TPU v7x, 32 devices: a whole 2x2x4 slice. The times are simulated.
32 devices in a mesh: gx: 2 (over y), gy: 4 (over z), gz: 4 (over x, core).
Axes of the slice: x: 2, y: 2, z: 4, core: 2. Of those that a mesh axis runs over, the one named last changes fastest.
Arguments:
- features: bfloat16 [64, 2, 4, 8192], P(None, 'gx', 'gy', 'gz'), may hold values from -6 to 6
- tiles: bfloat16 [2, 4, 128, 64, 512], P('gx', 'gy', 'gz'), may hold values from -0.25 to 0.25
- scales: float32 [2, 4, 128, 8], P('gx', 'gy', 'gz'), may hold values from 0.5 to 2
- slots: int32 [2, 4, 128, 8], P('gx', 'gy', 'gz'), may hold values from 0 to 175, as said below
- live: int32 [2, 4, 128], P('gx', 'gy', 'gz'), may hold values from 2 to 8, as said below
- times: float32 [64], replicated, may hold values from 0.6 to 1.6
Outputs:
- diffused: bfloat16 [64, 2, 4, 8192], P(None, 'gx', 'gy', 'gz')
Inputs may be any that keep to these rules, and one draw needn't show every extreme that they name: Slot 0 of every block row is the row's own block; slots 1 to 3 hold blocks of the row's own device, the others blocks from the shared set. `live`: each device has some block row with all 8 slots used.
All inputs are finite; a program needn't handle non-finite values.
Results may differ from a plain program's by a relative error of at most 0.0032.
Values may be sent and summed in bfloat16 or wider, within the bound.
No kernel may reach another device: no remote copies, remote signals or barrier semaphores. Data moves between devices by JAX's collectives and lax.ppermute only.
A program may use at most 64 MiB of HBM per device.

v0:
```python
import jax
import jax.numpy as jnp
from jax import lax
from jax.sharding import PartitionSpec as P

PB = 64
TERMS = 3


def with_halo(cells, sides, width):
    for axis, dim in sides:
        count = lax.axis_size(axis)
        ends = count - 1
        head = lax.slice_in_dim(cells, 0, width, axis=dim)
        tail = lax.slice_in_dim(cells, cells.shape[dim] - width, cells.shape[dim], axis=dim)
        cells = jnp.concatenate(
            [
                lax.ppermute(tail, axis, [(i, (i + 1) % count) for i in range(ends)]),
                cells,
                lax.ppermute(head, axis, [((i + 1) % count, i) for i in range(ends)]),
            ],
            axis=dim,
        )
    return cells


def to_blocks(value):
    count = value.shape[3] // PB
    return (
        value.reshape(value.shape[0], count, PB)
        .transpose(1, 0, 2)
        .reshape(count, value.shape[0] * PB)
    )


def shared_blocks(rim_rows):
    width = rim_rows.shape[1]
    panel = lax.all_gather(rim_rows, "gz", axis=0, tiled=True)
    grid = with_halo(panel.reshape(1, 1, panel.shape[0], width), (("gx", 0), ("gy", 1)), 1)
    return grid.reshape(-1, width)


def apply_operator(value, tile_rows, scale_rows, slot_rows, live_rows):
    blocks = to_blocks(value)
    count = blocks.shape[0]
    slot_count = slot_rows.shape[1]
    rim_count = max(1, count // 8)
    source = jnp.concatenate([blocks, shared_blocks(blocks[:rim_count])], 0)
    picked = jnp.take(source, slot_rows.reshape(-1), axis=0).reshape(
        count, slot_count, value.shape[0], PB
    )
    tile_parts = tile_rows.reshape(count, PB, slot_count, PB)
    used = (lax.broadcasted_iota(jnp.int32, (count, slot_count), 1) < live_rows[:, None]).astype(
        jnp.float32
    )
    weights = scale_rows * used
    result = jnp.zeros((count, value.shape[0], PB), jnp.float32)
    for slot in range(slot_count):
        partial_rows = jnp.einsum(
            "bfc,brc->bfr",
            picked[:, slot],
            tile_parts[:, :, slot],
            preferred_element_type=jnp.float32,
        )
        result = result + weights[:, slot][:, None, None] * partial_rows
    return result.transpose(1, 0, 2).reshape(value.shape[0], 1, 1, count * PB)


def body(features, tiles, scales, slots, live, times):
    count = tiles.shape[2]
    tile_rows = tiles.reshape(count, PB, tiles.shape[4])
    scale_rows = scales.reshape(count, scales.shape[3])
    slot_rows = slots.reshape(count, slots.shape[3])
    live_rows = live.reshape(count)
    total = features.astype(jnp.float32)
    factor = jnp.ones(times.shape, jnp.float32)
    value = features
    for term in range(1, TERMS + 1):
        image = apply_operator(value, tile_rows, scale_rows, slot_rows, live_rows)
        factor = factor * -times / jnp.float32(term)
        total = total + factor[:, None, None, None] * image
        value = image.astype(jnp.bfloat16)
    return total.astype(jnp.bfloat16)


def solution(mesh):
    return jax.shard_map(
        body,
        mesh=mesh,
        in_specs=(
            P(None, "gx", "gy", "gz"),
            P("gx", "gy", "gz", None, None),
            P("gx", "gy", "gz", None),
            P("gx", "gy", "gz", None),
            P("gx", "gy", "gz"),
            P(),
        ),
        out_specs=P(None, "gx", "gy", "gz"),
        check_vma=False,
    )
```

profile of v0, /device:TPU:0, one launch (start us, length us, event | category | flops | bytes accessed | tf_op | source)
XLA Modules:
  0.0 181.4 jit_solution(16395035376558209992)
XLA Ops:
  0.0 1.6 reshape.173
  2.0 6.5 %all-gather = bf16[4,4,4096]{2,1,0:T(4,128)(2,1)S(1)} all-gather(bf16[1,4,4096]{2,1,0:T(4,128)(2,1)S(1)} %reshape.216), channel_id=1, replica_groups=mesh['gx'=2,'gy'=4,'gz'=4] {'gz'}, dimensions={0}, use_global_device_ids=true | all-gather | bytes 163840 | tf_op jit(solution)/shard_map/all_gather | solution.py:38
  8.5 3.8 %collective-permute-start = (bf16[1,1,16,4096]{3,2,1,0:T(8,128)(2,1)S(1)}, bf16[1,1,16,4096]{3,2,1,0:T(8,128)(2,1)S(1)}, u32[]{:S(2)}, u32[]{:S(2)}) collective-permute-start(bf16[1,1,16,4096]{3,2,1,0:T(8,128)(2,1)S(1)} %reshape.175), channel_id=1, source_target_pairs={{0,16},{1,17},{2,18},{3,19},{4,20},{5,21},{6,22},{7,23},{8,24},{9,... | collective-permute-start | bytes 393224 | tf_op jit(solution)/shard_map/ppermute | solution.py:18
  12.3 1.3 collective-permute-start.1
  13.6 0.8 copy.45
  14.5 3.7 %reshape_reshape.5 = bf16[32,64,8,64]{3,2,1,0:T(8,128)(2,1)} reshape(bf16[1,1,32,64,512]{4,3,2,1,0:T(8,128)(2,1)S(1)} %copy-done.29) | data formatting | bytes 4194304 | tf_op jit(solution)/shard_map/reshape;reshape | solution.py:52
  18.1 23.5 %fusion.22 = (bf16[32,64,1,64]{3,2,1,0:T(2,128)(2,1)}, bf16[32,64,1,64]{3,2,1,0:T(2,128)(2,1)}, bf16[32,64,1,64]{3,2,1,0:T(2,128)(2,1)}, bf16[32,64,1,64]{3,2,1,...) fusion(bf16[32,64,8,64]{3,2,1,0:T(8,128)(2,1)} %reshape_reshape.5), kind=kLoop, calls=%fused_computation.116 | loop fusion | bytes 4194304 | tf_op jit(solution)/shard_map/slice | solution.py:62
  41.7 0.5 reshape.174
  42.2 3.5 %collective-permute-start.2 = (bf16[3,1,16,4096]{3,2,1,0:T(8,128)(2,1)S(1)}, bf16[3,1,16,4096]{3,2,1,0:T(8,128)(2,1)S(1)}, u32[]{:S(2)}, u32[]{:S(2)}) collective-permute-start(bf16[3,1,16,4096]{3,2,1,0:T(8,128)(2,1)S(1)} %constant_dynamic-update-slice_fusion), channel_id=1, source_target_pairs={{0,4},{4,8},{8,12},{1,5},{5,9},{9,13},{2,6},{6,10},{10,14},{3,7},{... | collective-permute-start | bytes 1179656 | tf_op jit(solution)/shard_map/ppermute | solution.py:18
  45.7 1.3 collective-permute-start.3
  47.0 0.5 compare_and_fusion
  47.6 0.6 slice_bitcast_fusion.48
  48.2 6.1 %collective-permute-done.2 = bf16[3,1,16,4096]{3,2,1,0:T(8,128)(2,1)S(1)} collective-permute-done((bf16[3,1,16,4096]{3,2,1,0:T(8,128)(2,1)S(1)}, bf16[3,1,16,4096]{3,2,1,0:T(8,128)(2,1)S(1)}, u32[]{:S(2)}, u32[]{:S(2)}) %collective-permute-start.2) | collective-permute-done | bytes 393248 | tf_op jit(solution)/shard_map/ppermute | solution.py:18
  54.3 4.1 %collective-permute-done.3 = bf16[3,1,16,4096]{3,2,1,0:T(8,128)(2,1)S(1)} collective-permute-done((bf16[3,1,16,4096]{3,2,1,0:T(8,128)(2,1)S(1)}, bf16[3,1,16,4096]{3,2,1,0:T(8,128)(2,1)S(1)}, u32[]{:S(2)}, u32[]{:S(2)}) %collective-permute-start.3) | collective-permute-done | bytes 393248 | tf_op jit(solution)/shard_map/ppermute | solution.py:20
  58.7 1.8 %gather_fusion = bf16[256,4096]{1,0:T(8,128)(2,1)S(1)} fusion(bf16[176,4096]{1,0:T(8,128)(2,1)S(1)} %pad_maximum_fusion, s32[1024]{0:T(1024)S(1)} %pad_clamp_fusion), kind=kCustom, calls=%fused_computation.clone | custom fusion | bytes 4195328 | tf_op jit(solution)/shard_map/jit(_take)/gather | solution.py:49
  60.6 2.3 %broadcast_select_fusion.2 = bf16[256,4096]{1,0:T(8,128)(2,1)} fusion(bf16[256,4096]{1,0:T(8,128)(2,1)S(1)} %gather_fusion, pred[256]{0:T(512)(128)(4,1)} %compare_and_fusion), kind=kLoop, calls=%fused_computation.5 | loop fusion | flops 1048576 | bytes 4194560 | tf_op jit(solution)/shard_map/jit(_take)/select_n | solution.py:49
  62.9 7.0 %reshape.177 = bf16[32,8,64,64]{3,2,1,0:T(8,128)(2,1)} reshape(bf16[256,4096]{1,0:T(8,128)(2,1)} %broadcast_select_fusion.2) | data formatting | bytes 4194304 | tf_op jit(solution)/shard_map/reshape | solution.py:49
  69.9 1.6 convolution_multiply_fusion.23
  71.6 1.6 fusion.21
  73.2 0.4 fusion.20
  76.2 1.4 fusion.24
  77.7 5.4 %all-gather.1 = bf16[4,4,4096]{2,1,0:T(4,128)(2,1)S(1)} all-gather(bf16[1,4,4096]{2,1,0:T(4,128)(2,1)S(1)} %reshape.218), channel_id=1, replica_groups=mesh['gx'=2,'gy'=4,'gz'=4] {'gz'}, dimensions={0}, use_global_device_ids=true | all-gather | bytes 163840 | tf_op jit(solution)/shard_map/all_gather | solution.py:38
  83.2 4.3 %collective-permute-start.4 = (bf16[1,1,16,4096]{3,2,1,0:T(8,128)(2,1)S(1)}, bf16[1,1,16,4096]{3,2,1,0:T(8,128)(2,1)S(1)}, u32[]{:S(2)}, u32[]{:S(2)}) collective-permute-start(bf16[1,1,16,4096]{3,2,1,0:T(8,128)(2,1)S(1)} %reshape.180), channel_id=1, source_target_pairs={{0,16},{1,17},{2,18},{3,19},{4,20},{5,21},{6,22},{7,23},{8,24},{9,... | collective-permute-start | bytes 393224 | tf_op jit(solution)/shard_map/ppermute | solution.py:18
  87.5 1.3 collective-permute-start.5
  88.8 1.9 %collective-permute-done.4 = bf16[1,1,16,4096]{3,2,1,0:T(8,128)(2,1)S(1)} collective-permute-done((bf16[1,1,16,4096]{3,2,1,0:T(8,128)(2,1)S(1)}, bf16[1,1,16,4096]{3,2,1,0:T(8,128)(2,1)S(1)}, u32[]{:S(2)}, u32[]{:S(2)}) %collective-permute-start.4) | collective-permute-done | bytes 131104 | tf_op jit(solution)/shard_map/ppermute | solution.py:18
  90.8 4.1 %collective-permute-done.5 = bf16[1,1,16,4096]{3,2,1,0:T(8,128)(2,1)S(1)} collective-permute-done((bf16[1,1,16,4096]{3,2,1,0:T(8,128)(2,1)S(1)}, bf16[1,1,16,4096]{3,2,1,0:T(8,128)(2,1)S(1)}, u32[]{:S(2)}, u32[]{:S(2)}) %collective-permute-start.5) | collective-permute-done | bytes 131104 | tf_op jit(solution)/shard_map/ppermute | solution.py:20
  94.9 3.5 %collective-permute-start.6 = (bf16[3,1,16,4096]{3,2,1,0:T(8,128)(2,1)S(1)}, bf16[3,1,16,4096]{3,2,1,0:T(8,128)(2,1)S(1)}, u32[]{:S(2)}, u32[]{:S(2)}) collective-permute-start(bf16[3,1,16,4096]{3,2,1,0:T(8,128)(2,1)S(1)} %constant_dynamic-update-slice_fusion.3), channel_id=1, source_target_pairs={{0,4},{4,8},{8,12},{1,5},{5,9},{9,13},{2,6},{6,10},{10,14},{3,7},{... | collective-permute-start | bytes 1179656 | tf_op jit(solution)/shard_map/ppermute | solution.py:18
  98.4 1.5 collective-permute-start.7
  99.8 0.5 reshape.179
  100.3 5.8 %collective-permute-done.6 = bf16[3,1,16,4096]{3,2,1,0:T(8,128)(2,1)S(1)} collective-permute-done((bf16[3,1,16,4096]{3,2,1,0:T(8,128)(2,1)S(1)}, bf16[3,1,16,4096]{3,2,1,0:T(8,128)(2,1)S(1)}, u32[]{:S(2)}, u32[]{:S(2)}) %collective-permute-start.6) | collective-permute-done | bytes 393248 | tf_op jit(solution)/shard_map/ppermute | solution.py:18
  106.1 4.1 %collective-permute-done.7 = bf16[3,1,16,4096]{3,2,1,0:T(8,128)(2,1)S(1)} collective-permute-done((bf16[3,1,16,4096]{3,2,1,0:T(8,128)(2,1)S(1)}, bf16[3,1,16,4096]{3,2,1,0:T(8,128)(2,1)S(1)}, u32[]{:S(2)}, u32[]{:S(2)}) %collective-permute-start.7) | collective-permute-done | bytes 393248 | tf_op jit(solution)/shard_map/ppermute | solution.py:20
  110.5 1.8 %gather_fusion.1 = bf16[256,4096]{1,0:T(8,128)(2,1)S(1)} fusion(bf16[176,4096]{1,0:T(8,128)(2,1)S(1)} %pad_maximum_fusion.1, s32[1024]{0:T(1024)S(1)} %pad_clamp_fusion), kind=kCustom, calls=%fused_computation.1.clone | custom fusion | bytes 4195328 | tf_op jit(solution)/shard_map/jit(_take)/gather | solution.py:49
  112.3 2.3 %broadcast_select_fusion.1 = bf16[256,4096]{1,0:T(8,128)(2,1)} fusion(bf16[256,4096]{1,0:T(8,128)(2,1)S(1)} %gather_fusion.1, pred[256]{0:T(512)(128)(4,1)} %compare_and_fusion), kind=kLoop, calls=%fused_computation.4 | loop fusion | flops 1048576 | bytes 4194560 | tf_op jit(solution)/shard_map/jit(_take)/select_n | solution.py:49
  114.6 7.0 %reshape.182 = bf16[32,8,64,64]{3,2,1,0:T(8,128)(2,1)} reshape(bf16[256,4096]{1,0:T(8,128)(2,1)} %broadcast_select_fusion.1) | data formatting | bytes 4194304 | tf_op jit(solution)/shard_map/reshape | solution.py:49
  121.7 1.6 convolution_multiply_fusion.15
  123.3 1.6 fusion.14
  125.4 0.4 fusion.12
  128.0 0.4 fusion.25
  128.4 0.8 copy-done.28
  129.3 5.4 %all-gather.2 = bf16[4,4,4096]{2,1,0:T(4,128)(2,1)S(1)} all-gather(bf16[1,4,4096]{2,1,0:T(4,128)(2,1)S(1)} %reshape.220), channel_id=1, replica_groups=mesh['gx'=2,'gy'=4,'gz'=4] {'gz'}, dimensions={0}, use_global_device_ids=true | all-gather | bytes 163840 | tf_op jit(solution)/shard_map/all_gather | solution.py:38
  134.8 1.5 collective-permute-start.8
  136.3 1.3 collective-permute-start.9
  137.6 2.1 %collective-permute-done.8 = bf16[1,1,16,4096]{3,2,1,0:T(8,128)(2,1)S(1)} collective-permute-done((bf16[1,1,16,4096]{3,2,1,0:T(8,128)(2,1)S(1)}, bf16[1,1,16,4096]{3,2,1,0:T(8,128)(2,1)S(1)}, u32[]{:S(2)}, u32[]{:S(2)}) %collective-permute-start.8) | collective-permute-done | bytes 131104 | tf_op jit(solution)/shard_map/ppermute | solution.py:18
  139.7 4.1 %collective-permute-done.9 = bf16[1,1,16,4096]{3,2,1,0:T(8,128)(2,1)S(1)} collective-permute-done((bf16[1,1,16,4096]{3,2,1,0:T(8,128)(2,1)S(1)}, bf16[1,1,16,4096]{3,2,1,0:T(8,128)(2,1)S(1)}, u32[]{:S(2)}, u32[]{:S(2)}) %collective-permute-start.9) | collective-permute-done | bytes 131104 | tf_op jit(solution)/shard_map/ppermute | solution.py:20
  143.8 4.2 %collective-permute-start.10 = (bf16[3,1,16,4096]{3,2,1,0:T(8,128)(2,1)S(1)}, bf16[3,1,16,4096]{3,2,1,0:T(8,128)(2,1)}, u32[]{:S(2)}, u32[]{:S(2)}) collective-permute-start(bf16[3,1,16,4096]{3,2,1,0:T(8,128)(2,1)S(1)} %constant_dynamic-update-slice_fusion.6), channel_id=1, source_target_pairs={{0,4},{4,8},{8,12},{1,5},{5,9},{9,13},{2,6},{6,10},{10,14},{3,7},{... | collective-permute-start | bytes 1179656 | tf_op jit(solution)/shard_map/ppermute | solution.py:18
  148.0 1.5 collective-permute-start.11
  149.5 0.6 fusion.23
  150.1 0.6 copy.63
  150.7 1.2 reshape.178
  151.9 1.5 reshape.184
  153.4 0.6 copy.72
  154.0 1.2 reshape.183
  155.2 4.9 %collective-permute-done.11 = bf16[3,1,16,4096]{3,2,1,0:T(8,128)(2,1)} collective-permute-done((bf16[3,1,16,4096]{3,2,1,0:T(8,128)(2,1)S(1)}, bf16[3,1,16,4096]{3,2,1,0:T(8,128)(2,1)}, u32[]{:S(2)}, u32[]{:S(2)}) %collective-permute-start.11) | collective-permute-done | bytes 393248 | tf_op jit(solution)/shard_map/ppermute | solution.py:20
  160.1 1.2 pad_maximum_fusion.5
  161.5 1.8 %gather_fusion.2 = bf16[256,4096]{1,0:T(8,128)(2,1)S(1)} fusion(bf16[176,4096]{1,0:T(8,128)(2,1)S(1)} %pad_maximum_fusion.2, s32[1024]{0:T(1024)S(1)} %pad_clamp_fusion), kind=kCustom, calls=%fused_computation.2.clone | custom fusion | bytes 4195328 | tf_op jit(solution)/shard_map/jit(_take)/gather | solution.py:49
  163.3 2.3 %broadcast_select_fusion = bf16[256,4096]{1,0:T(8,128)(2,1)} fusion(bf16[256,4096]{1,0:T(8,128)(2,1)S(1)} %gather_fusion.2, pred[256]{0:T(512)(128)(4,1)} %compare_and_fusion), kind=kLoop, calls=%fused_computation.3 | loop fusion | flops 1048576 | bytes 4194560 | tf_op jit(solution)/shard_map/jit(_take)/select_n | solution.py:49
  165.6 7.0 %reshape.187 = bf16[32,8,64,64]{3,2,1,0:T(8,128)(2,1)} reshape(bf16[256,4096]{1,0:T(8,128)(2,1)} %broadcast_select_fusion) | data formatting | bytes 4194304 | tf_op jit(solution)/shard_map/reshape | solution.py:49
  172.7 1.6 convolution_multiply_fusion.7
  174.3 1.6 fusion.7
  176.0 0.4 fusion.6
  176.4 0.4 fusion.5
  179.0 0.4 fusion.1
  179.5 0.6 copy.81
  180.5 0.9 add_convert_fusion
  (150 shorter events, 9.3 us)
Async XLA Ops:
  0.0 14.5 %copy-start.29 = (bf16[1,1,32,64,512]{4,3,2,1,0:T(8,128)(2,1)S(1)}, bf16[1,1,32,64,512]{4,3,2,1,0:T(8,128)(2,1)}, u32[]{:S(2)}) copy-start(bf16[1,1,32,64,512]{4,3,2,1,0:T(8,128)(2,1)} %param.9) | copy-start | bytes 6291460
  8.5 33.7 %collective-permute-start = (bf16[1,1,16,4096]{3,2,1,0:T(8,128)(2,1)S(1)}, bf16[1,1,16,4096]{3,2,1,0:T(8,128)(2,1)S(1)}, u32[]{:S(2)}, u32[]{:S(2)}) collective-permute-start(bf16[1,1,16,4096]{3,2,1,0:T(8,128)(2,1)S(1)} %reshape.175), channel_id=1, source_target_pairs={{0,16},{1,17},{2,18},{3,19},{4,20},{5,21},{6,22},{7,23},{8,24},{9,... | collective-permute-start | bytes 393224 | tf_op jit(solution)/shard_map/ppermute | solution.py:18
  12.3 29.9 %collective-permute-start.1 = (bf16[1,1,16,4096]{3,2,1,0:T(8,128)(2,1)S(1)}, bf16[1,1,16,4096]{3,2,1,0:T(8,128)(2,1)S(1)}, u32[]{:S(2)}, u32[]{:S(2)}) collective-permute-start(bf16[1,1,16,4096]{3,2,1,0:T(8,128)(2,1)S(1)} %reshape.175), channel_id=1, source_target_pairs={{16,0},{17,1},{18,2},{19,3},{20,4},{21,5},{22,6},{23,7},{24,8},{25... | collective-permute-start | bytes 393224 | tf_op jit(solution)/shard_map/ppermute | solution.py:20
  18.1 23.5 %copy-start.48 = (f32[1,1,32,8]{2,3,1,0:T(8,128)S(1)}, f32[1,1,32,8]{2,3,1,0:T(8,128)}, u32[]{:S(2)}) copy-start(f32[1,1,32,8]{2,3,1,0:T(8,128)} %param.10) | copy-start | bytes 3076
  18.1 23.5 %copy-start.52 = (s32[1,1,32]{2,1,0:T(1,128)S(1)}, s32[1,1,32]{2,1,0:T(1,128)}, u32[]{:S(2)}) copy-start(s32[1,1,32]{2,1,0:T(1,128)} %param.12) | copy-start | bytes 388
  42.2 12.1 %collective-permute-start.2 = (bf16[3,1,16,4096]{3,2,1,0:T(8,128)(2,1)S(1)}, bf16[3,1,16,4096]{3,2,1,0:T(8,128)(2,1)S(1)}, u32[]{:S(2)}, u32[]{:S(2)}) collective-permute-start(bf16[3,1,16,4096]{3,2,1,0:T(8,128)(2,1)S(1)} %constant_dynamic-update-slice_fusion), channel_id=1, source_target_pairs={{0,4},{4,8},{8,12},{1,5},{5,9},{9,13},{2,6},{6,10},{10,14},{3,7},{... | collective-permute-start | bytes 1179656 | tf_op jit(solution)/shard_map/ppermute | solution.py:18
  45.7 12.7 %collective-permute-start.3 = (bf16[3,1,16,4096]{3,2,1,0:T(8,128)(2,1)S(1)}, bf16[3,1,16,4096]{3,2,1,0:T(8,128)(2,1)S(1)}, u32[]{:S(2)}, u32[]{:S(2)}) collective-permute-start(bf16[3,1,16,4096]{3,2,1,0:T(8,128)(2,1)S(1)} %constant_dynamic-update-slice_fusion), channel_id=1, source_target_pairs={{4,0},{8,4},{12,8},{5,1},{9,5},{13,9},{6,2},{10,6},{14,10},{7,3},{... | collective-permute-start | bytes 1179656 | tf_op jit(solution)/shard_map/ppermute | solution.py:20
  62.8 7.1 %copy-start.3 = (bf16[32,64,1,64]{3,2,1,0:T(2,128)(2,1)S(1)}, bf16[32,64,1,64]{3,2,1,0:T(2,128)(2,1)}, u32[]{:S(2)}) copy-start(bf16[32,64,1,64]{3,2,1,0:T(2,128)(2,1)} %get-tuple-element.13) | copy-start | bytes 786436
  62.8 8.7 %copy-start.24 = (bf16[32,64,1,64]{3,2,1,0:T(2,128)(2,1)S(1)}, bf16[32,64,1,64]{3,2,1,0:T(2,128)(2,1)}, u32[]{:S(2)}) copy-start(bf16[32,64,1,64]{3,2,1,0:T(2,128)(2,1)} %get-tuple-element.12) | copy-start | bytes 786436
  62.9 8.7 %copy-start.42 = (f32[32]{0:T(128)S(1)}, f32[32]{0:T(128)}, u32[]{:S(2)}) copy-start(f32[32]{0:T(128)} %get-tuple-element.20) | copy-start | bytes 388
  69.9 3.2 %copy-start.1 = (bf16[32,8,64,64]{3,2,1,0:T(8,128)(2,1)S(1)}, bf16[32,8,64,64]{3,2,1,0:T(8,128)(2,1)}, u32[]{:S(2)}) copy-start(bf16[32,8,64,64]{3,2,1,0:T(8,128)(2,1)} %reshape.177) | copy-start | bytes 6291460
  69.9 3.2 %copy-start.21 = (bf16[32,64,1,64]{3,2,1,0:T(2,128)(2,1)S(1)}, bf16[32,64,1,64]{3,2,1,0:T(2,128)(2,1)}, u32[]{:S(2)}) copy-start(bf16[32,64,1,64]{3,2,1,0:T(2,128)(2,1)} %get-tuple-element.11) | copy-start | bytes 786436
  69.9 3.3 %copy-start.39 = (f32[32]{0:T(128)S(1)}, f32[32]{0:T(128)}, u32[]{:S(2)}) copy-start(f32[32]{0:T(128)} %get-tuple-element.19) | copy-start | bytes 388
  71.5 2.1 %copy-start.18 = (bf16[32,64,1,64]{3,2,1,0:T(2,128)(2,1)S(1)}, bf16[32,64,1,64]{3,2,1,0:T(2,128)(2,1)}, u32[]{:S(2)}) copy-start(bf16[32,64,1,64]{3,2,1,0:T(2,128)(2,1)} %get-tuple-element.10) | copy-start | bytes 786436
  71.5 2.1 %copy-start.36 = (f32[32]{0:T(128)S(1)}, f32[32]{0:T(128)}, u32[]{:S(2)}) copy-start(f32[32]{0:T(128)} %get-tuple-element.18) | copy-start | bytes 388
  73.2 1.2 copy-start.15
  73.2 1.2 copy-start.33
  73.6 1.3 copy-start.12
  74.4 1.3 copy-start.9
  74.9 1.3 copy-start.6
  74.9 1.3 copy-start.45
  83.2 7.5 %collective-permute-start.4 = (bf16[1,1,16,4096]{3,2,1,0:T(8,128)(2,1)S(1)}, bf16[1,1,16,4096]{3,2,1,0:T(8,128)(2,1)S(1)}, u32[]{:S(2)}, u32[]{:S(2)}) collective-permute-start(bf16[1,1,16,4096]{3,2,1,0:T(8,128)(2,1)S(1)} %reshape.180), channel_id=1, source_target_pairs={{0,16},{1,17},{2,18},{3,19},{4,20},{5,21},{6,22},{7,23},{8,24},{9,... | collective-permute-start | bytes 393224 | tf_op jit(solution)/shard_map/ppermute | solution.py:18
  87.5 7.4 %collective-permute-start.5 = (bf16[1,1,16,4096]{3,2,1,0:T(8,128)(2,1)S(1)}, bf16[1,1,16,4096]{3,2,1,0:T(8,128)(2,1)S(1)}, u32[]{:S(2)}, u32[]{:S(2)}) collective-permute-start(bf16[1,1,16,4096]{3,2,1,0:T(8,128)(2,1)S(1)} %reshape.180), channel_id=1, source_target_pairs={{16,0},{17,1},{18,2},{19,3},{20,4},{21,5},{22,6},{23,7},{24,8},{25... | collective-permute-start | bytes 393224 | tf_op jit(solution)/shard_map/ppermute | solution.py:20
  94.9 11.2 %collective-permute-start.6 = (bf16[3,1,16,4096]{3,2,1,0:T(8,128)(2,1)S(1)}, bf16[3,1,16,4096]{3,2,1,0:T(8,128)(2,1)S(1)}, u32[]{:S(2)}, u32[]{:S(2)}) collective-permute-start(bf16[3,1,16,4096]{3,2,1,0:T(8,128)(2,1)S(1)} %constant_dynamic-update-slice_fusion.3), channel_id=1, source_target_pairs={{0,4},{4,8},{8,12},{1,5},{5,9},{9,13},{2,6},{6,10},{10,14},{3,7},{... | collective-permute-start | bytes 1179656 | tf_op jit(solution)/shard_map/ppermute | solution.py:18
  98.4 11.9 %collective-permute-start.7 = (bf16[3,1,16,4096]{3,2,1,0:T(8,128)(2,1)S(1)}, bf16[3,1,16,4096]{3,2,1,0:T(8,128)(2,1)S(1)}, u32[]{:S(2)}, u32[]{:S(2)}) collective-permute-start(bf16[3,1,16,4096]{3,2,1,0:T(8,128)(2,1)S(1)} %constant_dynamic-update-slice_fusion.3), channel_id=1, source_target_pairs={{4,0},{8,4},{12,8},{5,1},{9,5},{13,9},{6,2},{10,6},{14,10},{7,3},{... | collective-permute-start | bytes 1179656 | tf_op jit(solution)/shard_map/ppermute | solution.py:20
  114.6 7.1 %copy-start.4 = (bf16[32,64,1,64]{3,2,1,0:T(2,128)(2,1)S(1)}, bf16[32,64,1,64]{3,2,1,0:T(2,128)(2,1)}, u32[]{:S(2)}) copy-start(bf16[32,64,1,64]{3,2,1,0:T(2,128)(2,1)} %get-tuple-element.13) | copy-start | bytes 786436
  114.6 8.7 %copy-start.25 = (bf16[32,64,1,64]{3,2,1,0:T(2,128)(2,1)S(1)}, bf16[32,64,1,64]{3,2,1,0:T(2,128)(2,1)}, u32[]{:S(2)}) copy-start(bf16[32,64,1,64]{3,2,1,0:T(2,128)(2,1)} %get-tuple-element.12) | copy-start | bytes 786436
  114.6 8.7 %copy-start.43 = (f32[32]{0:T(128)S(1)}, f32[32]{0:T(128)}, u32[]{:S(2)}) copy-start(f32[32]{0:T(128)} %get-tuple-element.20) | copy-start | bytes 388
  121.7 3.2 %copy-start.2 = (bf16[32,8,64,64]{3,2,1,0:T(8,128)(2,1)S(1)}, bf16[32,8,64,64]{3,2,1,0:T(8,128)(2,1)}, u32[]{:S(2)}) copy-start(bf16[32,8,64,64]{3,2,1,0:T(8,128)(2,1)} %reshape.182) | copy-start | bytes 6291460
  121.7 3.2 %copy-start.22 = (bf16[32,64,1,64]{3,2,1,0:T(2,128)(2,1)S(1)}, bf16[32,64,1,64]{3,2,1,0:T(2,128)(2,1)}, u32[]{:S(2)}) copy-start(bf16[32,64,1,64]{3,2,1,0:T(2,128)(2,1)} %get-tuple-element.11) | copy-start | bytes 786436
  121.7 3.3 %copy-start.40 = (f32[32]{0:T(128)S(1)}, f32[32]{0:T(128)}, u32[]{:S(2)}) copy-start(f32[32]{0:T(128)} %get-tuple-element.19) | copy-start | bytes 388
  123.3 2.1 %copy-start.19 = (bf16[32,64,1,64]{3,2,1,0:T(2,128)(2,1)S(1)}, bf16[32,64,1,64]{3,2,1,0:T(2,128)(2,1)}, u32[]{:S(2)}) copy-start(bf16[32,64,1,64]{3,2,1,0:T(2,128)(2,1)} %get-tuple-element.10) | copy-start | bytes 786436
  123.3 2.1 %copy-start.37 = (f32[32]{0:T(128)S(1)}, f32[32]{0:T(128)}, u32[]{:S(2)}) copy-start(f32[32]{0:T(128)} %get-tuple-element.18) | copy-start | bytes 388
  124.9 1.2 copy-start.16
  125.4 1.3 copy-start.13
  126.2 1.3 copy-start.10
  126.7 1.3 copy-start.7
  126.7 1.3 copy-start.46
  128.0 21.5 %copy-start.53 = (f32[64]{0:T(128)S(1)}, f32[64]{0:T(128)}, u32[]{:S(2)}) copy-start(f32[64]{0:T(128)} %param.13) | copy-start | bytes 772
  128.0 22.1 %copy-start.27 = (f32[32,64,64]{2,1,0:T(8,128)S(1)}, f32[32,64,64]{2,1,0:T(8,128)}, u32[]{:S(2)}) copy-start(f32[32,64,64]{2,1,0:T(8,128)} %get-tuple-element.26) | copy-start | bytes 1572868
  134.8 4.8 %collective-permute-start.8 = (bf16[1,1,16,4096]{3,2,1,0:T(8,128)(2,1)S(1)}, bf16[1,1,16,4096]{3,2,1,0:T(8,128)(2,1)S(1)}, u32[]{:S(2)}, u32[]{:S(2)}) collective-permute-start(bf16[1,1,16,4096]{3,2,1,0:T(8,128)(2,1)S(1)} %reshape.185), channel_id=1, source_target_pairs={{0,16},{1,17},{2,18},{3,19},{4,20},{5,21},{6,22},{7,23},{8,24},{9,... | collective-permute-start | bytes 393224 | tf_op jit(solution)/shard_map/ppermute | solution.py:18
  136.3 7.5 %collective-permute-start.9 = (bf16[1,1,16,4096]{3,2,1,0:T(8,128)(2,1)S(1)}, bf16[1,1,16,4096]{3,2,1,0:T(8,128)(2,1)S(1)}, u32[]{:S(2)}, u32[]{:S(2)}) collective-permute-start(bf16[1,1,16,4096]{3,2,1,0:T(8,128)(2,1)S(1)} %reshape.185), channel_id=1, source_target_pairs={{16,0},{17,1},{18,2},{19,3},{20,4},{21,5},{22,6},{23,7},{24,8},{25... | collective-permute-start | bytes 393224 | tf_op jit(solution)/shard_map/ppermute | solution.py:20
  143.8 11.4 %collective-permute-start.10 = (bf16[3,1,16,4096]{3,2,1,0:T(8,128)(2,1)S(1)}, bf16[3,1,16,4096]{3,2,1,0:T(8,128)(2,1)}, u32[]{:S(2)}, u32[]{:S(2)}) collective-permute-start(bf16[3,1,16,4096]{3,2,1,0:T(8,128)(2,1)S(1)} %constant_dynamic-update-slice_fusion.6), channel_id=1, source_target_pairs={{0,4},{4,8},{8,12},{1,5},{5,9},{9,13},{2,6},{6,10},{10,14},{3,7},{... | collective-permute-start | bytes 1179656 | tf_op jit(solution)/shard_map/ppermute | solution.py:18
  148.0 12.1 %collective-permute-start.11 = (bf16[3,1,16,4096]{3,2,1,0:T(8,128)(2,1)S(1)}, bf16[3,1,16,4096]{3,2,1,0:T(8,128)(2,1)}, u32[]{:S(2)}, u32[]{:S(2)}) collective-permute-start(bf16[3,1,16,4096]{3,2,1,0:T(8,128)(2,1)S(1)} %constant_dynamic-update-slice_fusion.6), channel_id=1, source_target_pairs={{4,0},{8,4},{12,8},{5,1},{9,5},{13,9},{6,2},{10,6},{14,10},{7,3},{... | collective-permute-start | bytes 1179656 | tf_op jit(solution)/shard_map/ppermute | solution.py:20
  165.6 7.1 %copy-start.5 = (bf16[32,64,1,64]{3,2,1,0:T(2,128)(2,1)S(1)}, bf16[32,64,1,64]{3,2,1,0:T(2,128)(2,1)}, u32[]{:S(2)}) copy-start(bf16[32,64,1,64]{3,2,1,0:T(2,128)(2,1)} %get-tuple-element.13) | copy-start | bytes 786436
  165.6 8.7 %copy-start.26 = (bf16[32,64,1,64]{3,2,1,0:T(2,128)(2,1)S(1)}, bf16[32,64,1,64]{3,2,1,0:T(2,128)(2,1)}, u32[]{:S(2)}) copy-start(bf16[32,64,1,64]{3,2,1,0:T(2,128)(2,1)} %get-tuple-element.12) | copy-start | bytes 786436
  165.6 8.7 %copy-start.44 = (f32[32]{0:T(128)S(1)}, f32[32]{0:T(128)}, u32[]{:S(2)}) copy-start(f32[32]{0:T(128)} %get-tuple-element.20) | copy-start | bytes 388
  172.7 3.2 %copy-start = (bf16[32,8,64,64]{3,2,1,0:T(8,128)(2,1)S(1)}, bf16[32,8,64,64]{3,2,1,0:T(8,128)(2,1)}, u32[]{:S(2)}) copy-start(bf16[32,8,64,64]{3,2,1,0:T(8,128)(2,1)} %reshape.187) | copy-start | bytes 6291460
  172.7 3.2 %copy-start.23 = (bf16[32,64,1,64]{3,2,1,0:T(2,128)(2,1)S(1)}, bf16[32,64,1,64]{3,2,1,0:T(2,128)(2,1)}, u32[]{:S(2)}) copy-start(bf16[32,64,1,64]{3,2,1,0:T(2,128)(2,1)} %get-tuple-element.11) | copy-start | bytes 786436
  172.7 3.3 %copy-start.41 = (f32[32]{0:T(128)S(1)}, f32[32]{0:T(128)}, u32[]{:S(2)}) copy-start(f32[32]{0:T(128)} %get-tuple-element.19) | copy-start | bytes 388
  174.3 2.1 %copy-start.20 = (bf16[32,64,1,64]{3,2,1,0:T(2,128)(2,1)S(1)}, bf16[32,64,1,64]{3,2,1,0:T(2,128)(2,1)}, u32[]{:S(2)}) copy-start(bf16[32,64,1,64]{3,2,1,0:T(2,128)(2,1)} %get-tuple-element.10) | copy-start | bytes 786436
  174.3 2.1 %copy-start.38 = (f32[32]{0:T(128)S(1)}, f32[32]{0:T(128)}, u32[]{:S(2)}) copy-start(f32[32]{0:T(128)} %get-tuple-element.18) | copy-start | bytes 388
  175.9 1.2 copy-start.17
  176.0 1.2 copy-start.35
  176.4 1.3 copy-start.14
  177.2 1.3 copy-start.11
  177.7 1.3 copy-start.8
  177.7 1.3 copy-start.47
  179.0 1.4 copy-start.30
  179.0 1.4 copy-start.31
  179.0 1.4 copy-start.32
  179.0 1.4 copy-start.49
  179.0 1.4 copy-start.50
  179.0 1.4 copy-start.51
  (2 other events, 2.0 us)
where the time goes:
time: 182 us; the launch traced here: 181 us
  local copies, waits for them, and re-layouts  68.4 us (38%)
  waiting for transfers between devices  37.3 us (20%)
  starting transfers between devices  28.9 us (16%)
  matrix products  17.7 us (10%)
  blocking collectives  17.3 us (10%)
  other arithmetic  10.8 us (6%)
    slice x1, local copies, waits for them, and re-layouts, apply_operator(): tile_parts[:, :, slot]  23.5 us
    ppermute x6, waiting for transfers between devices, with_halo(): lax.ppermute(head, axis, [((i + 1) % count, i) for i in range(ends)])  21.4 us
    reshape x3, local copies, waits for them, and re-layouts, apply_operator(): jnp.take(source, slot_rows.reshape(-1), axis=0)  21.1 us
    ppermute x6, starting transfers between devices, with_halo(): lax.ppermute(tail, axis, [(i, (i + 1) % count) for i in range(ends)])  20.8 us
    dot_general x24, matrix products, apply_operator(): jnp.einsum('bfc,brc->bfr', picked[:, slot], tile_parts[:, :, slot], prefe...  17.7 us
    all_gather x3, blocking collectives, shared_blocks(): panel = lax.all_gather(rim_rows, 'gz', axis=0, tiled=True)  17.3 us
    ppermute x6, waiting for transfers between devices, with_halo(): lax.ppermute(tail, axis, [(i, (i + 1) % count) for i in range(ends)])  15.9 us
    ppermute x6, starting transfers between devices, with_halo(): lax.ppermute(head, axis, [((i + 1) % count, i) for i in range(ends)])  8.14 us
  transfers between devices with their start and end apart: 12, of which 9 were waited for; matrix products, arithmetic and copies ran while one was open for 20% of the time, Pallas kernels for 0%

commit v1 on v0

v1 whole, which is shorter than its diff:
```python
import functools

import jax
import jax.numpy as jnp
from jax import lax
from jax.experimental import pallas as pl
from jax.experimental.pallas import tpu as pltpu
from jax.sharding import PartitionSpec as P

PB = 64
TERMS = 3
LANES = 2 * PB


def pairings(count):
    first = [(i, i ^ 1) for i in range(count)]
    second = [(i, (i + 1) % count if i % 2 else (i - 1) % count) for i in range(count)]
    return [first] if count == 2 else [first, second]


def partner_rank(here, step, count):
    forward = jnp.where(here % 2 == 0, 1, 2)
    backward = 3 - forward
    rank = jnp.where(step == 1, 0, jnp.where(step == 2, forward, backward))
    there = here + step - 1
    return rank, (there >= 0) & (there < count)


def exchange(rim):
    rows = jnp.stack([rim] + [lax.ppermute(rim, "gy", p) for p in pairings(lax.axis_size("gy"))])
    if lax.axis_size("gx") == 2:
        both = lax.all_gather(rows, ("gx", "gz"), axis=0, tiled=False)
        return both
    grid = jnp.stack([rows] + [lax.ppermute(rows, "gx", p) for p in pairings(lax.axis_size("gx"))])
    return lax.all_gather(grid, "gz", axis=0, tiled=False)


def source_index(slots, count, rim_count):
    layers = lax.axis_size("gz")
    x_size, y_size = lax.axis_size("gx"), lax.axis_size("gy")
    x_at, y_at = lax.axis_index("gx"), lax.axis_index("gy")
    rest = jnp.maximum(slots - count, 0)
    r = rest % rim_count
    m = (rest // rim_count) % layers
    c = (rest // (rim_count * layers)) % 3
    a = rest // (rim_count * layers * 3)
    y_rank, y_in = partner_rank(y_at, c, y_size)
    y_count = len(pairings(y_size)) + 1
    if x_size == 2:
        x_there = x_at + a - 1
        x_in = (x_there >= 0) & (x_there < 2)
        panel = (x_there * layers + m) * y_count + y_rank
        panels = 2 * layers * y_count
    else:
        x_rank, x_in = partner_rank(x_at, a, x_size)
        x_count = len(pairings(x_size)) + 1
        panel = (m * x_count + x_rank) * y_count + y_rank
        panels = layers * x_count * y_count
    far = count + panel * rim_count + r
    zero = count + panels * rim_count
    index = jnp.where(slots < count, slots, jnp.where(x_in & y_in, far, zero))
    return index.astype(jnp.int32), panels


def term_kernel(index_ref, value_ref, far_ref, tile_ref, total_ref, factor_ref, *rest, last):
    if last:
        total_out, source = rest
    else:
        value_out, rim_out, total_out, source = rest
    features, points = value_ref.shape
    panels, _, rim = far_ref.shape
    count = points // PB
    slot_count = tile_ref.shape[1] // PB
    left = lax.broadcasted_iota(jnp.int32, (features, LANES), 1) < PB

    def spread(pair, at):
        turned = jnp.concatenate([pair[:, PB:], pair[:, :PB]], axis=1)
        source[at] = jnp.where(left, pair, turned)
        source[at + 1] = jnp.where(left, turned, pair)

    for t in range(points // LANES):
        spread(value_ref[:, t * LANES : (t + 1) * LANES], 2 * t)

    @pl.loop(0, panels)
    def _(panel):
        for t in range(rim // LANES):
            spread(
                far_ref[panel, :, t * LANES : (t + 1) * LANES],
                count + panel * (rim // PB) + 2 * t,
            )

    source[count + panels * (rim // PB)] = jnp.zeros((features, LANES), source.dtype)
    factor = factor_ref[...]

    def picked(row):
        base = row * slot_count
        return jnp.concatenate(
            [
                jnp.where(left, source[index_ref[base + k]], source[index_ref[base + k + 1]])
                for k in range(0, slot_count, 2)
            ],
            axis=1,
        )

    for t in range(points // LANES):
        at = pl.ds(t * LANES, LANES)
        both = lax.dot_general(
            jnp.concatenate([picked(2 * t), picked(2 * t + 1)], axis=0),
            tile_ref[at, :],
            (((1,), (1,)), ((), ())),
            preferred_element_type=jnp.float32,
        )
        image = jnp.where(left, both[:features], both[features:])
        total = total_ref[:, at].astype(jnp.float32) + factor * image
        total_out[:, at] = total.astype(total_out.dtype)
        if not last:
            rounded = image.astype(value_out.dtype)
            value_out[:, at] = rounded
            if t < rim // LANES:
                rim_out[:, at] = rounded


def term(index, value, far, tiles, total, factor, last):
    features, points = value.shape
    vmem = pl.BlockSpec(memory_space=pltpu.VMEM)
    whole = jax.ShapeDtypeStruct(value.shape, jnp.bfloat16)
    if last:
        out_shape = whole
        out_specs = vmem
    else:
        out_shape = (
            whole,
            jax.ShapeDtypeStruct((features, far.shape[2]), jnp.bfloat16),
            jax.ShapeDtypeStruct(value.shape, jnp.float32),
        )
        out_specs = (vmem,) * 3
    blocks = points // PB + far.shape[0] * (far.shape[2] // PB) + 1
    return pl.pallas_call(
        functools.partial(term_kernel, last=last),
        out_shape=out_shape,
        in_specs=[pl.BlockSpec(memory_space=pltpu.SMEM)] + [vmem] * 5,
        out_specs=out_specs,
        scratch_shapes=[pltpu.VMEM((blocks, features, LANES), jnp.bfloat16)],
        compiler_params=pltpu.CompilerParams(vmem_limit_bytes=32 * 1024 * 1024),
        cost_estimate=pl.CostEstimate(
            flops=2 * features * tiles.size, bytes_accessed=2 * tiles.size, transcendentals=0
        ),
    )(index, value, far, tiles, total, factor)


def body(features, tiles, scales, slots, live, times):
    count, width = tiles.shape[2], tiles.shape[4]
    slot_count = scales.shape[3]
    size = features.shape[0]
    rim_count = max(1, count // 8)
    value = features.reshape(size, count * PB)
    rim = value[:, : rim_count * PB]
    index, panels = source_index(slots.reshape(count * slot_count), count, rim_count)
    used = lax.broadcasted_iota(jnp.int32, (count, slot_count), 1) < live.reshape(count, 1)
    weights = scales.reshape(count, slot_count) * used.astype(jnp.float32)
    lanes = jnp.repeat(weights, PB, axis=1)
    scaled = tiles.reshape(count, PB, width).astype(jnp.float32) * lanes[:, None, :]
    scaled = scaled.astype(jnp.bfloat16).reshape(count * PB, width)
    total = value
    factor = jnp.ones(times.shape, jnp.float32)
    for step in range(1, TERMS + 1):
        far = exchange(rim).reshape(panels, size, rim_count * PB)
        factor = factor * -times / jnp.float32(step)
        out = term(index, value, far, scaled, total, factor[:, None], step == TERMS)
        if step < TERMS:
            value, rim, total = out
    return out.reshape(features.shape)


def solution(mesh):
    return jax.shard_map(
        body,
        mesh=mesh,
        in_specs=(
            P(None, "gx", "gy", "gz"),
            P("gx", "gy", "gz", None, None),
            P("gx", "gy", "gz", None),
            P("gx", "gy", "gz", None),
            P("gx", "gy", "gz"),
            P(),
        ),
        out_specs=P(None, "gx", "gy", "gz"),
        check_vma=False,
    )
```

time: 182 us -> 66.7 us (0.37)
  local copies, waits for them, and re-layouts: 68.4 us -> 3.81 us
  waiting for transfers between devices: 37.3 us -> 9.35 us
  starting transfers between devices: 28.9 us -> 8.25 us
  matrix products: 17.7 us -> 0 us
  blocking collectives: 17.3 us -> 30.2 us
  Pallas kernels: 0 us -> 11.1 us
  other arithmetic: 10.8 us -> 3.48 us
    reshape x14 -> x1, local copies, waits for them, and re-layouts: 28.2 us -> 0.09 us  [body(): slots.reshape(count * slot_count)]
    ppermute x12 -> x6, waiting for transfers between devices: 37.3 us -> 9.35 us  [exchange(): lax.ppermute(rim, 'gy', p)]
    slice x4 -> x0, local copies, waits for them, and re-layouts: 23.5 us -> none  [the longest x1 23.5 us: apply_operator(): tile_parts[:, :, slot]]
    ppermute x12 -> x6, starting transfers between devices: 28.9 us -> 8.25 us  [exchange(): lax.ppermute(rim, 'gy', p)]
    dot_general x24 -> x0, matrix products: 17.7 us -> none  [apply_operator(): jnp.einsum('bfc,brc->bfr', picked[:, slot], tile_parts[:, :, slot], prefe...]
    all_gather x3, blocking collectives: 17.3 us -> 30.2 us  [exchange(): both = lax.all_gather(rows, ('gx', 'gz'), axis=0, tiled=False)]
    pallas_call x0 -> x3, Pallas kernels: none -> 11.1 us  [term(): pl.pallas_call(functools.partial(term_kernel, last=last), out_shape=out_s...]
    select_n x4 -> x1, other arithmetic: 6.82 us -> 0.03 us  [source_index(): index = jnp.where(slots < count, slots, jnp.where(x_in & y_in, far, zero))]
  transfers between devices with their start and end apart: 12 -> 6, of which waited for: 9 -> 4; matrix products, arithmetic and copies ran while one was open for 20% -> 7% of each run, Pallas kernels for 0% -> 0%
where the time goes in v1:
time: 66.7 us; the launch traced here: 66.3 us
  blocking collectives  30.2 us (45%)
  Pallas kernels  11.1 us (17%)
  waiting for transfers between devices  9.35 us (14%)
  starting transfers between devices  8.25 us (12%)
  local copies, waits for them, and re-layouts  3.81 us (6%)
  other arithmetic  3.48 us (5%)
    all_gather x3, blocking collectives, exchange(): both = lax.all_gather(rows, ('gx', 'gz'), axis=0, tiled=False)  30.2 us
    pallas_call x3, Pallas kernels, term(): pl.pallas_call(functools.partial(term_kernel, last=last), out_shape=out_s...  11.1 us
    ppermute x6, waiting for transfers between devices, exchange(): lax.ppermute(rim, 'gy', p)  9.35 us
    ppermute x6, starting transfers between devices, exchange(): lax.ppermute(rim, 'gy', p)  8.25 us
    unnamed x7, local copies, waits for them, and re-layouts  2.41 us
    convert_element_type x1, other arithmetic, body(): scaled = scaled.astype(jnp.bfloat16).reshape(count * PB, width)  2.06 us
  transfers between devices with their start and end apart: 6, of which 4 were waited for; matrix products, arithmetic and copies ran while one was open for 7% of the time, Pallas kernels for 0%

profile of v1, /device:TPU:0, one launch (start us, length us, event | category | flops | bytes accessed | tf_op | source)
XLA Modules:
  0.0 66.3 jit_solution(1505657771389573741)
XLA Ops:
  0.0 0.8 %slice_bitcast_fusion = (bf16[1,64,256]{2,1,0:T(8,128)(2,1)S(1)}, bf16[64,256]{1,0:T(8,128)(2,1)S(1)}) fusion(bf16[64,2048]{1,0:T(8,128)(2,1)} %bitcast.28), kind=kLoop, calls=%fused_computation.30 | loop fusion | bytes 98304 | tf_op jit(solution)/shard_map/stack | solution.py:30
  0.8 3.0 %collective-permute-start = (bf16[64,256]{1,0:T(8,128)(2,1)S(1)}, bf16[64,256]{1,0:T(8,128)(2,1)S(1)}, u32[]{:S(2)}, u32[]{:S(2)}) collective-permute-start(bf16[64,256]{1,0:T(8,128)(2,1)S(1)} %get-tuple-element.18), channel_id=1, source_target_pairs={{0,4},{4,0},{8,12},{12,8},{1,5},{5,1},{9,13},{13,9},{2,6},{6,2},{1... | collective-permute-start | bytes 98312 | tf_op jit(solution)/shard_map/ppermute | solution.py:30
  3.8 2.5 %collective-permute-start.1 = (bf16[64,256]{1,0:T(8,128)(2,1)S(1)}, bf16[64,256]{1,0:T(8,128)(2,1)S(1)}, u32[]{:S(2)}, u32[]{:S(2)}) collective-permute-start(bf16[64,256]{1,0:T(8,128)(2,1)S(1)} %get-tuple-element.18), channel_id=1, source_target_pairs={{0,12},{4,8},{8,4},{12,0},{1,13},{5,9},{9,5},{13,1},{2,14},{6,10},... | collective-permute-start | bytes 98312 | tf_op jit(solution)/shard_map/ppermute | solution.py:30
  6.3 0.8 %copy.16 = s32[1,1,32,8]{3,2,1,0:T(8,128)S(1)} copy(s32[1,1,32,8]{2,3,1,0:T(8,128)} %param.9) | data formatting | bytes 2048 | tf_op args[3]
  7.0 0.1 reshape.30
  7.1 0.7 %multiply_bitcast_fusion = (f32[64,1]{0,1:T(1,128)S(1)}, f32[64,1]{0,1:T(1,128)S(1)}, f32[64,1]{0,1:T(1,128)S(1)}) fusion(f32[64]{0:T(128)} %param.11), kind=kLoop, calls=%fused_computation.26 | loop fusion | flops 320 | bytes 1024 | tf_op jit(solution)/shard_map/broadcast_in_dim | solution.py:169
  7.8 0.7 %bitcast_select_fusion = f32[32,8]{0,1:T(8,128)S(1)} fusion(f32[1,1,32,8]{2,3,1,0:T(8,128)} %param.8, s32[32]{0:T(128)} %bitcast.39), kind=kLoop, calls=%fused_computation.5 | loop fusion | flops 512 | bytes 2176 | tf_op jit(solution)/shard_map/mul | solution.py:160
  8.5 0.1 copy.17
  8.6 0.1 broadcast_in_dim.29
  8.7 0.1 mul.36
  8.8 0.1 copy.18.factor_ref
  8.9 0.0 copy-start
  8.9 2.1 %fusion.tile_ref = bf16[2048,512]{1,0:T(8,128)(2,1)S(1)} fusion(bf16[1,1,32,64,512]{4,3,2,1,0:T(8,128)(2,1)} %param.7, f32[32,512]{1,0:T(8,128)S(1)} %mul.36), kind=kLoop, calls=%fused_computation.1 | loop fusion | flops 3145728 | bytes 4259840 | tf_op jit(solution)/shard_map/convert_element_type | solution.py:163
  10.9 0.0 collective-permute-done
  10.9 0.0 collective-permute-done.1
  11.0 10.4 %all-gather.far_ref = bf16[24,64,256]{2,1,0:T(8,128)(2,1)S(1)} all-gather(bf16[3,64,256]{2,1,0:T(8,128)(2,1)S(1)} %pad_maximum_fusion), channel_id=2, replica_groups=mesh['gx'=2,'gy'=4,'gz'=4] {'gx','gz'}, dimensions={0}, use_global_device_ids=true | all-gather | bytes 884736 | tf_op jit(solution)/shard_map/all_gather | solution.py:32
  21.4 0.0 copy-done
  21.4 3.5 %shard_map.64 = (bf16[64,2048]{1,0:T(8,128)(2,1)S(1)}, bf16[64,256]{1,0:T(8,128)(2,1)S(1)}, f32[64,2048]{1,0:T(8,128)S(1)}) custom-call(s32[256]{0:T(256)S(1)} %compare_select_fusion.index_ref, bf16[64,2048]{1,0:T(8,128)(2,1)S(1)} %bitcast.29, bf16[24,64,256]{2,1,0:T(8,128)(2,1)S(1)} %all-gather.far_ref, bf16[2048,512]{1,0:T(8,128)(2,1)S(1)} %fusion.tile_ref, ...), custom_call_target="tpu_custom_call" | custom-call | flops 134217728 | bytes 2097152 | tf_op jit(solution)/shard_map/pallas_call | solution.py:138
  24.9 0.0 copy-start.1
  24.9 0.7 %copy-done.1 = bf16[64,2048]{1,0:T(8,128)(2,1)} copy-done((bf16[64,2048]{1,0:T(8,128)(2,1)}, bf16[64,2048]{1,0:T(8,128)(2,1)S(1)}, u32[]{:S(2)}) %copy-start.1) | copy-done | bytes 262168
  25.6 0.7 %collective-permute-start.2 = (bf16[64,256]{1,0:T(8,128)(2,1)S(1)}, bf16[64,256]{1,0:T(8,128)(2,1)S(1)}, u32[]{:S(2)}, u32[]{:S(2)}) collective-permute-start(bf16[64,256]{1,0:T(8,128)(2,1)S(1)} %get-tuple-element.12), channel_id=1, source_target_pairs={{0,4},{4,0},{8,12},{12,8},{1,5},{5,1},{9,13},{13,9},{2,6},{6,2},{1... | collective-permute-start | bytes 98312 | tf_op jit(solution)/shard_map/ppermute | solution.py:30
  26.2 0.9 %collective-permute-start.3 = (bf16[64,256]{1,0:T(8,128)(2,1)S(1)}, bf16[64,256]{1,0:T(8,128)(2,1)S(1)}, u32[]{:S(2)}, u32[]{:S(2)}) collective-permute-start(bf16[64,256]{1,0:T(8,128)(2,1)S(1)} %get-tuple-element.12), channel_id=1, source_target_pairs={{0,12},{4,8},{8,4},{12,0},{1,13},{5,9},{9,5},{13,1},{2,14},{6,10},... | collective-permute-start | bytes 98312 | tf_op jit(solution)/shard_map/ppermute | solution.py:30
  27.1 0.1 copy.19.factor_ref
  27.2 2.2 %collective-permute-done.2 = bf16[64,256]{1,0:T(8,128)(2,1)S(1)} collective-permute-done((bf16[64,256]{1,0:T(8,128)(2,1)S(1)}, bf16[64,256]{1,0:T(8,128)(2,1)S(1)}, u32[]{:S(2)}, u32[]{:S(2)}) %collective-permute-start.2) | collective-permute-done | bytes 32800 | tf_op jit(solution)/shard_map/ppermute | solution.py:30
  29.5 2.5 %collective-permute-done.3 = bf16[64,256]{1,0:T(8,128)(2,1)S(1)} collective-permute-done((bf16[64,256]{1,0:T(8,128)(2,1)S(1)}, bf16[64,256]{1,0:T(8,128)(2,1)S(1)}, u32[]{:S(2)}, u32[]{:S(2)}) %collective-permute-start.3) | collective-permute-done | bytes 32800 | tf_op jit(solution)/shard_map/ppermute | solution.py:30
  32.0 10.4 %all-gather.1.far_ref = bf16[24,64,256]{2,1,0:T(8,128)(2,1)S(1)} all-gather(bf16[3,64,256]{2,1,0:T(8,128)(2,1)S(1)} %pad_maximum_fusion.1), channel_id=3, replica_groups=mesh['gx'=2,'gy'=4,'gz'=4] {'gx','gz'}, dimensions={0}, use_global_device_ids=true | all-gather | bytes 884736 | tf_op jit(solution)/shard_map/all_gather | solution.py:32
  42.4 0.0 copy-start.2
  42.4 0.9 %copy-done.2 = bf16[64,2048]{1,0:T(8,128)(2,1)S(1)} copy-done((bf16[64,2048]{1,0:T(8,128)(2,1)S(1)}, bf16[64,2048]{1,0:T(8,128)(2,1)}, u32[]{:S(2)}) %copy-start.2) | copy-done | bytes 262168
  43.3 3.5 %shard_map.65 = (bf16[64,2048]{1,0:T(8,128)(2,1)S(1)}, bf16[64,256]{1,0:T(8,128)(2,1)S(1)}, f32[64,2048]{1,0:T(8,128)S(1)}) custom-call(s32[256]{0:T(256)S(1)} %compare_select_fusion.index_ref, bf16[64,2048]{1,0:T(8,128)(2,1)S(1)} %copy-done.2, bf16[24,64,256]{2,1,0:T(8,128)(2,1)S(1)} %all-gather.1.far_ref, bf16[2048,512]{1,0:T(8,128)(2,1)S(1)} %fusion.tile_ref, ...), custom_call_target="tpu_custom_call" | custom-call | flops 134217728 | bytes 2097152 | tf_op jit(solution)/shard_map/pallas_call | solution.py:138
  46.8 0.1 collective-permute-start.4
  46.9 1.1 %collective-permute-start.5 = (bf16[64,256]{1,0:T(8,128)(2,1)S(1)}, bf16[64,256]{1,0:T(8,128)(2,1)S(1)}, u32[]{:S(2)}, u32[]{:S(2)}) collective-permute-start(bf16[64,256]{1,0:T(8,128)(2,1)S(1)} %get-tuple-element.15), channel_id=1, source_target_pairs={{0,12},{4,8},{8,4},{12,0},{1,13},{5,9},{9,5},{13,1},{2,14},{6,10},... | collective-permute-start | bytes 98312 | tf_op jit(solution)/shard_map/ppermute | solution.py:30
  48.0 0.1 copy.20.factor_ref
  48.1 2.7 %collective-permute-done.4 = bf16[64,256]{1,0:T(8,128)(2,1)S(1)} collective-permute-done((bf16[64,256]{1,0:T(8,128)(2,1)S(1)}, bf16[64,256]{1,0:T(8,128)(2,1)S(1)}, u32[]{:S(2)}, u32[]{:S(2)}) %collective-permute-start.4) | collective-permute-done | bytes 32800 | tf_op jit(solution)/shard_map/ppermute | solution.py:30
  50.8 1.9 %collective-permute-done.5 = bf16[64,256]{1,0:T(8,128)(2,1)S(1)} collective-permute-done((bf16[64,256]{1,0:T(8,128)(2,1)S(1)}, bf16[64,256]{1,0:T(8,128)(2,1)S(1)}, u32[]{:S(2)}, u32[]{:S(2)}) %collective-permute-start.5) | collective-permute-done | bytes 32800 | tf_op jit(solution)/shard_map/ppermute | solution.py:30
  52.7 9.4 %all-gather.2.far_ref = bf16[24,64,256]{2,1,0:T(8,128)(2,1)S(1)} all-gather(bf16[3,64,256]{2,1,0:T(8,128)(2,1)S(1)} %pad_maximum_fusion.2), channel_id=4, replica_groups=mesh['gx'=2,'gy'=4,'gz'=4] {'gx','gz'}, dimensions={0}, use_global_device_ids=true | all-gather | bytes 884736 | tf_op jit(solution)/shard_map/all_gather | solution.py:32
  62.1 4.2 %shard_map.66 = bf16[64,2048]{1,0:T(8,128)(2,1)} custom-call(s32[256]{0:T(256)S(1)} %compare_select_fusion.index_ref, bf16[64,2048]{1,0:T(8,128)(2,1)S(1)} %get-tuple-element.14.value_ref, bf16[24,64,256]{2,1,0:T(8,128)(2,1)S(1)} %all-gather.2.far_ref, bf16[2048,512]{1,0:T(8,128)(2,1)S(1)} %fusion.tile_ref, f32[64,2048]{1,0:T(8,128)S(1)} %get-tuple-element.16.total_ref, ...), custom_call_target="tpu_custom_call" | custom-call | flops 134217728 | bytes 2097152 | tf_op jit(solution)/shard_map/pallas_call | solution.py:138
  (4 shorter events, 0.1 us)
Async XLA Ops:
  0.8 10.2 %collective-permute-start = (bf16[64,256]{1,0:T(8,128)(2,1)S(1)}, bf16[64,256]{1,0:T(8,128)(2,1)S(1)}, u32[]{:S(2)}, u32[]{:S(2)}) collective-permute-start(bf16[64,256]{1,0:T(8,128)(2,1)S(1)} %get-tuple-element.18), channel_id=1, source_target_pairs={{0,4},{4,0},{8,12},{12,8},{1,5},{5,1},{9,13},{13,9},{2,6},{6,2},{1... | collective-permute-start | bytes 98312 | tf_op jit(solution)/shard_map/ppermute | solution.py:30
  3.8 7.2 %collective-permute-start.1 = (bf16[64,256]{1,0:T(8,128)(2,1)S(1)}, bf16[64,256]{1,0:T(8,128)(2,1)S(1)}, u32[]{:S(2)}, u32[]{:S(2)}) collective-permute-start(bf16[64,256]{1,0:T(8,128)(2,1)S(1)} %get-tuple-element.18), channel_id=1, source_target_pairs={{0,12},{4,8},{8,4},{12,0},{1,13},{5,9},{9,5},{13,1},{2,14},{6,10},... | collective-permute-start | bytes 98312 | tf_op jit(solution)/shard_map/ppermute | solution.py:30
  8.9 12.5 %copy-start = (bf16[64,1,1,2048]{3,0,2,1:T(8,128)(2,1)S(1)}, bf16[64,1,1,2048]{3,0,2,1:T(8,128)(2,1)}, u32[]{:S(2)}) copy-start(bf16[64,1,1,2048]{3,0,2,1:T(8,128)(2,1)} %param.6) | copy-start | bytes 786436
  24.9 0.7 %copy-start.1 = (bf16[64,2048]{1,0:T(8,128)(2,1)}, bf16[64,2048]{1,0:T(8,128)(2,1)S(1)}, u32[]{:S(2)}) copy-start(bf16[64,2048]{1,0:T(8,128)(2,1)S(1)} %get-tuple-element.11.value_ref) | copy-start | bytes 786436
  25.6 3.9 %collective-permute-start.2 = (bf16[64,256]{1,0:T(8,128)(2,1)S(1)}, bf16[64,256]{1,0:T(8,128)(2,1)S(1)}, u32[]{:S(2)}, u32[]{:S(2)}) collective-permute-start(bf16[64,256]{1,0:T(8,128)(2,1)S(1)} %get-tuple-element.12), channel_id=1, source_target_pairs={{0,4},{4,0},{8,12},{12,8},{1,5},{5,1},{9,13},{13,9},{2,6},{6,2},{1... | collective-permute-start | bytes 98312 | tf_op jit(solution)/shard_map/ppermute | solution.py:30
  26.2 5.7 %collective-permute-start.3 = (bf16[64,256]{1,0:T(8,128)(2,1)S(1)}, bf16[64,256]{1,0:T(8,128)(2,1)S(1)}, u32[]{:S(2)}, u32[]{:S(2)}) collective-permute-start(bf16[64,256]{1,0:T(8,128)(2,1)S(1)} %get-tuple-element.12), channel_id=1, source_target_pairs={{0,12},{4,8},{8,4},{12,0},{1,13},{5,9},{9,5},{13,1},{2,14},{6,10},... | collective-permute-start | bytes 98312 | tf_op jit(solution)/shard_map/ppermute | solution.py:30
  42.4 0.9 %copy-start.2 = (bf16[64,2048]{1,0:T(8,128)(2,1)S(1)}, bf16[64,2048]{1,0:T(8,128)(2,1)}, u32[]{:S(2)}) copy-start(bf16[64,2048]{1,0:T(8,128)(2,1)} %copy-done.1) | copy-start | bytes 786436
  46.8 4.0 %collective-permute-start.4 = (bf16[64,256]{1,0:T(8,128)(2,1)S(1)}, bf16[64,256]{1,0:T(8,128)(2,1)S(1)}, u32[]{:S(2)}, u32[]{:S(2)}) collective-permute-start(bf16[64,256]{1,0:T(8,128)(2,1)S(1)} %get-tuple-element.15), channel_id=1, source_target_pairs={{0,4},{4,0},{8,12},{12,8},{1,5},{5,1},{9,13},{13,9},{2,6},{6,2},{1... | collective-permute-start | bytes 98312 | tf_op jit(solution)/shard_map/ppermute | solution.py:30
  46.9 5.8 %collective-permute-start.5 = (bf16[64,256]{1,0:T(8,128)(2,1)S(1)}, bf16[64,256]{1,0:T(8,128)(2,1)S(1)}, u32[]{:S(2)}, u32[]{:S(2)}) collective-permute-start(bf16[64,256]{1,0:T(8,128)(2,1)S(1)} %get-tuple-element.15), channel_id=1, source_target_pairs={{0,12},{4,8},{8,4},{12,0},{1,13},{5,9},{9,5},{13,1},{2,14},{6,10},... | collective-permute-start | bytes 98312 | tf_op jit(solution)/shard_map/ppermute | solution.py:30

commit v2 on v1

v2 whole, which is shorter than its diff:
```python
import functools

import jax
import jax.numpy as jnp
from jax import lax
from jax.experimental import pallas as pl
from jax.experimental.pallas import tpu as pltpu
from jax.sharding import PartitionSpec as P

PB = 64
TERMS = 3
LANES = 2 * PB
AXES = ("gx", "gy", "gz")


def pairings(count):
    first = [(i, i ^ 1) for i in range(count)]
    second = [(i, (i + 1) % count if i % 2 else (i - 1) % count) for i in range(count)]
    return [first] if count == 2 else [first, second]


def partner_rank(here, step, count):
    forward = jnp.where(here % 2 == 0, 1, 2)
    backward = 3 - forward
    rank = jnp.where(step == 1, 0, jnp.where(step == 2, forward, backward))
    there = here + step - 1
    return rank, (there >= 0) & (there < count)


def place(rank, here, count):
    return here if rank == 0 else dict(pairings(count)[rank - 1])[here]


def partners():
    x_count = len(pairings(lax.axis_size("gx"))) + 1
    y_count = len(pairings(lax.axis_size("gy"))) + 1
    pair_count = lax.axis_size("gz") // 2
    chips = [(x, b) for x in range(x_count) for b in range(pair_count)]
    side = [(x, y, b) for x, b in chips for y in range(1, y_count)]
    return side + [(x, 0, b) for x, b in chips[1:]]


def partner_number(x, y, b):
    x_count = len(pairings(lax.axis_size("gx"))) + 1
    y_count = len(pairings(lax.axis_size("gy"))) + 1
    pair_count = lax.axis_size("gz") // 2
    chip = x * pair_count + b
    return jnp.where(
        y > 0, chip * (y_count - 1) + y - 1, x_count * pair_count * (y_count - 1) + chip - 1
    )


def swap(value, by_core):
    sizes = [lax.axis_size(name) for name in AXES]
    pairs = []
    for i in range(sizes[0]):
        for j in range(sizes[1]):
            for k in range(sizes[2]):
                x, y, b = by_core[k % 2]
                to = (place(x, i, sizes[0]), place(y, j, sizes[1]), (k // 2 ^ b) * 2 + k % 2)
                pairs.append(
                    ((i * sizes[1] + j) * sizes[2] + k, (to[0] * sizes[1] + to[1]) * sizes[2] + to[2])
                )
    return lax.ppermute(value, AXES, pairs)


def swap_cores(value):
    return lax.ppermute(value, "gz", [(k, k ^ 1) for k in range(lax.axis_size("gz"))])


def exchange(rim):
    chips = partners()
    alone = [swap(rim, (chips[-1], chips[-1]))] if len(chips) % 2 else []
    other = swap_cores(rim)
    both = jnp.stack([rim, other])
    shares = [
        swap(both, (chips[t], chips[t + 1])) for t in range(0, len(chips) - len(chips) % 2, 2)
    ]
    received = jnp.concatenate(shares + [panel[None] for panel in alone])
    return received, swap_cores(received), other


def source_index(slots, count, rim_count):
    layers = lax.axis_size("gz")
    x_at, y_at, z_at = (lax.axis_index(name) for name in AXES)
    rest = jnp.maximum(slots - count, 0)
    r = rest % rim_count
    m = (rest // rim_count) % layers
    c = (rest // (rim_count * layers)) % 3
    a = rest // (rim_count * layers * 3)
    x_rank, x_in = partner_rank(x_at, a, lax.axis_size("gx"))
    y_rank, y_in = partner_rank(y_at, c, lax.axis_size("gy"))
    flip = (m // 2) ^ (z_at // 2)
    chips = len(partners())
    core, target = z_at % 2, m % 2
    number = partner_number(x_rank, y_rank, flip)
    single = (number == chips - 1) if chips % 2 else jnp.zeros(number.shape, bool)
    holder = jnp.where(single, target, number % 2)
    panel = jnp.where(single, chips - 1, number // 2 * 2 + (target ^ holder))
    panel = panel + jnp.where(holder == core, 0, chips)
    here = (x_rank == 0) & (y_rank == 0) & (flip == 0)
    panel = jnp.where(here, 2 * chips, panel)
    far = count + panel * rim_count + r
    far = jnp.where(here & (target == core), r, far)
    zero = count + (2 * chips + 1) * rim_count
    index = jnp.where(slots < count, slots, jnp.where(x_in & y_in, far, zero))
    return index.astype(jnp.int32)


def term_kernel(
    index_ref, value_ref, mine_ref, others_ref, other_ref, tile_ref, *rest, kind
):
    if kind == "rim":
        rim_out, source = rest
    elif kind == "full":
        total_ref, factor_ref, value_out, total_out, source = rest
    else:
        total_ref, factor_ref, total_out, source = rest
    features, points = value_ref.shape
    panels, _, rim = mine_ref.shape
    count, rim_count = points // PB, rim // PB
    slot_count = tile_ref.shape[1] // PB
    left = lax.broadcasted_iota(jnp.int32, (features, LANES), 1) < PB

    def spread(pair, at):
        turned = jnp.concatenate([pair[:, PB:], pair[:, :PB]], axis=1)
        source[at] = jnp.where(left, pair, turned)
        source[at + 1] = jnp.where(left, turned, pair)

    for t in range(points // LANES):
        spread(value_ref[:, t * LANES : (t + 1) * LANES], 2 * t)
    for t in range(rim // LANES):
        spread(
            other_ref[:, t * LANES : (t + 1) * LANES], count + 2 * panels * rim_count + 2 * t
        )

    @pl.loop(0, panels)
    def _(panel):
        for t in range(rim // LANES):
            cut = slice(t * LANES, (t + 1) * LANES)
            at = count + panel * rim_count + 2 * t
            spread(mine_ref[panel, :, cut], at)
            spread(others_ref[panel, :, cut], at + panels * rim_count)

    source[count + (2 * panels + 1) * rim_count] = jnp.zeros((features, LANES), source.dtype)

    def picked(row):
        base = row * slot_count
        return jnp.concatenate(
            [
                jnp.where(left, source[index_ref[base + k]], source[index_ref[base + k + 1]])
                for k in range(0, slot_count, 2)
            ],
            axis=1,
        )

    for t in range((rim if kind == "rim" else points) // LANES):
        at = pl.ds(t * LANES, LANES)
        both = lax.dot_general(
            jnp.concatenate([picked(2 * t), picked(2 * t + 1)], axis=0),
            tile_ref[at, :],
            (((1,), (1,)), ((), ())),
            preferred_element_type=jnp.float32,
        )
        image = jnp.where(left, both[:features], both[features:])
        if kind == "rim":
            rim_out[:, at] = image.astype(rim_out.dtype)
            continue
        total = total_ref[:, at].astype(jnp.float32) + factor_ref[...] * image
        total_out[:, at] = total.astype(total_out.dtype)
        if kind == "full":
            value_out[:, at] = image.astype(value_out.dtype)


def term(kind, index, value, rims, tiles, *accumulate):
    features, points = value.shape
    vmem = pl.BlockSpec(memory_space=pltpu.VMEM)
    whole = jax.ShapeDtypeStruct(value.shape, jnp.bfloat16)
    rim = rims[0].shape[2]
    if kind == "rim":
        tiles = tiles[:rim]
        out_shape = jax.ShapeDtypeStruct((features, rim), jnp.bfloat16)
        out_specs = vmem
    elif kind == "full":
        out_shape = (whole, jax.ShapeDtypeStruct(value.shape, jnp.float32))
        out_specs = (vmem, vmem)
    else:
        out_shape, out_specs = whole, vmem
    blocks = points // PB + (2 * rims[0].shape[0] + 1) * (rim // PB) + 1
    return pl.pallas_call(
        functools.partial(term_kernel, kind=kind),
        out_shape=out_shape,
        in_specs=[pl.BlockSpec(memory_space=pltpu.SMEM)] + [vmem] * (5 + len(accumulate)),
        out_specs=out_specs,
        scratch_shapes=[pltpu.VMEM((blocks, features, LANES), jnp.bfloat16)],
        compiler_params=pltpu.CompilerParams(vmem_limit_bytes=32 * 1024 * 1024),
        cost_estimate=pl.CostEstimate(
            flops=2 * features * tiles.size, bytes_accessed=2 * tiles.size, transcendentals=0
        ),
    )(index, value, *rims, tiles, *accumulate)


def body(features, tiles, scales, slots, live, times):
    count, width = tiles.shape[2], tiles.shape[4]
    slot_count = scales.shape[3]
    size = features.shape[0]
    rim_count = max(1, count // 8)
    value = features.reshape(size, count * PB)
    rim = value[:, : rim_count * PB]
    index = source_index(slots.reshape(count * slot_count), count, rim_count)
    used = lax.broadcasted_iota(jnp.int32, (count, slot_count), 1) < live.reshape(count, 1)
    weights = scales.reshape(count, slot_count) * used.astype(jnp.float32)
    lanes = jnp.repeat(weights, PB, axis=1)
    scaled = tiles.reshape(count, PB, width).astype(jnp.float32) * lanes[:, None, :]
    scaled = scaled.astype(jnp.bfloat16).reshape(count * PB, width)
    total = value
    factor = jnp.ones(times.shape, jnp.float32)
    for step in range(1, TERMS + 1):
        rims = exchange(rim)
        factor = factor * -times / jnp.float32(step)
        if step < TERMS:
            rim = term("rim", index, value, rims, scaled)
            value, total = term("full", index, value, rims, scaled, total, factor[:, None])
        else:
            total = term("last", index, value, rims, scaled, total, factor[:, None])
    return total.reshape(features.shape)


def solution(mesh):
    return jax.shard_map(
        body,
        mesh=mesh,
        in_specs=(
            P(None, "gx", "gy", "gz"),
            P("gx", "gy", "gz", None, None),
            P("gx", "gy", "gz", None),
            P("gx", "gy", "gz", None),
            P("gx", "gy", "gz"),
            P(),
        ),
        out_specs=P(None, "gx", "gy", "gz"),
        check_vma=False,
    )
```

time: 66.7 us -> 74.9 us (1.12)
  blocking collectives: 30.2 us -> 0 us
  starting transfers between devices: 8.25 us -> 34.4 us
  waiting for transfers between devices: 9.35 us -> 13.9 us
  other arithmetic: 3.48 us -> 7.31 us
  Pallas kernels: 11.1 us -> 13.8 us
  local copies, waits for them, and re-layouts: 3.81 us -> 4.63 us
    all_gather x3 -> x0, blocking collectives: 30.2 us -> none  [exchange(): both = lax.all_gather(rows, ('gx', 'gz'), axis=0, tiled=False)]
    ppermute x6 -> x24, starting transfers between devices: 8.25 us -> 34.4 us  [the longest x18 26.8 us: swap(): return lax.ppermute(value, AXES, pairs)]
    ppermute x6 -> x24, waiting for transfers between devices: 9.35 us -> 13.9 us  [the longest x18 11.7 us: swap(): return lax.ppermute(value, AXES, pairs)]
    convert_element_type x0 -> x1, other arithmetic: none -> 4.13 us  [body(): tiles.reshape(count, PB, width).astype(jnp.float32) * lanes[:, None, :]]
    pallas_call x3 -> x5, Pallas kernels: 11.1 us -> 13.8 us  [term(): pl.pallas_call(functools.partial(term_kernel, kind=kind), out_shape=out_s...]
    convert_element_type x1 -> x2, other arithmetic: 2.06 us -> 3.1 us  [body(): scaled = scaled.astype(jnp.bfloat16).reshape(count * PB, width)]
    unnamed x7 -> x38, local copies, waits for them, and re-layouts: 2.41 us -> 3.17 us
  transfers between devices with their start and end apart: 6 -> 24, of which waited for: 4 -> 11; matrix products, arithmetic and copies ran while one was open for 7% -> 11% of each run, Pallas kernels for 0% -> 7%
where the time goes in v2:
time: 74.9 us; the launch traced here: 74.4 us
  starting transfers between devices  34.4 us (46%)
  waiting for transfers between devices  13.9 us (19%)
  Pallas kernels  13.8 us (18%)
  other arithmetic  7.31 us (10%)
  local copies, waits for them, and re-layouts  4.63 us (6%)
    ppermute x18, starting transfers between devices, swap(): return lax.ppermute(value, AXES, pairs)  26.8 us
    pallas_call x5, Pallas kernels, term(): pl.pallas_call(functools.partial(term_kernel, kind=kind), out_shape=out_s...  13.8 us
    ppermute x18, waiting for transfers between devices, swap(): return lax.ppermute(value, AXES, pairs)  11.7 us
    ppermute x6, starting transfers between devices, swap_cores(): lax.ppermute(value, 'gz', [(k, k ^ 1) for k in range(lax.axis_size('gz'))])  7.57 us
    convert_element_type x1, other arithmetic, body(): tiles.reshape(count, PB, width).astype(jnp.float32) * lanes[:, None, :]  4.13 us
    unnamed x38, local copies, waits for them, and re-layouts  3.17 us
    convert_element_type x2, other arithmetic, body(): scaled = scaled.astype(jnp.bfloat16).reshape(count * PB, width)  3.1 us
    ppermute x6, waiting for transfers between devices, swap_cores(): lax.ppermute(value, 'gz', [(k, k ^ 1) for k in range(lax.axis_size('gz'))])  2.21 us
  transfers between devices with their start and end apart: 24, of which 11 were waited for; matrix products, arithmetic and copies ran while one was open for 11% of the time, Pallas kernels for 7%

profile of v2, /device:TPU:0, one launch (start us, length us, event | category | flops | bytes accessed | tf_op | source)
XLA Modules:
  0.0 74.4 jit_solution(17005832353576989638)
XLA Ops:
  0.0 0.8 %slice_bitcast_fusion = (bf16[1,64,256]{2,1,0:T(8,128)(2,1)S(1)}, bf16[64,256]{1,0:T(8,128)(2,1)S(1)}) fusion(bf16[64,2048]{1,0:T(8,128)(2,1)} %bitcast.35), kind=kLoop, calls=%fused_computation.66 | loop fusion | bytes 98304 | tf_op jit(solution)/shard_map/stack | solution.py:75
  0.8 0.5 collective-permute-start
  1.3 3.5 %collective-permute-start.6 = (bf16[64,256]{1,0:T(8,128)(2,1)S(1)}, bf16[64,256]{1,0:T(8,128)(2,1)S(1)}, u32[]{:S(2)}, u32[]{:S(2)}) collective-permute-start(bf16[64,256]{1,0:T(8,128)(2,1)S(1)} %get-tuple-element.14), channel_id=1, source_target_pairs={{0,18},{1,19},{2,16},{3,17},{4,22},{5,23},{6,20},{7,21},{8,26},{9,... | collective-permute-start | bytes 98312 | tf_op jit(solution)/shard_map/ppermute | solution.py:64
  4.8 4.1 %convert_bitcast_fusion = f32[32,64,512]{2,1,0:T(8,128)} fusion(bf16[1,1,32,64,512]{4,3,2,1,0:T(8,128)(2,1)} %param.7), kind=kLoop, calls=%fused_computation.2 | loop fusion | flops 1048576 | bytes 6291456 | tf_op jit(solution)/shard_map/convert_element_type | solution.py:214
  8.9 0.0 collective-permute-done.other_ref
  8.9 1.6 %collective-permute-start.1 = (bf16[2,64,256]{2,1,0:T(8,128)(2,1)S(1)}, bf16[2,64,256]{2,1,0:T(8,128)(2,1)S(1)}, u32[]{:S(2)}, u32[]{:S(2)}) collective-permute-start(bf16[2,64,256]{2,1,0:T(8,128)(2,1)S(1)} %pad_maximum_fusion), channel_id=1, source_target_pairs={{0,4},{1,13},{2,6},{3,15},{4,0},{5,9},{6,2},{7,11},{8,12},{9,5},{1... | collective-permute-start | bytes 196616 | tf_op jit(solution)/shard_map/ppermute | solution.py:64
  10.6 0.0 copy-start.10
  10.6 0.1 copy.11
  10.7 0.1 reshape.24
  10.8 0.1 copy.12
  10.9 0.1 broadcast_in_dim.61
  11.0 0.1 mul.41
  11.1 0.5 collective-permute-start.2
  11.6 1.5 %collective-permute-start.3 = (bf16[2,64,256]{2,1,0:T(8,128)(2,1)S(1)}, bf16[2,64,256]{2,1,0:T(8,128)(2,1)S(1)}, u32[]{:S(2)}, u32[]{:S(2)}) collective-permute-start(bf16[2,64,256]{2,1,0:T(8,128)(2,1)S(1)} %pad_maximum_fusion), channel_id=1, source_target_pairs={{0,20},{1,29},{2,22},{3,31},{4,16},{5,25},{6,18},{7,27},{8,28},{9,... | collective-permute-start | bytes 196616 | tf_op jit(solution)/shard_map/ppermute | solution.py:64
  13.1 2.3 %collective-permute-start.4 = (bf16[2,64,256]{2,1,0:T(8,128)(2,1)S(1)}, bf16[2,64,256]{2,1,0:T(8,128)(2,1)S(1)}, u32[]{:S(2)}, u32[]{:S(2)}) collective-permute-start(bf16[2,64,256]{2,1,0:T(8,128)(2,1)S(1)} %pad_maximum_fusion), channel_id=1, source_target_pairs={{0,22},{1,31},{2,20},{3,29},{4,18},{5,27},{6,16},{7,25},{8,30},{9,... | collective-permute-start | bytes 196616 | tf_op jit(solution)/shard_map/ppermute | solution.py:64
  15.5 0.5 collective-permute-start.5
  16.0 0.3 collective-permute-done.2
  16.3 0.4 collective-permute-done.3
  16.8 3.8 %collective-permute-done.4 = bf16[2,64,256]{2,1,0:T(8,128)(2,1)S(1)} collective-permute-done((bf16[2,64,256]{2,1,0:T(8,128)(2,1)S(1)}, bf16[2,64,256]{2,1,0:T(8,128)(2,1)S(1)}, u32[]{:S(2)}, u32[]{:S(2)}) %collective-permute-start.4) | collective-permute-done | bytes 65568 | tf_op jit(solution)/shard_map/ppermute | solution.py:64
  20.5 0.0 collective-permute-done.5
  20.6 2.5 %collective-permute-start.7 = (bf16[11,64,256]{2,1,0:T(8,128)(2,1)S(1)}, bf16[11,64,256]{2,1,0:T(8,128)(2,1)S(1)}, u32[]{:S(2)}, u32[]{:S(2)}) collective-permute-start(bf16[11,64,256]{2,1,0:T(8,128)(2,1)S(1)} %constant_dynamic-update-slice_fusion.mine_ref), channel_id=1, source_target_pairs={{0,1},{1,0},{2,3},{3,2},{4,5},{5,4},{6,7},{7,6},{8,9},{9,8},{10,11... | collective-permute-start | bytes 1081352 | tf_op jit(solution)/shard_map/ppermute | solution.py:68
  23.1 1.1 %fusion.1 = bf16[4,64,512]{2,1,0:T(8,128)(2,1)S(1)} fusion(f32[32,64,512]{2,1,0:T(8,128)} %convert_bitcast_fusion, f32[4,512]{1,0:T(4,128)S(1)} %slice.15), kind=kLoop, calls=%fused_computation.4 | loop fusion | flops 262144 | bytes 794624 | tf_op jit(solution)/shard_map/convert_element_type | solution.py:215
  24.2 0.2 collective-permute-done.7.others_ref
  24.4 1.9 %shard_map.65 = bf16[64,256]{1,0:T(8,128)(2,1)S(1)} custom-call(s32[256]{0:T(256)S(1)} %compare_select_fusion.index_ref, bf16[64,2048]{1,0:T(8,128)(2,1)S(1)} %bitcast.36, bf16[11,64,256]{2,1,0:T(8,128)(2,1)S(1)} %constant_dynamic-update-slice_fusion.mine_ref, bf16[11,64,256]{2,1,0:T(8,128)(2,1)S(1)} %collective-permute-done.7.others_ref, ...), custom_call_target="tpu_custom_call" | custom-call | flops 16777216 | bytes 262144 | tf_op jit(solution)/shard_map/pallas_call | solution.py:190
  26.3 0.4 collective-permute-start.8
  26.8 0.9 %collective-permute-done.8.other_ref = bf16[64,256]{1,0:T(8,128)(2,1)S(1)} collective-permute-done((bf16[64,256]{1,0:T(8,128)(2,1)S(1)}, bf16[64,256]{1,0:T(8,128)(2,1)S(1)}, u32[]{:S(2)}, u32[]{:S(2)}) %collective-permute-start.8) | collective-permute-done | bytes 32800 | tf_op jit(solution)/shard_map/ppermute | solution.py:68
  27.6 0.1 collective-permute-start.9
  27.7 2.5 %collective-permute-start.14 = (bf16[64,256]{1,0:T(8,128)(2,1)S(1)}, bf16[64,256]{1,0:T(8,128)(2,1)S(1)}, u32[]{:S(2)}, u32[]{:S(2)}) collective-permute-start(bf16[64,256]{1,0:T(8,128)(2,1)S(1)} %shard_map.65), channel_id=1, source_target_pairs={{0,18},{1,19},{2,16},{3,17},{4,22},{5,23},{6,20},{7,21},{8,26},{9,... | collective-permute-start | bytes 98312 | tf_op jit(solution)/shard_map/ppermute | solution.py:64
  30.2 1.9 %collective-permute-start.10 = (bf16[2,64,256]{2,1,0:T(8,128)(2,1)S(1)}, bf16[2,64,256]{2,1,0:T(8,128)(2,1)S(1)}, u32[]{:S(2)}, u32[]{:S(2)}) collective-permute-start(bf16[2,64,256]{2,1,0:T(8,128)(2,1)S(1)} %pad_maximum_fusion.1), channel_id=1, source_target_pairs={{0,6},{1,15},{2,4},{3,13},{4,2},{5,11},{6,0},{7,9},{8,14},{9,7},{1... | collective-permute-start | bytes 196616 | tf_op jit(solution)/shard_map/ppermute | solution.py:64
  32.1 0.0 collective-permute-start.11
  32.1 3.8 %collective-permute-start.12 = (bf16[2,64,256]{2,1,0:T(8,128)(2,1)S(1)}, bf16[2,64,256]{2,1,0:T(8,128)(2,1)S(1)}, u32[]{:S(2)}, u32[]{:S(2)}) collective-permute-start(bf16[2,64,256]{2,1,0:T(8,128)(2,1)S(1)} %pad_maximum_fusion.1), channel_id=1, source_target_pairs={{0,22},{1,31},{2,20},{3,29},{4,18},{5,27},{6,16},{7,25},{8,30},{9,... | collective-permute-start | bytes 196616 | tf_op jit(solution)/shard_map/ppermute | solution.py:64
  36.0 0.0 collective-permute-done.9
  36.0 0.5 collective-permute-start.13
  36.5 0.0 collective-permute-done.10
  36.5 1.1 %collective-permute-done.11 = bf16[2,64,256]{2,1,0:T(8,128)(2,1)S(1)} collective-permute-done((bf16[2,64,256]{2,1,0:T(8,128)(2,1)S(1)}, bf16[2,64,256]{2,1,0:T(8,128)(2,1)S(1)}, u32[]{:S(2)}, u32[]{:S(2)}) %collective-permute-start.11) | collective-permute-done | bytes 65568 | tf_op jit(solution)/shard_map/ppermute | solution.py:64
  37.7 1.3 %collective-permute-done.12 = bf16[2,64,256]{2,1,0:T(8,128)(2,1)S(1)} collective-permute-done((bf16[2,64,256]{2,1,0:T(8,128)(2,1)S(1)}, bf16[2,64,256]{2,1,0:T(8,128)(2,1)S(1)}, u32[]{:S(2)}, u32[]{:S(2)}) %collective-permute-start.12) | collective-permute-done | bytes 65568 | tf_op jit(solution)/shard_map/ppermute | solution.py:64
  39.0 1.2 %collective-permute-done.13 = bf16[2,64,256]{2,1,0:T(8,128)(2,1)S(1)} collective-permute-done((bf16[2,64,256]{2,1,0:T(8,128)(2,1)S(1)}, bf16[2,64,256]{2,1,0:T(8,128)(2,1)S(1)}, u32[]{:S(2)}, u32[]{:S(2)}) %collective-permute-start.13) | collective-permute-done | bytes 65568 | tf_op jit(solution)/shard_map/ppermute | solution.py:64
  40.3 2.2 %collective-permute-start.15 = (bf16[11,64,256]{2,1,0:T(8,128)(2,1)S(1)}, bf16[11,64,256]{2,1,0:T(8,128)(2,1)}, u32[]{:S(2)}, u32[]{:S(2)}) collective-permute-start(bf16[11,64,256]{2,1,0:T(8,128)(2,1)S(1)} %constant_dynamic-update-slice_fusion.6.mine_ref), channel_id=1, source_target_pairs={{0,1},{1,0},{2,3},{3,2},{4,5},{5,4},{6,7},{7,6},{8,9},{9,8},{10,11... | collective-permute-start | bytes 1081352 | tf_op jit(solution)/shard_map/ppermute | solution.py:68
  42.4 2.0 %fusion.tile_ref = bf16[2048,512]{1,0:T(8,128)(2,1)S(1)} fusion(f32[32,512]{1,0:T(8,128)S(1)} %mul.41, bf16[1,1,32,64,512]{4,3,2,1,0:T(8,128)(2,1)} %param.7), kind=kLoop, calls=%fused_computation.1 | loop fusion | flops 3145728 | bytes 4259840 | tf_op jit(solution)/shard_map/convert_element_type | solution.py:215
  44.5 0.1 copy.13.rest_1_
  44.6 1.0 %copy-done.2 = bf16[11,64,256]{2,1,0:T(8,128)(2,1)S(1)} copy-done((bf16[11,64,256]{2,1,0:T(8,128)(2,1)S(1)}, bf16[11,64,256]{2,1,0:T(8,128)(2,1)}, u32[]{:S(2)}) %copy-start.2) | copy-done | bytes 360472
  45.5 2.5 %shard_map.64 = (bf16[64,2048]{1,0:T(8,128)(2,1)S(1)}, f32[64,2048]{1,0:T(8,128)S(1)}) custom-call(s32[256]{0:T(256)S(1)} %compare_select_fusion.index_ref, bf16[64,2048]{1,0:T(8,128)(2,1)S(1)} %bitcast.37, bf16[11,64,256]{2,1,0:T(8,128)(2,1)S(1)} %constant_dynamic-update-slice_fusion.mine_ref, bf16[11,64,256]{2,1,0:T(8,128)(2,1)S(1)} %copy-done.2, ...), custom_call_target="tpu_custom_call" | custom-call | flops 134217728 | bytes 2097152 | tf_op jit(solution)/shard_map/pallas_call | solution.py:190
  48.1 0.0 copy-start.3
  48.1 0.0 collective-permute-done.15.others_ref
  48.1 2.6 %shard_map.67 = bf16[64,256]{1,0:T(8,128)(2,1)S(1)} custom-call(s32[256]{0:T(256)S(1)} %compare_select_fusion.index_ref, bf16[64,2048]{1,0:T(8,128)(2,1)S(1)} %get-tuple-element.9.value_ref, bf16[11,64,256]{2,1,0:T(8,128)(2,1)S(1)} %constant_dynamic-update-slice_fusion.6.mine_ref, bf16[11,64,256]{2,1,0:T(8,128)(2,1)} %collective-permute-done.15.others_ref, ...), custom_call_target="tpu_custom_call" | custom-call | flops 16777216 | bytes 262144 | tf_op jit(solution)/shard_map/pallas_call | solution.py:190
  50.8 0.1 collective-permute-start.16
  50.9 1.2 %collective-permute-done.16.other_ref = bf16[64,256]{1,0:T(8,128)(2,1)S(1)} collective-permute-done((bf16[64,256]{1,0:T(8,128)(2,1)S(1)}, bf16[64,256]{1,0:T(8,128)(2,1)S(1)}, u32[]{:S(2)}, u32[]{:S(2)}) %collective-permute-start.16) | collective-permute-done | bytes 32800 | tf_op jit(solution)/shard_map/ppermute | solution.py:68
  52.1 0.1 collective-permute-start.17
  52.2 0.6 collective-permute-start.22
  52.7 2.9 %collective-permute-start.18 = (bf16[2,64,256]{2,1,0:T(8,128)(2,1)S(1)}, bf16[2,64,256]{2,1,0:T(8,128)(2,1)S(1)}, u32[]{:S(2)}, u32[]{:S(2)}) collective-permute-start(bf16[2,64,256]{2,1,0:T(8,128)(2,1)S(1)} %pad_maximum_fusion.2), channel_id=1, source_target_pairs={{0,6},{1,15},{2,4},{3,13},{4,2},{5,11},{6,0},{7,9},{8,14},{9,7},{1... | collective-permute-start | bytes 196616 | tf_op jit(solution)/shard_map/ppermute | solution.py:64
  55.6 1.0 %collective-permute-start.19 = (bf16[2,64,256]{2,1,0:T(8,128)(2,1)S(1)}, bf16[2,64,256]{2,1,0:T(8,128)(2,1)S(1)}, u32[]{:S(2)}, u32[]{:S(2)}) collective-permute-start(bf16[2,64,256]{2,1,0:T(8,128)(2,1)S(1)} %pad_maximum_fusion.2), channel_id=1, source_target_pairs={{0,20},{1,29},{2,22},{3,31},{4,16},{5,25},{6,18},{7,27},{8,28},{9,... | collective-permute-start | bytes 196616 | tf_op jit(solution)/shard_map/ppermute | solution.py:64
  56.6 1.9 %collective-permute-start.20 = (bf16[2,64,256]{2,1,0:T(8,128)(2,1)S(1)}, bf16[2,64,256]{2,1,0:T(8,128)(2,1)S(1)}, u32[]{:S(2)}, u32[]{:S(2)}) collective-permute-start(bf16[2,64,256]{2,1,0:T(8,128)(2,1)S(1)} %pad_maximum_fusion.2), channel_id=1, source_target_pairs={{0,22},{1,31},{2,20},{3,29},{4,18},{5,27},{6,16},{7,25},{8,30},{9,... | collective-permute-start | bytes 196616 | tf_op jit(solution)/shard_map/ppermute | solution.py:64
  58.5 1.5 %collective-permute-start.21 = (bf16[2,64,256]{2,1,0:T(8,128)(2,1)S(1)}, bf16[2,64,256]{2,1,0:T(8,128)(2,1)S(1)}, u32[]{:S(2)}, u32[]{:S(2)}) collective-permute-start(bf16[2,64,256]{2,1,0:T(8,128)(2,1)S(1)} %pad_maximum_fusion.2), channel_id=1, source_target_pairs={{0,2},{1,17},{2,0},{3,19},{4,6},{5,21},{6,4},{7,23},{8,10},{9,25},... | collective-permute-start | bytes 196616 | tf_op jit(solution)/shard_map/ppermute | solution.py:64
  60.0 1.3 %collective-permute-done.19 = bf16[2,64,256]{2,1,0:T(8,128)(2,1)S(1)} collective-permute-done((bf16[2,64,256]{2,1,0:T(8,128)(2,1)S(1)}, bf16[2,64,256]{2,1,0:T(8,128)(2,1)S(1)}, u32[]{:S(2)}, u32[]{:S(2)}) %collective-permute-start.19) | collective-permute-done | bytes 65568 | tf_op jit(solution)/shard_map/ppermute | solution.py:64
  61.3 2.2 %collective-permute-done.20 = bf16[2,64,256]{2,1,0:T(8,128)(2,1)S(1)} collective-permute-done((bf16[2,64,256]{2,1,0:T(8,128)(2,1)S(1)}, bf16[2,64,256]{2,1,0:T(8,128)(2,1)S(1)}, u32[]{:S(2)}, u32[]{:S(2)}) %collective-permute-start.20) | collective-permute-done | bytes 65568 | tf_op jit(solution)/shard_map/ppermute | solution.py:64
  63.5 0.0 collective-permute-done.21
  63.6 1.9 %collective-permute-start.23 = (bf16[11,64,256]{2,1,0:T(8,128)(2,1)S(1)}, bf16[11,64,256]{2,1,0:T(8,128)(2,1)}, u32[]{:S(2)}, u32[]{:S(2)}) collective-permute-start(bf16[11,64,256]{2,1,0:T(8,128)(2,1)S(1)} %constant_dynamic-update-slice_fusion.12.mine_ref), channel_id=1, source_target_pairs={{0,1},{1,0},{2,3},{3,2},{4,5},{5,4},{6,7},{7,6},{8,9},{9,8},{10,11... | collective-permute-start | bytes 1081352 | tf_op jit(solution)/shard_map/ppermute | solution.py:68
  65.5 0.1 copy.14.rest_1_
  65.6 0.1 copy.15.rest_1_
  65.7 0.9 %copy-done.4 = bf16[64,2048]{1,0:T(8,128)(2,1)S(1)} copy-done((bf16[64,2048]{1,0:T(8,128)(2,1)S(1)}, bf16[64,2048]{1,0:T(8,128)(2,1)}, u32[]{:S(2)}) %copy-start.4) | copy-done | bytes 262168
  66.6 1.0 %copy-done.6 = f32[64,2048]{1,0:T(8,128)S(1)} copy-done((f32[64,2048]{1,0:T(8,128)S(1)}, f32[64,2048]{1,0:T(8,128)}, u32[]{:S(2)}) %copy-start.6) | copy-done | bytes 524312
  67.7 3.0 %shard_map.66 = (bf16[64,2048]{1,0:T(8,128)(2,1)S(1)}, f32[64,2048]{1,0:T(8,128)S(1)}) custom-call(s32[256]{0:T(256)S(1)} %compare_select_fusion.index_ref, bf16[64,2048]{1,0:T(8,128)(2,1)S(1)} %copy-done.4, bf16[11,64,256]{2,1,0:T(8,128)(2,1)S(1)} %constant_dynamic-update-slice_fusion.6.mine_ref, bf16[11,64,256]{2,1,0:T(8,128)(2,1)} %collective-permute-done.15.others_ref, ...), custom_call_target="tpu_custom_call" | custom-call | flops 134217728 | bytes 2097152 | tf_op jit(solution)/shard_map/pallas_call | solution.py:190
  70.7 0.0 collective-permute-done.23.others_ref
  70.7 3.7 %shard_map.68 = bf16[64,2048]{1,0:T(8,128)(2,1)} custom-call(s32[256]{0:T(256)S(1)} %compare_select_fusion.index_ref, bf16[64,2048]{1,0:T(8,128)(2,1)S(1)} %get-tuple-element.11.value_ref, bf16[11,64,256]{2,1,0:T(8,128)(2,1)S(1)} %constant_dynamic-update-slice_fusion.12.mine_ref, bf16[11,64,256]{2,1,0:T(8,128)(2,1)} %collective-permute-done.23.others_ref, ...), custom_call_target="tpu_custom_call" | custom-call | flops 134217728 | bytes 2097152 | tf_op jit(solution)/shard_map/pallas_call | solution.py:190
  (48 shorter events, 0.2 us)
Async XLA Ops:
  0.0 10.6 %copy-start.9 = (s32[1,1,32]{2,1,0:T(1,128)S(1)}, s32[1,1,32]{2,1,0:T(1,128)}, u32[]{:S(2)}) copy-start(s32[1,1,32]{2,1,0:T(1,128)} %param.10) | copy-start | bytes 388
  0.0 10.6 %copy-start.8 = (f32[1,1,32,8]{2,3,1,0:T(8,128)S(1)}, f32[1,1,32,8]{2,3,1,0:T(8,128)}, u32[]{:S(2)}) copy-start(f32[1,1,32,8]{2,3,1,0:T(8,128)} %param.8) | copy-start | bytes 3076
  0.0 10.6 %copy-start.7 = (s32[1,1,32,8]{2,3,1,0:T(8,128)S(1)}, s32[1,1,32,8]{2,3,1,0:T(8,128)}, u32[]{:S(2)}) copy-start(s32[1,1,32,8]{2,3,1,0:T(8,128)} %param.9) | copy-start | bytes 3076
  0.8 23.6 %copy-start = (bf16[64,1,1,2048]{3,0,2,1:T(8,128)(2,1)S(1)}, bf16[64,1,1,2048]{3,0,2,1:T(8,128)(2,1)}, u32[]{:S(2)}) copy-start(bf16[64,1,1,2048]{3,0,2,1:T(8,128)(2,1)} %param.6) | copy-start | bytes 786436
  0.8 8.1 %collective-permute-start = (bf16[64,256]{1,0:T(8,128)(2,1)S(1)}, bf16[64,256]{1,0:T(8,128)(2,1)S(1)}, u32[]{:S(2)}, u32[]{:S(2)}) collective-permute-start(bf16[64,256]{1,0:T(8,128)(2,1)S(1)} %get-tuple-element.14), channel_id=1, source_target_pairs={{0,1},{1,0},{2,3},{3,2},{4,5},{5,4},{6,7},{7,6},{8,9},{9,8},{10,11... | collective-permute-start | bytes 98312 | tf_op jit(solution)/shard_map/ppermute | solution.py:68
  1.3 19.3 %collective-permute-start.6 = (bf16[64,256]{1,0:T(8,128)(2,1)S(1)}, bf16[64,256]{1,0:T(8,128)(2,1)S(1)}, u32[]{:S(2)}, u32[]{:S(2)}) collective-permute-start(bf16[64,256]{1,0:T(8,128)(2,1)S(1)} %get-tuple-element.14), channel_id=1, source_target_pairs={{0,18},{1,19},{2,16},{3,17},{4,22},{5,23},{6,20},{7,21},{8,26},{9,... | collective-permute-start | bytes 98312 | tf_op jit(solution)/shard_map/ppermute | solution.py:64
  8.9 6.5 %collective-permute-start.1 = (bf16[2,64,256]{2,1,0:T(8,128)(2,1)S(1)}, bf16[2,64,256]{2,1,0:T(8,128)(2,1)S(1)}, u32[]{:S(2)}, u32[]{:S(2)}) collective-permute-start(bf16[2,64,256]{2,1,0:T(8,128)(2,1)S(1)} %pad_maximum_fusion), channel_id=1, source_target_pairs={{0,4},{1,13},{2,6},{3,15},{4,0},{5,9},{6,2},{7,11},{8,12},{9,5},{1... | collective-permute-start | bytes 196616 | tf_op jit(solution)/shard_map/ppermute | solution.py:64
  10.6 33.8 %copy-start.10 = (f32[64]{0:T(128)S(1)}, f32[64]{0:T(128)}, u32[]{:S(2)}) copy-start(f32[64]{0:T(128)} %param.11) | copy-start | bytes 772
  11.1 5.2 %collective-permute-start.2 = (bf16[2,64,256]{2,1,0:T(8,128)(2,1)S(1)}, bf16[2,64,256]{2,1,0:T(8,128)(2,1)S(1)}, u32[]{:S(2)}, u32[]{:S(2)}) collective-permute-start(bf16[2,64,256]{2,1,0:T(8,128)(2,1)S(1)} %pad_maximum_fusion), channel_id=1, source_target_pairs={{0,6},{1,15},{2,4},{3,13},{4,2},{5,11},{6,0},{7,9},{8,14},{9,7},{1... | collective-permute-start | bytes 196616 | tf_op jit(solution)/shard_map/ppermute | solution.py:64
  11.6 5.2 %collective-permute-start.3 = (bf16[2,64,256]{2,1,0:T(8,128)(2,1)S(1)}, bf16[2,64,256]{2,1,0:T(8,128)(2,1)S(1)}, u32[]{:S(2)}, u32[]{:S(2)}) collective-permute-start(bf16[2,64,256]{2,1,0:T(8,128)(2,1)S(1)} %pad_maximum_fusion), channel_id=1, source_target_pairs={{0,20},{1,29},{2,22},{3,31},{4,16},{5,25},{6,18},{7,27},{8,28},{9,... | collective-permute-start | bytes 196616 | tf_op jit(solution)/shard_map/ppermute | solution.py:64
  13.1 7.4 %collective-permute-start.4 = (bf16[2,64,256]{2,1,0:T(8,128)(2,1)S(1)}, bf16[2,64,256]{2,1,0:T(8,128)(2,1)S(1)}, u32[]{:S(2)}, u32[]{:S(2)}) collective-permute-start(bf16[2,64,256]{2,1,0:T(8,128)(2,1)S(1)} %pad_maximum_fusion), channel_id=1, source_target_pairs={{0,22},{1,31},{2,20},{3,29},{4,18},{5,27},{6,16},{7,25},{8,30},{9,... | collective-permute-start | bytes 196616 | tf_op jit(solution)/shard_map/ppermute | solution.py:64
  15.5 5.1 %collective-permute-start.5 = (bf16[2,64,256]{2,1,0:T(8,128)(2,1)S(1)}, bf16[2,64,256]{2,1,0:T(8,128)(2,1)S(1)}, u32[]{:S(2)}, u32[]{:S(2)}) collective-permute-start(bf16[2,64,256]{2,1,0:T(8,128)(2,1)S(1)} %pad_maximum_fusion), channel_id=1, source_target_pairs={{0,2},{1,17},{2,0},{3,19},{4,6},{5,21},{6,4},{7,23},{8,10},{9,25},... | collective-permute-start | bytes 196616 | tf_op jit(solution)/shard_map/ppermute | solution.py:64
  20.6 3.8 %collective-permute-start.7 = (bf16[11,64,256]{2,1,0:T(8,128)(2,1)S(1)}, bf16[11,64,256]{2,1,0:T(8,128)(2,1)S(1)}, u32[]{:S(2)}, u32[]{:S(2)}) collective-permute-start(bf16[11,64,256]{2,1,0:T(8,128)(2,1)S(1)} %constant_dynamic-update-slice_fusion.mine_ref), channel_id=1, source_target_pairs={{0,1},{1,0},{2,3},{3,2},{4,5},{5,4},{6,7},{7,6},{8,9},{9,8},{10,11... | collective-permute-start | bytes 1081352 | tf_op jit(solution)/shard_map/ppermute | solution.py:68
  24.4 15.9 %copy-start.1 = (bf16[11,64,256]{2,1,0:T(8,128)(2,1)}, bf16[11,64,256]{2,1,0:T(8,128)(2,1)S(1)}, u32[]{:S(2)}) copy-start(bf16[11,64,256]{2,1,0:T(8,128)(2,1)S(1)} %collective-permute-done.7.others_ref) | copy-start | bytes 1081348
  26.3 1.3 %collective-permute-start.8 = (bf16[64,256]{1,0:T(8,128)(2,1)S(1)}, bf16[64,256]{1,0:T(8,128)(2,1)S(1)}, u32[]{:S(2)}, u32[]{:S(2)}) collective-permute-start(bf16[64,256]{1,0:T(8,128)(2,1)S(1)} %shard_map.65), channel_id=1, source_target_pairs={{0,1},{1,0},{2,3},{3,2},{4,5},{5,4},{6,7},{7,6},{8,9},{9,8},{10,11... | collective-permute-start | bytes 98312 | tf_op jit(solution)/shard_map/ppermute | solution.py:68
  27.6 8.4 %collective-permute-start.9 = (bf16[2,64,256]{2,1,0:T(8,128)(2,1)S(1)}, bf16[2,64,256]{2,1,0:T(8,128)(2,1)S(1)}, u32[]{:S(2)}, u32[]{:S(2)}) collective-permute-start(bf16[2,64,256]{2,1,0:T(8,128)(2,1)S(1)} %pad_maximum_fusion.1), channel_id=1, source_target_pairs={{0,4},{1,13},{2,6},{3,15},{4,0},{5,9},{6,2},{7,11},{8,12},{9,5},{1... | collective-permute-start | bytes 196616 | tf_op jit(solution)/shard_map/ppermute | solution.py:64
  27.7 12.6 %collective-permute-start.14 = (bf16[64,256]{1,0:T(8,128)(2,1)S(1)}, bf16[64,256]{1,0:T(8,128)(2,1)S(1)}, u32[]{:S(2)}, u32[]{:S(2)}) collective-permute-start(bf16[64,256]{1,0:T(8,128)(2,1)S(1)} %shard_map.65), channel_id=1, source_target_pairs={{0,18},{1,19},{2,16},{3,17},{4,22},{5,23},{6,20},{7,21},{8,26},{9,... | collective-permute-start | bytes 98312 | tf_op jit(solution)/shard_map/ppermute | solution.py:64
  30.2 6.3 %collective-permute-start.10 = (bf16[2,64,256]{2,1,0:T(8,128)(2,1)S(1)}, bf16[2,64,256]{2,1,0:T(8,128)(2,1)S(1)}, u32[]{:S(2)}, u32[]{:S(2)}) collective-permute-start(bf16[2,64,256]{2,1,0:T(8,128)(2,1)S(1)} %pad_maximum_fusion.1), channel_id=1, source_target_pairs={{0,6},{1,15},{2,4},{3,13},{4,2},{5,11},{6,0},{7,9},{8,14},{9,7},{1... | collective-permute-start | bytes 196616 | tf_op jit(solution)/shard_map/ppermute | solution.py:64
  32.1 5.6 %collective-permute-start.11 = (bf16[2,64,256]{2,1,0:T(8,128)(2,1)S(1)}, bf16[2,64,256]{2,1,0:T(8,128)(2,1)S(1)}, u32[]{:S(2)}, u32[]{:S(2)}) collective-permute-start(bf16[2,64,256]{2,1,0:T(8,128)(2,1)S(1)} %pad_maximum_fusion.1), channel_id=1, source_target_pairs={{0,20},{1,29},{2,22},{3,31},{4,16},{5,25},{6,18},{7,27},{8,28},{9,... | collective-permute-start | bytes 196616 | tf_op jit(solution)/shard_map/ppermute | solution.py:64
  32.1 6.9 %collective-permute-start.12 = (bf16[2,64,256]{2,1,0:T(8,128)(2,1)S(1)}, bf16[2,64,256]{2,1,0:T(8,128)(2,1)S(1)}, u32[]{:S(2)}, u32[]{:S(2)}) collective-permute-start(bf16[2,64,256]{2,1,0:T(8,128)(2,1)S(1)} %pad_maximum_fusion.1), channel_id=1, source_target_pairs={{0,22},{1,31},{2,20},{3,29},{4,18},{5,27},{6,16},{7,25},{8,30},{9,... | collective-permute-start | bytes 196616 | tf_op jit(solution)/shard_map/ppermute | solution.py:64
  36.0 4.3 %collective-permute-start.13 = (bf16[2,64,256]{2,1,0:T(8,128)(2,1)S(1)}, bf16[2,64,256]{2,1,0:T(8,128)(2,1)S(1)}, u32[]{:S(2)}, u32[]{:S(2)}) collective-permute-start(bf16[2,64,256]{2,1,0:T(8,128)(2,1)S(1)} %pad_maximum_fusion.1), channel_id=1, source_target_pairs={{0,2},{1,17},{2,0},{3,19},{4,6},{5,21},{6,4},{7,23},{8,10},{9,25},... | collective-permute-start | bytes 196616 | tf_op jit(solution)/shard_map/ppermute | solution.py:64
  40.3 7.8 %collective-permute-start.15 = (bf16[11,64,256]{2,1,0:T(8,128)(2,1)S(1)}, bf16[11,64,256]{2,1,0:T(8,128)(2,1)}, u32[]{:S(2)}, u32[]{:S(2)}) collective-permute-start(bf16[11,64,256]{2,1,0:T(8,128)(2,1)S(1)} %constant_dynamic-update-slice_fusion.6.mine_ref), channel_id=1, source_target_pairs={{0,1},{1,0},{2,3},{3,2},{4,5},{5,4},{6,7},{7,6},{8,9},{9,8},{10,11... | collective-permute-start | bytes 1081352 | tf_op jit(solution)/shard_map/ppermute | solution.py:68
  44.6 1.0 %copy-start.2 = (bf16[11,64,256]{2,1,0:T(8,128)(2,1)S(1)}, bf16[11,64,256]{2,1,0:T(8,128)(2,1)}, u32[]{:S(2)}) copy-start(bf16[11,64,256]{2,1,0:T(8,128)(2,1)} %copy-done.1) | copy-start | bytes 1081348
  48.1 2.7 %copy-start.3 = (bf16[64,2048]{1,0:T(8,128)(2,1)}, bf16[64,2048]{1,0:T(8,128)(2,1)S(1)}, u32[]{:S(2)}) copy-start(bf16[64,2048]{1,0:T(8,128)(2,1)S(1)} %get-tuple-element.9.value_ref) | copy-start | bytes 786436
  48.1 2.8 %copy-start.5 = (f32[64,2048]{1,0:T(8,128)}, f32[64,2048]{1,0:T(8,128)S(1)}, u32[]{:S(2)}) copy-start(f32[64,2048]{1,0:T(8,128)S(1)} %get-tuple-element.10.rest_0_) | copy-start | bytes 1572868
  50.8 1.3 %collective-permute-start.16 = (bf16[64,256]{1,0:T(8,128)(2,1)S(1)}, bf16[64,256]{1,0:T(8,128)(2,1)S(1)}, u32[]{:S(2)}, u32[]{:S(2)}) collective-permute-start(bf16[64,256]{1,0:T(8,128)(2,1)S(1)} %shard_map.67), channel_id=1, source_target_pairs={{0,1},{1,0},{2,3},{3,2},{4,5},{5,4},{6,7},{7,6},{8,9},{9,8},{10,11... | collective-permute-start | bytes 98312 | tf_op jit(solution)/shard_map/ppermute | solution.py:68
  52.1 6.4 %collective-permute-start.17 = (bf16[2,64,256]{2,1,0:T(8,128)(2,1)S(1)}, bf16[2,64,256]{2,1,0:T(8,128)(2,1)S(1)}, u32[]{:S(2)}, u32[]{:S(2)}) collective-permute-start(bf16[2,64,256]{2,1,0:T(8,128)(2,1)S(1)} %pad_maximum_fusion.2), channel_id=1, source_target_pairs={{0,4},{1,13},{2,6},{3,15},{4,0},{5,9},{6,2},{7,11},{8,12},{9,5},{1... | collective-permute-start | bytes 196616 | tf_op jit(solution)/shard_map/ppermute | solution.py:64
  52.2 11.4 %collective-permute-start.22 = (bf16[64,256]{1,0:T(8,128)(2,1)S(1)}, bf16[64,256]{1,0:T(8,128)(2,1)S(1)}, u32[]{:S(2)}, u32[]{:S(2)}) collective-permute-start(bf16[64,256]{1,0:T(8,128)(2,1)S(1)} %shard_map.67), channel_id=1, source_target_pairs={{0,18},{1,19},{2,16},{3,17},{4,22},{5,23},{6,20},{7,21},{8,26},{9,... | collective-permute-start | bytes 98312 | tf_op jit(solution)/shard_map/ppermute | solution.py:64
  52.7 7.3 %collective-permute-start.18 = (bf16[2,64,256]{2,1,0:T(8,128)(2,1)S(1)}, bf16[2,64,256]{2,1,0:T(8,128)(2,1)S(1)}, u32[]{:S(2)}, u32[]{:S(2)}) collective-permute-start(bf16[2,64,256]{2,1,0:T(8,128)(2,1)S(1)} %pad_maximum_fusion.2), channel_id=1, source_target_pairs={{0,6},{1,15},{2,4},{3,13},{4,2},{5,11},{6,0},{7,9},{8,14},{9,7},{1... | collective-permute-start | bytes 196616 | tf_op jit(solution)/shard_map/ppermute | solution.py:64
  55.6 5.7 %collective-permute-start.19 = (bf16[2,64,256]{2,1,0:T(8,128)(2,1)S(1)}, bf16[2,64,256]{2,1,0:T(8,128)(2,1)S(1)}, u32[]{:S(2)}, u32[]{:S(2)}) collective-permute-start(bf16[2,64,256]{2,1,0:T(8,128)(2,1)S(1)} %pad_maximum_fusion.2), channel_id=1, source_target_pairs={{0,20},{1,29},{2,22},{3,31},{4,16},{5,25},{6,18},{7,27},{8,28},{9,... | collective-permute-start | bytes 196616 | tf_op jit(solution)/shard_map/ppermute | solution.py:64
  56.6 6.9 %collective-permute-start.20 = (bf16[2,64,256]{2,1,0:T(8,128)(2,1)S(1)}, bf16[2,64,256]{2,1,0:T(8,128)(2,1)S(1)}, u32[]{:S(2)}, u32[]{:S(2)}) collective-permute-start(bf16[2,64,256]{2,1,0:T(8,128)(2,1)S(1)} %pad_maximum_fusion.2), channel_id=1, source_target_pairs={{0,22},{1,31},{2,20},{3,29},{4,18},{5,27},{6,16},{7,25},{8,30},{9,... | collective-permute-start | bytes 196616 | tf_op jit(solution)/shard_map/ppermute | solution.py:64
  58.5 5.0 %collective-permute-start.21 = (bf16[2,64,256]{2,1,0:T(8,128)(2,1)S(1)}, bf16[2,64,256]{2,1,0:T(8,128)(2,1)S(1)}, u32[]{:S(2)}, u32[]{:S(2)}) collective-permute-start(bf16[2,64,256]{2,1,0:T(8,128)(2,1)S(1)} %pad_maximum_fusion.2), channel_id=1, source_target_pairs={{0,2},{1,17},{2,0},{3,19},{4,6},{5,21},{6,4},{7,23},{8,10},{9,25},... | collective-permute-start | bytes 196616 | tf_op jit(solution)/shard_map/ppermute | solution.py:64
  63.6 7.1 %collective-permute-start.23 = (bf16[11,64,256]{2,1,0:T(8,128)(2,1)S(1)}, bf16[11,64,256]{2,1,0:T(8,128)(2,1)}, u32[]{:S(2)}, u32[]{:S(2)}) collective-permute-start(bf16[11,64,256]{2,1,0:T(8,128)(2,1)S(1)} %constant_dynamic-update-slice_fusion.12.mine_ref), channel_id=1, source_target_pairs={{0,1},{1,0},{2,3},{3,2},{4,5},{5,4},{6,7},{7,6},{8,9},{9,8},{10,11... | collective-permute-start | bytes 1081352 | tf_op jit(solution)/shard_map/ppermute | solution.py:68
  65.7 0.9 %copy-start.4 = (bf16[64,2048]{1,0:T(8,128)(2,1)S(1)}, bf16[64,2048]{1,0:T(8,128)(2,1)}, u32[]{:S(2)}) copy-start(bf16[64,2048]{1,0:T(8,128)(2,1)} %copy-done.3) | copy-start | bytes 786436
  66.6 1.0 %copy-start.6 = (f32[64,2048]{1,0:T(8,128)S(1)}, f32[64,2048]{1,0:T(8,128)}, u32[]{:S(2)}) copy-start(f32[64,2048]{1,0:T(8,128)} %copy-done.5) | copy-start | bytes 1572868

commit v3 on v2

v3 whole, which is shorter than its diff:
```python
import functools

import jax
import jax.numpy as jnp
from jax import lax
from jax.experimental import pallas as pl
from jax.experimental.pallas import tpu as pltpu
from jax.sharding import PartitionSpec as P

PB = 64
TERMS = 3
FEATURES = 64
NEAR = 4
LANES = 2 * PB
AXES = ("gx", "gy", "gz")


def pairings(count):
    first = [(i, i ^ 1) for i in range(count)]
    second = [(i, (i + 1) % count if i % 2 else (i - 1) % count) for i in range(count)]
    return [first] if count == 2 else [first, second]


def partner_rank(here, step, count):
    forward = jnp.where(here % 2 == 0, 1, 2)
    backward = 3 - forward
    rank = jnp.where(step == 1, 0, jnp.where(step == 2, forward, backward))
    there = here + step - 1
    return rank, (there >= 0) & (there < count)


def place(rank, here, count):
    there = here if rank == 0 else dict(pairings(count)[rank - 1])[here]
    return there if abs(there - here) <= 1 else None


def partners():
    x_count = len(pairings(lax.axis_size("gx"))) + 1
    y_count = len(pairings(lax.axis_size("gy"))) + 1
    pair_count = lax.axis_size("gz") // 2
    chips = [(x, b) for x in range(x_count) for b in range(pair_count)]
    side = [(x, y, b) for x, b in chips for y in range(1, y_count)]
    return side + [(x, 0, b) for x, b in chips[1:]]


def partner_number(x, y, b):
    x_count = len(pairings(lax.axis_size("gx"))) + 1
    y_count = len(pairings(lax.axis_size("gy"))) + 1
    pair_count = lax.axis_size("gz") // 2
    chip = x * pair_count + b
    return jnp.where(
        y > 0, chip * (y_count - 1) + y - 1, x_count * pair_count * (y_count - 1) + chip - 1
    )


def swap(value, by_core):
    sizes = [lax.axis_size(name) for name in AXES]
    pairs = []
    for i in range(sizes[0]):
        for j in range(sizes[1]):
            for k in range(sizes[2]):
                x, y, b = by_core[k % 2]
                to = (place(x, i, sizes[0]), place(y, j, sizes[1]), (k // 2 ^ b) * 2 + k % 2)
                if None in to:
                    to = (i, j, (k // 2 ^ 1) * 2 + k % 2)
                pairs.append(
                    ((i * sizes[1] + j) * sizes[2] + k, (to[0] * sizes[1] + to[1]) * sizes[2] + to[2])
                )
    return lax.ppermute(value, AXES, pairs)


def swap_cores(value):
    return lax.ppermute(value, "gz", [(k, k ^ 1) for k in range(lax.axis_size("gz"))])


def exchange(rim, work):
    chips = partners()
    alone = [swap(rim, (chips[-1], chips[-1]))] if len(chips) % 2 else []
    other = swap_cores(rim)
    both = jnp.stack([rim, other])
    steps = reversed(range(0, len(chips) - len(chips) % 2, 2))
    shares = [swap(both, (chips[t], chips[t + 1])) for t in steps][::-1]
    received = jnp.concatenate(shares + [panel[None] for panel in alone])
    received, work = lax.optimization_barrier((received, work))
    return (received, swap_cores(received), other, rim), work


def source_index(slots, count, rim_count):
    layers = lax.axis_size("gz")
    x_at, y_at, z_at = (lax.axis_index(name) for name in AXES)
    rest = jnp.maximum(slots - count, 0)
    r = rest % rim_count
    m = (rest // rim_count) % layers
    c = (rest // (rim_count * layers)) % 3
    a = rest // (rim_count * layers * 3)
    x_rank, x_in = partner_rank(x_at, a, lax.axis_size("gx"))
    y_rank, y_in = partner_rank(y_at, c, lax.axis_size("gy"))
    flip = (m // 2) ^ (z_at // 2)
    chips = len(partners())
    core, target = z_at % 2, m % 2
    number = partner_number(x_rank, y_rank, flip)
    single = (number == chips - 1) if chips % 2 else jnp.zeros(number.shape, bool)
    holder = jnp.where(single, target, number % 2)
    panel = jnp.where(single, chips - 1, number // 2 * 2 + (target ^ holder))
    panel = panel + jnp.where(holder == core, 0, chips)
    here = (x_rank == 0) & (y_rank == 0) & (flip == 0)
    panel = jnp.where(here, 2 * chips + jnp.where(target == core, 1, 0), panel)
    zero = (2 * chips + 2) * rim_count
    far = jnp.where(x_in & y_in, panel * rim_count + r, zero)
    index = jnp.where(slots < count, slots, far)
    return index.astype(jnp.int32)


def left_half():
    return lax.broadcasted_iota(jnp.int32, (FEATURES, LANES), 1) < PB


def turn(pair):
    return jnp.concatenate([pair[:, PB:], pair[:, :PB]], axis=1)


def spread(pair, store, at):
    turned = turn(pair)
    store[at] = jnp.where(left_half(), pair, turned)
    store[at + 1] = jnp.where(left_half(), turned, pair)


def each_rim(rims, place_pair):
    mine_ref, others_ref, other_ref, own_ref = rims
    panels, _, rim = mine_ref.shape
    rim_count = rim // PB

    @pl.loop(0, panels)
    def _(panel):
        for t in range(rim // LANES):
            cut = slice(t * LANES, (t + 1) * LANES)
            at = panel * rim_count + 2 * t
            place_pair(mine_ref[panel, :, cut], at)
            place_pair(others_ref[panel, :, cut], at + panels * rim_count)

    for t in range(rim // LANES):
        cut = slice(t * LANES, (t + 1) * LANES)
        at = 2 * panels * rim_count + 2 * t
        place_pair(other_ref[:, cut], at)
        place_pair(own_ref[:, cut], at + rim_count)


def product(first, second, tile):
    both = lax.dot_general(
        jnp.concatenate([first, second], axis=0),
        tile,
        (((1,), (1,)), ((), ())),
        preferred_element_type=jnp.float32,
    )
    return jnp.where(left_half(), both[:FEATURES], both[FEATURES:])


def picked(store, index_ref, at):
    return jnp.concatenate(
        [
            jnp.where(left_half(), store[index_ref[at + k]], store[index_ref[at + k + 1]])
            for k in range(0, NEAR, 2)
        ],
        axis=1,
    )


def near_image(index_ref, store, tile_ref, near_out):
    slot_count = tile_ref.shape[1] // PB
    for t in range(near_out.shape[1] // LANES):
        at = pl.ds(t * LANES, LANES)
        near_out[:, at] = product(
            picked(store, index_ref, 2 * t * slot_count),
            picked(store, index_ref, (2 * t + 1) * slot_count),
            tile_ref[at, : NEAR * PB],
        )


def first_kernel(index_ref, value_ref, raw_ref, scale_ref, live_ref, tile_out, near_out, store):
    count, slot_count = scale_ref.shape
    used = lax.broadcasted_iota(jnp.int32, (count, slot_count), 1) < live_ref[...]
    weights = jnp.where(used, scale_ref[...], 0.0)
    lanes = jnp.concatenate(
        [jnp.broadcast_to(weights[:, k : k + 1], (count, PB)) for k in range(slot_count)], axis=1
    )
    for b in range(count):
        at = pl.ds(b * PB, PB)
        scaled = raw_ref[at, :].astype(jnp.float32) * lanes[b : b + 1, :]
        tile_out[at, :] = scaled.astype(tile_out.dtype)
    for t in range(value_ref.shape[1] // LANES):
        spread(value_ref[:, t * LANES : (t + 1) * LANES], store, 2 * t)
    near_image(index_ref, store, tile_out, near_out)


def rim_kernel(index_ref, *refs):
    rims, (tile_ref, near_ref, rim_out, store) = refs[:4], refs[4:]
    slot_count = tile_ref.shape[1] // PB

    def keep(pair, number):
        store[number // 2] = pair

    each_rim(rims, keep)
    store[store.shape[0] - 1] = jnp.zeros(store.shape[1:], store.dtype)

    def sources(row):
        base = row * slot_count + NEAR
        parts = []
        for k in range(0, NEAR, 2):
            halves = []
            for side in range(2):
                number = index_ref[base + k + side]
                pair = store[number // 2]
                halves.append(jnp.where(number % 2 == side, pair, turn(pair)))
            parts.append(jnp.where(left_half(), halves[0], halves[1]))
        return jnp.concatenate(parts, axis=1)

    for t in range(rim_out.shape[1] // LANES):
        at = pl.ds(t * LANES, LANES)
        far = product(sources(2 * t), sources(2 * t + 1), tile_ref[at, NEAR * PB :])
        rim_out[:, at] = (near_ref[:, at] + far).astype(rim_out.dtype)


def far_kernel(step, last, index_ref, *refs):
    rims, (tile_ref, near_ref, total_ref, times_ref) = refs[:4], refs[4:8]
    if last:
        total_out, store = refs[8:]
    else:
        total_out, near_out, store, own_store = refs[8:]
    slot_count = tile_ref.shape[1] // PB
    each_rim(rims, lambda pair, number: spread(pair, store, number))
    store[store.shape[0] - 1] = jnp.zeros(store.shape[1:], store.dtype)
    factor = jnp.ones(times_ref.shape, jnp.float32)
    for n in range(1, step + 1):
        factor = factor * -times_ref[...] / jnp.float32(n)
    for t in range(near_ref.shape[1] // LANES):
        at = pl.ds(t * LANES, LANES)
        image = near_ref[:, at] + product(
            picked(store, index_ref, 2 * t * slot_count + NEAR),
            picked(store, index_ref, (2 * t + 1) * slot_count + NEAR),
            tile_ref[at, NEAR * PB :],
        )
        total = total_ref[:, at].astype(jnp.float32) + factor * image
        total_out[:, at] = total.astype(total_out.dtype)
        if not last:
            spread(image.astype(jnp.bfloat16), own_store, 2 * t)
    if not last:
        near_image(index_ref, own_store, tile_ref, near_out)


def call(kernel, out_shape, scratch, flops, index, *arrays):
    vmem = pl.BlockSpec(memory_space=pltpu.VMEM)
    return pl.pallas_call(
        kernel,
        out_shape=out_shape,
        in_specs=[pl.BlockSpec(memory_space=pltpu.SMEM)] + [vmem] * len(arrays),
        out_specs=jax.tree.map(lambda _: vmem, out_shape),
        scratch_shapes=[pltpu.VMEM(shape, jnp.bfloat16) for shape in scratch],
        compiler_params=pltpu.CompilerParams(vmem_limit_bytes=16 * 1024 * 1024),
        cost_estimate=pl.CostEstimate(flops=flops, bytes_accessed=flops // 64, transcendentals=0),
    )(index, *arrays)


def body(features, tiles, scales, slots, live, times):
    count, width = tiles.shape[2], tiles.shape[4]
    slot_count = scales.shape[3]
    rim_count = max(1, count // 8)
    points = count * PB
    value = features.reshape(FEATURES, points)
    rim = value[:, : rim_count * PB]
    index = source_index(slots.reshape(count * slot_count), count, rim_count)
    image_shape = jax.ShapeDtypeStruct(value.shape, jnp.float32)
    rim_shape = jax.ShapeDtypeStruct(rim.shape, jnp.bfloat16)
    own_store = (count, FEATURES, LANES)
    rims_held = 2 * len(partners()) + 2
    far_store = (rims_held * rim_count + 1, FEATURES, LANES)
    pair_store = (rims_held * rim_count // 2 + 1, FEATURES, LANES)
    half = FEATURES * points * width
    scaled, near = call(
        first_kernel,
        (jax.ShapeDtypeStruct((points, width), jnp.bfloat16), image_shape),
        [own_store],
        half,
        index,
        value,
        tiles.reshape(points, width),
        scales.reshape(count, slot_count),
        live.reshape(count, 1),
    )
    times = times[:, None]
    total = value
    for step in range(1, TERMS + 1):
        rims, (scaled, near, total) = exchange(rim, (scaled, near, total))
        if step < TERMS:
            rim = call(rim_kernel, rim_shape, [pair_store], half // 8, index, *rims, scaled, near)
        last = step == TERMS
        out = call(
            functools.partial(far_kernel, step, last),
            jax.ShapeDtypeStruct(value.shape, jnp.bfloat16) if last else (image_shape,) * 2,
            [far_store] if last else [far_store, own_store],
            half if last else 2 * half,
            index,
            *rims,
            scaled,
            near,
            total,
            times,
        )
        if not last:
            total, near = out
    return out.reshape(features.shape)


def solution(mesh):
    return jax.shard_map(
        body,
        mesh=mesh,
        in_specs=(
            P(None, "gx", "gy", "gz"),
            P("gx", "gy", "gz", None, None),
            P("gx", "gy", "gz", None),
            P("gx", "gy", "gz", None),
            P("gx", "gy", "gz"),
            P(),
        ),
        out_specs=P(None, "gx", "gy", "gz"),
        check_vma=False,
    )
```

time: 74.9 us -> 65.8 us (0.88)
  other arithmetic: 7.31 us -> 0.7 us
  starting transfers between devices: 34.4 us -> 27.8 us
  waiting for transfers between devices: 13.9 us -> 17.3 us
  local copies, waits for them, and re-layouts: 4.63 us -> 7.63 us
  Pallas kernels: 13.8 us -> 11.9 us
    convert_element_type x3 -> x0, other arithmetic: 7.23 us -> none  [the longest x1 4.13 us: body(): tiles.reshape(count, PB, width).astype(jnp.float32) * lanes[:, None, :]]
    ppermute x6, starting transfers between devices: 7.57 us -> 1.07 us  [swap_cores(): lax.ppermute(value, 'gz', [(k, k ^ 1) for k in range(lax.axis_size('gz'))])]
    ppermute x6, waiting for transfers between devices: 2.21 us -> 7.13 us  [swap_cores(): lax.ppermute(value, 'gz', [(k, k ^ 1) for k in range(lax.axis_size('gz'))])]
    unnamed x38 -> x25, local copies, waits for them, and re-layouts: 3.17 us -> 5.94 us
    pallas_call x5 -> x6, Pallas kernels: 13.8 us -> 11.9 us  [call(): pl.pallas_call(kernel, out_shape=out_shape, in_specs=[pl.BlockSpec(memory...]
    ppermute x18, waiting for transfers between devices: 11.7 us -> 10.1 us  [swap(): return lax.ppermute(value, AXES, pairs)]
  transfers between devices with their start and end apart: 24 -> 24, of which waited for: 11 -> 15; matrix products, arithmetic and copies ran while one was open for 11% -> 5% of each run, Pallas kernels for 7% -> 10%
where the time goes in v3:
time: 65.8 us; the launch traced here: 65.4 us
  starting transfers between devices  27.8 us (42%)
  waiting for transfers between devices  17.3 us (26%)
  Pallas kernels  11.9 us (18%)
  local copies, waits for them, and re-layouts  7.63 us (12%)
  other arithmetic  0.7 us (1%)
    ppermute x18, starting transfers between devices, swap(): return lax.ppermute(value, AXES, pairs)  26.7 us
    pallas_call x6, Pallas kernels, call(): pl.pallas_call(kernel, out_shape=out_shape, in_specs=[pl.BlockSpec(memory...  11.9 us
    ppermute x18, waiting for transfers between devices, swap(): return lax.ppermute(value, AXES, pairs)  10.1 us
    ppermute x6, waiting for transfers between devices, swap_cores(): lax.ppermute(value, 'gz', [(k, k ^ 1) for k in range(lax.axis_size('gz'))])  7.13 us
    unnamed x25, local copies, waits for them, and re-layouts  5.94 us
  transfers between devices with their start and end apart: 24, of which 15 were waited for; matrix products, arithmetic and copies ran while one was open for 5% of the time, Pallas kernels for 10%

profile of v3, /device:TPU:0, one launch (start us, length us, event | category | flops | bytes accessed | tf_op | source)
XLA Modules:
  0.0 65.4 jit_solution(16903465369909471872)
XLA Ops:
  0.0 0.8 %slice_bitcast_fusion = (bf16[1,64,256]{2,1,0:T(8,128)(2,1)S(1)}, bf16[64,256]{1,0:T(8,128)(2,1)S(1)}) fusion(bf16[64,2048]{1,0:T(8,128)(2,1)} %bitcast.22), kind=kLoop, calls=%fused_computation.55 | loop fusion | bytes 98304 | tf_op jit(solution)/shard_map/stack | solution.py:80
  0.8 0.5 collective-permute-start
  1.2 3.4 %collective-permute-start.6 = (bf16[64,256]{1,0:T(8,128)(2,1)S(1)}, bf16[64,256]{1,0:T(8,128)(2,1)S(1)}, u32[]{:S(2)}, u32[]{:S(2)}) collective-permute-start(bf16[64,256]{1,0:T(8,128)(2,1)S(1)} %get-tuple-element.42.refs_3_), channel_id=1, source_target_pairs={{0,18},{1,19},{2,16},{3,17},{4,22},{5,23},{6,20},{7,21},{8,26},{9,... | collective-permute-start | bytes 98312 | tf_op jit(solution)/shard_map/ppermute | solution.py:69
  4.7 0.8 %copy.12 = s32[1,1,32,8]{3,2,1,0:T(8,128)S(1)} copy(s32[1,1,32,8]{2,3,1,0:T(8,128)} %param.9) | data formatting | bytes 2048 | tf_op args[3]
  5.4 0.1 reshape.18
  5.5 0.0 collective-permute-done.refs_2_
  5.6 1.6 %collective-permute-start.1 = (bf16[2,64,256]{2,1,0:T(8,128)(2,1)S(1)}, bf16[2,64,256]{2,1,0:T(8,128)(2,1)S(1)}, u32[]{:S(2)}, u32[]{:S(2)}) collective-permute-start(bf16[2,64,256]{2,1,0:T(8,128)(2,1)S(1)} %pad_maximum_fusion), channel_id=1, source_target_pairs={{0,4},{1,3},{2,6},{3,1},{4,0},{5,9},{6,2},{7,11},{8,12},{9,5},{10,... | collective-permute-start | bytes 196616 | tf_op jit(solution)/shard_map/ppermute | solution.py:69
  7.2 0.8 %copy.13 = f32[1,1,32,8]{3,2,1,0:T(8,128)S(1)} copy(f32[1,1,32,8]{2,3,1,0:T(8,128)} %param.8) | data formatting | bytes 2048 | tf_op args[2]
  8.0 0.7 %copy.14.live_ref = s32[32,1]{1,0:T(8,128)S(1)} copy(s32[32,1]{0,1:T(1,128)} %bitcast.32) | data formatting | bytes 256 | tf_op jit(solution)/shard_map/reshape | solution.py:287
  8.7 1.6 %copy-done = bf16[1,1,32,64,512]{4,3,2,1,0:T(8,128)(2,1)S(1)} copy-done((bf16[1,1,32,64,512]{4,3,2,1,0:T(8,128)(2,1)S(1)}, bf16[1,1,32,64,512]{4,3,2,1,0:T(8,128)(2,1)}, u32[]{:S(2)}) %copy-start) | copy-done | bytes 2097176
  10.3 0.9 %copy-done.1 = bf16[64,1,1,2048]{3,0,2,1:T(8,128)(2,1)S(1)} copy-done((bf16[64,1,1,2048]{3,0,2,1:T(8,128)(2,1)S(1)}, bf16[64,1,1,2048]{3,0,2,1:T(8,128)(2,1)}, u32[]{:S(2)}) %copy-start.1) | copy-done | bytes 262168
  11.3 1.5 %shard_map.64 = (bf16[2048,512]{1,0:T(8,128)(2,1)S(1)}, f32[64,2048]{1,0:T(8,128)S(1)}) custom-call(s32[256]{0:T(256)S(1)} %compare_select_fusion.index_ref, bf16[64,2048]{1,0:T(8,128)(2,1)S(1)} %bitcast.23, bf16[2048,512]{1,0:T(8,128)(2,1)S(1)} %bitcast.21, f32[32,8]{1,0:T(8,128)S(1)} %bitcast.30, s32[32,1]{1,0:T(8,128)S(1)} %copy.14.live_ref), custom_call_target="tpu_custom_call" | custom-call | flops 67108864 | bytes 1048576 | tf_op jit(solution)/shard_map/pallas_call | solution.py:252
  12.8 0.5 collective-permute-start.2
  13.3 1.5 %collective-permute-start.3 = (bf16[2,64,256]{2,1,0:T(8,128)(2,1)S(1)}, bf16[2,64,256]{2,1,0:T(8,128)(2,1)S(1)}, u32[]{:S(2)}, u32[]{:S(2)}) collective-permute-start(bf16[2,64,256]{2,1,0:T(8,128)(2,1)S(1)} %pad_maximum_fusion), channel_id=1, source_target_pairs={{0,20},{1,3},{2,22},{3,1},{4,16},{5,25},{6,18},{7,27},{8,28},{9,21... | collective-permute-start | bytes 196616 | tf_op jit(solution)/shard_map/ppermute | solution.py:69
  14.8 2.3 %collective-permute-start.4 = (bf16[2,64,256]{2,1,0:T(8,128)(2,1)S(1)}, bf16[2,64,256]{2,1,0:T(8,128)(2,1)S(1)}, u32[]{:S(2)}, u32[]{:S(2)}) collective-permute-start(bf16[2,64,256]{2,1,0:T(8,128)(2,1)S(1)} %pad_maximum_fusion), channel_id=1, source_target_pairs={{0,22},{1,3},{2,20},{3,1},{4,18},{5,27},{6,16},{7,25},{8,30},{9,23... | collective-permute-start | bytes 196616 | tf_op jit(solution)/shard_map/ppermute | solution.py:69
  17.2 0.0 collective-permute-done.1
  17.2 0.5 collective-permute-start.5
  17.7 0.3 collective-permute-done.2
  18.1 0.4 collective-permute-done.3
  18.5 2.4 %collective-permute-done.4 = bf16[2,64,256]{2,1,0:T(8,128)(2,1)S(1)} collective-permute-done((bf16[2,64,256]{2,1,0:T(8,128)(2,1)S(1)}, bf16[2,64,256]{2,1,0:T(8,128)(2,1)S(1)}, u32[]{:S(2)}, u32[]{:S(2)}) %collective-permute-start.4) | collective-permute-done | bytes 65568 | tf_op jit(solution)/shard_map/ppermute | solution.py:69
  20.9 0.7 %collective-permute-done.5 = bf16[2,64,256]{2,1,0:T(8,128)(2,1)S(1)} collective-permute-done((bf16[2,64,256]{2,1,0:T(8,128)(2,1)S(1)}, bf16[2,64,256]{2,1,0:T(8,128)(2,1)S(1)}, u32[]{:S(2)}, u32[]{:S(2)}) %collective-permute-start.5) | collective-permute-done | bytes 65568 | tf_op jit(solution)/shard_map/ppermute | solution.py:69
  21.7 0.0 collective-permute-done.6
  21.7 0.1 collective-permute-start.7
  21.8 1.7 %collective-permute-done.7.refs_1_ = bf16[11,64,256]{2,1,0:T(8,128)(2,1)S(1)} collective-permute-done((bf16[11,64,256]{2,1,0:T(8,128)(2,1)S(1)}, bf16[11,64,256]{2,1,0:T(8,128)(2,1)S(1)}, u32[]{:S(2)}, u32[]{:S(2)}) %collective-permute-start.7) | collective-permute-done | bytes 360480 | tf_op jit(solution)/shard_map/ppermute | solution.py:73
  23.4 1.2 %shard_map.65.refs_3_ = bf16[64,256]{1,0:T(8,128)(2,1)S(1)} custom-call(s32[256]{0:T(256)S(1)} %compare_select_fusion.index_ref, bf16[11,64,256]{2,1,0:T(8,128)(2,1)S(1)} %constant_dynamic-update-slice_fusion.refs_0_, bf16[11,64,256]{2,1,0:T(8,128)(2,1)S(1)} %collective-permute-done.7.refs_1_, bf16[64,256]{1,0:T(8,128)(2,1)S(1)} %collective-permute-done.refs_2_, ...), custom_call_target="tpu_custom_call" | custom-call | flops 8388608 | bytes 131072 | tf_op jit(solution)/shard_map/pallas_call | solution.py:252
  24.6 0.2 collective-permute-start.8
  24.8 1.1 %collective-permute-done.8.refs_2_ = bf16[64,256]{1,0:T(8,128)(2,1)S(1)} collective-permute-done((bf16[64,256]{1,0:T(8,128)(2,1)S(1)}, bf16[64,256]{1,0:T(8,128)(2,1)S(1)}, u32[]{:S(2)}, u32[]{:S(2)}) %collective-permute-start.8) | collective-permute-done | bytes 32800 | tf_op jit(solution)/shard_map/ppermute | solution.py:73
  25.9 0.6 pad_maximum_fusion.1
  26.5 1.4 %collective-permute-start.9 = (bf16[2,64,256]{2,1,0:T(8,128)(2,1)}, bf16[2,64,256]{2,1,0:T(8,128)(2,1)}, u32[]{:S(2)}, u32[]{:S(2)}) collective-permute-start(bf16[2,64,256]{2,1,0:T(8,128)(2,1)} %pad_maximum_fusion.1), channel_id=1, source_target_pairs={{0,4},{1,3},{2,6},{3,1},{4,0},{5,9},{6,2},{7,11},{8,12},{9,5},{10,... | collective-permute-start | bytes 196616 | tf_op jit(solution)/shard_map/ppermute | solution.py:69
  27.9 0.1 copy.15.refs_7_
  28.0 1.1 %collective-permute-start.14 = (bf16[64,256]{1,0:T(8,128)(2,1)S(1)}, bf16[64,256]{1,0:T(8,128)(2,1)S(1)}, u32[]{:S(2)}, u32[]{:S(2)}) collective-permute-start(bf16[64,256]{1,0:T(8,128)(2,1)S(1)} %shard_map.65.refs_3_), channel_id=1, source_target_pairs={{0,18},{1,19},{2,16},{3,17},{4,22},{5,23},{6,20},{7,21},{8,26},{9,... | collective-permute-start | bytes 98312 | tf_op jit(solution)/shard_map/ppermute | solution.py:69
  29.1 0.9 %copy-done.2 = bf16[64,1,1,2048]{3,0,2,1:T(8,128)(2,1)S(1)} copy-done((bf16[64,1,1,2048]{3,0,2,1:T(8,128)(2,1)S(1)}, bf16[64,1,1,2048]{3,0,2,1:T(8,128)(2,1)}, u32[]{:S(2)}) %copy-start.2) | copy-done | bytes 262168
  30.0 2.6 %shard_map.66 = (f32[64,2048]{1,0:T(8,128)S(1)}, f32[64,2048]{1,0:T(8,128)S(1)}) custom-call(s32[256]{0:T(256)S(1)} %compare_select_fusion.index_ref, bf16[11,64,256]{2,1,0:T(8,128)(2,1)S(1)} %constant_dynamic-update-slice_fusion.refs_0_, bf16[11,64,256]{2,1,0:T(8,128)(2,1)S(1)} %collective-permute-done.7.refs_1_, ...), custom_call_target="tpu_custom_call" | custom-call | flops 134217728 | bytes 2097152 | tf_op jit(solution)/shard_map/pallas_call | solution.py:252
  32.6 1.4 %collective-permute-start.10 = (bf16[2,64,256]{2,1,0:T(8,128)(2,1)}, bf16[2,64,256]{2,1,0:T(8,128)(2,1)S(1)}, u32[]{:S(2)}, u32[]{:S(2)}) collective-permute-start(bf16[2,64,256]{2,1,0:T(8,128)(2,1)} %pad_maximum_fusion.1), channel_id=1, source_target_pairs={{0,6},{1,3},{2,4},{3,1},{4,2},{5,11},{6,0},{7,9},{8,14},{9,7},{10,... | collective-permute-start | bytes 196616 | tf_op jit(solution)/shard_map/ppermute | solution.py:69
  34.0 2.0 %collective-permute-start.11 = (bf16[2,64,256]{2,1,0:T(8,128)(2,1)}, bf16[2,64,256]{2,1,0:T(8,128)(2,1)S(1)}, u32[]{:S(2)}, u32[]{:S(2)}) collective-permute-start(bf16[2,64,256]{2,1,0:T(8,128)(2,1)} %pad_maximum_fusion.1), channel_id=1, source_target_pairs={{0,20},{1,3},{2,22},{3,1},{4,16},{5,25},{6,18},{7,27},{8,28},{9,21... | collective-permute-start | bytes 196616 | tf_op jit(solution)/shard_map/ppermute | solution.py:69
  36.0 1.9 %collective-permute-start.12 = (bf16[2,64,256]{2,1,0:T(8,128)(2,1)}, bf16[2,64,256]{2,1,0:T(8,128)(2,1)S(1)}, u32[]{:S(2)}, u32[]{:S(2)}) collective-permute-start(bf16[2,64,256]{2,1,0:T(8,128)(2,1)} %pad_maximum_fusion.1), channel_id=1, source_target_pairs={{0,22},{1,3},{2,20},{3,1},{4,18},{5,27},{6,16},{7,25},{8,30},{9,23... | collective-permute-start | bytes 196616 | tf_op jit(solution)/shard_map/ppermute | solution.py:69
  37.9 0.0 collective-permute-done.9
  37.9 0.4 collective-permute-start.13
  38.4 0.8 %constant_dynamic-update-slice_fusion.11 = bf16[11,64,256]{2,1,0:T(8,128)(2,1)S(1)} fusion(bf16[2,64,256]{2,1,0:T(8,128)(2,1)} %collective-permute-done.9), kind=kLoop, calls=%fused_computation.14 | loop fusion | bytes 131072
  39.2 0.0 collective-permute-done.10
  39.2 0.1 collective-permute-done.11
  39.4 3.0 %collective-permute-done.12 = bf16[2,64,256]{2,1,0:T(8,128)(2,1)S(1)} collective-permute-done((bf16[2,64,256]{2,1,0:T(8,128)(2,1)}, bf16[2,64,256]{2,1,0:T(8,128)(2,1)S(1)}, u32[]{:S(2)}, u32[]{:S(2)}) %collective-permute-start.12) | collective-permute-done | bytes 65568 | tf_op jit(solution)/shard_map/ppermute | solution.py:69
  42.3 0.1 collective-permute-done.13
  42.4 0.0 collective-permute-done.14
  42.4 0.1 collective-permute-start.15
  42.5 1.7 %collective-permute-done.15.refs_1_ = bf16[11,64,256]{2,1,0:T(8,128)(2,1)S(1)} collective-permute-done((bf16[11,64,256]{2,1,0:T(8,128)(2,1)S(1)}, bf16[11,64,256]{2,1,0:T(8,128)(2,1)S(1)}, u32[]{:S(2)}, u32[]{:S(2)}) %collective-permute-start.15) | collective-permute-done | bytes 360480 | tf_op jit(solution)/shard_map/ppermute | solution.py:73
  44.2 1.2 %shard_map.67.refs_3_ = bf16[64,256]{1,0:T(8,128)(2,1)S(1)} custom-call(s32[256]{0:T(256)S(1)} %compare_select_fusion.index_ref, bf16[11,64,256]{2,1,0:T(8,128)(2,1)S(1)} %constant_dynamic-update-slice_fusion.6.refs_0_, bf16[11,64,256]{2,1,0:T(8,128)(2,1)S(1)} %collective-permute-done.15.refs_1_, bf16[64,256]{1,0:T(8,128)(2,1)S(1)} %collective-permute-done.8.refs_2_, ...), custom_call_target="tpu_custom_call" | custom-call | flops 8388608 | bytes 131072 | tf_op jit(solution)/shard_map/pallas_call | solution.py:252
  45.3 0.2 collective-permute-start.16
  45.5 1.1 %collective-permute-done.16.refs_2_ = bf16[64,256]{1,0:T(8,128)(2,1)S(1)} collective-permute-done((bf16[64,256]{1,0:T(8,128)(2,1)S(1)}, bf16[64,256]{1,0:T(8,128)(2,1)S(1)}, u32[]{:S(2)}, u32[]{:S(2)}) %collective-permute-start.16) | collective-permute-done | bytes 32800 | tf_op jit(solution)/shard_map/ppermute | solution.py:73
  46.6 0.7 %collective-permute-start.17 = (bf16[2,64,256]{2,1,0:T(8,128)(2,1)S(1)}, bf16[2,64,256]{2,1,0:T(8,128)(2,1)S(1)}, u32[]{:S(2)}, u32[]{:S(2)}) collective-permute-start(bf16[2,64,256]{2,1,0:T(8,128)(2,1)S(1)} %pad_maximum_fusion.2), channel_id=1, source_target_pairs={{0,4},{1,3},{2,6},{3,1},{4,0},{5,9},{6,2},{7,11},{8,12},{9,5},{10,... | collective-permute-start | bytes 196616 | tf_op jit(solution)/shard_map/ppermute | solution.py:69
  47.3 1.8 %collective-permute-start.22 = (bf16[64,256]{1,0:T(8,128)(2,1)S(1)}, bf16[64,256]{1,0:T(8,128)(2,1)S(1)}, u32[]{:S(2)}, u32[]{:S(2)}) collective-permute-start(bf16[64,256]{1,0:T(8,128)(2,1)S(1)} %shard_map.67.refs_3_), channel_id=1, source_target_pairs={{0,18},{1,19},{2,16},{3,17},{4,22},{5,23},{6,20},{7,21},{8,26},{9,... | collective-permute-start | bytes 98312 | tf_op jit(solution)/shard_map/ppermute | solution.py:69
  49.2 2.6 %shard_map.68 = (f32[64,2048]{1,0:T(8,128)S(1)}, f32[64,2048]{1,0:T(8,128)S(1)}) custom-call(s32[256]{0:T(256)S(1)} %compare_select_fusion.index_ref, bf16[11,64,256]{2,1,0:T(8,128)(2,1)S(1)} %constant_dynamic-update-slice_fusion.6.refs_0_, bf16[11,64,256]{2,1,0:T(8,128)(2,1)S(1)} %collective-permute-done.15.refs_1_, ...), custom_call_target="tpu_custom_call" | custom-call | flops 134217728 | bytes 2097152 | tf_op jit(solution)/shard_map/pallas_call | solution.py:252
  51.8 1.7 %collective-permute-start.18 = (bf16[2,64,256]{2,1,0:T(8,128)(2,1)S(1)}, bf16[2,64,256]{2,1,0:T(8,128)(2,1)S(1)}, u32[]{:S(2)}, u32[]{:S(2)}) collective-permute-start(bf16[2,64,256]{2,1,0:T(8,128)(2,1)S(1)} %pad_maximum_fusion.2), channel_id=1, source_target_pairs={{0,6},{1,3},{2,4},{3,1},{4,2},{5,11},{6,0},{7,9},{8,14},{9,7},{10,... | collective-permute-start | bytes 196616 | tf_op jit(solution)/shard_map/ppermute | solution.py:69
  53.4 0.9 %collective-permute-start.19 = (bf16[2,64,256]{2,1,0:T(8,128)(2,1)S(1)}, bf16[2,64,256]{2,1,0:T(8,128)(2,1)S(1)}, u32[]{:S(2)}, u32[]{:S(2)}) collective-permute-start(bf16[2,64,256]{2,1,0:T(8,128)(2,1)S(1)} %pad_maximum_fusion.2), channel_id=1, source_target_pairs={{0,20},{1,3},{2,22},{3,1},{4,16},{5,25},{6,18},{7,27},{8,28},{9,21... | collective-permute-start | bytes 196616 | tf_op jit(solution)/shard_map/ppermute | solution.py:69
  54.4 2.2 %collective-permute-start.20 = (bf16[2,64,256]{2,1,0:T(8,128)(2,1)S(1)}, bf16[2,64,256]{2,1,0:T(8,128)(2,1)S(1)}, u32[]{:S(2)}, u32[]{:S(2)}) collective-permute-start(bf16[2,64,256]{2,1,0:T(8,128)(2,1)S(1)} %pad_maximum_fusion.2), channel_id=1, source_target_pairs={{0,22},{1,3},{2,20},{3,1},{4,18},{5,27},{6,16},{7,25},{8,30},{9,23... | collective-permute-start | bytes 196616 | tf_op jit(solution)/shard_map/ppermute | solution.py:69
  56.6 0.0 collective-permute-done.17
  56.6 1.2 %collective-permute-start.21 = (bf16[2,64,256]{2,1,0:T(8,128)(2,1)S(1)}, bf16[2,64,256]{2,1,0:T(8,128)(2,1)S(1)}, u32[]{:S(2)}, u32[]{:S(2)}) collective-permute-start(bf16[2,64,256]{2,1,0:T(8,128)(2,1)S(1)} %pad_maximum_fusion.2), channel_id=1, source_target_pairs={{0,2},{1,17},{2,0},{3,19},{4,6},{5,21},{6,4},{7,23},{8,10},{9,25},... | collective-permute-start | bytes 196616 | tf_op jit(solution)/shard_map/ppermute | solution.py:69
  57.8 0.0 collective-permute-done.18
  57.8 0.7 %collective-permute-done.19 = bf16[2,64,256]{2,1,0:T(8,128)(2,1)S(1)} collective-permute-done((bf16[2,64,256]{2,1,0:T(8,128)(2,1)S(1)}, bf16[2,64,256]{2,1,0:T(8,128)(2,1)S(1)}, u32[]{:S(2)}, u32[]{:S(2)}) %collective-permute-start.19) | collective-permute-done | bytes 65568 | tf_op jit(solution)/shard_map/ppermute | solution.py:69
  58.6 1.8 %collective-permute-done.20 = bf16[2,64,256]{2,1,0:T(8,128)(2,1)S(1)} collective-permute-done((bf16[2,64,256]{2,1,0:T(8,128)(2,1)S(1)}, bf16[2,64,256]{2,1,0:T(8,128)(2,1)S(1)}, u32[]{:S(2)}, u32[]{:S(2)}) %collective-permute-start.20) | collective-permute-done | bytes 65568 | tf_op jit(solution)/shard_map/ppermute | solution.py:69
  60.4 0.4 collective-permute-done.21
  60.9 0.1 collective-permute-start.23
  61.0 1.7 %collective-permute-done.23.refs_1_ = bf16[11,64,256]{2,1,0:T(8,128)(2,1)S(1)} collective-permute-done((bf16[11,64,256]{2,1,0:T(8,128)(2,1)S(1)}, bf16[11,64,256]{2,1,0:T(8,128)(2,1)S(1)}, u32[]{:S(2)}, u32[]{:S(2)}) %collective-permute-start.23) | collective-permute-done | bytes 360480 | tf_op jit(solution)/shard_map/ppermute | solution.py:73
  62.6 2.8 %shard_map.69 = bf16[64,2048]{1,0:T(8,128)(2,1)} custom-call(s32[256]{0:T(256)S(1)} %compare_select_fusion.index_ref, bf16[11,64,256]{2,1,0:T(8,128)(2,1)S(1)} %constant_dynamic-update-slice_fusion.12.refs_0_, bf16[11,64,256]{2,1,0:T(8,128)(2,1)S(1)} %collective-permute-done.23.refs_1_, bf16[64,256]{1,0:T(8,128)(2,1)S(1)} %collective-permute-done.16.refs_2_, ...), custom_call_target="tpu_custom_call" | custom-call | flops 67108864 | bytes 1048576 | tf_op jit(solution)/shard_map/pallas_call | solution.py:252
  (26 shorter events, 0.2 us)
Async XLA Ops:
  0.8 4.8 %collective-permute-start = (bf16[64,256]{1,0:T(8,128)(2,1)S(1)}, bf16[64,256]{1,0:T(8,128)(2,1)S(1)}, u32[]{:S(2)}, u32[]{:S(2)}) collective-permute-start(bf16[64,256]{1,0:T(8,128)(2,1)S(1)} %get-tuple-element.42.refs_3_), channel_id=1, source_target_pairs={{0,1},{1,0},{2,3},{3,2},{4,5},{5,4},{6,7},{7,6},{8,9},{9,8},{10,11... | collective-permute-start | bytes 98312 | tf_op jit(solution)/shard_map/ppermute | solution.py:73
  1.2 20.4 %collective-permute-start.6 = (bf16[64,256]{1,0:T(8,128)(2,1)S(1)}, bf16[64,256]{1,0:T(8,128)(2,1)S(1)}, u32[]{:S(2)}, u32[]{:S(2)}) collective-permute-start(bf16[64,256]{1,0:T(8,128)(2,1)S(1)} %get-tuple-element.42.refs_3_), channel_id=1, source_target_pairs={{0,18},{1,19},{2,16},{3,17},{4,22},{5,23},{6,20},{7,21},{8,26},{9,... | collective-permute-start | bytes 98312 | tf_op jit(solution)/shard_map/ppermute | solution.py:69
  5.6 11.6 %collective-permute-start.1 = (bf16[2,64,256]{2,1,0:T(8,128)(2,1)S(1)}, bf16[2,64,256]{2,1,0:T(8,128)(2,1)S(1)}, u32[]{:S(2)}, u32[]{:S(2)}) collective-permute-start(bf16[2,64,256]{2,1,0:T(8,128)(2,1)S(1)} %pad_maximum_fusion), channel_id=1, source_target_pairs={{0,4},{1,3},{2,6},{3,1},{4,0},{5,9},{6,2},{7,11},{8,12},{9,5},{10,... | collective-permute-start | bytes 196616 | tf_op jit(solution)/shard_map/ppermute | solution.py:69
  8.7 1.6 %copy-start = (bf16[1,1,32,64,512]{4,3,2,1,0:T(8,128)(2,1)S(1)}, bf16[1,1,32,64,512]{4,3,2,1,0:T(8,128)(2,1)}, u32[]{:S(2)}) copy-start(bf16[1,1,32,64,512]{4,3,2,1,0:T(8,128)(2,1)} %param.7) | copy-start | bytes 6291460
  10.3 0.9 %copy-start.1 = (bf16[64,1,1,2048]{3,0,2,1:T(8,128)(2,1)S(1)}, bf16[64,1,1,2048]{3,0,2,1:T(8,128)(2,1)}, u32[]{:S(2)}) copy-start(bf16[64,1,1,2048]{3,0,2,1:T(8,128)(2,1)} %param.6) | copy-start | bytes 786436
  12.8 5.2 %collective-permute-start.2 = (bf16[2,64,256]{2,1,0:T(8,128)(2,1)S(1)}, bf16[2,64,256]{2,1,0:T(8,128)(2,1)S(1)}, u32[]{:S(2)}, u32[]{:S(2)}) collective-permute-start(bf16[2,64,256]{2,1,0:T(8,128)(2,1)S(1)} %pad_maximum_fusion), channel_id=1, source_target_pairs={{0,6},{1,3},{2,4},{3,1},{4,2},{5,11},{6,0},{7,9},{8,14},{9,7},{10,... | collective-permute-start | bytes 196616 | tf_op jit(solution)/shard_map/ppermute | solution.py:69
  13.3 5.2 %collective-permute-start.3 = (bf16[2,64,256]{2,1,0:T(8,128)(2,1)S(1)}, bf16[2,64,256]{2,1,0:T(8,128)(2,1)S(1)}, u32[]{:S(2)}, u32[]{:S(2)}) collective-permute-start(bf16[2,64,256]{2,1,0:T(8,128)(2,1)S(1)} %pad_maximum_fusion), channel_id=1, source_target_pairs={{0,20},{1,3},{2,22},{3,1},{4,16},{5,25},{6,18},{7,27},{8,28},{9,21... | collective-permute-start | bytes 196616 | tf_op jit(solution)/shard_map/ppermute | solution.py:69
  14.8 6.1 %collective-permute-start.4 = (bf16[2,64,256]{2,1,0:T(8,128)(2,1)S(1)}, bf16[2,64,256]{2,1,0:T(8,128)(2,1)S(1)}, u32[]{:S(2)}, u32[]{:S(2)}) collective-permute-start(bf16[2,64,256]{2,1,0:T(8,128)(2,1)S(1)} %pad_maximum_fusion), channel_id=1, source_target_pairs={{0,22},{1,3},{2,20},{3,1},{4,18},{5,27},{6,16},{7,25},{8,30},{9,23... | collective-permute-start | bytes 196616 | tf_op jit(solution)/shard_map/ppermute | solution.py:69
  17.2 4.5 %collective-permute-start.5 = (bf16[2,64,256]{2,1,0:T(8,128)(2,1)S(1)}, bf16[2,64,256]{2,1,0:T(8,128)(2,1)S(1)}, u32[]{:S(2)}, u32[]{:S(2)}) collective-permute-start(bf16[2,64,256]{2,1,0:T(8,128)(2,1)S(1)} %pad_maximum_fusion), channel_id=1, source_target_pairs={{0,2},{1,17},{2,0},{3,19},{4,6},{5,21},{6,4},{7,23},{8,10},{9,25},... | collective-permute-start | bytes 196616 | tf_op jit(solution)/shard_map/ppermute | solution.py:69
  17.7 10.2 %copy-start.3 = (f32[64]{0:T(128)S(1)}, f32[64]{0:T(128)}, u32[]{:S(2)}) copy-start(f32[64]{0:T(128)} %param.11) | copy-start | bytes 772
  21.7 1.7 %collective-permute-start.7 = (bf16[11,64,256]{2,1,0:T(8,128)(2,1)S(1)}, bf16[11,64,256]{2,1,0:T(8,128)(2,1)S(1)}, u32[]{:S(2)}, u32[]{:S(2)}) collective-permute-start(bf16[11,64,256]{2,1,0:T(8,128)(2,1)S(1)} %constant_dynamic-update-slice_fusion.refs_0_), channel_id=1, source_target_pairs={{0,1},{1,0},{2,3},{3,2},{4,5},{5,4},{6,7},{7,6},{8,9},{9,8},{10,11... | collective-permute-start | bytes 1081352 | tf_op jit(solution)/shard_map/ppermute | solution.py:73
  24.6 1.3 %collective-permute-start.8 = (bf16[64,256]{1,0:T(8,128)(2,1)S(1)}, bf16[64,256]{1,0:T(8,128)(2,1)S(1)}, u32[]{:S(2)}, u32[]{:S(2)}) collective-permute-start(bf16[64,256]{1,0:T(8,128)(2,1)S(1)} %shard_map.65.refs_3_), channel_id=1, source_target_pairs={{0,1},{1,0},{2,3},{3,2},{4,5},{5,4},{6,7},{7,6},{8,9},{9,8},{10,11... | collective-permute-start | bytes 98312 | tf_op jit(solution)/shard_map/ppermute | solution.py:73
  26.5 11.4 %collective-permute-start.9 = (bf16[2,64,256]{2,1,0:T(8,128)(2,1)}, bf16[2,64,256]{2,1,0:T(8,128)(2,1)}, u32[]{:S(2)}, u32[]{:S(2)}) collective-permute-start(bf16[2,64,256]{2,1,0:T(8,128)(2,1)} %pad_maximum_fusion.1), channel_id=1, source_target_pairs={{0,4},{1,3},{2,6},{3,1},{4,0},{5,9},{6,2},{7,11},{8,12},{9,5},{10,... | collective-permute-start | bytes 196616 | tf_op jit(solution)/shard_map/ppermute | solution.py:69
  28.0 14.4 %collective-permute-start.14 = (bf16[64,256]{1,0:T(8,128)(2,1)S(1)}, bf16[64,256]{1,0:T(8,128)(2,1)S(1)}, u32[]{:S(2)}, u32[]{:S(2)}) collective-permute-start(bf16[64,256]{1,0:T(8,128)(2,1)S(1)} %shard_map.65.refs_3_), channel_id=1, source_target_pairs={{0,18},{1,19},{2,16},{3,17},{4,22},{5,23},{6,20},{7,21},{8,26},{9,... | collective-permute-start | bytes 98312 | tf_op jit(solution)/shard_map/ppermute | solution.py:69
  29.1 0.9 %copy-start.2 = (bf16[64,1,1,2048]{3,0,2,1:T(8,128)(2,1)S(1)}, bf16[64,1,1,2048]{3,0,2,1:T(8,128)(2,1)}, u32[]{:S(2)}) copy-start(bf16[64,1,1,2048]{3,0,2,1:T(8,128)(2,1)} %param.6) | copy-start | bytes 786436
  32.6 6.6 %collective-permute-start.10 = (bf16[2,64,256]{2,1,0:T(8,128)(2,1)}, bf16[2,64,256]{2,1,0:T(8,128)(2,1)S(1)}, u32[]{:S(2)}, u32[]{:S(2)}) collective-permute-start(bf16[2,64,256]{2,1,0:T(8,128)(2,1)} %pad_maximum_fusion.1), channel_id=1, source_target_pairs={{0,6},{1,3},{2,4},{3,1},{4,2},{5,11},{6,0},{7,9},{8,14},{9,7},{10,... | collective-permute-start | bytes 196616 | tf_op jit(solution)/shard_map/ppermute | solution.py:69
  34.0 5.4 %collective-permute-start.11 = (bf16[2,64,256]{2,1,0:T(8,128)(2,1)}, bf16[2,64,256]{2,1,0:T(8,128)(2,1)S(1)}, u32[]{:S(2)}, u32[]{:S(2)}) collective-permute-start(bf16[2,64,256]{2,1,0:T(8,128)(2,1)} %pad_maximum_fusion.1), channel_id=1, source_target_pairs={{0,20},{1,3},{2,22},{3,1},{4,16},{5,25},{6,18},{7,27},{8,28},{9,21... | collective-permute-start | bytes 196616 | tf_op jit(solution)/shard_map/ppermute | solution.py:69
  36.0 6.3 %collective-permute-start.12 = (bf16[2,64,256]{2,1,0:T(8,128)(2,1)}, bf16[2,64,256]{2,1,0:T(8,128)(2,1)S(1)}, u32[]{:S(2)}, u32[]{:S(2)}) collective-permute-start(bf16[2,64,256]{2,1,0:T(8,128)(2,1)} %pad_maximum_fusion.1), channel_id=1, source_target_pairs={{0,22},{1,3},{2,20},{3,1},{4,18},{5,27},{6,16},{7,25},{8,30},{9,23... | collective-permute-start | bytes 196616 | tf_op jit(solution)/shard_map/ppermute | solution.py:69
  37.9 4.5 %collective-permute-start.13 = (bf16[2,64,256]{2,1,0:T(8,128)(2,1)}, bf16[2,64,256]{2,1,0:T(8,128)(2,1)S(1)}, u32[]{:S(2)}, u32[]{:S(2)}) collective-permute-start(bf16[2,64,256]{2,1,0:T(8,128)(2,1)} %pad_maximum_fusion.1), channel_id=1, source_target_pairs={{0,2},{1,17},{2,0},{3,19},{4,6},{5,21},{6,4},{7,23},{8,10},{9,25},... | collective-permute-start | bytes 196616 | tf_op jit(solution)/shard_map/ppermute | solution.py:69
  42.4 1.7 %collective-permute-start.15 = (bf16[11,64,256]{2,1,0:T(8,128)(2,1)S(1)}, bf16[11,64,256]{2,1,0:T(8,128)(2,1)S(1)}, u32[]{:S(2)}, u32[]{:S(2)}) collective-permute-start(bf16[11,64,256]{2,1,0:T(8,128)(2,1)S(1)} %constant_dynamic-update-slice_fusion.6.refs_0_), channel_id=1, source_target_pairs={{0,1},{1,0},{2,3},{3,2},{4,5},{5,4},{6,7},{7,6},{8,9},{9,8},{10,11... | collective-permute-start | bytes 1081352 | tf_op jit(solution)/shard_map/ppermute | solution.py:73
  45.3 1.3 %collective-permute-start.16 = (bf16[64,256]{1,0:T(8,128)(2,1)S(1)}, bf16[64,256]{1,0:T(8,128)(2,1)S(1)}, u32[]{:S(2)}, u32[]{:S(2)}) collective-permute-start(bf16[64,256]{1,0:T(8,128)(2,1)S(1)} %shard_map.67.refs_3_), channel_id=1, source_target_pairs={{0,1},{1,0},{2,3},{3,2},{4,5},{5,4},{6,7},{7,6},{8,9},{9,8},{10,11... | collective-permute-start | bytes 98312 | tf_op jit(solution)/shard_map/ppermute | solution.py:73
  46.6 10.0 %collective-permute-start.17 = (bf16[2,64,256]{2,1,0:T(8,128)(2,1)S(1)}, bf16[2,64,256]{2,1,0:T(8,128)(2,1)S(1)}, u32[]{:S(2)}, u32[]{:S(2)}) collective-permute-start(bf16[2,64,256]{2,1,0:T(8,128)(2,1)S(1)} %pad_maximum_fusion.2), channel_id=1, source_target_pairs={{0,4},{1,3},{2,6},{3,1},{4,0},{5,9},{6,2},{7,11},{8,12},{9,5},{10,... | collective-permute-start | bytes 196616 | tf_op jit(solution)/shard_map/ppermute | solution.py:69
  47.3 13.6 %collective-permute-start.22 = (bf16[64,256]{1,0:T(8,128)(2,1)S(1)}, bf16[64,256]{1,0:T(8,128)(2,1)S(1)}, u32[]{:S(2)}, u32[]{:S(2)}) collective-permute-start(bf16[64,256]{1,0:T(8,128)(2,1)S(1)} %shard_map.67.refs_3_), channel_id=1, source_target_pairs={{0,18},{1,19},{2,16},{3,17},{4,22},{5,23},{6,20},{7,21},{8,26},{9,... | collective-permute-start | bytes 98312 | tf_op jit(solution)/shard_map/ppermute | solution.py:69
  51.8 6.1 %collective-permute-start.18 = (bf16[2,64,256]{2,1,0:T(8,128)(2,1)S(1)}, bf16[2,64,256]{2,1,0:T(8,128)(2,1)S(1)}, u32[]{:S(2)}, u32[]{:S(2)}) collective-permute-start(bf16[2,64,256]{2,1,0:T(8,128)(2,1)S(1)} %pad_maximum_fusion.2), channel_id=1, source_target_pairs={{0,6},{1,3},{2,4},{3,1},{4,2},{5,11},{6,0},{7,9},{8,14},{9,7},{10,... | collective-permute-start | bytes 196616 | tf_op jit(solution)/shard_map/ppermute | solution.py:69
  53.4 5.2 %collective-permute-start.19 = (bf16[2,64,256]{2,1,0:T(8,128)(2,1)S(1)}, bf16[2,64,256]{2,1,0:T(8,128)(2,1)S(1)}, u32[]{:S(2)}, u32[]{:S(2)}) collective-permute-start(bf16[2,64,256]{2,1,0:T(8,128)(2,1)S(1)} %pad_maximum_fusion.2), channel_id=1, source_target_pairs={{0,20},{1,3},{2,22},{3,1},{4,16},{5,25},{6,18},{7,27},{8,28},{9,21... | collective-permute-start | bytes 196616 | tf_op jit(solution)/shard_map/ppermute | solution.py:69
  54.4 6.1 %collective-permute-start.20 = (bf16[2,64,256]{2,1,0:T(8,128)(2,1)S(1)}, bf16[2,64,256]{2,1,0:T(8,128)(2,1)S(1)}, u32[]{:S(2)}, u32[]{:S(2)}) collective-permute-start(bf16[2,64,256]{2,1,0:T(8,128)(2,1)S(1)} %pad_maximum_fusion.2), channel_id=1, source_target_pairs={{0,22},{1,3},{2,20},{3,1},{4,18},{5,27},{6,16},{7,25},{8,30},{9,23... | collective-permute-start | bytes 196616 | tf_op jit(solution)/shard_map/ppermute | solution.py:69
  56.6 4.3 %collective-permute-start.21 = (bf16[2,64,256]{2,1,0:T(8,128)(2,1)S(1)}, bf16[2,64,256]{2,1,0:T(8,128)(2,1)S(1)}, u32[]{:S(2)}, u32[]{:S(2)}) collective-permute-start(bf16[2,64,256]{2,1,0:T(8,128)(2,1)S(1)} %pad_maximum_fusion.2), channel_id=1, source_target_pairs={{0,2},{1,17},{2,0},{3,19},{4,6},{5,21},{6,4},{7,23},{8,10},{9,25},... | collective-permute-start | bytes 196616 | tf_op jit(solution)/shard_map/ppermute | solution.py:69
  60.9 1.7 %collective-permute-start.23 = (bf16[11,64,256]{2,1,0:T(8,128)(2,1)S(1)}, bf16[11,64,256]{2,1,0:T(8,128)(2,1)S(1)}, u32[]{:S(2)}, u32[]{:S(2)}) collective-permute-start(bf16[11,64,256]{2,1,0:T(8,128)(2,1)S(1)} %constant_dynamic-update-slice_fusion.12.refs_0_), channel_id=1, source_target_pairs={{0,1},{1,0},{2,3},{3,2},{4,5},{5,4},{6,7},{7,6},{8,9},{9,8},{10,11... | collective-permute-start | bytes 1081352 | tf_op jit(solution)/shard_map/ppermute | solution.py:73

commit v4 on v3

--- a/solution.py
+++ b/solution.py
@@ -11,6 +11,7 @@
 TERMS = 3
 FEATURES = 64
 NEAR = 4
+PARTS = 4
 LANES = 2 * PB
 AXES = ("gx", "gy", "gz")
 
@@ -79,13 +80,14 @@
     other = swap_cores(rim)
     both = jnp.stack([rim, other])
     steps = reversed(range(0, len(chips) - len(chips) % 2, 2))
-    shares = [swap(both, (chips[t], chips[t + 1])) for t in steps][::-1]
-    received = jnp.concatenate(shares + [panel[None] for panel in alone])
-    received, work = lax.optimization_barrier((received, work))
-    return (received, swap_cores(received), other, rim), work
-
-
-def source_index(slots, count, rim_count):
+    shares = [swap(both, (chips[t], chips[t + 1])) for t in steps]
+    shares[1], *results = work(shares[1])
+    received = jnp.concatenate(shares[::-1] + [panel[None] for panel in alone])
+    return (received, swap_cores(received), other, rim), results
+
+
+def source_index(slots, live, rim_count):
+    count, slot_count = slots.shape
     layers = lax.axis_size("gz")
     x_at, y_at, z_at = (lax.axis_index(name) for name in AXES)
     rest = jnp.maximum(slots - count, 0)
@@ -107,7 +109,10 @@
     panel = jnp.where(here, 2 * chips + jnp.where(target == core, 1, 0), panel)
     zero = (2 * chips + 2) * rim_count
     far = jnp.where(x_in & y_in, panel * rim_count + r, zero)
-    index = jnp.where(slots < count, slots, far)
+    place = lax.broadcasted_iota(jnp.int32, slots.shape, 1)
+    far = jnp.where(place < live, far, zero)
+    index = jnp.where(place < NEAR, jnp.where(place < live, slots, count), far)
+    index = index.reshape(count * slot_count)
     return index.astype(jnp.int32)
 
 
@@ -176,20 +181,47 @@
         )
 
 
-def first_kernel(index_ref, value_ref, raw_ref, scale_ref, live_ref, tile_out, near_out, store):
+def first_kernel(
+    index_ref, _, value_hbm, raw_hbm, scale_hbm,
+    __, tile_out, near_out, total_out,
+    store, value_ref, raw_ref, scale_ref, arrived,
+):
     count, slot_count = scale_ref.shape
-    used = lax.broadcasted_iota(jnp.int32, (count, slot_count), 1) < live_ref[...]
-    weights = jnp.where(used, scale_ref[...], 0.0)
+    rows = raw_ref.shape[0] // PARTS
+    fetches = [
+        pltpu.make_async_copy(source, target, arrived.at[n])
+        for n, (source, target) in enumerate(
+            [(scale_hbm, scale_ref), (value_hbm, value_ref)]
+            + [
+                (raw_hbm.at[pl.ds(p * rows, rows)], raw_ref.at[pl.ds(p * rows, rows)])
+                for p in range(PARTS)
+            ]
+        )
+    ]
+    for fetch in fetches:
+        fetch.start()
+    for fetch in fetches[:2]:
+        fetch.wait()
+    scales = scale_ref[...]
     lanes = jnp.concatenate(
-        [jnp.broadcast_to(weights[:, k : k + 1], (count, PB)) for k in range(slot_count)], axis=1
-    )
-    for b in range(count):
-        at = pl.ds(b * PB, PB)
-        scaled = raw_ref[at, :].astype(jnp.float32) * lanes[b : b + 1, :]
-        tile_out[at, :] = scaled.astype(tile_out.dtype)
+        [jnp.broadcast_to(scales[:, k : k + 1], (count, PB)) for k in range(slot_count)], axis=1
+    )
     for t in range(value_ref.shape[1] // LANES):
-        spread(value_ref[:, t * LANES : (t + 1) * LANES], store, 2 * t)
+        pair = value_ref[:, t * LANES : (t + 1) * LANES]
+        total_out[:, t * LANES : (t + 1) * LANES] = pair.astype(total_out.dtype)
+        spread(pair, store, 2 * t)
+    clear_last(store)
+    for p in range(PARTS):
+        fetches[2 + p].wait()
+        for b in range(p * rows // PB, (p + 1) * rows // PB):
+            at = pl.ds(b * PB, PB)
+            scaled = raw_ref[at, :].astype(jnp.float32) * lanes[b : b + 1, :]
+            tile_out[at, :] = scaled.astype(tile_out.dtype)
     near_image(index_ref, store, tile_out, near_out)
+
+
+def clear_last(store):
+    store[store.shape[0] - 1] = jnp.zeros(store.shape[1:], store.dtype)
 
 
 def rim_kernel(index_ref, *refs):
@@ -200,7 +232,7 @@
         store[number // 2] = pair
 
     each_rim(rims, keep)
-    store[store.shape[0] - 1] = jnp.zeros(store.shape[1:], store.dtype)
+    clear_last(store)
 
     def sources(row):
         base = row * slot_count + NEAR
@@ -221,14 +253,17 @@
 
 
 def far_kernel(step, last, index_ref, *refs):
+    if not last:
+        refs = refs[1:]
     rims, (tile_ref, near_ref, total_ref, times_ref) = refs[:4], refs[4:8]
     if last:
         total_out, store = refs[8:]
     else:
-        total_out, near_out, store, own_store = refs[8:]
+        _, total_out, near_out, store, own_store = refs[8:]
+        clear_last(own_store)
     slot_count = tile_ref.shape[1] // PB
     each_rim(rims, lambda pair, number: spread(pair, store, number))
-    store[store.shape[0] - 1] = jnp.zeros(store.shape[1:], store.dtype)
+    clear_last(store)
     factor = jnp.ones(times_ref.shape, jnp.float32)
     for n in range(1, step + 1):
         factor = factor * -times_ref[...] / jnp.float32(n)
@@ -247,17 +282,22 @@
         near_image(index_ref, own_store, tile_ref, near_out)
 
 
-def call(kernel, out_shape, scratch, flops, index, *arrays):
-    vmem = pl.BlockSpec(memory_space=pltpu.VMEM)
+def call(kernel, out_shape, scratch, flops, index, *arrays, space=pltpu.VMEM, through=None):
+    handed = () if through is None else (through,)
+    out_shape = tuple(jax.ShapeDtypeStruct(x.shape, x.dtype) for x in handed) + out_shape
     return pl.pallas_call(
         kernel,
         out_shape=out_shape,
-        in_specs=[pl.BlockSpec(memory_space=pltpu.SMEM)] + [vmem] * len(arrays),
-        out_specs=jax.tree.map(lambda _: vmem, out_shape),
-        scratch_shapes=[pltpu.VMEM(shape, jnp.bfloat16) for shape in scratch],
+        in_specs=[pl.BlockSpec(memory_space=pltpu.SMEM)]
+        + [pl.BlockSpec(memory_space=pl.ANY)] * len(handed)
+        + [pl.BlockSpec(memory_space=space)] * len(arrays),
+        out_specs=(pl.BlockSpec(memory_space=pl.ANY),) * len(handed)
+        + (pl.BlockSpec(memory_space=pltpu.VMEM),) * (len(out_shape) - len(handed)),
+        scratch_shapes=scratch,
+        input_output_aliases={1: 0} if handed else {},
         compiler_params=pltpu.CompilerParams(vmem_limit_bytes=16 * 1024 * 1024),
         cost_estimate=pl.CostEstimate(flops=flops, bytes_accessed=flops // 64, transcendentals=0),
-    )(index, *arrays)
+    )(index, *handed, *arrays)
 
 
 def body(features, tiles, scales, slots, live, times):
@@ -267,46 +307,71 @@
     points = count * PB
     value = features.reshape(FEATURES, points)
     rim = value[:, : rim_count * PB]
-    index = source_index(slots.reshape(count * slot_count), count, rim_count)
+    index = source_index(slots.reshape(count, slot_count), live.reshape(count, 1), rim_count)
+    rims_held = 2 * len(partners()) + 2
+    half = FEATURES * points * width
+
+    def blocks(number):
+        return pltpu.VMEM((number, FEATURES, LANES), jnp.bfloat16)
+
+    own_store = blocks(count + 1)
+    far_store = blocks(rims_held * rim_count + 1)
+    pair_store = blocks(rims_held * rim_count // 2 + 1)
     image_shape = jax.ShapeDtypeStruct(value.shape, jnp.float32)
     rim_shape = jax.ShapeDtypeStruct(rim.shape, jnp.bfloat16)
-    own_store = (count, FEATURES, LANES)
-    rims_held = 2 * len(partners()) + 2
-    far_store = (rims_held * rim_count + 1, FEATURES, LANES)
-    pair_store = (rims_held * rim_count // 2 + 1, FEATURES, LANES)
-    half = FEATURES * points * width
-    scaled, near = call(
-        first_kernel,
-        (jax.ShapeDtypeStruct((points, width), jnp.bfloat16), image_shape),
-        [own_store],
+    tile_shape = jax.ShapeDtypeStruct((points, width), jnp.bfloat16)
+
+    def first(through):
+        return call(
+            first_kernel,
+            (tile_shape, image_shape, image_shape),
+            [
+                own_store,
+                pltpu.VMEM(value.shape, jnp.bfloat16),
+                pltpu.VMEM((points, width), jnp.bfloat16),
+                pltpu.VMEM((count, slot_count), jnp.float32),
+                pltpu.SemaphoreType.DMA((2 + PARTS,)),
+            ],
+            half,
+            index,
+            value,
+            tiles.reshape(points, width),
+            scales.reshape(count, slot_count),
+            space=pltpu.HBM,
+            through=through,
+        )
+
+    rims, (scaled, near, total) = exchange(rim, first)
+    times = times[:, None]
+    for step in range(1, TERMS):
+        arrays = (index, *rims, scaled, near)
+        (rim,) = call(rim_kernel, (rim_shape,), [pair_store], half // 8, *arrays)
+
+        def rest(through):
+            return call(
+                functools.partial(far_kernel, step, False),
+                (image_shape, image_shape),
+                [far_store, own_store],
+                2 * half,
+                *arrays,
+                total,
+                times,
+                through=through,
+            )
+
+        rims, (total, near) = exchange(rim, rest)
+    (out,) = call(
+        functools.partial(far_kernel, TERMS, True),
+        (jax.ShapeDtypeStruct(value.shape, jnp.bfloat16),),
+        [far_store],
         half,
         index,
-        value,
-        tiles.reshape(points, width),
-        scales.reshape(count, slot_count),
-        live.reshape(count, 1),
-    )
-    times = times[:, None]
-    total = value
-    for step in range(1, TERMS + 1):
-        rims, (scaled, near, total) = exchange(rim, (scaled, near, total))
-        if step < TERMS:
-            rim = call(rim_kernel, rim_shape, [pair_store], half // 8, index, *rims, scaled, near)
-        last = step == TERMS
-        out = call(
-            functools.partial(far_kernel, step, last),
-            jax.ShapeDtypeStruct(value.shape, jnp.bfloat16) if last else (image_shape,) * 2,
-            [far_store] if last else [far_store, own_store],
-            half if last else 2 * half,
-            index,
-            *rims,
-            scaled,
-            near,
-            total,
-            times,
-        )
-        if not last:
-            total, near = out
+        *rims,
+        scaled,
+        near,
+        total,
+        times,
+    )
     return out.reshape(features.shape)
 
 

time: 65.8 us -> 62.3 us (0.947)
  waiting for transfers between devices: 17.3 us -> 12.7 us
  other arithmetic: 0.7 us -> 1.43 us
    ppermute x18, waiting for transfers between devices: 10.1 us -> 5.57 us  [swap(): return lax.ppermute(value, AXES, pairs)]
    reshape x2 -> x1, local copies, waits for them, and re-layouts: 0.82 us -> 0.09 us  [body(): slots.reshape(count, slot_count)]
    lt x0 -> x2, other arithmetic: none -> 0.73 us  [source_index(): index = jnp.where(place < NEAR, jnp.where(place < live, slots, count), far)]
    unnamed x25 -> x27, local copies, waits for them, and re-layouts: 5.94 us -> 6.04 us
  transfers between devices with their start and end apart: 24 -> 24, of which waited for: 15 -> 11; matrix products, arithmetic and copies ran while one was open for 5% -> 6% of each run, Pallas kernels for 10% -> 11%
where the time goes in v4:
time: 62.3 us; the launch traced here: 61.9 us
  starting transfers between devices  28.2 us (45%)
  waiting for transfers between devices  12.7 us (20%)
  Pallas kernels  12.1 us (19%)
  local copies, waits for them, and re-layouts  7.19 us (12%)
  other arithmetic  1.43 us (2%)
    ppermute x18, starting transfers between devices, swap(): return lax.ppermute(value, AXES, pairs)  27.1 us
    pallas_call x6, Pallas kernels, call(): pl.pallas_call(kernel, out_shape=out_shape, in_specs=[pl.BlockSpec(memory...  12.1 us
    ppermute x6, waiting for transfers between devices, swap_cores(): lax.ppermute(value, 'gz', [(k, k ^ 1) for k in range(lax.axis_size('gz'))])  7.13 us
    unnamed x27, local copies, waits for them, and re-layouts  6.04 us
    ppermute x18, waiting for transfers between devices, swap(): return lax.ppermute(value, AXES, pairs)  5.57 us
  transfers between devices with their start and end apart: 24, of which 11 were waited for; matrix products, arithmetic and copies ran while one was open for 6% of the time, Pallas kernels for 11%

profile of v4, /device:TPU:0, one launch (start us, length us, event | category | flops | bytes accessed | tf_op | source)
XLA Modules:
  0.0 61.9 jit_solution(6710722264444691138)
XLA Ops:
  0.0 0.8 %slice_bitcast_fusion = (bf16[1,64,256]{2,1,0:T(8,128)(2,1)S(1)}, bf16[64,256]{1,0:T(8,128)(2,1)S(1)}) fusion(bf16[64,2048]{1,0:T(8,128)(2,1)} %bitcast.23), kind=kLoop, calls=%fused_computation.57 | loop fusion | bytes 98304 | tf_op jit(solution)/shard_map/stack | solution.py:81
  0.8 0.5 collective-permute-start
  1.2 3.4 %collective-permute-start.6 = (bf16[64,256]{1,0:T(8,128)(2,1)S(1)}, bf16[64,256]{1,0:T(8,128)(2,1)S(1)}, u32[]{:S(2)}, u32[]{:S(2)}) collective-permute-start(bf16[64,256]{1,0:T(8,128)(2,1)S(1)} %get-tuple-element.26.refs_3_.refs_4_), channel_id=1, source_target_pairs={{0,18},{1,19},{2,16},{3,17},{4,22},{5,23},{6,20},{7,21},{8,26},{9,... | collective-permute-start | bytes 98312 | tf_op jit(solution)/shard_map/ppermute | solution.py:70
  4.7 0.7 %iota_compare_fusion = pred[32,8]{1,0:T(8,128)(4,1)S(1)} fusion(s32[32]{0:T(128)} %bitcast.31), kind=kLoop, calls=%fused_computation.21 | loop fusion | flops 256 | bytes 384 | tf_op jit(solution)/shard_map/lt | solution.py:114
  5.4 0.8 %copy.14 = s32[1,1,32,8]{3,2,1,0:T(8,128)S(1)} copy(s32[1,1,32,8]{2,3,1,0:T(8,128)} %param.9) | data formatting | bytes 2048 | tf_op args[3]
  6.2 0.1 reshape.23
  6.3 0.1 iota.13
  6.4 0.1 lt.70
  6.5 1.6 %collective-permute-start.1 = (bf16[2,64,256]{2,1,0:T(8,128)(2,1)S(1)}, bf16[2,64,256]{2,1,0:T(8,128)(2,1)S(1)}, u32[]{:S(2)}, u32[]{:S(2)}) collective-permute-start(bf16[2,64,256]{2,1,0:T(8,128)(2,1)S(1)} %pad_maximum_fusion), channel_id=1, source_target_pairs={{0,4},{1,3},{2,6},{3,1},{4,0},{5,9},{6,2},{7,11},{8,12},{9,5},{10,... | collective-permute-start | bytes 196616 | tf_op jit(solution)/shard_map/ppermute | solution.py:70
  8.2 0.8 %copy.15 = f32[1,1,32,8]{3,2,1,0:T(8,128)S(1)} copy(f32[1,1,32,8]{2,3,1,0:T(8,128)} %param.8) | data formatting | bytes 2048 | tf_op args[2]
  9.0 0.0 collective-permute-start.4
  9.0 2.9 %collective-permute-start.2 = (bf16[2,64,256]{2,1,0:T(8,128)(2,1)S(1)}, bf16[2,64,256]{2,1,0:T(8,128)(2,1)S(1)}, u32[]{:S(2)}, u32[]{:S(2)}) collective-permute-start(bf16[2,64,256]{2,1,0:T(8,128)(2,1)S(1)} %pad_maximum_fusion), channel_id=1, source_target_pairs={{0,6},{1,3},{2,4},{3,1},{4,2},{5,11},{6,0},{7,9},{8,14},{9,7},{10,... | collective-permute-start | bytes 196616 | tf_op jit(solution)/shard_map/ppermute | solution.py:70
  11.9 1.4 %collective-permute-start.3 = (bf16[2,64,256]{2,1,0:T(8,128)(2,1)S(1)}, bf16[2,64,256]{2,1,0:T(8,128)(2,1)S(1)}, u32[]{:S(2)}, u32[]{:S(2)}) collective-permute-start(bf16[2,64,256]{2,1,0:T(8,128)(2,1)S(1)} %pad_maximum_fusion), channel_id=1, source_target_pairs={{0,20},{1,3},{2,22},{3,1},{4,16},{5,25},{6,18},{7,27},{8,28},{9,21... | collective-permute-start | bytes 196616 | tf_op jit(solution)/shard_map/ppermute | solution.py:70
  13.3 0.0 collective-permute-done.1
  13.3 0.5 collective-permute-start.5
  13.8 1.0 %collective-permute-done.2 = bf16[2,64,256]{2,1,0:T(8,128)(2,1)S(1)} collective-permute-done((bf16[2,64,256]{2,1,0:T(8,128)(2,1)S(1)}, bf16[2,64,256]{2,1,0:T(8,128)(2,1)S(1)}, u32[]{:S(2)}, u32[]{:S(2)}) %collective-permute-start.2) | collective-permute-done | bytes 65568 | tf_op jit(solution)/shard_map/ppermute | solution.py:70
  14.8 2.2 %collective-permute-done.3 = bf16[2,64,256]{2,1,0:T(8,128)(2,1)S(1)} collective-permute-done((bf16[2,64,256]{2,1,0:T(8,128)(2,1)S(1)}, bf16[2,64,256]{2,1,0:T(8,128)(2,1)S(1)}, u32[]{:S(2)}, u32[]{:S(2)}) %collective-permute-start.3) | collective-permute-done | bytes 65568 | tf_op jit(solution)/shard_map/ppermute | solution.py:70
  17.0 0.0 copy-start
  17.1 1.6 %copy-done = bf16[1,1,32,64,512]{4,3,2,1,0:T(8,128)(2,1)S(1)} copy-done((bf16[1,1,32,64,512]{4,3,2,1,0:T(8,128)(2,1)S(1)}, bf16[1,1,32,64,512]{4,3,2,1,0:T(8,128)(2,1)}, u32[]{:S(2)}) %copy-start) | copy-done | bytes 2097176
  18.6 0.9 %copy-done.3 = bf16[64,1,1,2048]{3,0,2,1:T(8,128)(2,1)S(1)} copy-done((bf16[64,1,1,2048]{3,0,2,1:T(8,128)(2,1)S(1)}, bf16[64,1,1,2048]{3,0,2,1:T(8,128)(2,1)}, u32[]{:S(2)}) %copy-start.3) | copy-done | bytes 262168
  19.6 1.7 %shard_map.64 = (bf16[2,64,256]{2,1,0:T(8,128)(2,1)S(1)}, bf16[2048,512]{1,0:T(8,128)(2,1)S(1)}, f32[64,2048]{1,0:T(8,128)S(1)}, f32[64,2048]{1,0:T(8,128)S(1)}) custom-call(s32[256]{0:T(256)S(1)} %select_select_fusion.index_ref, bf16[2,64,256]{2,1,0:T(8,128)(2,1)S(1)} %collective-permute-done.4._, ...), custom_call_target="tpu_custom_call", output_to_operand_aliasing={{0}: (1, {})} | custom-call | flops 67108864 | bytes 1048576 | tf_op jit(solution)/shard_map/pallas_call | solution.py:288
  21.3 0.0 copy-start.4
  21.4 0.0 collective-permute-done.5
  21.4 0.0 collective-permute-done.6
  21.4 0.1 collective-permute-start.7
  21.5 1.7 %collective-permute-done.7.refs_1_.refs_2_ = bf16[11,64,256]{2,1,0:T(8,128)(2,1)S(1)} collective-permute-done((bf16[11,64,256]{2,1,0:T(8,128)(2,1)S(1)}, bf16[11,64,256]{2,1,0:T(8,128)(2,1)S(1)}, u32[]{:S(2)}, u32[]{:S(2)}) %collective-permute-start.7) | collective-permute-done | bytes 360480 | tf_op jit(solution)/shard_map/ppermute | solution.py:74
  23.2 1.2 %shard_map.65.refs_3_.refs_4_ = bf16[64,256]{1,0:T(8,128)(2,1)S(1)} custom-call(s32[256]{0:T(256)S(1)} %select_select_fusion.index_ref, bf16[11,64,256]{2,1,0:T(8,128)(2,1)S(1)} %constant_dynamic-update-slice_fusion.refs_0_.refs_1_, bf16[11,64,256]{2,1,0:T(8,128)(2,1)S(1)} %collective-permute-done.7.refs_1_.refs_2_, ...), custom_call_target="tpu_custom_call" | custom-call | flops 8388608 | bytes 131072 | tf_op jit(solution)/shard_map/pallas_call | solution.py:288
  24.3 0.2 collective-permute-start.8
  24.5 1.1 %collective-permute-done.8.refs_2_.refs_3_ = bf16[64,256]{1,0:T(8,128)(2,1)S(1)} collective-permute-done((bf16[64,256]{1,0:T(8,128)(2,1)S(1)}, bf16[64,256]{1,0:T(8,128)(2,1)S(1)}, u32[]{:S(2)}, u32[]{:S(2)}) %collective-permute-start.8) | collective-permute-done | bytes 32800 | tf_op jit(solution)/shard_map/ppermute | solution.py:74
  25.6 0.6 %pad_maximum_fusion.1 = bf16[2,64,256]{2,1,0:T(8,128)(2,1)} fusion(bf16[1,64,256]{2,1,0:T(8,128)(2,1)S(1)} %bitcast.26, bf16[1,64,256]{2,1,0:T(8,128)(2,1)S(1)} %bitcast.22), kind=kLoop, calls=%fused_computation.1 | loop fusion | flops 32768 | bytes 131072 | tf_op jit(solution)/shard_map/stack | solution.py:81
  26.2 0.8 %collective-permute-start.9 = (bf16[2,64,256]{2,1,0:T(8,128)(2,1)}, bf16[2,64,256]{2,1,0:T(8,128)(2,1)}, u32[]{:S(2)}, u32[]{:S(2)}) collective-permute-start(bf16[2,64,256]{2,1,0:T(8,128)(2,1)} %pad_maximum_fusion.1), channel_id=1, source_target_pairs={{0,4},{1,3},{2,6},{3,1},{4,0},{5,9},{6,2},{7,11},{8,12},{9,5},{10,... | collective-permute-start | bytes 196616 | tf_op jit(solution)/shard_map/ppermute | solution.py:70
  27.1 0.1 copy.16.refs_8_.refs_7_
  27.2 1.4 %collective-permute-start.14 = (bf16[64,256]{1,0:T(8,128)(2,1)S(1)}, bf16[64,256]{1,0:T(8,128)(2,1)S(1)}, u32[]{:S(2)}, u32[]{:S(2)}) collective-permute-start(bf16[64,256]{1,0:T(8,128)(2,1)S(1)} %shard_map.65.refs_3_.refs_4_), channel_id=1, source_target_pairs={{0,18},{1,19},{2,16},{3,17},{4,22},{5,23},{6,20},{7,21},{8,26},{9,... | collective-permute-start | bytes 98312 | tf_op jit(solution)/shard_map/ppermute | solution.py:70
  28.6 2.2 %collective-permute-start.12 = (bf16[2,64,256]{2,1,0:T(8,128)(2,1)}, bf16[2,64,256]{2,1,0:T(8,128)(2,1)S(1)}, u32[]{:S(2)}, u32[]{:S(2)}) collective-permute-start(bf16[2,64,256]{2,1,0:T(8,128)(2,1)} %pad_maximum_fusion.1), channel_id=1, source_target_pairs={{0,22},{1,3},{2,20},{3,1},{4,18},{5,27},{6,16},{7,25},{8,30},{9,23... | collective-permute-start | bytes 196616 | tf_op jit(solution)/shard_map/ppermute | solution.py:70
  30.8 1.2 %collective-permute-start.10 = (bf16[2,64,256]{2,1,0:T(8,128)(2,1)}, bf16[2,64,256]{2,1,0:T(8,128)(2,1)S(1)}, u32[]{:S(2)}, u32[]{:S(2)}) collective-permute-start(bf16[2,64,256]{2,1,0:T(8,128)(2,1)} %pad_maximum_fusion.1), channel_id=1, source_target_pairs={{0,6},{1,3},{2,4},{3,1},{4,2},{5,11},{6,0},{7,9},{8,14},{9,7},{10,... | collective-permute-start | bytes 196616 | tf_op jit(solution)/shard_map/ppermute | solution.py:70
  31.9 1.8 %collective-permute-start.11 = (bf16[2,64,256]{2,1,0:T(8,128)(2,1)}, bf16[2,64,256]{2,1,0:T(8,128)(2,1)S(1)}, u32[]{:S(2)}, u32[]{:S(2)}) collective-permute-start(bf16[2,64,256]{2,1,0:T(8,128)(2,1)} %pad_maximum_fusion.1), channel_id=1, source_target_pairs={{0,20},{1,3},{2,22},{3,1},{4,16},{5,25},{6,18},{7,27},{8,28},{9,21... | collective-permute-start | bytes 196616 | tf_op jit(solution)/shard_map/ppermute | solution.py:70
  33.7 1.5 %collective-permute-start.13 = (bf16[2,64,256]{2,1,0:T(8,128)(2,1)}, bf16[2,64,256]{2,1,0:T(8,128)(2,1)S(1)}, u32[]{:S(2)}, u32[]{:S(2)}) collective-permute-start(bf16[2,64,256]{2,1,0:T(8,128)(2,1)} %pad_maximum_fusion.1), channel_id=1, source_target_pairs={{0,2},{1,17},{2,0},{3,19},{4,6},{5,21},{6,4},{7,23},{8,10},{9,25},... | collective-permute-start | bytes 196616 | tf_op jit(solution)/shard_map/ppermute | solution.py:70
  35.2 0.8 %constant_dynamic-update-slice_fusion.11 = bf16[11,64,256]{2,1,0:T(8,128)(2,1)S(1)} fusion(bf16[2,64,256]{2,1,0:T(8,128)(2,1)} %collective-permute-done.9), kind=kLoop, calls=%fused_computation.14 | loop fusion | bytes 131072
  36.1 0.1 collective-permute-done.10
  36.1 1.2 %collective-permute-done.11 = bf16[2,64,256]{2,1,0:T(8,128)(2,1)S(1)} collective-permute-done((bf16[2,64,256]{2,1,0:T(8,128)(2,1)}, bf16[2,64,256]{2,1,0:T(8,128)(2,1)S(1)}, u32[]{:S(2)}, u32[]{:S(2)}) %collective-permute-start.11) | collective-permute-done | bytes 65568 | tf_op jit(solution)/shard_map/ppermute | solution.py:70
  37.3 0.0 collective-permute-done.12.refs_0_
  37.3 1.0 %copy-done.2 = f32[64,2048]{1,0:T(8,128)S(1)} copy-done((f32[64,2048]{1,0:T(8,128)S(1)}, f32[64,2048]{1,0:T(8,128)}, u32[]{:S(2)}) %copy-start.2) | copy-done | bytes 524312
  38.4 2.6 %shard_map.66 = (bf16[2,64,256]{2,1,0:T(8,128)(2,1)S(1)}, f32[64,2048]{1,0:T(8,128)S(1)}, f32[64,2048]{1,0:T(8,128)S(1)}) custom-call(s32[256]{0:T(256)S(1)} %select_select_fusion.index_ref, bf16[2,64,256]{2,1,0:T(8,128)(2,1)S(1)} %collective-permute-done.12.refs_0_, ...), custom_call_target="tpu_custom_call", output_to_operand_aliasing={{0}: (1, {})} | custom-call | flops 134217728 | bytes 2097152 | tf_op jit(solution)/shard_map/pallas_call | solution.py:288
  41.0 0.0 collective-permute-done.13
  41.0 0.1 collective-permute-start.15
  41.1 1.7 %collective-permute-done.15.refs_1_.refs_2_ = bf16[11,64,256]{2,1,0:T(8,128)(2,1)S(1)} collective-permute-done((bf16[11,64,256]{2,1,0:T(8,128)(2,1)S(1)}, bf16[11,64,256]{2,1,0:T(8,128)(2,1)S(1)}, u32[]{:S(2)}, u32[]{:S(2)}) %collective-permute-start.15) | collective-permute-done | bytes 360480 | tf_op jit(solution)/shard_map/ppermute | solution.py:74
  42.8 1.2 %shard_map.67.refs_3_ = bf16[64,256]{1,0:T(8,128)(2,1)S(1)} custom-call(s32[256]{0:T(256)S(1)} %select_select_fusion.index_ref, bf16[11,64,256]{2,1,0:T(8,128)(2,1)S(1)} %constant_dynamic-update-slice_fusion.6.refs_0_.refs_1_, bf16[11,64,256]{2,1,0:T(8,128)(2,1)S(1)} %collective-permute-done.15.refs_1_.refs_2_, ...), custom_call_target="tpu_custom_call" | custom-call | flops 8388608 | bytes 131072 | tf_op jit(solution)/shard_map/pallas_call | solution.py:288
  44.0 0.2 collective-permute-start.16
  44.2 1.1 %collective-permute-done.16.refs_2_ = bf16[64,256]{1,0:T(8,128)(2,1)S(1)} collective-permute-done((bf16[64,256]{1,0:T(8,128)(2,1)S(1)}, bf16[64,256]{1,0:T(8,128)(2,1)S(1)}, u32[]{:S(2)}, u32[]{:S(2)}) %collective-permute-start.16) | collective-permute-done | bytes 32800 | tf_op jit(solution)/shard_map/ppermute | solution.py:74
  45.2 2.8 %collective-permute-start.20 = (bf16[2,64,256]{2,1,0:T(8,128)(2,1)S(1)}, bf16[2,64,256]{2,1,0:T(8,128)(2,1)S(1)}, u32[]{:S(2)}, u32[]{:S(2)}) collective-permute-start(bf16[2,64,256]{2,1,0:T(8,128)(2,1)S(1)} %pad_maximum_fusion.2), channel_id=1, source_target_pairs={{0,22},{1,3},{2,20},{3,1},{4,18},{5,27},{6,16},{7,25},{8,30},{9,23... | collective-permute-start | bytes 196616 | tf_op jit(solution)/shard_map/ppermute | solution.py:70
  48.0 0.7 %collective-permute-start.17 = (bf16[2,64,256]{2,1,0:T(8,128)(2,1)S(1)}, bf16[2,64,256]{2,1,0:T(8,128)(2,1)S(1)}, u32[]{:S(2)}, u32[]{:S(2)}) collective-permute-start(bf16[2,64,256]{2,1,0:T(8,128)(2,1)S(1)} %pad_maximum_fusion.2), channel_id=1, source_target_pairs={{0,4},{1,3},{2,6},{3,1},{4,0},{5,9},{6,2},{7,11},{8,12},{9,5},{10,... | collective-permute-start | bytes 196616 | tf_op jit(solution)/shard_map/ppermute | solution.py:70
  48.7 1.0 %collective-permute-start.22 = (bf16[64,256]{1,0:T(8,128)(2,1)S(1)}, bf16[64,256]{1,0:T(8,128)(2,1)S(1)}, u32[]{:S(2)}, u32[]{:S(2)}) collective-permute-start(bf16[64,256]{1,0:T(8,128)(2,1)S(1)} %shard_map.67.refs_3_), channel_id=1, source_target_pairs={{0,18},{1,19},{2,16},{3,17},{4,22},{5,23},{6,20},{7,21},{8,26},{9,... | collective-permute-start | bytes 98312 | tf_op jit(solution)/shard_map/ppermute | solution.py:70
  49.7 1.9 %collective-permute-start.18 = (bf16[2,64,256]{2,1,0:T(8,128)(2,1)S(1)}, bf16[2,64,256]{2,1,0:T(8,128)(2,1)S(1)}, u32[]{:S(2)}, u32[]{:S(2)}) collective-permute-start(bf16[2,64,256]{2,1,0:T(8,128)(2,1)S(1)} %pad_maximum_fusion.2), channel_id=1, source_target_pairs={{0,6},{1,3},{2,4},{3,1},{4,2},{5,11},{6,0},{7,9},{8,14},{9,7},{10,... | collective-permute-start | bytes 196616 | tf_op jit(solution)/shard_map/ppermute | solution.py:70
  51.6 1.5 %collective-permute-start.19 = (bf16[2,64,256]{2,1,0:T(8,128)(2,1)S(1)}, bf16[2,64,256]{2,1,0:T(8,128)(2,1)S(1)}, u32[]{:S(2)}, u32[]{:S(2)}) collective-permute-start(bf16[2,64,256]{2,1,0:T(8,128)(2,1)S(1)} %pad_maximum_fusion.2), channel_id=1, source_target_pairs={{0,20},{1,3},{2,22},{3,1},{4,16},{5,25},{6,18},{7,27},{8,28},{9,21... | collective-permute-start | bytes 196616 | tf_op jit(solution)/shard_map/ppermute | solution.py:70
  53.1 0.5 collective-permute-start.21
  53.6 2.6 %shard_map.68 = (bf16[2,64,256]{2,1,0:T(8,128)(2,1)S(1)}, f32[64,2048]{1,0:T(8,128)S(1)}, f32[64,2048]{1,0:T(8,128)S(1)}) custom-call(s32[256]{0:T(256)S(1)} %select_select_fusion.index_ref, bf16[2,64,256]{2,1,0:T(8,128)(2,1)S(1)} %collective-permute-done.20.refs_0_, ...), custom_call_target="tpu_custom_call", output_to_operand_aliasing={{0}: (1, {})} | custom-call | flops 134217728 | bytes 2097152 | tf_op jit(solution)/shard_map/pallas_call | solution.py:288
  56.2 0.0 collective-permute-done.17
  56.2 0.0 collective-permute-done.18
  56.3 0.5 collective-permute-done.19
  56.7 0.6 collective-permute-done.21
  57.4 0.0 collective-permute-done.22
  57.4 0.1 collective-permute-start.23
  57.5 1.7 %collective-permute-done.23.refs_1_ = bf16[11,64,256]{2,1,0:T(8,128)(2,1)S(1)} collective-permute-done((bf16[11,64,256]{2,1,0:T(8,128)(2,1)S(1)}, bf16[11,64,256]{2,1,0:T(8,128)(2,1)S(1)}, u32[]{:S(2)}, u32[]{:S(2)}) %collective-permute-start.23) | collective-permute-done | bytes 360480 | tf_op jit(solution)/shard_map/ppermute | solution.py:74
  59.1 2.8 %shard_map.69 = bf16[64,2048]{1,0:T(8,128)(2,1)} custom-call(s32[256]{0:T(256)S(1)} %select_select_fusion.index_ref, bf16[11,64,256]{2,1,0:T(8,128)(2,1)S(1)} %constant_dynamic-update-slice_fusion.12.refs_0_, bf16[11,64,256]{2,1,0:T(8,128)(2,1)S(1)} %collective-permute-done.23.refs_1_, bf16[64,256]{1,0:T(8,128)(2,1)S(1)} %collective-permute-done.16.refs_2_, ...), custom_call_target="tpu_custom_call" | custom-call | flops 67108864 | bytes 1048576 | tf_op jit(solution)/shard_map/pallas_call | solution.py:288
  (32 shorter events, 0.2 us)
Async XLA Ops:
  0.8 5.8 %collective-permute-start = (bf16[64,256]{1,0:T(8,128)(2,1)S(1)}, bf16[64,256]{1,0:T(8,128)(2,1)S(1)}, u32[]{:S(2)}, u32[]{:S(2)}) collective-permute-start(bf16[64,256]{1,0:T(8,128)(2,1)S(1)} %get-tuple-element.26.refs_3_.refs_4_), channel_id=1, source_target_pairs={{0,1},{1,0},{2,3},{3,2},{4,5},{5,4},{6,7},{7,6},{8,9},{9,8},{10,11... | collective-permute-start | bytes 98312 | tf_op jit(solution)/shard_map/ppermute | solution.py:74
  1.2 20.2 %collective-permute-start.6 = (bf16[64,256]{1,0:T(8,128)(2,1)S(1)}, bf16[64,256]{1,0:T(8,128)(2,1)S(1)}, u32[]{:S(2)}, u32[]{:S(2)}) collective-permute-start(bf16[64,256]{1,0:T(8,128)(2,1)S(1)} %get-tuple-element.26.refs_3_.refs_4_), channel_id=1, source_target_pairs={{0,18},{1,19},{2,16},{3,17},{4,22},{5,23},{6,20},{7,21},{8,26},{9,... | collective-permute-start | bytes 98312 | tf_op jit(solution)/shard_map/ppermute | solution.py:70
  6.5 6.7 %collective-permute-start.1 = (bf16[2,64,256]{2,1,0:T(8,128)(2,1)S(1)}, bf16[2,64,256]{2,1,0:T(8,128)(2,1)S(1)}, u32[]{:S(2)}, u32[]{:S(2)}) collective-permute-start(bf16[2,64,256]{2,1,0:T(8,128)(2,1)S(1)} %pad_maximum_fusion), channel_id=1, source_target_pairs={{0,4},{1,3},{2,6},{3,1},{4,0},{5,9},{6,2},{7,11},{8,12},{9,5},{10,... | collective-permute-start | bytes 196616 | tf_op jit(solution)/shard_map/ppermute | solution.py:70
  9.0 8.0 %collective-permute-start.4 = (bf16[2,64,256]{2,1,0:T(8,128)(2,1)S(1)}, bf16[2,64,256]{2,1,0:T(8,128)(2,1)S(1)}, u32[]{:S(2)}, u32[]{:S(2)}) collective-permute-start(bf16[2,64,256]{2,1,0:T(8,128)(2,1)S(1)} %pad_maximum_fusion), channel_id=1, source_target_pairs={{0,22},{1,3},{2,20},{3,1},{4,18},{5,27},{6,16},{7,25},{8,30},{9,23... | collective-permute-start | bytes 196616 | tf_op jit(solution)/shard_map/ppermute | solution.py:70
  9.0 5.8 %collective-permute-start.2 = (bf16[2,64,256]{2,1,0:T(8,128)(2,1)S(1)}, bf16[2,64,256]{2,1,0:T(8,128)(2,1)S(1)}, u32[]{:S(2)}, u32[]{:S(2)}) collective-permute-start(bf16[2,64,256]{2,1,0:T(8,128)(2,1)S(1)} %pad_maximum_fusion), channel_id=1, source_target_pairs={{0,6},{1,3},{2,4},{3,1},{4,2},{5,11},{6,0},{7,9},{8,14},{9,7},{10,... | collective-permute-start | bytes 196616 | tf_op jit(solution)/shard_map/ppermute | solution.py:70
  11.9 5.2 %collective-permute-start.3 = (bf16[2,64,256]{2,1,0:T(8,128)(2,1)S(1)}, bf16[2,64,256]{2,1,0:T(8,128)(2,1)S(1)}, u32[]{:S(2)}, u32[]{:S(2)}) collective-permute-start(bf16[2,64,256]{2,1,0:T(8,128)(2,1)S(1)} %pad_maximum_fusion), channel_id=1, source_target_pairs={{0,20},{1,3},{2,22},{3,1},{4,16},{5,25},{6,18},{7,27},{8,28},{9,21... | collective-permute-start | bytes 196616 | tf_op jit(solution)/shard_map/ppermute | solution.py:70
  13.3 8.1 %collective-permute-start.5 = (bf16[2,64,256]{2,1,0:T(8,128)(2,1)S(1)}, bf16[2,64,256]{2,1,0:T(8,128)(2,1)S(1)}, u32[]{:S(2)}, u32[]{:S(2)}) collective-permute-start(bf16[2,64,256]{2,1,0:T(8,128)(2,1)S(1)} %pad_maximum_fusion), channel_id=1, source_target_pairs={{0,2},{1,17},{2,0},{3,19},{4,6},{5,21},{6,4},{7,23},{8,10},{9,25},... | collective-permute-start | bytes 196616 | tf_op jit(solution)/shard_map/ppermute | solution.py:70
  17.0 1.6 %copy-start = (bf16[1,1,32,64,512]{4,3,2,1,0:T(8,128)(2,1)S(1)}, bf16[1,1,32,64,512]{4,3,2,1,0:T(8,128)(2,1)}, u32[]{:S(2)}) copy-start(bf16[1,1,32,64,512]{4,3,2,1,0:T(8,128)(2,1)} %param.7) | copy-start | bytes 6291460
  18.6 0.9 %copy-start.3 = (bf16[64,1,1,2048]{3,0,2,1:T(8,128)(2,1)S(1)}, bf16[64,1,1,2048]{3,0,2,1:T(8,128)(2,1)}, u32[]{:S(2)}) copy-start(bf16[64,1,1,2048]{3,0,2,1:T(8,128)(2,1)} %param.6) | copy-start | bytes 786436
  21.3 5.7 %copy-start.1 = (f32[64,2048]{1,0:T(8,128)}, f32[64,2048]{1,0:T(8,128)S(1)}, u32[]{:S(2)}) copy-start(f32[64,2048]{1,0:T(8,128)S(1)} %get-tuple-element.18.refs_7_) | copy-start | bytes 1572868
  21.3 5.7 %copy-start.4 = (f32[64]{0:T(128)S(1)}, f32[64]{0:T(128)}, u32[]{:S(2)}) copy-start(f32[64]{0:T(128)} %param.11) | copy-start | bytes 772
  21.4 1.7 %collective-permute-start.7 = (bf16[11,64,256]{2,1,0:T(8,128)(2,1)S(1)}, bf16[11,64,256]{2,1,0:T(8,128)(2,1)S(1)}, u32[]{:S(2)}, u32[]{:S(2)}) collective-permute-start(bf16[11,64,256]{2,1,0:T(8,128)(2,1)S(1)} %constant_dynamic-update-slice_fusion.refs_0_.refs_1_), channel_id=1, source_target_pairs={{0,1},{1,0},{2,3},{3,2},{4,5},{5,4},{6,7},{7,6},{8,9},{9,8},{10,11... | collective-permute-start | bytes 1081352 | tf_op jit(solution)/shard_map/ppermute | solution.py:74
  24.3 1.3 %collective-permute-start.8 = (bf16[64,256]{1,0:T(8,128)(2,1)S(1)}, bf16[64,256]{1,0:T(8,128)(2,1)S(1)}, u32[]{:S(2)}, u32[]{:S(2)}) collective-permute-start(bf16[64,256]{1,0:T(8,128)(2,1)S(1)} %shard_map.65.refs_3_.refs_4_), channel_id=1, source_target_pairs={{0,1},{1,0},{2,3},{3,2},{4,5},{5,4},{6,7},{7,6},{8,9},{9,8},{10,11... | collective-permute-start | bytes 98312 | tf_op jit(solution)/shard_map/ppermute | solution.py:74
  26.2 7.5 %collective-permute-start.9 = (bf16[2,64,256]{2,1,0:T(8,128)(2,1)}, bf16[2,64,256]{2,1,0:T(8,128)(2,1)}, u32[]{:S(2)}, u32[]{:S(2)}) collective-permute-start(bf16[2,64,256]{2,1,0:T(8,128)(2,1)} %pad_maximum_fusion.1), channel_id=1, source_target_pairs={{0,4},{1,3},{2,6},{3,1},{4,0},{5,9},{6,2},{7,11},{8,12},{9,5},{10,... | collective-permute-start | bytes 196616 | tf_op jit(solution)/shard_map/ppermute | solution.py:70
  27.2 13.8 %collective-permute-start.14 = (bf16[64,256]{1,0:T(8,128)(2,1)S(1)}, bf16[64,256]{1,0:T(8,128)(2,1)S(1)}, u32[]{:S(2)}, u32[]{:S(2)}) collective-permute-start(bf16[64,256]{1,0:T(8,128)(2,1)S(1)} %shard_map.65.refs_3_.refs_4_), channel_id=1, source_target_pairs={{0,18},{1,19},{2,16},{3,17},{4,22},{5,23},{6,20},{7,21},{8,26},{9,... | collective-permute-start | bytes 98312 | tf_op jit(solution)/shard_map/ppermute | solution.py:70
  28.6 8.8 %collective-permute-start.12 = (bf16[2,64,256]{2,1,0:T(8,128)(2,1)}, bf16[2,64,256]{2,1,0:T(8,128)(2,1)S(1)}, u32[]{:S(2)}, u32[]{:S(2)}) collective-permute-start(bf16[2,64,256]{2,1,0:T(8,128)(2,1)} %pad_maximum_fusion.1), channel_id=1, source_target_pairs={{0,22},{1,3},{2,20},{3,1},{4,18},{5,27},{6,16},{7,25},{8,30},{9,23... | collective-permute-start | bytes 196616 | tf_op jit(solution)/shard_map/ppermute | solution.py:70
  30.8 5.4 %collective-permute-start.10 = (bf16[2,64,256]{2,1,0:T(8,128)(2,1)}, bf16[2,64,256]{2,1,0:T(8,128)(2,1)S(1)}, u32[]{:S(2)}, u32[]{:S(2)}) collective-permute-start(bf16[2,64,256]{2,1,0:T(8,128)(2,1)} %pad_maximum_fusion.1), channel_id=1, source_target_pairs={{0,6},{1,3},{2,4},{3,1},{4,2},{5,11},{6,0},{7,9},{8,14},{9,7},{10,... | collective-permute-start | bytes 196616 | tf_op jit(solution)/shard_map/ppermute | solution.py:70
  31.9 5.4 %collective-permute-start.11 = (bf16[2,64,256]{2,1,0:T(8,128)(2,1)}, bf16[2,64,256]{2,1,0:T(8,128)(2,1)S(1)}, u32[]{:S(2)}, u32[]{:S(2)}) collective-permute-start(bf16[2,64,256]{2,1,0:T(8,128)(2,1)} %pad_maximum_fusion.1), channel_id=1, source_target_pairs={{0,20},{1,3},{2,22},{3,1},{4,16},{5,25},{6,18},{7,27},{8,28},{9,21... | collective-permute-start | bytes 196616 | tf_op jit(solution)/shard_map/ppermute | solution.py:70
  33.7 7.3 %collective-permute-start.13 = (bf16[2,64,256]{2,1,0:T(8,128)(2,1)}, bf16[2,64,256]{2,1,0:T(8,128)(2,1)S(1)}, u32[]{:S(2)}, u32[]{:S(2)}) collective-permute-start(bf16[2,64,256]{2,1,0:T(8,128)(2,1)} %pad_maximum_fusion.1), channel_id=1, source_target_pairs={{0,2},{1,17},{2,0},{3,19},{4,6},{5,21},{6,4},{7,23},{8,10},{9,25},... | collective-permute-start | bytes 196616 | tf_op jit(solution)/shard_map/ppermute | solution.py:70
  37.3 1.0 %copy-start.2 = (f32[64,2048]{1,0:T(8,128)S(1)}, f32[64,2048]{1,0:T(8,128)}, u32[]{:S(2)}) copy-start(f32[64,2048]{1,0:T(8,128)} %copy-done.1) | copy-start | bytes 1572868
  41.0 1.7 %collective-permute-start.15 = (bf16[11,64,256]{2,1,0:T(8,128)(2,1)S(1)}, bf16[11,64,256]{2,1,0:T(8,128)(2,1)S(1)}, u32[]{:S(2)}, u32[]{:S(2)}) collective-permute-start(bf16[11,64,256]{2,1,0:T(8,128)(2,1)S(1)} %constant_dynamic-update-slice_fusion.6.refs_0_.refs_1_), channel_id=1, source_target_pairs={{0,1},{1,0},{2,3},{3,2},{4,5},{5,4},{6,7},{7,6},{8,9},{9,8},{10,11... | collective-permute-start | bytes 1081352 | tf_op jit(solution)/shard_map/ppermute | solution.py:74
  44.0 1.3 %collective-permute-start.16 = (bf16[64,256]{1,0:T(8,128)(2,1)S(1)}, bf16[64,256]{1,0:T(8,128)(2,1)S(1)}, u32[]{:S(2)}, u32[]{:S(2)}) collective-permute-start(bf16[64,256]{1,0:T(8,128)(2,1)S(1)} %shard_map.67.refs_3_), channel_id=1, source_target_pairs={{0,1},{1,0},{2,3},{3,2},{4,5},{5,4},{6,7},{7,6},{8,9},{9,8},{10,11... | collective-permute-start | bytes 98312 | tf_op jit(solution)/shard_map/ppermute | solution.py:74
  45.2 7.8 %collective-permute-start.20 = (bf16[2,64,256]{2,1,0:T(8,128)(2,1)S(1)}, bf16[2,64,256]{2,1,0:T(8,128)(2,1)S(1)}, u32[]{:S(2)}, u32[]{:S(2)}) collective-permute-start(bf16[2,64,256]{2,1,0:T(8,128)(2,1)S(1)} %pad_maximum_fusion.2), channel_id=1, source_target_pairs={{0,22},{1,3},{2,20},{3,1},{4,18},{5,27},{6,16},{7,25},{8,30},{9,23... | collective-permute-start | bytes 196616 | tf_op jit(solution)/shard_map/ppermute | solution.py:70
  48.0 8.2 %collective-permute-start.17 = (bf16[2,64,256]{2,1,0:T(8,128)(2,1)S(1)}, bf16[2,64,256]{2,1,0:T(8,128)(2,1)S(1)}, u32[]{:S(2)}, u32[]{:S(2)}) collective-permute-start(bf16[2,64,256]{2,1,0:T(8,128)(2,1)S(1)} %pad_maximum_fusion.2), channel_id=1, source_target_pairs={{0,4},{1,3},{2,6},{3,1},{4,0},{5,9},{6,2},{7,11},{8,12},{9,5},{10,... | collective-permute-start | bytes 196616 | tf_op jit(solution)/shard_map/ppermute | solution.py:70
  48.7 8.7 %collective-permute-start.22 = (bf16[64,256]{1,0:T(8,128)(2,1)S(1)}, bf16[64,256]{1,0:T(8,128)(2,1)S(1)}, u32[]{:S(2)}, u32[]{:S(2)}) collective-permute-start(bf16[64,256]{1,0:T(8,128)(2,1)S(1)} %shard_map.67.refs_3_), channel_id=1, source_target_pairs={{0,18},{1,19},{2,16},{3,17},{4,22},{5,23},{6,20},{7,21},{8,26},{9,... | collective-permute-start | bytes 98312 | tf_op jit(solution)/shard_map/ppermute | solution.py:70
  49.7 6.6 %collective-permute-start.18 = (bf16[2,64,256]{2,1,0:T(8,128)(2,1)S(1)}, bf16[2,64,256]{2,1,0:T(8,128)(2,1)S(1)}, u32[]{:S(2)}, u32[]{:S(2)}) collective-permute-start(bf16[2,64,256]{2,1,0:T(8,128)(2,1)S(1)} %pad_maximum_fusion.2), channel_id=1, source_target_pairs={{0,6},{1,3},{2,4},{3,1},{4,2},{5,11},{6,0},{7,9},{8,14},{9,7},{10,... | collective-permute-start | bytes 196616 | tf_op jit(solution)/shard_map/ppermute | solution.py:70
  51.6 5.2 %collective-permute-start.19 = (bf16[2,64,256]{2,1,0:T(8,128)(2,1)S(1)}, bf16[2,64,256]{2,1,0:T(8,128)(2,1)S(1)}, u32[]{:S(2)}, u32[]{:S(2)}) collective-permute-start(bf16[2,64,256]{2,1,0:T(8,128)(2,1)S(1)} %pad_maximum_fusion.2), channel_id=1, source_target_pairs={{0,20},{1,3},{2,22},{3,1},{4,16},{5,25},{6,18},{7,27},{8,28},{9,21... | collective-permute-start | bytes 196616 | tf_op jit(solution)/shard_map/ppermute | solution.py:70
  53.1 4.3 %collective-permute-start.21 = (bf16[2,64,256]{2,1,0:T(8,128)(2,1)S(1)}, bf16[2,64,256]{2,1,0:T(8,128)(2,1)S(1)}, u32[]{:S(2)}, u32[]{:S(2)}) collective-permute-start(bf16[2,64,256]{2,1,0:T(8,128)(2,1)S(1)} %pad_maximum_fusion.2), channel_id=1, source_target_pairs={{0,2},{1,17},{2,0},{3,19},{4,6},{5,21},{6,4},{7,23},{8,10},{9,25},... | collective-permute-start | bytes 196616 | tf_op jit(solution)/shard_map/ppermute | solution.py:70
  57.4 1.7 %collective-permute-start.23 = (bf16[11,64,256]{2,1,0:T(8,128)(2,1)S(1)}, bf16[11,64,256]{2,1,0:T(8,128)(2,1)S(1)}, u32[]{:S(2)}, u32[]{:S(2)}) collective-permute-start(bf16[11,64,256]{2,1,0:T(8,128)(2,1)S(1)} %constant_dynamic-update-slice_fusion.12.refs_0_), channel_id=1, source_target_pairs={{0,1},{1,0},{2,3},{3,2},{4,5},{5,4},{6,7},{7,6},{8,9},{9,8},{10,11... | collective-permute-start | bytes 1081352 | tf_op jit(solution)/shard_map/ppermute | solution.py:74

commit v5 on v4

--- a/solution.py
+++ b/solution.py
@@ -12,6 +12,7 @@
 FEATURES = 64
 NEAR = 4
 PARTS = 4
+VMEM_MIB = 16
 LANES = 2 * PB
 AXES = ("gx", "gy", "gz")
 
@@ -76,13 +77,18 @@
 
 def exchange(rim, work):
     chips = partners()
-    alone = [swap(rim, (chips[-1], chips[-1]))] if len(chips) % 2 else []
+    sides = len(pairings(lax.axis_size("gy")))
+    plane = chips[-((len(chips) - sides) // (sides + 1)) :]
     other = swap_cores(rim)
     both = jnp.stack([rim, other])
-    steps = reversed(range(0, len(chips) - len(chips) % 2, 2))
-    shares = [swap(both, (chips[t], chips[t + 1])) for t in steps]
-    shares[1], *results = work(shares[1])
-    received = jnp.concatenate(shares[::-1] + [panel[None] for panel in alone])
+    side = swap(both, (chips[0], chips[sides - 1]))
+    alone = [swap(rim, (plane[-1], plane[-1]))] if len(plane) % 2 else []
+    own = [
+        swap(both, (plane[t], plane[t + 1])) for t in range(0, len(plane) - len(plane) % 2, 2)
+    ]
+    passed = [swap(side, (chip, chip)) for chip in plane[::-1]]
+    passed[0], *results = work(passed[0])
+    received = jnp.concatenate([side] + passed[::-1] + own + [panel[None] for panel in alone])
     return (received, swap_cores(received), other, rim), results
 
 
@@ -183,7 +189,7 @@
 
 def first_kernel(
     index_ref, _, value_hbm, raw_hbm, scale_hbm,
-    __, tile_out, near_out, total_out,
+    __, tile_out, near_out,
     store, value_ref, raw_ref, scale_ref, arrived,
 ):
     count, slot_count = scale_ref.shape
@@ -208,7 +214,6 @@
     )
     for t in range(value_ref.shape[1] // LANES):
         pair = value_ref[:, t * LANES : (t + 1) * LANES]
-        total_out[:, t * LANES : (t + 1) * LANES] = pair.astype(total_out.dtype)
         spread(pair, store, 2 * t)
     clear_last(store)
     for p in range(PARTS):
@@ -255,15 +260,21 @@
 def far_kernel(step, last, index_ref, *refs):
     if not last:
         refs = refs[1:]
-    rims, (tile_ref, near_ref, total_ref, times_ref) = refs[:4], refs[4:8]
+    rims, (tile_ref, near_ref, times_ref, total_ref) = refs[:4], refs[4:8]
     if last:
         total_out, store = refs[8:]
     else:
-        _, total_out, near_out, store, own_store = refs[8:]
+        _, total_out, near_out, store, own_store, *fetching = refs[8:]
         clear_last(own_store)
+        if fetching:
+            features_hbm, (total_ref, arrived) = total_ref, fetching
+            fetch = pltpu.make_async_copy(features_hbm, total_ref, arrived)
+            fetch.start()
     slot_count = tile_ref.shape[1] // PB
     each_rim(rims, lambda pair, number: spread(pair, store, number))
     clear_last(store)
+    if not last and fetching:
+        fetch.wait()
     factor = jnp.ones(times_ref.shape, jnp.float32)
     for n in range(1, step + 1):
         factor = factor * -times_ref[...] / jnp.float32(n)
@@ -282,22 +293,24 @@
         near_image(index_ref, own_store, tile_ref, near_out)
 
 
-def call(kernel, out_shape, scratch, flops, index, *arrays, space=pltpu.VMEM, through=None):
+def call(kernel, out_shape, scratch, flops, index, *arrays, fetched=(), through=None):
     handed = () if through is None else (through,)
     out_shape = tuple(jax.ShapeDtypeStruct(x.shape, x.dtype) for x in handed) + out_shape
+    anywhere, vmem = pl.BlockSpec(memory_space=pl.ANY), pl.BlockSpec(memory_space=pltpu.VMEM)
+    fetched = [pltpu.with_memory_space_constraint(x, pltpu.HBM) for x in fetched]
     return pl.pallas_call(
         kernel,
         out_shape=out_shape,
         in_specs=[pl.BlockSpec(memory_space=pltpu.SMEM)]
-        + [pl.BlockSpec(memory_space=pl.ANY)] * len(handed)
-        + [pl.BlockSpec(memory_space=space)] * len(arrays),
-        out_specs=(pl.BlockSpec(memory_space=pl.ANY),) * len(handed)
-        + (pl.BlockSpec(memory_space=pltpu.VMEM),) * (len(out_shape) - len(handed)),
+        + [anywhere] * len(handed)
+        + [vmem] * len(arrays)
+        + [pl.BlockSpec(memory_space=pltpu.HBM)] * len(fetched),
+        out_specs=(anywhere,) * len(handed) + (vmem,) * (len(out_shape) - len(handed)),
         scratch_shapes=scratch,
         input_output_aliases={1: 0} if handed else {},
-        compiler_params=pltpu.CompilerParams(vmem_limit_bytes=16 * 1024 * 1024),
+        compiler_params=pltpu.CompilerParams(vmem_limit_bytes=VMEM_MIB * 1024 * 1024),
         cost_estimate=pl.CostEstimate(flops=flops, bytes_accessed=flops // 64, transcendentals=0),
-    )(index, *handed, *arrays)
+    )(index, *handed, *arrays, *fetched)
 
 
 def body(features, tiles, scales, slots, live, times):
@@ -324,7 +337,7 @@
     def first(through):
         return call(
             first_kernel,
-            (tile_shape, image_shape, image_shape),
+            (tile_shape, image_shape),
             [
                 own_store,
                 pltpu.VMEM(value.shape, jnp.bfloat16),
@@ -334,28 +347,28 @@
             ],
             half,
             index,
-            value,
-            tiles.reshape(points, width),
-            scales.reshape(count, slot_count),
-            space=pltpu.HBM,
+            fetched=(value, tiles.reshape(points, width), scales.reshape(count, slot_count)),
             through=through,
         )
 
-    rims, (scaled, near, total) = exchange(rim, first)
+    rims, (scaled, near) = exchange(rim, first)
     times = times[:, None]
     for step in range(1, TERMS):
         arrays = (index, *rims, scaled, near)
         (rim,) = call(rim_kernel, (rim_shape,), [pair_store], half // 8, *arrays)
 
         def rest(through):
+            begun = step > 1
+            fetch = [pltpu.VMEM(value.shape, jnp.bfloat16), pltpu.SemaphoreType.DMA]
             return call(
                 functools.partial(far_kernel, step, False),
                 (image_shape, image_shape),
-                [far_store, own_store],
+                [far_store, own_store] + ([] if begun else fetch),
                 2 * half,
                 *arrays,
-                total,
                 times,
+                *([total] if begun else []),
+                fetched=() if begun else (value,),
                 through=through,
             )
 
@@ -369,8 +382,8 @@
         *rims,
         scaled,
         near,
+        times,
         total,
-        times,
     )
     return out.reshape(features.shape)
 

time: 62.3 us -> 59.1 us (0.949)
  local copies, waits for them, and re-layouts: 7.19 us -> 4.26 us
  starting transfers between devices: 28.2 us -> 26.2 us
  Pallas kernels: 12.1 us -> 13 us
  waiting for transfers between devices: 12.7 us -> 13.5 us
    unnamed x27 -> x19, local copies, waits for them, and re-layouts: 6.04 us -> 3.1 us
    ppermute x18, starting transfers between devices: 27.1 us -> 25.1 us  [swap(): return lax.ppermute(value, AXES, pairs)]
    pallas_call x6, Pallas kernels: 12.1 us -> 13 us  [call(): pl.pallas_call(kernel, out_shape=out_shape, in_specs=[pl.BlockSpec(memory...]
    ppermute x18, waiting for transfers between devices: 5.57 us -> 6.37 us  [swap(): return lax.ppermute(value, AXES, pairs)]
  transfers between devices with their start and end apart: 24 -> 24, of which waited for: 11 -> 11; matrix products, arithmetic and copies ran while one was open for 6% -> 7% of each run, Pallas kernels for 11% -> 13%
where the time goes in v5:
time: 59.1 us; the launch traced here: 58.8 us
  starting transfers between devices  26.2 us (44%)
  waiting for transfers between devices  13.5 us (23%)
  Pallas kernels  13 us (22%)
  local copies, waits for them, and re-layouts  4.26 us (7%)
  other arithmetic  1.43 us (2%)
    ppermute x18, starting transfers between devices, swap(): return lax.ppermute(value, AXES, pairs)  25.1 us
    pallas_call x6, Pallas kernels, call(): pl.pallas_call(kernel, out_shape=out_shape, in_specs=[pl.BlockSpec(memory...  13 us
    ppermute x6, waiting for transfers between devices, swap_cores(): lax.ppermute(value, 'gz', [(k, k ^ 1) for k in range(lax.axis_size('gz'))])  7.13 us
    ppermute x18, waiting for transfers between devices, swap(): return lax.ppermute(value, AXES, pairs)  6.37 us
    unnamed x19, local copies, waits for them, and re-layouts  3.1 us
  transfers between devices with their start and end apart: 24, of which 11 were waited for; matrix products, arithmetic and copies ran while one was open for 7% of the time, Pallas kernels for 13%

profile of v5, /device:TPU:0, one launch (start us, length us, event | category | flops | bytes accessed | tf_op | source)
XLA Modules:
  0.0 58.8 jit_solution(11025973277954932076)
XLA Ops:
  0.0 0.8 %slice_bitcast_fusion = (bf16[1,64,256]{2,1,0:T(8,128)(2,1)S(1)}, bf16[64,256]{1,0:T(8,128)(2,1)S(1)}) fusion(bf16[64,2048]{1,0:T(8,128)(2,1)} %bitcast.27), kind=kLoop, calls=%fused_computation.57 | loop fusion | bytes 98304 | tf_op jit(solution)/shard_map/stack | solution.py:83
  0.8 0.5 collective-permute-start
  1.2 3.4 %collective-permute-start.6 = (bf16[64,256]{1,0:T(8,128)(2,1)S(1)}, bf16[64,256]{1,0:T(8,128)(2,1)S(1)}, u32[]{:S(2)}, u32[]{:S(2)}) collective-permute-start(bf16[64,256]{1,0:T(8,128)(2,1)S(1)} %get-tuple-element.24.refs_3_.refs_4_), channel_id=1, source_target_pairs={{0,18},{1,19},{2,16},{3,17},{4,22},{5,23},{6,20},{7,21},{8,26},{9,... | collective-permute-start | bytes 98312 | tf_op jit(solution)/shard_map/ppermute | solution.py:71
  4.7 0.7 %iota_compare_fusion = pred[32,8]{1,0:T(8,128)(4,1)S(1)} fusion(s32[32]{0:T(128)} %bitcast.32), kind=kLoop, calls=%fused_computation.21 | loop fusion | flops 256 | bytes 384 | tf_op jit(solution)/shard_map/lt | solution.py:120
  5.4 0.8 %copy.14 = s32[1,1,32,8]{3,2,1,0:T(8,128)S(1)} copy(s32[1,1,32,8]{2,3,1,0:T(8,128)} %param.9) | data formatting | bytes 2048 | tf_op args[3]
  6.2 0.1 reshape.23
  6.3 0.1 iota.13
  6.4 0.1 lt.70
  6.5 0.0 collective-permute-done.refs_2_.refs_3_
  6.5 1.6 %collective-permute-start.1 = (bf16[2,64,256]{2,1,0:T(8,128)(2,1)S(1)}, bf16[2,64,256]{2,1,0:T(8,128)(2,1)S(1)}, u32[]{:S(2)}, u32[]{:S(2)}) collective-permute-start(bf16[2,64,256]{2,1,0:T(8,128)(2,1)S(1)} %pad_maximum_fusion), channel_id=1, source_target_pairs={{0,4},{1,3},{2,6},{3,1},{4,0},{5,9},{6,2},{7,11},{8,12},{9,5},{10,... | collective-permute-start | bytes 196616 | tf_op jit(solution)/shard_map/ppermute | solution.py:71
  8.2 1.4 %copy.15 = f32[1,1,32,8]{3,2,1,0:T(8,128)} copy(f32[1,1,32,8]{2,3,1,0:T(8,128)} %param.8) | data formatting | bytes 2048 | tf_op args[2]
  9.6 0.5 collective-permute-start.5
  10.1 0.7 %collective-permute-done.1 = bf16[2,64,256]{2,1,0:T(8,128)(2,1)S(1)} collective-permute-done((bf16[2,64,256]{2,1,0:T(8,128)(2,1)S(1)}, bf16[2,64,256]{2,1,0:T(8,128)(2,1)S(1)}, u32[]{:S(2)}, u32[]{:S(2)}) %collective-permute-start.1) | collective-permute-done | bytes 65568 | tf_op jit(solution)/shard_map/ppermute | solution.py:71
  10.9 0.7 %collective-permute-start.4 = (bf16[2,64,256]{2,1,0:T(8,128)(2,1)S(1)}, bf16[2,64,256]{2,1,0:T(8,128)(2,1)S(1)}, u32[]{:S(2)}, u32[]{:S(2)}) collective-permute-start(bf16[2,64,256]{2,1,0:T(8,128)(2,1)S(1)} %collective-permute-done.1), channel_id=1, source_target_pairs={{0,18},{1,19},{2,16},{3,17},{4,22},{5,23},{6,20},{7,21},{8,26},{9,... | collective-permute-start | bytes 196616 | tf_op jit(solution)/shard_map/ppermute | solution.py:71
  11.6 1.3 %collective-permute-start.2 = (bf16[2,64,256]{2,1,0:T(8,128)(2,1)S(1)}, bf16[2,64,256]{2,1,0:T(8,128)(2,1)S(1)}, u32[]{:S(2)}, u32[]{:S(2)}) collective-permute-start(bf16[2,64,256]{2,1,0:T(8,128)(2,1)S(1)} %collective-permute-done.1), channel_id=1, source_target_pairs={{0,2},{1,3},{2,0},{3,1},{4,6},{5,7},{6,4},{7,5},{8,10},{9,11},{10,... | collective-permute-start | bytes 196616 | tf_op jit(solution)/shard_map/ppermute | solution.py:71
  12.8 1.5 %collective-permute-start.3 = (bf16[2,64,256]{2,1,0:T(8,128)(2,1)S(1)}, bf16[2,64,256]{2,1,0:T(8,128)(2,1)S(1)}, u32[]{:S(2)}, u32[]{:S(2)}) collective-permute-start(bf16[2,64,256]{2,1,0:T(8,128)(2,1)S(1)} %collective-permute-done.1), channel_id=1, source_target_pairs={{0,16},{1,17},{2,18},{3,19},{4,20},{5,21},{6,22},{7,23},{8,24},{9,... | collective-permute-start | bytes 196616 | tf_op jit(solution)/shard_map/ppermute | solution.py:71
  14.4 1.6 %collective-permute-done.2 = bf16[2,64,256]{2,1,0:T(8,128)(2,1)S(1)} collective-permute-done((bf16[2,64,256]{2,1,0:T(8,128)(2,1)S(1)}, bf16[2,64,256]{2,1,0:T(8,128)(2,1)S(1)}, u32[]{:S(2)}, u32[]{:S(2)}) %collective-permute-start.2) | collective-permute-done | bytes 65568 | tf_op jit(solution)/shard_map/ppermute | solution.py:71
  16.0 1.1 %collective-permute-done.3 = bf16[2,64,256]{2,1,0:T(8,128)(2,1)S(1)} collective-permute-done((bf16[2,64,256]{2,1,0:T(8,128)(2,1)S(1)}, bf16[2,64,256]{2,1,0:T(8,128)(2,1)S(1)}, u32[]{:S(2)}, u32[]{:S(2)}) %collective-permute-start.3) | collective-permute-done | bytes 65568 | tf_op jit(solution)/shard_map/ppermute | solution.py:71
  17.1 0.0 collective-permute-done.4._
  17.1 2.7 %shard_map.64 = (bf16[2,64,256]{2,1,0:T(8,128)(2,1)S(1)}, bf16[2048,512]{1,0:T(8,128)(2,1)S(1)}, f32[64,2048]{1,0:T(8,128)S(1)}) custom-call(s32[256]{0:T(256)S(1)} %select_select_fusion.index_ref, bf16[2,64,256]{2,1,0:T(8,128)(2,1)S(1)} %collective-permute-done.4._, bf16[64,2048]{1,0:T(8,128)(2,1)} %bitcast.28, ...), custom_call_target="tpu_custom_call", output_to_operand_aliasing={{0}: (1, {})} | custom-call | flops 67108864 | bytes 1048576 | tf_op jit(solution)/shard_map/pallas_call | solution.py:301
  19.8 0.0 copy-start
  19.8 0.0 collective-permute-done.5
  19.9 0.0 collective-permute-done.6
  19.9 0.1 collective-permute-start.7
  20.0 1.7 %collective-permute-done.7.refs_1_.refs_2_ = bf16[11,64,256]{2,1,0:T(8,128)(2,1)S(1)} collective-permute-done((bf16[11,64,256]{2,1,0:T(8,128)(2,1)S(1)}, bf16[11,64,256]{2,1,0:T(8,128)(2,1)S(1)}, u32[]{:S(2)}, u32[]{:S(2)}) %collective-permute-start.7) | collective-permute-done | bytes 360480 | tf_op jit(solution)/shard_map/ppermute | solution.py:75
  21.6 1.2 %shard_map.65.refs_3_.refs_4_ = bf16[64,256]{1,0:T(8,128)(2,1)S(1)} custom-call(s32[256]{0:T(256)S(1)} %select_select_fusion.index_ref, bf16[11,64,256]{2,1,0:T(8,128)(2,1)S(1)} %constant_dynamic-update-slice_fusion.refs_0_.refs_1_, bf16[11,64,256]{2,1,0:T(8,128)(2,1)S(1)} %collective-permute-done.7.refs_1_.refs_2_, ...), custom_call_target="tpu_custom_call" | custom-call | flops 8388608 | bytes 131072 | tf_op jit(solution)/shard_map/pallas_call | solution.py:301
  22.8 0.2 collective-permute-start.8
  23.0 1.1 %collective-permute-done.8.refs_2_.refs_3_ = bf16[64,256]{1,0:T(8,128)(2,1)S(1)} collective-permute-done((bf16[64,256]{1,0:T(8,128)(2,1)S(1)}, bf16[64,256]{1,0:T(8,128)(2,1)S(1)}, u32[]{:S(2)}, u32[]{:S(2)}) %collective-permute-start.8) | collective-permute-done | bytes 32800 | tf_op jit(solution)/shard_map/ppermute | solution.py:75
  24.1 0.6 %pad_maximum_fusion.1 = bf16[2,64,256]{2,1,0:T(8,128)(2,1)} fusion(bf16[1,64,256]{2,1,0:T(8,128)(2,1)S(1)} %bitcast.23, bf16[1,64,256]{2,1,0:T(8,128)(2,1)S(1)} %bitcast.21), kind=kLoop, calls=%fused_computation.1 | loop fusion | flops 32768 | bytes 131072 | tf_op jit(solution)/shard_map/stack | solution.py:83
  24.7 1.6 %collective-permute-start.9 = (bf16[2,64,256]{2,1,0:T(8,128)(2,1)}, bf16[2,64,256]{2,1,0:T(8,128)(2,1)}, u32[]{:S(2)}, u32[]{:S(2)}) collective-permute-start(bf16[2,64,256]{2,1,0:T(8,128)(2,1)} %pad_maximum_fusion.1), channel_id=1, source_target_pairs={{0,4},{1,3},{2,6},{3,1},{4,0},{5,9},{6,2},{7,11},{8,12},{9,5},{10,... | collective-permute-start | bytes 196616 | tf_op jit(solution)/shard_map/ppermute | solution.py:71
  26.3 0.1 copy.16.refs_7_.refs_6_
  26.4 1.5 %collective-permute-start.14 = (bf16[64,256]{1,0:T(8,128)(2,1)S(1)}, bf16[64,256]{1,0:T(8,128)(2,1)S(1)}, u32[]{:S(2)}, u32[]{:S(2)}) collective-permute-start(bf16[64,256]{1,0:T(8,128)(2,1)S(1)} %shard_map.65.refs_3_.refs_4_), channel_id=1, source_target_pairs={{0,18},{1,19},{2,16},{3,17},{4,22},{5,23},{6,20},{7,21},{8,26},{9,... | collective-permute-start | bytes 98312 | tf_op jit(solution)/shard_map/ppermute | solution.py:71
  27.9 1.5 %collective-permute-start.13 = (bf16[2,64,256]{2,1,0:T(8,128)(2,1)}, bf16[2,64,256]{2,1,0:T(8,128)(2,1)S(1)}, u32[]{:S(2)}, u32[]{:S(2)}) collective-permute-start(bf16[2,64,256]{2,1,0:T(8,128)(2,1)} %pad_maximum_fusion.1), channel_id=1, source_target_pairs={{0,2},{1,17},{2,0},{3,19},{4,6},{5,21},{6,4},{7,23},{8,10},{9,25},... | collective-permute-start | bytes 196616 | tf_op jit(solution)/shard_map/ppermute | solution.py:71
  29.4 0.0 collective-permute-done.9
  29.4 1.6 %collective-permute-start.12 = (bf16[2,64,256]{2,1,0:T(8,128)(2,1)}, bf16[2,64,256]{2,1,0:T(8,128)(2,1)S(1)}, u32[]{:S(2)}, u32[]{:S(2)}) collective-permute-start(bf16[2,64,256]{2,1,0:T(8,128)(2,1)} %collective-permute-done.9), channel_id=1, source_target_pairs={{0,18},{1,19},{2,16},{3,17},{4,22},{5,23},{6,20},{7,21},{8,26},{9,... | collective-permute-start | bytes 196616 | tf_op jit(solution)/shard_map/ppermute | solution.py:71
  31.0 1.3 %collective-permute-start.10 = (bf16[2,64,256]{2,1,0:T(8,128)(2,1)}, bf16[2,64,256]{2,1,0:T(8,128)(2,1)S(1)}, u32[]{:S(2)}, u32[]{:S(2)}) collective-permute-start(bf16[2,64,256]{2,1,0:T(8,128)(2,1)} %collective-permute-done.9), channel_id=1, source_target_pairs={{0,2},{1,3},{2,0},{3,1},{4,6},{5,7},{6,4},{7,5},{8,10},{9,11},{10,... | collective-permute-start | bytes 196616 | tf_op jit(solution)/shard_map/ppermute | solution.py:71
  32.3 0.9 %constant_dynamic-update-slice_fusion.11 = bf16[11,64,256]{2,1,0:T(8,128)(2,1)S(1)} fusion(bf16[2,64,256]{2,1,0:T(8,128)(2,1)} %collective-permute-done.9), kind=kLoop, calls=%fused_computation.14 | loop fusion | bytes 131072
  33.2 0.6 %collective-permute-start.11 = (bf16[2,64,256]{2,1,0:T(8,128)(2,1)}, bf16[2,64,256]{2,1,0:T(8,128)(2,1)S(1)}, u32[]{:S(2)}, u32[]{:S(2)}) collective-permute-start(bf16[2,64,256]{2,1,0:T(8,128)(2,1)} %collective-permute-done.9), channel_id=1, source_target_pairs={{0,16},{1,17},{2,18},{3,19},{4,20},{5,21},{6,22},{7,23},{8,24},{9,... | collective-permute-start | bytes 196616 | tf_op jit(solution)/shard_map/ppermute | solution.py:71
  33.8 1.0 %collective-permute-done.12.refs_0_ = bf16[2,64,256]{2,1,0:T(8,128)(2,1)S(1)} collective-permute-done((bf16[2,64,256]{2,1,0:T(8,128)(2,1)}, bf16[2,64,256]{2,1,0:T(8,128)(2,1)S(1)}, u32[]{:S(2)}, u32[]{:S(2)}) %collective-permute-start.12) | collective-permute-done | bytes 65568 | tf_op jit(solution)/shard_map/ppermute | solution.py:71
  34.8 2.6 %shard_map.66 = (bf16[2,64,256]{2,1,0:T(8,128)(2,1)S(1)}, f32[64,2048]{1,0:T(8,128)S(1)}, f32[64,2048]{1,0:T(8,128)S(1)}) custom-call(s32[256]{0:T(256)S(1)} %select_select_fusion.index_ref, bf16[2,64,256]{2,1,0:T(8,128)(2,1)S(1)} %collective-permute-done.12.refs_0_, ...), custom_call_target="tpu_custom_call", output_to_operand_aliasing={{0}: (1, {})} | custom-call | flops 134217728 | bytes 2097152 | tf_op jit(solution)/shard_map/pallas_call | solution.py:301
  37.5 0.0 collective-permute-done.10
  37.5 0.2 collective-permute-done.11
  37.7 0.0 collective-permute-done.13
  37.7 0.0 collective-permute-done.14
  37.7 0.1 collective-permute-start.15
  37.8 1.7 %collective-permute-done.15.refs_1_.refs_2_ = bf16[11,64,256]{2,1,0:T(8,128)(2,1)S(1)} collective-permute-done((bf16[11,64,256]{2,1,0:T(8,128)(2,1)S(1)}, bf16[11,64,256]{2,1,0:T(8,128)(2,1)S(1)}, u32[]{:S(2)}, u32[]{:S(2)}) %collective-permute-start.15) | collective-permute-done | bytes 360480 | tf_op jit(solution)/shard_map/ppermute | solution.py:75
  39.4 1.2 %shard_map.67.refs_3_ = bf16[64,256]{1,0:T(8,128)(2,1)S(1)} custom-call(s32[256]{0:T(256)S(1)} %select_select_fusion.index_ref, bf16[11,64,256]{2,1,0:T(8,128)(2,1)S(1)} %constant_dynamic-update-slice_fusion.6.refs_0_.refs_1_, bf16[11,64,256]{2,1,0:T(8,128)(2,1)S(1)} %collective-permute-done.15.refs_1_.refs_2_, ...), custom_call_target="tpu_custom_call" | custom-call | flops 8388608 | bytes 131072 | tf_op jit(solution)/shard_map/pallas_call | solution.py:301
  40.6 0.2 collective-permute-start.16
  40.8 1.1 %collective-permute-done.16.refs_2_ = bf16[64,256]{1,0:T(8,128)(2,1)S(1)} collective-permute-done((bf16[64,256]{1,0:T(8,128)(2,1)S(1)}, bf16[64,256]{1,0:T(8,128)(2,1)S(1)}, u32[]{:S(2)}, u32[]{:S(2)}) %collective-permute-start.16) | collective-permute-done | bytes 32800 | tf_op jit(solution)/shard_map/ppermute | solution.py:75
  41.9 1.6 %collective-permute-start.17 = (bf16[2,64,256]{2,1,0:T(8,128)(2,1)S(1)}, bf16[2,64,256]{2,1,0:T(8,128)(2,1)S(1)}, u32[]{:S(2)}, u32[]{:S(2)}) collective-permute-start(bf16[2,64,256]{2,1,0:T(8,128)(2,1)S(1)} %pad_maximum_fusion.2), channel_id=1, source_target_pairs={{0,4},{1,3},{2,6},{3,1},{4,0},{5,9},{6,2},{7,11},{8,12},{9,5},{10,... | collective-permute-start | bytes 196616 | tf_op jit(solution)/shard_map/ppermute | solution.py:71
  43.5 1.3 %collective-permute-start.22 = (bf16[64,256]{1,0:T(8,128)(2,1)S(1)}, bf16[64,256]{1,0:T(8,128)(2,1)S(1)}, u32[]{:S(2)}, u32[]{:S(2)}) collective-permute-start(bf16[64,256]{1,0:T(8,128)(2,1)S(1)} %shard_map.67.refs_3_), channel_id=1, source_target_pairs={{0,18},{1,19},{2,16},{3,17},{4,22},{5,23},{6,20},{7,21},{8,26},{9,... | collective-permute-start | bytes 98312 | tf_op jit(solution)/shard_map/ppermute | solution.py:71
  44.9 1.5 %collective-permute-start.21 = (bf16[2,64,256]{2,1,0:T(8,128)(2,1)S(1)}, bf16[2,64,256]{2,1,0:T(8,128)(2,1)S(1)}, u32[]{:S(2)}, u32[]{:S(2)}) collective-permute-start(bf16[2,64,256]{2,1,0:T(8,128)(2,1)S(1)} %pad_maximum_fusion.2), channel_id=1, source_target_pairs={{0,2},{1,17},{2,0},{3,19},{4,6},{5,21},{6,4},{7,23},{8,10},{9,25},... | collective-permute-start | bytes 196616 | tf_op jit(solution)/shard_map/ppermute | solution.py:71
  46.4 0.0 collective-permute-done.17
  46.4 1.5 %collective-permute-start.20 = (bf16[2,64,256]{2,1,0:T(8,128)(2,1)S(1)}, bf16[2,64,256]{2,1,0:T(8,128)(2,1)S(1)}, u32[]{:S(2)}, u32[]{:S(2)}) collective-permute-start(bf16[2,64,256]{2,1,0:T(8,128)(2,1)S(1)} %collective-permute-done.17), channel_id=1, source_target_pairs={{0,18},{1,19},{2,16},{3,17},{4,22},{5,23},{6,20},{7,21},{8,26},{9,... | collective-permute-start | bytes 196616 | tf_op jit(solution)/shard_map/ppermute | solution.py:71
  47.8 1.2 %collective-permute-start.18 = (bf16[2,64,256]{2,1,0:T(8,128)(2,1)S(1)}, bf16[2,64,256]{2,1,0:T(8,128)(2,1)S(1)}, u32[]{:S(2)}, u32[]{:S(2)}) collective-permute-start(bf16[2,64,256]{2,1,0:T(8,128)(2,1)S(1)} %collective-permute-done.17), channel_id=1, source_target_pairs={{0,2},{1,3},{2,0},{3,1},{4,6},{5,7},{6,4},{7,5},{8,10},{9,11},{10,... | collective-permute-start | bytes 196616 | tf_op jit(solution)/shard_map/ppermute | solution.py:71
  49.1 0.8 %collective-permute-start.19 = (bf16[2,64,256]{2,1,0:T(8,128)(2,1)S(1)}, bf16[2,64,256]{2,1,0:T(8,128)(2,1)S(1)}, u32[]{:S(2)}, u32[]{:S(2)}) collective-permute-start(bf16[2,64,256]{2,1,0:T(8,128)(2,1)S(1)} %collective-permute-done.17), channel_id=1, source_target_pairs={{0,16},{1,17},{2,18},{3,19},{4,20},{5,21},{6,22},{7,23},{8,24},{9,... | collective-permute-start | bytes 196616 | tf_op jit(solution)/shard_map/ppermute | solution.py:71
  49.9 1.7 %collective-permute-done.20.refs_0_ = bf16[2,64,256]{2,1,0:T(8,128)(2,1)S(1)} collective-permute-done((bf16[2,64,256]{2,1,0:T(8,128)(2,1)S(1)}, bf16[2,64,256]{2,1,0:T(8,128)(2,1)S(1)}, u32[]{:S(2)}, u32[]{:S(2)}) %collective-permute-start.20) | collective-permute-done | bytes 65568 | tf_op jit(solution)/shard_map/ppermute | solution.py:71
  51.5 2.6 %shard_map.68 = (bf16[2,64,256]{2,1,0:T(8,128)(2,1)S(1)}, f32[64,2048]{1,0:T(8,128)S(1)}, f32[64,2048]{1,0:T(8,128)S(1)}) custom-call(s32[256]{0:T(256)S(1)} %select_select_fusion.index_ref, bf16[2,64,256]{2,1,0:T(8,128)(2,1)S(1)} %collective-permute-done.20.refs_0_, ...), custom_call_target="tpu_custom_call", output_to_operand_aliasing={{0}: (1, {})} | custom-call | flops 134217728 | bytes 2097152 | tf_op jit(solution)/shard_map/pallas_call | solution.py:301
  54.1 0.0 collective-permute-done.18
  54.2 0.0 collective-permute-done.19
  54.2 0.0 collective-permute-done.21
  54.3 0.1 collective-permute-start.23
  54.3 1.7 %collective-permute-done.23.refs_1_ = bf16[11,64,256]{2,1,0:T(8,128)(2,1)S(1)} collective-permute-done((bf16[11,64,256]{2,1,0:T(8,128)(2,1)S(1)}, bf16[11,64,256]{2,1,0:T(8,128)(2,1)S(1)}, u32[]{:S(2)}, u32[]{:S(2)}) %collective-permute-start.23) | collective-permute-done | bytes 360480 | tf_op jit(solution)/shard_map/ppermute | solution.py:75
  56.0 2.8 %shard_map.69 = bf16[64,2048]{1,0:T(8,128)(2,1)} custom-call(s32[256]{0:T(256)S(1)} %select_select_fusion.index_ref, bf16[11,64,256]{2,1,0:T(8,128)(2,1)S(1)} %constant_dynamic-update-slice_fusion.12.refs_0_, bf16[11,64,256]{2,1,0:T(8,128)(2,1)S(1)} %collective-permute-done.23.refs_1_, bf16[64,256]{1,0:T(8,128)(2,1)S(1)} %collective-permute-done.16.refs_2_, ...), custom_call_target="tpu_custom_call" | custom-call | flops 67108864 | bytes 1048576 | tf_op jit(solution)/shard_map/pallas_call | solution.py:301
  (24 shorter events, 0.2 us)
Async XLA Ops:
  0.8 5.8 %collective-permute-start = (bf16[64,256]{1,0:T(8,128)(2,1)S(1)}, bf16[64,256]{1,0:T(8,128)(2,1)S(1)}, u32[]{:S(2)}, u32[]{:S(2)}) collective-permute-start(bf16[64,256]{1,0:T(8,128)(2,1)S(1)} %get-tuple-element.24.refs_3_.refs_4_), channel_id=1, source_target_pairs={{0,1},{1,0},{2,3},{3,2},{4,5},{5,4},{6,7},{7,6},{8,9},{9,8},{10,11... | collective-permute-start | bytes 98312 | tf_op jit(solution)/shard_map/ppermute | solution.py:75
  1.2 18.7 %collective-permute-start.6 = (bf16[64,256]{1,0:T(8,128)(2,1)S(1)}, bf16[64,256]{1,0:T(8,128)(2,1)S(1)}, u32[]{:S(2)}, u32[]{:S(2)}) collective-permute-start(bf16[64,256]{1,0:T(8,128)(2,1)S(1)} %get-tuple-element.24.refs_3_.refs_4_), channel_id=1, source_target_pairs={{0,18},{1,19},{2,16},{3,17},{4,22},{5,23},{6,20},{7,21},{8,26},{9,... | collective-permute-start | bytes 98312 | tf_op jit(solution)/shard_map/ppermute | solution.py:71
  6.5 4.3 %collective-permute-start.1 = (bf16[2,64,256]{2,1,0:T(8,128)(2,1)S(1)}, bf16[2,64,256]{2,1,0:T(8,128)(2,1)S(1)}, u32[]{:S(2)}, u32[]{:S(2)}) collective-permute-start(bf16[2,64,256]{2,1,0:T(8,128)(2,1)S(1)} %pad_maximum_fusion), channel_id=1, source_target_pairs={{0,4},{1,3},{2,6},{3,1},{4,0},{5,9},{6,2},{7,11},{8,12},{9,5},{10,... | collective-permute-start | bytes 196616 | tf_op jit(solution)/shard_map/ppermute | solution.py:71
  9.6 10.2 %collective-permute-start.5 = (bf16[2,64,256]{2,1,0:T(8,128)(2,1)S(1)}, bf16[2,64,256]{2,1,0:T(8,128)(2,1)S(1)}, u32[]{:S(2)}, u32[]{:S(2)}) collective-permute-start(bf16[2,64,256]{2,1,0:T(8,128)(2,1)S(1)} %pad_maximum_fusion), channel_id=1, source_target_pairs={{0,2},{1,17},{2,0},{3,19},{4,6},{5,21},{6,4},{7,23},{8,10},{9,25},... | collective-permute-start | bytes 196616 | tf_op jit(solution)/shard_map/ppermute | solution.py:71
  10.9 6.2 %collective-permute-start.4 = (bf16[2,64,256]{2,1,0:T(8,128)(2,1)S(1)}, bf16[2,64,256]{2,1,0:T(8,128)(2,1)S(1)}, u32[]{:S(2)}, u32[]{:S(2)}) collective-permute-start(bf16[2,64,256]{2,1,0:T(8,128)(2,1)S(1)} %collective-permute-done.1), channel_id=1, source_target_pairs={{0,18},{1,19},{2,16},{3,17},{4,22},{5,23},{6,20},{7,21},{8,26},{9,... | collective-permute-start | bytes 196616 | tf_op jit(solution)/shard_map/ppermute | solution.py:71
  11.6 4.4 %collective-permute-start.2 = (bf16[2,64,256]{2,1,0:T(8,128)(2,1)S(1)}, bf16[2,64,256]{2,1,0:T(8,128)(2,1)S(1)}, u32[]{:S(2)}, u32[]{:S(2)}) collective-permute-start(bf16[2,64,256]{2,1,0:T(8,128)(2,1)S(1)} %collective-permute-done.1), channel_id=1, source_target_pairs={{0,2},{1,3},{2,0},{3,1},{4,6},{5,7},{6,4},{7,5},{8,10},{9,11},{10,... | collective-permute-start | bytes 196616 | tf_op jit(solution)/shard_map/ppermute | solution.py:71
  12.8 4.3 %collective-permute-start.3 = (bf16[2,64,256]{2,1,0:T(8,128)(2,1)S(1)}, bf16[2,64,256]{2,1,0:T(8,128)(2,1)S(1)}, u32[]{:S(2)}, u32[]{:S(2)}) collective-permute-start(bf16[2,64,256]{2,1,0:T(8,128)(2,1)S(1)} %collective-permute-done.1), channel_id=1, source_target_pairs={{0,16},{1,17},{2,18},{3,19},{4,20},{5,21},{6,22},{7,23},{8,24},{9,... | collective-permute-start | bytes 196616 | tf_op jit(solution)/shard_map/ppermute | solution.py:71
  19.8 6.5 %copy-start = (f32[64]{0:T(128)S(1)}, f32[64]{0:T(128)}, u32[]{:S(2)}) copy-start(f32[64]{0:T(128)} %param.11) | copy-start | bytes 772
  19.9 1.7 %collective-permute-start.7 = (bf16[11,64,256]{2,1,0:T(8,128)(2,1)S(1)}, bf16[11,64,256]{2,1,0:T(8,128)(2,1)S(1)}, u32[]{:S(2)}, u32[]{:S(2)}) collective-permute-start(bf16[11,64,256]{2,1,0:T(8,128)(2,1)S(1)} %constant_dynamic-update-slice_fusion.refs_0_.refs_1_), channel_id=1, source_target_pairs={{0,1},{1,0},{2,3},{3,2},{4,5},{5,4},{6,7},{7,6},{8,9},{9,8},{10,11... | collective-permute-start | bytes 1081352 | tf_op jit(solution)/shard_map/ppermute | solution.py:75
  22.8 1.3 %collective-permute-start.8 = (bf16[64,256]{1,0:T(8,128)(2,1)S(1)}, bf16[64,256]{1,0:T(8,128)(2,1)S(1)}, u32[]{:S(2)}, u32[]{:S(2)}) collective-permute-start(bf16[64,256]{1,0:T(8,128)(2,1)S(1)} %shard_map.65.refs_3_.refs_4_), channel_id=1, source_target_pairs={{0,1},{1,0},{2,3},{3,2},{4,5},{5,4},{6,7},{7,6},{8,9},{9,8},{10,11... | collective-permute-start | bytes 98312 | tf_op jit(solution)/shard_map/ppermute | solution.py:75
  24.7 4.7 %collective-permute-start.9 = (bf16[2,64,256]{2,1,0:T(8,128)(2,1)}, bf16[2,64,256]{2,1,0:T(8,128)(2,1)}, u32[]{:S(2)}, u32[]{:S(2)}) collective-permute-start(bf16[2,64,256]{2,1,0:T(8,128)(2,1)} %pad_maximum_fusion.1), channel_id=1, source_target_pairs={{0,4},{1,3},{2,6},{3,1},{4,0},{5,9},{6,2},{7,11},{8,12},{9,5},{10,... | collective-permute-start | bytes 196616 | tf_op jit(solution)/shard_map/ppermute | solution.py:71
  26.4 11.3 %collective-permute-start.14 = (bf16[64,256]{1,0:T(8,128)(2,1)S(1)}, bf16[64,256]{1,0:T(8,128)(2,1)S(1)}, u32[]{:S(2)}, u32[]{:S(2)}) collective-permute-start(bf16[64,256]{1,0:T(8,128)(2,1)S(1)} %shard_map.65.refs_3_.refs_4_), channel_id=1, source_target_pairs={{0,18},{1,19},{2,16},{3,17},{4,22},{5,23},{6,20},{7,21},{8,26},{9,... | collective-permute-start | bytes 98312 | tf_op jit(solution)/shard_map/ppermute | solution.py:71
  27.9 9.8 %collective-permute-start.13 = (bf16[2,64,256]{2,1,0:T(8,128)(2,1)}, bf16[2,64,256]{2,1,0:T(8,128)(2,1)S(1)}, u32[]{:S(2)}, u32[]{:S(2)}) collective-permute-start(bf16[2,64,256]{2,1,0:T(8,128)(2,1)} %pad_maximum_fusion.1), channel_id=1, source_target_pairs={{0,2},{1,17},{2,0},{3,19},{4,6},{5,21},{6,4},{7,23},{8,10},{9,25},... | collective-permute-start | bytes 196616 | tf_op jit(solution)/shard_map/ppermute | solution.py:71
  29.4 5.4 %collective-permute-start.12 = (bf16[2,64,256]{2,1,0:T(8,128)(2,1)}, bf16[2,64,256]{2,1,0:T(8,128)(2,1)S(1)}, u32[]{:S(2)}, u32[]{:S(2)}) collective-permute-start(bf16[2,64,256]{2,1,0:T(8,128)(2,1)} %collective-permute-done.9), channel_id=1, source_target_pairs={{0,18},{1,19},{2,16},{3,17},{4,22},{5,23},{6,20},{7,21},{8,26},{9,... | collective-permute-start | bytes 196616 | tf_op jit(solution)/shard_map/ppermute | solution.py:71
  31.0 6.4 %collective-permute-start.10 = (bf16[2,64,256]{2,1,0:T(8,128)(2,1)}, bf16[2,64,256]{2,1,0:T(8,128)(2,1)S(1)}, u32[]{:S(2)}, u32[]{:S(2)}) collective-permute-start(bf16[2,64,256]{2,1,0:T(8,128)(2,1)} %collective-permute-done.9), channel_id=1, source_target_pairs={{0,2},{1,3},{2,0},{3,1},{4,6},{5,7},{6,4},{7,5},{8,10},{9,11},{10,... | collective-permute-start | bytes 196616 | tf_op jit(solution)/shard_map/ppermute | solution.py:71
  33.2 4.5 %collective-permute-start.11 = (bf16[2,64,256]{2,1,0:T(8,128)(2,1)}, bf16[2,64,256]{2,1,0:T(8,128)(2,1)S(1)}, u32[]{:S(2)}, u32[]{:S(2)}) collective-permute-start(bf16[2,64,256]{2,1,0:T(8,128)(2,1)} %collective-permute-done.9), channel_id=1, source_target_pairs={{0,16},{1,17},{2,18},{3,19},{4,20},{5,21},{6,22},{7,23},{8,24},{9,... | collective-permute-start | bytes 196616 | tf_op jit(solution)/shard_map/ppermute | solution.py:71
  37.7 1.7 %collective-permute-start.15 = (bf16[11,64,256]{2,1,0:T(8,128)(2,1)S(1)}, bf16[11,64,256]{2,1,0:T(8,128)(2,1)S(1)}, u32[]{:S(2)}, u32[]{:S(2)}) collective-permute-start(bf16[11,64,256]{2,1,0:T(8,128)(2,1)S(1)} %constant_dynamic-update-slice_fusion.6.refs_0_.refs_1_), channel_id=1, source_target_pairs={{0,1},{1,0},{2,3},{3,2},{4,5},{5,4},{6,7},{7,6},{8,9},{9,8},{10,11... | collective-permute-start | bytes 1081352 | tf_op jit(solution)/shard_map/ppermute | solution.py:75
  40.6 1.3 %collective-permute-start.16 = (bf16[64,256]{1,0:T(8,128)(2,1)S(1)}, bf16[64,256]{1,0:T(8,128)(2,1)S(1)}, u32[]{:S(2)}, u32[]{:S(2)}) collective-permute-start(bf16[64,256]{1,0:T(8,128)(2,1)S(1)} %shard_map.67.refs_3_), channel_id=1, source_target_pairs={{0,1},{1,0},{2,3},{3,2},{4,5},{5,4},{6,7},{7,6},{8,9},{9,8},{10,11... | collective-permute-start | bytes 98312 | tf_op jit(solution)/shard_map/ppermute | solution.py:75
  41.9 4.5 %collective-permute-start.17 = (bf16[2,64,256]{2,1,0:T(8,128)(2,1)S(1)}, bf16[2,64,256]{2,1,0:T(8,128)(2,1)S(1)}, u32[]{:S(2)}, u32[]{:S(2)}) collective-permute-start(bf16[2,64,256]{2,1,0:T(8,128)(2,1)S(1)} %pad_maximum_fusion.2), channel_id=1, source_target_pairs={{0,4},{1,3},{2,6},{3,1},{4,0},{5,9},{6,2},{7,11},{8,12},{9,5},{10,... | collective-permute-start | bytes 196616 | tf_op jit(solution)/shard_map/ppermute | solution.py:71
  43.5 10.7 %collective-permute-start.22 = (bf16[64,256]{1,0:T(8,128)(2,1)S(1)}, bf16[64,256]{1,0:T(8,128)(2,1)S(1)}, u32[]{:S(2)}, u32[]{:S(2)}) collective-permute-start(bf16[64,256]{1,0:T(8,128)(2,1)S(1)} %shard_map.67.refs_3_), channel_id=1, source_target_pairs={{0,18},{1,19},{2,16},{3,17},{4,22},{5,23},{6,20},{7,21},{8,26},{9,... | collective-permute-start | bytes 98312 | tf_op jit(solution)/shard_map/ppermute | solution.py:71
  44.9 9.3 %collective-permute-start.21 = (bf16[2,64,256]{2,1,0:T(8,128)(2,1)S(1)}, bf16[2,64,256]{2,1,0:T(8,128)(2,1)S(1)}, u32[]{:S(2)}, u32[]{:S(2)}) collective-permute-start(bf16[2,64,256]{2,1,0:T(8,128)(2,1)S(1)} %pad_maximum_fusion.2), channel_id=1, source_target_pairs={{0,2},{1,17},{2,0},{3,19},{4,6},{5,21},{6,4},{7,23},{8,10},{9,25},... | collective-permute-start | bytes 196616 | tf_op jit(solution)/shard_map/ppermute | solution.py:71
  46.4 5.2 %collective-permute-start.20 = (bf16[2,64,256]{2,1,0:T(8,128)(2,1)S(1)}, bf16[2,64,256]{2,1,0:T(8,128)(2,1)S(1)}, u32[]{:S(2)}, u32[]{:S(2)}) collective-permute-start(bf16[2,64,256]{2,1,0:T(8,128)(2,1)S(1)} %collective-permute-done.17), channel_id=1, source_target_pairs={{0,18},{1,19},{2,16},{3,17},{4,22},{5,23},{6,20},{7,21},{8,26},{9,... | collective-permute-start | bytes 196616 | tf_op jit(solution)/shard_map/ppermute | solution.py:71
  47.8 6.3 %collective-permute-start.18 = (bf16[2,64,256]{2,1,0:T(8,128)(2,1)S(1)}, bf16[2,64,256]{2,1,0:T(8,128)(2,1)S(1)}, u32[]{:S(2)}, u32[]{:S(2)}) collective-permute-start(bf16[2,64,256]{2,1,0:T(8,128)(2,1)S(1)} %collective-permute-done.17), channel_id=1, source_target_pairs={{0,2},{1,3},{2,0},{3,1},{4,6},{5,7},{6,4},{7,5},{8,10},{9,11},{10,... | collective-permute-start | bytes 196616 | tf_op jit(solution)/shard_map/ppermute | solution.py:71
  49.1 5.1 %collective-permute-start.19 = (bf16[2,64,256]{2,1,0:T(8,128)(2,1)S(1)}, bf16[2,64,256]{2,1,0:T(8,128)(2,1)S(1)}, u32[]{:S(2)}, u32[]{:S(2)}) collective-permute-start(bf16[2,64,256]{2,1,0:T(8,128)(2,1)S(1)} %collective-permute-done.17), channel_id=1, source_target_pairs={{0,16},{1,17},{2,18},{3,19},{4,20},{5,21},{6,22},{7,23},{8,24},{9,... | collective-permute-start | bytes 196616 | tf_op jit(solution)/shard_map/ppermute | solution.py:71
  54.3 1.7 %collective-permute-start.23 = (bf16[11,64,256]{2,1,0:T(8,128)(2,1)S(1)}, bf16[11,64,256]{2,1,0:T(8,128)(2,1)S(1)}, u32[]{:S(2)}, u32[]{:S(2)}) collective-permute-start(bf16[11,64,256]{2,1,0:T(8,128)(2,1)S(1)} %constant_dynamic-update-slice_fusion.12.refs_0_), channel_id=1, source_target_pairs={{0,1},{1,0},{2,3},{3,2},{4,5},{5,4},{6,7},{7,6},{8,9},{9,8},{10,11... | collective-permute-start | bytes 1081352 | tf_op jit(solution)/shard_map/ppermute | solution.py:75

commit v6 on v5

v6 whole, which is shorter than its diff:
```python
import functools

import jax
import jax.numpy as jnp
from jax import lax
from jax.experimental import pallas as pl
from jax.experimental.pallas import tpu as pltpu
from jax.sharding import PartitionSpec as P

PB = 64
TERMS = 3
FEATURES = 64
NEAR = 4
PARTS = 4
VMEM_MIB = 16
LANES = 2 * PB
AXES = ("gx", "gy", "gz")


def pairings(count):
    first = [(i, i ^ 1) for i in range(count)]
    second = [(i, (i + 1) % count if i % 2 else (i - 1) % count) for i in range(count)]
    return [first] if count == 2 else [first, second]


def partner_rank(here, step, count):
    forward = jnp.where((here & 1) == 0, 1, 2)
    backward = 3 - forward
    rank = jnp.where(step == 1, 0, jnp.where(step == 2, forward, backward))
    there = here + step - 1
    return rank, (there >= 0) & (there < count)


def place(rank, here, count):
    there = here if rank == 0 else dict(pairings(count)[rank - 1])[here]
    return there if abs(there - here) <= 1 else None


def partners():
    x_count = len(pairings(lax.axis_size("gx"))) + 1
    y_count = len(pairings(lax.axis_size("gy"))) + 1
    pair_count = lax.axis_size("gz") // 2
    chips = [(x, b) for x in range(x_count) for b in range(pair_count)]
    side = [(x, y, b) for x, b in chips for y in range(1, y_count)]
    return side + [(x, 0, b) for x, b in chips[1:]]


def partner_number(x, y, b):
    x_count = len(pairings(lax.axis_size("gx"))) + 1
    y_count = len(pairings(lax.axis_size("gy"))) + 1
    pair_count = lax.axis_size("gz") // 2
    chip = x * pair_count + b
    return jnp.where(
        y > 0, chip * (y_count - 1) + y - 1, x_count * pair_count * (y_count - 1) + chip - 1
    )


def swap(value, by_core):
    sizes = [lax.axis_size(name) for name in AXES]
    pairs = []
    for i in range(sizes[0]):
        for j in range(sizes[1]):
            for k in range(sizes[2]):
                x, y, b = by_core[k % 2]
                to = (place(x, i, sizes[0]), place(y, j, sizes[1]), (k // 2 ^ b) * 2 + k % 2)
                if None in to:
                    to = (i, j, (k // 2 ^ 1) * 2 + k % 2)
                pairs.append(
                    ((i * sizes[1] + j) * sizes[2] + k, (to[0] * sizes[1] + to[1]) * sizes[2] + to[2])
                )
    return lax.ppermute(value, AXES, pairs)


def swap_cores(value):
    return lax.ppermute(value, "gz", [(k, k ^ 1) for k in range(lax.axis_size("gz"))])


def exchange(rim, work):
    chips = partners()
    sides = len(pairings(lax.axis_size("gy")))
    plane = chips[-((len(chips) - sides) // (sides + 1)) :]
    other = swap_cores(rim)
    both = jnp.stack([rim, other])
    side = swap(both, (chips[0], chips[sides - 1]))
    alone = [swap(rim, (plane[-1], plane[-1]))] if len(plane) % 2 else []
    own = [
        swap(both, (plane[t], plane[t + 1])) for t in range(0, len(plane) - len(plane) % 2, 2)
    ]
    passed = [swap(side, (chip, chip)) for chip in plane[::-1]]
    own[0], *results = work(own[0])
    received = jnp.concatenate([side] + passed[::-1] + own + [panel[None] for panel in alone])
    return (received, swap_cores(received), other, rim), results


def source_index(slots, live, count, rim_count):
    layers = lax.axis_size("gz")
    x_at, y_at, z_at = (lax.axis_index(name) for name in AXES)
    rest = jnp.maximum(slots - count, 0)
    column = sum((rest >= rim_count * layers * n).astype(jnp.int32) for n in range(1, 9))
    a = (column >= 3).astype(jnp.int32) + (column >= 6).astype(jnp.int32)
    c = column - 3 * a
    inside = rest - rim_count * layers * column
    m = sum((inside >= rim_count * n).astype(jnp.int32) for n in range(1, layers))
    r = inside - rim_count * m
    x_rank, x_in = partner_rank(x_at, a, lax.axis_size("gx"))
    y_rank, y_in = partner_rank(y_at, c, lax.axis_size("gy"))
    flip = (m >> 1) ^ (z_at >> 1)
    chips = len(partners())
    core, target = z_at & 1, m & 1
    number = partner_number(x_rank, y_rank, flip)
    holder, panel = number & 1, (number & -2) + (target ^ (number & 1))
    if chips % 2:
        holder = jnp.where(number == chips - 1, target, holder)
        panel = jnp.where(number == chips - 1, chips - 1, panel)
    panel = panel + jnp.where(holder == core, 0, chips)
    here = (x_rank == 0) & (y_rank == 0) & (flip == 0)
    panel = jnp.where(here, 2 * chips + jnp.where(target == core, 1, 0), panel)
    zero = (2 * chips + 2) * rim_count
    place = lax.broadcasted_iota(jnp.int32, slots.shape, 0)
    used = place < live
    far = jnp.where(x_in & y_in & used, panel * rim_count + r, zero)
    return jnp.where(place < NEAR, jnp.where(used, slots, count), far)


def left_half():
    return lax.broadcasted_iota(jnp.int32, (FEATURES, LANES), 1) < PB


def turn(pair):
    return jnp.concatenate([pair[:, PB:], pair[:, :PB]], axis=1)


def spread(pair, store, at):
    turned = turn(pair)
    store[at] = jnp.where(left_half(), pair, turned)
    store[at + 1] = jnp.where(left_half(), turned, pair)


def each_rim(rims, place_pair):
    mine_ref, others_ref, other_ref, own_ref = rims
    panels, _, rim = mine_ref.shape
    rim_count = rim // PB

    @pl.loop(0, panels)
    def _(panel):
        for t in range(rim // LANES):
            cut = slice(t * LANES, (t + 1) * LANES)
            at = panel * rim_count + 2 * t
            place_pair(mine_ref[panel, :, cut], at)
            place_pair(others_ref[panel, :, cut], at + panels * rim_count)

    for t in range(rim // LANES):
        cut = slice(t * LANES, (t + 1) * LANES)
        at = 2 * panels * rim_count + 2 * t
        place_pair(other_ref[:, cut], at)
        place_pair(own_ref[:, cut], at + rim_count)


def product(first, second, tile):
    both = lax.dot_general(
        jnp.concatenate([first, second], axis=0),
        tile,
        (((1,), (1,)), ((), ())),
        preferred_element_type=jnp.float32,
    )
    return jnp.where(left_half(), both[:FEATURES], both[FEATURES:])


def picked(store, index_ref, first, row):
    return jnp.concatenate(
        [
            jnp.where(left_half(), store[index_ref[k, row]], store[index_ref[k + 1, row]])
            for k in range(first, first + NEAR, 2)
        ],
        axis=1,
    )


def fold_kernel(
    _, raw_hbm, slot_hbm, live_hbm, scale_hbm,
    __, tile_out, index_out,
    raw_ref, slot_ref, live_ref, scale_ref, arrived, *, rim_count,
):
    count = slot_ref.shape[1]
    rows = raw_ref.shape[0] // PARTS
    fetches = [
        pltpu.make_async_copy(source, target, arrived.at[n])
        for n, (source, target) in enumerate(
            [(scale_hbm, scale_ref), (slot_hbm, slot_ref), (live_hbm, live_ref)]
            + [
                (raw_hbm.at[pl.ds(p * rows, rows)], raw_ref.at[pl.ds(p * rows, rows)])
                for p in range(PARTS)
            ]
        )
    ]
    for fetch in fetches:
        fetch.start()
    half = lax.broadcasted_iota(jnp.int32, (PB, LANES), 1) < PB
    for fetch in fetches[:3]:
        fetch.wait()
    index_out[...] = source_index(slot_ref[...], live_ref[...], count, rim_count)
    for p in range(PARTS):
        fetches[3 + p].wait()
        for b in range(p * rows // PB, (p + 1) * rows // PB):
            for k in range(0, scale_ref.shape[0], 2):
                at = pl.ds(b * PB, PB), pl.ds(k * PB, LANES)
                scale = jnp.where(half, scale_ref[k, b], scale_ref[k + 1, b])
                tile_out[at] = (raw_ref[at].astype(jnp.float32) * scale).astype(tile_out.dtype)


def near_kernel(index_ref, value_ref, tile_ref, near_out, store):
    for t in range(value_ref.shape[1] // LANES):
        spread(value_ref[:, t * LANES : (t + 1) * LANES], store, 2 * t)
    clear_last(store)
    for t in range(near_out.shape[1] // LANES):
        at = pl.ds(t * LANES, LANES)
        near_out[:, at] = product(
            picked(store, index_ref, 0, 2 * t),
            picked(store, index_ref, 0, 2 * t + 1),
            tile_ref[at, : NEAR * PB],
        )


def clear_last(store):
    store[store.shape[0] - 1] = jnp.zeros(store.shape[1:], store.dtype)


def rim_kernel(index_ref, *refs):
    rims, (tile_ref, near_ref, rim_out, store) = refs[:4], refs[4:]

    def keep(pair, number):
        store[number // 2] = pair

    each_rim(rims, keep)
    clear_last(store)

    def sources(row):
        parts = []
        for k in range(NEAR, 2 * NEAR, 2):
            halves = []
            for side in range(2):
                number = index_ref[k + side, row]
                pair = store[number >> 1]
                halves.append(jnp.where((number & 1) == side, pair, turn(pair)))
            parts.append(jnp.where(left_half(), halves[0], halves[1]))
        return jnp.concatenate(parts, axis=1)

    for t in range(rim_out.shape[1] // LANES):
        at = pl.ds(t * LANES, LANES)
        far = product(sources(2 * t), sources(2 * t + 1), tile_ref[at, NEAR * PB :])
        rim_out[:, at] = (near_ref[:, at] + far).astype(rim_out.dtype)


def far_kernel(step, last, index_ref, *refs):
    if not last:
        refs = refs[1:]
    rims, (tile_ref, near_ref, times_ref, total_ref) = refs[:4], refs[4:8]
    if last:
        result_hbm, store, total_out, sent = refs[8:]
    else:
        _, total_out, value_out, store, *fetching = refs[8:]
        if fetching:
            features_hbm, (total_ref, arrived) = total_ref, fetching
            fetch = pltpu.make_async_copy(features_hbm, total_ref, arrived)
            fetch.start()
    each_rim(rims, lambda pair, number: spread(pair, store, number))
    clear_last(store)
    if not last and fetching:
        fetch.wait()
    factor = jnp.ones(times_ref.shape, jnp.float32)
    for n in range(1, step + 1):
        factor = factor * -times_ref[...] / jnp.float32(n)
    pairs = near_ref.shape[1] // LANES
    sends = []
    for t in range(pairs):
        at = pl.ds(t * LANES, LANES)
        image = near_ref[:, at] + product(
            picked(store, index_ref, NEAR, 2 * t),
            picked(store, index_ref, NEAR, 2 * t + 1),
            tile_ref[at, NEAR * PB :],
        )
        total = total_ref[:, at].astype(jnp.float32) + factor * image
        total_out[:, at] = total.astype(total_out.dtype)
        if not last:
            value_out[:, at] = image.astype(value_out.dtype)
        elif (t + 1) % (pairs // PARTS) == 0:
            part = pl.ds((t + 1 - pairs // PARTS) * LANES, pairs // PARTS * LANES)
            send = pltpu.make_async_copy(
                total_out.at[:, part], result_hbm.at[:, part], sent.at[len(sends)]
            )
            send.start()
            sends.append(send)
    for send in sends:
        send.wait()


def call(kernel, results, scratch, flops, index, *arrays, fetched=(), through=None, to_hbm=False):
    scalars = () if index is None else (index,)
    handed = () if through is None else (through,)
    out_shape = tuple(jax.ShapeDtypeStruct(x.shape, x.dtype) for x in handed) + results
    anywhere, vmem = pl.BlockSpec(memory_space=pl.ANY), pl.BlockSpec(memory_space=pltpu.VMEM)
    hbm = pl.BlockSpec(memory_space=pltpu.HBM)
    fetched = [pltpu.with_memory_space_constraint(x, pltpu.HBM) for x in fetched]
    return pl.pallas_call(
        kernel,
        out_shape=out_shape,
        in_specs=[pl.BlockSpec(memory_space=pltpu.SMEM)] * len(scalars)
        + [anywhere] * len(handed)
        + [vmem] * len(arrays)
        + [hbm] * len(fetched),
        out_specs=(anywhere,) * len(handed) + (hbm if to_hbm else vmem,) * len(results),
        scratch_shapes=scratch,
        input_output_aliases={len(scalars): 0} if handed else {},
        compiler_params=pltpu.CompilerParams(vmem_limit_bytes=VMEM_MIB * 1024 * 1024),
        cost_estimate=pl.CostEstimate(flops=flops, bytes_accessed=flops // 64, transcendentals=0),
    )(*scalars, *handed, *arrays, *fetched)


def body(features, tiles, scales, slots, live, times):
    count, width = tiles.shape[2], tiles.shape[4]
    slot_count = scales.shape[3]
    rim_count = max(1, count // 8)
    points = count * PB
    value = features.reshape(FEATURES, points)
    rim = value[:, : rim_count * PB]
    scales = scales.reshape(count, slot_count).T
    slots = slots.reshape(count, slot_count).T
    rims_held = 2 * len(partners()) + 2
    half = FEATURES * points * width

    def blocks(number):
        return pltpu.VMEM((number, FEATURES, LANES), jnp.bfloat16)

    own_store = blocks(count + 1)
    far_store = blocks(rims_held * rim_count + 1)
    pair_store = blocks(rims_held * rim_count // 2 + 1)
    image_shape = jax.ShapeDtypeStruct(value.shape, jnp.float32)
    value_shape = jax.ShapeDtypeStruct(value.shape, jnp.bfloat16)
    rim_shape = jax.ShapeDtypeStruct(rim.shape, jnp.bfloat16)
    tile_shape = jax.ShapeDtypeStruct((points, width), jnp.bfloat16)
    index_shape = jax.ShapeDtypeStruct(slots.shape, jnp.int32)

    def fold(through):
        return call(
            functools.partial(fold_kernel, rim_count=rim_count),
            (tile_shape, index_shape),
            [
                pltpu.VMEM((points, width), jnp.bfloat16),
                pltpu.VMEM(slots.shape, jnp.int32),
                pltpu.VMEM((1, count), jnp.int32),
                pltpu.SMEM(scales.shape, jnp.float32),
                pltpu.SemaphoreType.DMA((PARTS + 3,)),
            ],
            half,
            None,
            fetched=(tiles.reshape(points, width), slots, live.reshape(1, count), scales),
            through=through,
        )

    rims, (scaled, index) = exchange(rim, fold)
    (near,) = call(near_kernel, (image_shape,), [own_store], half, index, value, scaled)
    times = times[:, None]
    total = value
    for step in range(1, TERMS):
        arrays = (index, *rims, scaled, near)
        (rim,) = call(rim_kernel, (rim_shape,), [pair_store], half // 8, *arrays)

        def rest(through):
            begun = step > 1
            fetch = [pltpu.VMEM(value.shape, jnp.bfloat16), pltpu.SemaphoreType.DMA]
            return call(
                functools.partial(far_kernel, step, False),
                (image_shape, value_shape),
                [far_store] + ([] if begun else fetch),
                half,
                *arrays,
                times,
                *([total] if begun else []),
                fetched=() if begun else (value,),
                through=through,
            )

        rims, (total, value) = exchange(rim, rest)
        (near,) = call(near_kernel, (image_shape,), [own_store], half, index, value, scaled)
    (out,) = call(
        functools.partial(far_kernel, TERMS, True),
        (value_shape,),
        [
            far_store,
            pltpu.VMEM(value.shape, jnp.bfloat16),
            pltpu.SemaphoreType.DMA((PARTS,)),
        ],
        half,
        index,
        *rims,
        scaled,
        near,
        times,
        total,
        to_hbm=True,
    )
    return out.reshape(features.shape)


def solution(mesh):
    return jax.shard_map(
        body,
        mesh=mesh,
        in_specs=(
            P(None, "gx", "gy", "gz"),
            P("gx", "gy", "gz", None, None),
            P("gx", "gy", "gz", None),
            P("gx", "gy", "gz", None),
            P("gx", "gy", "gz"),
            P(),
        ),
        out_specs=P(None, "gx", "gy", "gz"),
        check_vma=False,
    )
```

time: 59.1 us -> 54.3 us (0.919)
  waiting for transfers between devices: 13.5 us -> 10.4 us
  Pallas kernels: 13 us -> 14.7 us
  local copies, waits for them, and re-layouts: 4.26 us -> 2.72 us
  starting transfers between devices: 26.2 us -> 25.4 us
  other arithmetic: 1.43 us -> 0.65 us
    ppermute x6, waiting for transfers between devices: 7.13 us -> 4.45 us  [swap_cores(): lax.ppermute(value, 'gz', [(k, k ^ 1) for k in range(lax.axis_size('gz'))])]
    pallas_call x6 -> x9, Pallas kernels: 13 us -> 14.7 us  [call(): pl.pallas_call(kernel, out_shape=out_shape, in_specs=[pl.BlockSpec(memory...]
    unnamed x19, local copies, waits for them, and re-layouts: 3.1 us -> 1.78 us
    ppermute x18, starting transfers between devices: 25.1 us -> 24.3 us  [swap(): return lax.ppermute(value, AXES, pairs)]
    lt x2 -> x0, other arithmetic: 0.73 us -> none  [source_index(): index = jnp.where(place < NEAR, jnp.where(place < live, slots, count), far)]
  transfers between devices with their start and end apart: 24 -> 24, of which waited for: 11 -> 12; matrix products, arithmetic and copies ran while one was open for 7% -> 3% of each run, Pallas kernels for 13% -> 18%
where the time goes in v6:
time: 54.3 us; the launch traced here: 54.1 us
  starting transfers between devices  25.4 us (47%)
  Pallas kernels  14.7 us (27%)
  waiting for transfers between devices  10.4 us (19%)
  local copies, waits for them, and re-layouts  2.72 us (5%)
  other arithmetic  0.65 us (1%)
    ppermute x18, starting transfers between devices, swap(): return lax.ppermute(value, AXES, pairs)  24.3 us
    pallas_call x9, Pallas kernels, call(): pl.pallas_call(kernel, out_shape=out_shape, in_specs=[pl.BlockSpec(memory...  14.7 us
    ppermute x18, waiting for transfers between devices, swap(): return lax.ppermute(value, AXES, pairs)  5.95 us
    ppermute x6, waiting for transfers between devices, swap_cores(): lax.ppermute(value, 'gz', [(k, k ^ 1) for k in range(lax.axis_size('gz'))])  4.45 us
    unnamed x19, local copies, waits for them, and re-layouts  1.78 us
  transfers between devices with their start and end apart: 24, of which 12 were waited for; matrix products, arithmetic and copies ran while one was open for 3% of the time, Pallas kernels for 18%

profile of v6, /device:TPU:0, one launch (start us, length us, event | category | flops | bytes accessed | tf_op | source)
XLA Modules:
  0.0 54.1 jit_solution(13995379963566511663)
XLA Ops:
  0.0 0.8 %slice_bitcast_fusion = (bf16[1,64,256]{2,1,0:T(8,128)(2,1)S(1)}, bf16[64,256]{1,0:T(8,128)(2,1)S(1)}) fusion(bf16[64,2048]{1,0:T(8,128)(2,1)} %bitcast.24), kind=kLoop, calls=%fused_computation.21 | loop fusion | bytes 98304 | tf_op jit(solution)/shard_map/stack | solution.py:83
  0.8 0.5 collective-permute-start
  1.3 0.9 %collective-permute-done.refs_2_.refs_3_ = bf16[64,256]{1,0:T(8,128)(2,1)S(1)} collective-permute-done((bf16[64,256]{1,0:T(8,128)(2,1)S(1)}, bf16[64,256]{1,0:T(8,128)(2,1)S(1)}, u32[]{:S(2)}, u32[]{:S(2)}) %collective-permute-start) | collective-permute-done | bytes 32800 | tf_op jit(solution)/shard_map/ppermute | solution.py:75
  2.2 3.0 %collective-permute-start.2 = (bf16[2,64,256]{2,1,0:T(8,128)(2,1)S(1)}, bf16[2,64,256]{2,1,0:T(8,128)(2,1)S(1)}, u32[]{:S(2)}, u32[]{:S(2)}) collective-permute-start(bf16[2,64,256]{2,1,0:T(8,128)(2,1)S(1)} %pad_maximum_fusion), channel_id=1, source_target_pairs={{0,4},{1,3},{2,6},{3,1},{4,0},{5,9},{6,2},{7,11},{8,12},{9,5},{10,... | collective-permute-start | bytes 196616 | tf_op jit(solution)/shard_map/ppermute | solution.py:71
  5.1 1.5 %collective-permute-start.1 = (bf16[2,64,256]{2,1,0:T(8,128)(2,1)S(1)}, bf16[2,64,256]{2,1,0:T(8,128)(2,1)S(1)}, u32[]{:S(2)}, u32[]{:S(2)}) collective-permute-start(bf16[2,64,256]{2,1,0:T(8,128)(2,1)S(1)} %pad_maximum_fusion), channel_id=1, source_target_pairs={{0,2},{1,17},{2,0},{3,19},{4,6},{5,21},{6,4},{7,23},{8,10},{9,25},... | collective-permute-start | bytes 196616 | tf_op jit(solution)/shard_map/ppermute | solution.py:71
  6.6 1.5 %collective-permute-start.6 = (bf16[64,256]{1,0:T(8,128)(2,1)S(1)}, bf16[64,256]{1,0:T(8,128)(2,1)S(1)}, u32[]{:S(2)}, u32[]{:S(2)}) collective-permute-start(bf16[64,256]{1,0:T(8,128)(2,1)S(1)} %get-tuple-element.24.refs_3_.refs_4_), channel_id=1, source_target_pairs={{0,18},{1,19},{2,16},{3,17},{4,22},{5,23},{6,20},{7,21},{8,26},{9,... | collective-permute-start | bytes 98312 | tf_op jit(solution)/shard_map/ppermute | solution.py:71
  8.1 0.0 collective-permute-done.2
  8.1 1.5 %collective-permute-start.3 = (bf16[2,64,256]{2,1,0:T(8,128)(2,1)S(1)}, bf16[2,64,256]{2,1,0:T(8,128)(2,1)S(1)}, u32[]{:S(2)}, u32[]{:S(2)}) collective-permute-start(bf16[2,64,256]{2,1,0:T(8,128)(2,1)S(1)} %collective-permute-done.2), channel_id=1, source_target_pairs={{0,2},{1,3},{2,0},{3,1},{4,6},{5,7},{6,4},{7,5},{8,10},{9,11},{10,... | collective-permute-start | bytes 196616 | tf_op jit(solution)/shard_map/ppermute | solution.py:71
  9.6 1.2 %collective-permute-start.4 = (bf16[2,64,256]{2,1,0:T(8,128)(2,1)S(1)}, bf16[2,64,256]{2,1,0:T(8,128)(2,1)S(1)}, u32[]{:S(2)}, u32[]{:S(2)}) collective-permute-start(bf16[2,64,256]{2,1,0:T(8,128)(2,1)S(1)} %collective-permute-done.2), channel_id=1, source_target_pairs={{0,16},{1,17},{2,18},{3,19},{4,20},{5,21},{6,22},{7,23},{8,24},{9,... | collective-permute-start | bytes 196616 | tf_op jit(solution)/shard_map/ppermute | solution.py:71
  10.8 0.8 %collective-permute-start.5 = (bf16[2,64,256]{2,1,0:T(8,128)(2,1)S(1)}, bf16[2,64,256]{2,1,0:T(8,128)(2,1)S(1)}, u32[]{:S(2)}, u32[]{:S(2)}) collective-permute-start(bf16[2,64,256]{2,1,0:T(8,128)(2,1)S(1)} %collective-permute-done.2), channel_id=1, source_target_pairs={{0,18},{1,19},{2,16},{3,17},{4,22},{5,23},{6,20},{7,21},{8,26},{9,... | collective-permute-start | bytes 196616 | tf_op jit(solution)/shard_map/ppermute | solution.py:71
  11.6 0.0 collective-permute-done.1._
  11.6 1.7 %shard_map.64 = (bf16[2,64,256]{2,1,0:T(8,128)(2,1)S(1)}, bf16[2048,512]{1,0:T(8,128)(2,1)S(1)}, s32[8,32]{1,0:T(8,128)S(1)}) custom-call(bf16[2,64,256]{2,1,0:T(8,128)(2,1)S(1)} %collective-permute-done.1._, bf16[2048,512]{1,0:T(8,128)(2,1)} %bitcast.32, s32[8,32]{1,0:T(8,128)} %bitcast.33, s32[1,32]{1,0:T(1,128)} %bitcast.35, ...), custom_call_target="tpu_custom_call", output_to_operand_aliasing={{0}: (0, {})} | custom-call | flops 67108864 | bytes 1048576 | tf_op jit(solution)/shard_map/pallas_call | solution.py:304
  13.4 0.0 collective-permute-done.3
  13.4 0.9 %collective-permute-done.4 = bf16[2,64,256]{2,1,0:T(8,128)(2,1)S(1)} collective-permute-done((bf16[2,64,256]{2,1,0:T(8,128)(2,1)S(1)}, bf16[2,64,256]{2,1,0:T(8,128)(2,1)S(1)}, u32[]{:S(2)}, u32[]{:S(2)}) %collective-permute-start.4) | collective-permute-done | bytes 65568 | tf_op jit(solution)/shard_map/ppermute | solution.py:71
  14.3 1.7 %collective-permute-done.5 = bf16[2,64,256]{2,1,0:T(8,128)(2,1)S(1)} collective-permute-done((bf16[2,64,256]{2,1,0:T(8,128)(2,1)S(1)}, bf16[2,64,256]{2,1,0:T(8,128)(2,1)S(1)}, u32[]{:S(2)}, u32[]{:S(2)}) %collective-permute-start.5) | collective-permute-done | bytes 65568 | tf_op jit(solution)/shard_map/ppermute | solution.py:71
  16.0 0.0 collective-permute-done.6
  16.1 0.1 collective-permute-start.7
  16.1 0.0 copy-done
  16.1 1.2 %shard_map.65.refs_5_.refs_6_ = f32[64,2048]{1,0:T(8,128)S(1)} custom-call(s32[8,32]{1,0:T(8,128)S(1)} %get-tuple-element.14.index_ref, bf16[64,2048]{1,0:T(8,128)(2,1)S(1)} %bitcast.26, bf16[2048,512]{1,0:T(8,128)(2,1)S(1)} %get-tuple-element.16.tile_ref.refs_4_.refs_5_), custom_call_target="tpu_custom_call" | custom-call | flops 67108864 | bytes 1048576 | tf_op jit(solution)/shard_map/pallas_call | solution.py:304
  17.3 0.0 copy-start.1
  17.3 0.5 collective-permute-done.7.refs_1_.refs_2_
  17.8 1.2 %shard_map.66.refs_3_.refs_4_ = bf16[64,256]{1,0:T(8,128)(2,1)S(1)} custom-call(s32[8,32]{1,0:T(8,128)S(1)} %get-tuple-element.14.index_ref, bf16[11,64,256]{2,1,0:T(8,128)(2,1)S(1)} %constant_dynamic-update-slice_fusion.refs_0_.refs_1_, bf16[11,64,256]{2,1,0:T(8,128)(2,1)S(1)} %collective-permute-done.7.refs_1_.refs_2_, ...), custom_call_target="tpu_custom_call" | custom-call | flops 8388608 | bytes 131072 | tf_op jit(solution)/shard_map/pallas_call | solution.py:304
  19.0 0.2 collective-permute-start.8
  19.2 1.1 %collective-permute-done.8.refs_2_.refs_3_ = bf16[64,256]{1,0:T(8,128)(2,1)S(1)} collective-permute-done((bf16[64,256]{1,0:T(8,128)(2,1)S(1)}, bf16[64,256]{1,0:T(8,128)(2,1)S(1)}, u32[]{:S(2)}, u32[]{:S(2)}) %collective-permute-start.8) | collective-permute-done | bytes 32800 | tf_op jit(solution)/shard_map/ppermute | solution.py:75
  20.3 0.6 %pad_maximum_fusion.1 = bf16[2,64,256]{2,1,0:T(8,128)(2,1)} fusion(bf16[1,64,256]{2,1,0:T(8,128)(2,1)S(1)} %bitcast.28, bf16[1,64,256]{2,1,0:T(8,128)(2,1)S(1)} %bitcast.27), kind=kLoop, calls=%fused_computation.1 | loop fusion | flops 32768 | bytes 131072 | tf_op jit(solution)/shard_map/stack | solution.py:83
  20.9 1.6 %collective-permute-start.9 = (bf16[2,64,256]{2,1,0:T(8,128)(2,1)}, bf16[2,64,256]{2,1,0:T(8,128)(2,1)}, u32[]{:S(2)}, u32[]{:S(2)}) collective-permute-start(bf16[2,64,256]{2,1,0:T(8,128)(2,1)} %pad_maximum_fusion.1), channel_id=1, source_target_pairs={{0,4},{1,3},{2,6},{3,1},{4,0},{5,9},{6,2},{7,11},{8,12},{9,5},{10,... | collective-permute-start | bytes 196616 | tf_op jit(solution)/shard_map/ppermute | solution.py:71
  22.5 0.5 collective-permute-start.13
  23.0 0.1 copy.10.refs_7_.refs_6_
  23.1 1.5 %collective-permute-start.14 = (bf16[64,256]{1,0:T(8,128)(2,1)S(1)}, bf16[64,256]{1,0:T(8,128)(2,1)S(1)}, u32[]{:S(2)}, u32[]{:S(2)}) collective-permute-start(bf16[64,256]{1,0:T(8,128)(2,1)S(1)} %shard_map.66.refs_3_.refs_4_), channel_id=1, source_target_pairs={{0,18},{1,19},{2,16},{3,17},{4,22},{5,23},{6,20},{7,21},{8,26},{9,... | collective-permute-start | bytes 98312 | tf_op jit(solution)/shard_map/ppermute | solution.py:71
  24.6 0.9 %collective-permute-done.9 = bf16[2,64,256]{2,1,0:T(8,128)(2,1)} collective-permute-done((bf16[2,64,256]{2,1,0:T(8,128)(2,1)}, bf16[2,64,256]{2,1,0:T(8,128)(2,1)}, u32[]{:S(2)}, u32[]{:S(2)}) %collective-permute-start.9) | collective-permute-done | bytes 65568 | tf_op jit(solution)/shard_map/ppermute | solution.py:71
  25.5 0.5 collective-permute-start.10
  26.0 0.8 %collective-permute-start.11 = (bf16[2,64,256]{2,1,0:T(8,128)(2,1)}, bf16[2,64,256]{2,1,0:T(8,128)(2,1)S(1)}, u32[]{:S(2)}, u32[]{:S(2)}) collective-permute-start(bf16[2,64,256]{2,1,0:T(8,128)(2,1)} %collective-permute-done.9), channel_id=1, source_target_pairs={{0,16},{1,17},{2,18},{3,19},{4,20},{5,21},{6,22},{7,23},{8,24},{9,... | collective-permute-start | bytes 196616 | tf_op jit(solution)/shard_map/ppermute | solution.py:71
  26.8 2.1 %collective-permute-start.12 = (bf16[2,64,256]{2,1,0:T(8,128)(2,1)}, bf16[2,64,256]{2,1,0:T(8,128)(2,1)S(1)}, u32[]{:S(2)}, u32[]{:S(2)}) collective-permute-start(bf16[2,64,256]{2,1,0:T(8,128)(2,1)} %collective-permute-done.9), channel_id=1, source_target_pairs={{0,18},{1,19},{2,16},{3,17},{4,22},{5,23},{6,20},{7,21},{8,26},{9,... | collective-permute-start | bytes 196616 | tf_op jit(solution)/shard_map/ppermute | solution.py:71
  29.0 0.0 collective-permute-done.13.refs_0_
  29.0 2.2 %shard_map.67 = (bf16[2,64,256]{2,1,0:T(8,128)(2,1)}, f32[64,2048]{1,0:T(8,128)S(1)}, bf16[64,2048]{1,0:T(8,128)(2,1)S(1)}) custom-call(s32[8,32]{1,0:T(8,128)S(1)} %get-tuple-element.14.index_ref, bf16[2,64,256]{2,1,0:T(8,128)(2,1)} %collective-permute-done.13.refs_0_, ...), custom_call_target="tpu_custom_call", output_to_operand_aliasing={{0}: (1, {})} | custom-call | flops 67108864 | bytes 1048576 | tf_op jit(solution)/shard_map/pallas_call | solution.py:304
  31.1 0.8 %constant_dynamic-update-slice_fusion.11 = bf16[11,64,256]{2,1,0:T(8,128)(2,1)S(1)} fusion(bf16[2,64,256]{2,1,0:T(8,128)(2,1)} %collective-permute-done.9), kind=kLoop, calls=%fused_computation.14 | loop fusion | bytes 131072
  32.0 0.0 collective-permute-done.10
  32.0 0.0 collective-permute-done.11
  32.0 0.2 collective-permute-done.12
  32.2 0.8 %constant_dynamic-update-slice_fusion.7 = bf16[11,64,256]{2,1,0:T(8,128)(2,1)S(1)} fusion(bf16[11,64,256]{2,1,0:T(8,128)(2,1)S(1)} %constant_dynamic-update-slice_fusion.8, bf16[2,64,256]{2,1,0:T(8,128)(2,1)} %get-tuple-element.17), kind=kLoop, calls=%fused_computation.10 | loop fusion | bytes 131072
  33.0 0.0 collective-permute-done.14
  33.1 0.1 collective-permute-start.15
  33.1 1.2 %shard_map.68.refs_5_.refs_6_ = f32[64,2048]{1,0:T(8,128)S(1)} custom-call(s32[8,32]{1,0:T(8,128)S(1)} %get-tuple-element.14.index_ref, bf16[64,2048]{1,0:T(8,128)(2,1)S(1)} %get-tuple-element.18.value_ref, bf16[2048,512]{1,0:T(8,128)(2,1)S(1)} %get-tuple-element.16.tile_ref.refs_4_.refs_5_), custom_call_target="tpu_custom_call" | custom-call | flops 67108864 | bytes 1048576 | tf_op jit(solution)/shard_map/pallas_call | solution.py:304
  34.3 0.5 collective-permute-done.15.refs_1_.refs_2_
  34.8 1.2 %shard_map.69.refs_3_ = bf16[64,256]{1,0:T(8,128)(2,1)S(1)} custom-call(s32[8,32]{1,0:T(8,128)S(1)} %get-tuple-element.14.index_ref, bf16[11,64,256]{2,1,0:T(8,128)(2,1)S(1)} %constant_dynamic-update-slice_fusion.6.refs_0_.refs_1_, bf16[11,64,256]{2,1,0:T(8,128)(2,1)S(1)} %collective-permute-done.15.refs_1_.refs_2_, ...), custom_call_target="tpu_custom_call" | custom-call | flops 8388608 | bytes 131072 | tf_op jit(solution)/shard_map/pallas_call | solution.py:304
  36.0 0.2 collective-permute-start.16
  36.2 1.1 %collective-permute-done.16.refs_2_ = bf16[64,256]{1,0:T(8,128)(2,1)S(1)} collective-permute-done((bf16[64,256]{1,0:T(8,128)(2,1)S(1)}, bf16[64,256]{1,0:T(8,128)(2,1)S(1)}, u32[]{:S(2)}, u32[]{:S(2)}) %collective-permute-start.16) | collective-permute-done | bytes 32800 | tf_op jit(solution)/shard_map/ppermute | solution.py:75
  37.3 1.5 %collective-permute-start.17 = (bf16[2,64,256]{2,1,0:T(8,128)(2,1)S(1)}, bf16[2,64,256]{2,1,0:T(8,128)(2,1)S(1)}, u32[]{:S(2)}, u32[]{:S(2)}) collective-permute-start(bf16[2,64,256]{2,1,0:T(8,128)(2,1)S(1)} %pad_maximum_fusion.2), channel_id=1, source_target_pairs={{0,4},{1,3},{2,6},{3,1},{4,0},{5,9},{6,2},{7,11},{8,12},{9,5},{10,... | collective-permute-start | bytes 196616 | tf_op jit(solution)/shard_map/ppermute | solution.py:71
  38.8 1.3 %collective-permute-start.21 = (bf16[2,64,256]{2,1,0:T(8,128)(2,1)S(1)}, bf16[2,64,256]{2,1,0:T(8,128)(2,1)S(1)}, u32[]{:S(2)}, u32[]{:S(2)}) collective-permute-start(bf16[2,64,256]{2,1,0:T(8,128)(2,1)S(1)} %pad_maximum_fusion.2), channel_id=1, source_target_pairs={{0,2},{1,17},{2,0},{3,19},{4,6},{5,21},{6,4},{7,23},{8,10},{9,25},... | collective-permute-start | bytes 196616 | tf_op jit(solution)/shard_map/ppermute | solution.py:71
  40.1 1.5 %collective-permute-start.22 = (bf16[64,256]{1,0:T(8,128)(2,1)S(1)}, bf16[64,256]{1,0:T(8,128)(2,1)S(1)}, u32[]{:S(2)}, u32[]{:S(2)}) collective-permute-start(bf16[64,256]{1,0:T(8,128)(2,1)S(1)} %shard_map.69.refs_3_), channel_id=1, source_target_pairs={{0,18},{1,19},{2,16},{3,17},{4,22},{5,23},{6,20},{7,21},{8,26},{9,... | collective-permute-start | bytes 98312 | tf_op jit(solution)/shard_map/ppermute | solution.py:71
  41.6 0.0 collective-permute-done.17
  41.6 1.5 %collective-permute-start.18 = (bf16[2,64,256]{2,1,0:T(8,128)(2,1)S(1)}, bf16[2,64,256]{2,1,0:T(8,128)(2,1)S(1)}, u32[]{:S(2)}, u32[]{:S(2)}) collective-permute-start(bf16[2,64,256]{2,1,0:T(8,128)(2,1)S(1)} %collective-permute-done.17), channel_id=1, source_target_pairs={{0,2},{1,3},{2,0},{3,1},{4,6},{5,7},{6,4},{7,5},{8,10},{9,11},{10,... | collective-permute-start | bytes 196616 | tf_op jit(solution)/shard_map/ppermute | solution.py:71
  43.1 1.2 %collective-permute-start.19 = (bf16[2,64,256]{2,1,0:T(8,128)(2,1)S(1)}, bf16[2,64,256]{2,1,0:T(8,128)(2,1)S(1)}, u32[]{:S(2)}, u32[]{:S(2)}) collective-permute-start(bf16[2,64,256]{2,1,0:T(8,128)(2,1)S(1)} %collective-permute-done.17), channel_id=1, source_target_pairs={{0,16},{1,17},{2,18},{3,19},{4,20},{5,21},{6,22},{7,23},{8,24},{9,... | collective-permute-start | bytes 196616 | tf_op jit(solution)/shard_map/ppermute | solution.py:71
  44.3 0.8 %collective-permute-start.20 = (bf16[2,64,256]{2,1,0:T(8,128)(2,1)S(1)}, bf16[2,64,256]{2,1,0:T(8,128)(2,1)S(1)}, u32[]{:S(2)}, u32[]{:S(2)}) collective-permute-start(bf16[2,64,256]{2,1,0:T(8,128)(2,1)S(1)} %collective-permute-done.17), channel_id=1, source_target_pairs={{0,18},{1,19},{2,16},{3,17},{4,22},{5,23},{6,20},{7,21},{8,26},{9,... | collective-permute-start | bytes 196616 | tf_op jit(solution)/shard_map/ppermute | solution.py:71
  45.1 0.0 collective-permute-done.21.refs_0_
  45.1 2.1 %shard_map.70 = (bf16[2,64,256]{2,1,0:T(8,128)(2,1)S(1)}, f32[64,2048]{1,0:T(8,128)S(1)}, bf16[64,2048]{1,0:T(8,128)(2,1)S(1)}) custom-call(s32[8,32]{1,0:T(8,128)S(1)} %get-tuple-element.14.index_ref, bf16[2,64,256]{2,1,0:T(8,128)(2,1)S(1)} %collective-permute-done.21.refs_0_, ...), custom_call_target="tpu_custom_call", output_to_operand_aliasing={{0}: (1, {})} | custom-call | flops 67108864 | bytes 1048576 | tf_op jit(solution)/shard_map/pallas_call | solution.py:304
  47.2 0.0 collective-permute-done.18
  47.2 0.6 %collective-permute-done.19 = bf16[2,64,256]{2,1,0:T(8,128)(2,1)S(1)} collective-permute-done((bf16[2,64,256]{2,1,0:T(8,128)(2,1)S(1)}, bf16[2,64,256]{2,1,0:T(8,128)(2,1)S(1)}, u32[]{:S(2)}, u32[]{:S(2)}) %collective-permute-start.19) | collective-permute-done | bytes 65568 | tf_op jit(solution)/shard_map/ppermute | solution.py:71
  47.8 1.7 %collective-permute-done.20 = bf16[2,64,256]{2,1,0:T(8,128)(2,1)S(1)} collective-permute-done((bf16[2,64,256]{2,1,0:T(8,128)(2,1)S(1)}, bf16[2,64,256]{2,1,0:T(8,128)(2,1)S(1)}, u32[]{:S(2)}, u32[]{:S(2)}) %collective-permute-start.20) | collective-permute-done | bytes 65568 | tf_op jit(solution)/shard_map/ppermute | solution.py:71
  49.5 0.0 collective-permute-done.22
  49.5 0.1 collective-permute-start.23
  49.6 1.2 %shard_map.71.refs_5_ = f32[64,2048]{1,0:T(8,128)S(1)} custom-call(s32[8,32]{1,0:T(8,128)S(1)} %get-tuple-element.14.index_ref, bf16[64,2048]{1,0:T(8,128)(2,1)S(1)} %get-tuple-element.21.value_ref, bf16[2048,512]{1,0:T(8,128)(2,1)S(1)} %get-tuple-element.16.tile_ref.refs_4_.refs_5_), custom_call_target="tpu_custom_call" | custom-call | flops 67108864 | bytes 1048576 | tf_op jit(solution)/shard_map/pallas_call | solution.py:304
  50.8 0.5 collective-permute-done.23.refs_1_
  51.3 2.8 %shard_map.72 = bf16[64,2048]{1,0:T(8,128)(2,1)} custom-call(s32[8,32]{1,0:T(8,128)S(1)} %get-tuple-element.14.index_ref, bf16[11,64,256]{2,1,0:T(8,128)(2,1)S(1)} %constant_dynamic-update-slice_fusion.12.refs_0_, bf16[11,64,256]{2,1,0:T(8,128)(2,1)S(1)} %collective-permute-done.23.refs_1_, bf16[64,256]{1,0:T(8,128)(2,1)S(1)} %collective-permute-done.16.refs_2_, ...), custom_call_target="tpu_custom_call" | custom-call | flops 67108864 | bytes 1048576 | tf_op jit(solution)/shard_map/pallas_call | solution.py:304
  (20 shorter events, 0.1 us)
Async XLA Ops:
  0.0 16.1 %copy-start = (bf16[64,1,1,2048]{3,0,2,1:T(8,128)(2,1)S(1)}, bf16[64,1,1,2048]{3,0,2,1:T(8,128)(2,1)}, u32[]{:S(2)}) copy-start(bf16[64,1,1,2048]{3,0,2,1:T(8,128)(2,1)} %param.6) | copy-start | bytes 786436
  0.8 1.3 %collective-permute-start = (bf16[64,256]{1,0:T(8,128)(2,1)S(1)}, bf16[64,256]{1,0:T(8,128)(2,1)S(1)}, u32[]{:S(2)}, u32[]{:S(2)}) collective-permute-start(bf16[64,256]{1,0:T(8,128)(2,1)S(1)} %get-tuple-element.24.refs_3_.refs_4_), channel_id=1, source_target_pairs={{0,1},{1,0},{2,3},{3,2},{4,5},{5,4},{6,7},{7,6},{8,9},{9,8},{10,11... | collective-permute-start | bytes 98312 | tf_op jit(solution)/shard_map/ppermute | solution.py:75
  2.2 6.0 %collective-permute-start.2 = (bf16[2,64,256]{2,1,0:T(8,128)(2,1)S(1)}, bf16[2,64,256]{2,1,0:T(8,128)(2,1)S(1)}, u32[]{:S(2)}, u32[]{:S(2)}) collective-permute-start(bf16[2,64,256]{2,1,0:T(8,128)(2,1)S(1)} %pad_maximum_fusion), channel_id=1, source_target_pairs={{0,4},{1,3},{2,6},{3,1},{4,0},{5,9},{6,2},{7,11},{8,12},{9,5},{10,... | collective-permute-start | bytes 196616 | tf_op jit(solution)/shard_map/ppermute | solution.py:71
  5.1 6.5 %collective-permute-start.1 = (bf16[2,64,256]{2,1,0:T(8,128)(2,1)S(1)}, bf16[2,64,256]{2,1,0:T(8,128)(2,1)S(1)}, u32[]{:S(2)}, u32[]{:S(2)}) collective-permute-start(bf16[2,64,256]{2,1,0:T(8,128)(2,1)S(1)} %pad_maximum_fusion), channel_id=1, source_target_pairs={{0,2},{1,17},{2,0},{3,19},{4,6},{5,21},{6,4},{7,23},{8,10},{9,25},... | collective-permute-start | bytes 196616 | tf_op jit(solution)/shard_map/ppermute | solution.py:71
  6.6 9.4 %collective-permute-start.6 = (bf16[64,256]{1,0:T(8,128)(2,1)S(1)}, bf16[64,256]{1,0:T(8,128)(2,1)S(1)}, u32[]{:S(2)}, u32[]{:S(2)}) collective-permute-start(bf16[64,256]{1,0:T(8,128)(2,1)S(1)} %get-tuple-element.24.refs_3_.refs_4_), channel_id=1, source_target_pairs={{0,18},{1,19},{2,16},{3,17},{4,22},{5,23},{6,20},{7,21},{8,26},{9,... | collective-permute-start | bytes 98312 | tf_op jit(solution)/shard_map/ppermute | solution.py:71
  8.1 5.2 %collective-permute-start.3 = (bf16[2,64,256]{2,1,0:T(8,128)(2,1)S(1)}, bf16[2,64,256]{2,1,0:T(8,128)(2,1)S(1)}, u32[]{:S(2)}, u32[]{:S(2)}) collective-permute-start(bf16[2,64,256]{2,1,0:T(8,128)(2,1)S(1)} %collective-permute-done.2), channel_id=1, source_target_pairs={{0,2},{1,3},{2,0},{3,1},{4,6},{5,7},{6,4},{7,5},{8,10},{9,11},{10,... | collective-permute-start | bytes 196616 | tf_op jit(solution)/shard_map/ppermute | solution.py:71
  9.6 4.7 %collective-permute-start.4 = (bf16[2,64,256]{2,1,0:T(8,128)(2,1)S(1)}, bf16[2,64,256]{2,1,0:T(8,128)(2,1)S(1)}, u32[]{:S(2)}, u32[]{:S(2)}) collective-permute-start(bf16[2,64,256]{2,1,0:T(8,128)(2,1)S(1)} %collective-permute-done.2), channel_id=1, source_target_pairs={{0,16},{1,17},{2,18},{3,19},{4,20},{5,21},{6,22},{7,23},{8,24},{9,... | collective-permute-start | bytes 196616 | tf_op jit(solution)/shard_map/ppermute | solution.py:71
  10.8 5.2 %collective-permute-start.5 = (bf16[2,64,256]{2,1,0:T(8,128)(2,1)S(1)}, bf16[2,64,256]{2,1,0:T(8,128)(2,1)S(1)}, u32[]{:S(2)}, u32[]{:S(2)}) collective-permute-start(bf16[2,64,256]{2,1,0:T(8,128)(2,1)S(1)} %collective-permute-done.2), channel_id=1, source_target_pairs={{0,18},{1,19},{2,16},{3,17},{4,22},{5,23},{6,20},{7,21},{8,26},{9,... | collective-permute-start | bytes 196616 | tf_op jit(solution)/shard_map/ppermute | solution.py:71
  16.1 1.7 %collective-permute-start.7 = (bf16[11,64,256]{2,1,0:T(8,128)(2,1)S(1)}, bf16[11,64,256]{2,1,0:T(8,128)(2,1)S(1)}, u32[]{:S(2)}, u32[]{:S(2)}) collective-permute-start(bf16[11,64,256]{2,1,0:T(8,128)(2,1)S(1)} %constant_dynamic-update-slice_fusion.refs_0_.refs_1_), channel_id=1, source_target_pairs={{0,1},{1,0},{2,3},{3,2},{4,5},{5,4},{6,7},{7,6},{8,9},{9,8},{10,11... | collective-permute-start | bytes 1081352 | tf_op jit(solution)/shard_map/ppermute | solution.py:75
  17.3 5.7 %copy-start.1 = (f32[64]{0:T(128)S(1)}, f32[64]{0:T(128)}, u32[]{:S(2)}) copy-start(f32[64]{0:T(128)} %param.11) | copy-start | bytes 772
  19.0 1.3 %collective-permute-start.8 = (bf16[64,256]{1,0:T(8,128)(2,1)S(1)}, bf16[64,256]{1,0:T(8,128)(2,1)S(1)}, u32[]{:S(2)}, u32[]{:S(2)}) collective-permute-start(bf16[64,256]{1,0:T(8,128)(2,1)S(1)} %shard_map.66.refs_3_.refs_4_), channel_id=1, source_target_pairs={{0,1},{1,0},{2,3},{3,2},{4,5},{5,4},{6,7},{7,6},{8,9},{9,8},{10,11... | collective-permute-start | bytes 98312 | tf_op jit(solution)/shard_map/ppermute | solution.py:75
  20.9 4.6 %collective-permute-start.9 = (bf16[2,64,256]{2,1,0:T(8,128)(2,1)}, bf16[2,64,256]{2,1,0:T(8,128)(2,1)}, u32[]{:S(2)}, u32[]{:S(2)}) collective-permute-start(bf16[2,64,256]{2,1,0:T(8,128)(2,1)} %pad_maximum_fusion.1), channel_id=1, source_target_pairs={{0,4},{1,3},{2,6},{3,1},{4,0},{5,9},{6,2},{7,11},{8,12},{9,5},{10,... | collective-permute-start | bytes 196616 | tf_op jit(solution)/shard_map/ppermute | solution.py:71
  22.5 6.5 %collective-permute-start.13 = (bf16[2,64,256]{2,1,0:T(8,128)(2,1)}, bf16[2,64,256]{2,1,0:T(8,128)(2,1)}, u32[]{:S(2)}, u32[]{:S(2)}) collective-permute-start(bf16[2,64,256]{2,1,0:T(8,128)(2,1)} %pad_maximum_fusion.1), channel_id=1, source_target_pairs={{0,2},{1,17},{2,0},{3,19},{4,6},{5,21},{6,4},{7,23},{8,10},{9,25},... | collective-permute-start | bytes 196616 | tf_op jit(solution)/shard_map/ppermute | solution.py:71
  23.1 9.9 %collective-permute-start.14 = (bf16[64,256]{1,0:T(8,128)(2,1)S(1)}, bf16[64,256]{1,0:T(8,128)(2,1)S(1)}, u32[]{:S(2)}, u32[]{:S(2)}) collective-permute-start(bf16[64,256]{1,0:T(8,128)(2,1)S(1)} %shard_map.66.refs_3_.refs_4_), channel_id=1, source_target_pairs={{0,18},{1,19},{2,16},{3,17},{4,22},{5,23},{6,20},{7,21},{8,26},{9,... | collective-permute-start | bytes 98312 | tf_op jit(solution)/shard_map/ppermute | solution.py:71
  25.5 6.5 %collective-permute-start.10 = (bf16[2,64,256]{2,1,0:T(8,128)(2,1)}, bf16[2,64,256]{2,1,0:T(8,128)(2,1)S(1)}, u32[]{:S(2)}, u32[]{:S(2)}) collective-permute-start(bf16[2,64,256]{2,1,0:T(8,128)(2,1)} %collective-permute-done.9), channel_id=1, source_target_pairs={{0,2},{1,3},{2,0},{3,1},{4,6},{5,7},{6,4},{7,5},{8,10},{9,11},{10,... | collective-permute-start | bytes 196616 | tf_op jit(solution)/shard_map/ppermute | solution.py:71
  26.0 6.0 %collective-permute-start.11 = (bf16[2,64,256]{2,1,0:T(8,128)(2,1)}, bf16[2,64,256]{2,1,0:T(8,128)(2,1)S(1)}, u32[]{:S(2)}, u32[]{:S(2)}) collective-permute-start(bf16[2,64,256]{2,1,0:T(8,128)(2,1)} %collective-permute-done.9), channel_id=1, source_target_pairs={{0,16},{1,17},{2,18},{3,19},{4,20},{5,21},{6,22},{7,23},{8,24},{9,... | collective-permute-start | bytes 196616 | tf_op jit(solution)/shard_map/ppermute | solution.py:71
  26.8 5.4 %collective-permute-start.12 = (bf16[2,64,256]{2,1,0:T(8,128)(2,1)}, bf16[2,64,256]{2,1,0:T(8,128)(2,1)S(1)}, u32[]{:S(2)}, u32[]{:S(2)}) collective-permute-start(bf16[2,64,256]{2,1,0:T(8,128)(2,1)} %collective-permute-done.9), channel_id=1, source_target_pairs={{0,18},{1,19},{2,16},{3,17},{4,22},{5,23},{6,20},{7,21},{8,26},{9,... | collective-permute-start | bytes 196616 | tf_op jit(solution)/shard_map/ppermute | solution.py:71
  33.1 1.7 %collective-permute-start.15 = (bf16[11,64,256]{2,1,0:T(8,128)(2,1)S(1)}, bf16[11,64,256]{2,1,0:T(8,128)(2,1)S(1)}, u32[]{:S(2)}, u32[]{:S(2)}) collective-permute-start(bf16[11,64,256]{2,1,0:T(8,128)(2,1)S(1)} %constant_dynamic-update-slice_fusion.6.refs_0_.refs_1_), channel_id=1, source_target_pairs={{0,1},{1,0},{2,3},{3,2},{4,5},{5,4},{6,7},{7,6},{8,9},{9,8},{10,11... | collective-permute-start | bytes 1081352 | tf_op jit(solution)/shard_map/ppermute | solution.py:75
  36.0 1.3 %collective-permute-start.16 = (bf16[64,256]{1,0:T(8,128)(2,1)S(1)}, bf16[64,256]{1,0:T(8,128)(2,1)S(1)}, u32[]{:S(2)}, u32[]{:S(2)}) collective-permute-start(bf16[64,256]{1,0:T(8,128)(2,1)S(1)} %shard_map.69.refs_3_), channel_id=1, source_target_pairs={{0,1},{1,0},{2,3},{3,2},{4,5},{5,4},{6,7},{7,6},{8,9},{9,8},{10,11... | collective-permute-start | bytes 98312 | tf_op jit(solution)/shard_map/ppermute | solution.py:75
  37.3 4.3 %collective-permute-start.17 = (bf16[2,64,256]{2,1,0:T(8,128)(2,1)S(1)}, bf16[2,64,256]{2,1,0:T(8,128)(2,1)S(1)}, u32[]{:S(2)}, u32[]{:S(2)}) collective-permute-start(bf16[2,64,256]{2,1,0:T(8,128)(2,1)S(1)} %pad_maximum_fusion.2), channel_id=1, source_target_pairs={{0,4},{1,3},{2,6},{3,1},{4,0},{5,9},{6,2},{7,11},{8,12},{9,5},{10,... | collective-permute-start | bytes 196616 | tf_op jit(solution)/shard_map/ppermute | solution.py:71
  38.8 6.3 %collective-permute-start.21 = (bf16[2,64,256]{2,1,0:T(8,128)(2,1)S(1)}, bf16[2,64,256]{2,1,0:T(8,128)(2,1)S(1)}, u32[]{:S(2)}, u32[]{:S(2)}) collective-permute-start(bf16[2,64,256]{2,1,0:T(8,128)(2,1)S(1)} %pad_maximum_fusion.2), channel_id=1, source_target_pairs={{0,2},{1,17},{2,0},{3,19},{4,6},{5,21},{6,4},{7,23},{8,10},{9,25},... | collective-permute-start | bytes 196616 | tf_op jit(solution)/shard_map/ppermute | solution.py:71
  40.1 9.4 %collective-permute-start.22 = (bf16[64,256]{1,0:T(8,128)(2,1)S(1)}, bf16[64,256]{1,0:T(8,128)(2,1)S(1)}, u32[]{:S(2)}, u32[]{:S(2)}) collective-permute-start(bf16[64,256]{1,0:T(8,128)(2,1)S(1)} %shard_map.69.refs_3_), channel_id=1, source_target_pairs={{0,18},{1,19},{2,16},{3,17},{4,22},{5,23},{6,20},{7,21},{8,26},{9,... | collective-permute-start | bytes 98312 | tf_op jit(solution)/shard_map/ppermute | solution.py:71
  41.6 5.6 %collective-permute-start.18 = (bf16[2,64,256]{2,1,0:T(8,128)(2,1)S(1)}, bf16[2,64,256]{2,1,0:T(8,128)(2,1)S(1)}, u32[]{:S(2)}, u32[]{:S(2)}) collective-permute-start(bf16[2,64,256]{2,1,0:T(8,128)(2,1)S(1)} %collective-permute-done.17), channel_id=1, source_target_pairs={{0,2},{1,3},{2,0},{3,1},{4,6},{5,7},{6,4},{7,5},{8,10},{9,11},{10,... | collective-permute-start | bytes 196616 | tf_op jit(solution)/shard_map/ppermute | solution.py:71
  43.1 4.7 %collective-permute-start.19 = (bf16[2,64,256]{2,1,0:T(8,128)(2,1)S(1)}, bf16[2,64,256]{2,1,0:T(8,128)(2,1)S(1)}, u32[]{:S(2)}, u32[]{:S(2)}) collective-permute-start(bf16[2,64,256]{2,1,0:T(8,128)(2,1)S(1)} %collective-permute-done.17), channel_id=1, source_target_pairs={{0,16},{1,17},{2,18},{3,19},{4,20},{5,21},{6,22},{7,23},{8,24},{9,... | collective-permute-start | bytes 196616 | tf_op jit(solution)/shard_map/ppermute | solution.py:71
  44.3 5.2 %collective-permute-start.20 = (bf16[2,64,256]{2,1,0:T(8,128)(2,1)S(1)}, bf16[2,64,256]{2,1,0:T(8,128)(2,1)S(1)}, u32[]{:S(2)}, u32[]{:S(2)}) collective-permute-start(bf16[2,64,256]{2,1,0:T(8,128)(2,1)S(1)} %collective-permute-done.17), channel_id=1, source_target_pairs={{0,18},{1,19},{2,16},{3,17},{4,22},{5,23},{6,20},{7,21},{8,26},{9,... | collective-permute-start | bytes 196616 | tf_op jit(solution)/shard_map/ppermute | solution.py:71
  49.5 1.7 %collective-permute-start.23 = (bf16[11,64,256]{2,1,0:T(8,128)(2,1)S(1)}, bf16[11,64,256]{2,1,0:T(8,128)(2,1)S(1)}, u32[]{:S(2)}, u32[]{:S(2)}) collective-permute-start(bf16[11,64,256]{2,1,0:T(8,128)(2,1)S(1)} %constant_dynamic-update-slice_fusion.12.refs_0_), channel_id=1, source_target_pairs={{0,1},{1,0},{2,3},{3,2},{4,5},{5,4},{6,7},{7,6},{8,9},{9,8},{10,11... | collective-permute-start | bytes 1081352 | tf_op jit(solution)/shard_map/ppermute | solution.py:75

commit v7 on v6

--- a/solution.py
+++ b/solution.py
@@ -177,16 +177,16 @@
 
 
 def fold_kernel(
-    _, raw_hbm, slot_hbm, live_hbm, scale_hbm,
-    __, tile_out, index_out,
-    raw_ref, slot_ref, live_ref, scale_ref, arrived, *, rim_count,
+    _, raw_hbm, slot_hbm, live_hbm, scale_hbm, time_hbm,
+    __, tile_out, index_out, time_out,
+    raw_ref, slot_ref, live_ref, scale_ref, time_ref, arrived, *, rim_count,
 ):
     count = slot_ref.shape[1]
     rows = raw_ref.shape[0] // PARTS
     fetches = [
         pltpu.make_async_copy(source, target, arrived.at[n])
         for n, (source, target) in enumerate(
-            [(scale_hbm, scale_ref), (slot_hbm, slot_ref), (live_hbm, live_ref)]
+            [(scale_hbm, scale_ref), (slot_hbm, slot_ref), (live_hbm, live_ref), (time_hbm, time_ref)]
             + [
                 (raw_hbm.at[pl.ds(p * rows, rows)], raw_ref.at[pl.ds(p * rows, rows)])
                 for p in range(PARTS)
@@ -196,11 +196,15 @@
     for fetch in fetches:
         fetch.start()
     half = lax.broadcasted_iota(jnp.int32, (PB, LANES), 1) < PB
-    for fetch in fetches[:3]:
+    small = len(fetches) - PARTS
+    for fetch in fetches[:small]:
         fetch.wait()
+    eye = [lax.broadcasted_iota(jnp.int32, (FEATURES, FEATURES), n) for n in range(2)]
+    column = jnp.where(eye[0] == eye[1], time_ref[...], 0.0)
+    time_out[...] = jnp.sum(column, axis=1, keepdims=True)
     index_out[...] = source_index(slot_ref[...], live_ref[...], count, rim_count)
     for p in range(PARTS):
-        fetches[3 + p].wait()
+        fetches[small + p].wait()
         for b in range(p * rows // PB, (p + 1) * rows // PB):
             for k in range(0, scale_ref.shape[0], 2):
                 at = pl.ds(b * PB, PB), pl.ds(k * PB, LANES)
@@ -343,23 +347,29 @@
     def fold(through):
         return call(
             functools.partial(fold_kernel, rim_count=rim_count),
-            (tile_shape, index_shape),
+            (tile_shape, index_shape, jax.ShapeDtypeStruct((FEATURES, 1), jnp.float32)),
             [
                 pltpu.VMEM((points, width), jnp.bfloat16),
                 pltpu.VMEM(slots.shape, jnp.int32),
                 pltpu.VMEM((1, count), jnp.int32),
                 pltpu.SMEM(scales.shape, jnp.float32),
-                pltpu.SemaphoreType.DMA((PARTS + 3,)),
+                pltpu.VMEM((1, FEATURES), jnp.float32),
+                pltpu.SemaphoreType.DMA((PARTS + 4,)),
             ],
             half,
             None,
-            fetched=(tiles.reshape(points, width), slots, live.reshape(1, count), scales),
+            fetched=(
+                tiles.reshape(points, width),
+                slots,
+                live.reshape(1, count),
+                scales,
+                times.reshape(1, FEATURES),
+            ),
             through=through,
         )
 
-    rims, (scaled, index) = exchange(rim, fold)
+    rims, (scaled, index, times) = exchange(rim, fold)
     (near,) = call(near_kernel, (image_shape,), [own_store], half, index, value, scaled)
-    times = times[:, None]
     total = value
     for step in range(1, TERMS):
         arrays = (index, *rims, scaled, near)

time: 54.3 us -> 52.4 us (0.965)
  local copies, waits for them, and re-layouts: 2.72 us -> 0.94 us
  other arithmetic: 0.65 us -> 0.02 us
    unnamed x19 -> x17, local copies, waits for them, and re-layouts: 1.78 us -> 0.09 us
    another operation x3, other arithmetic: 0.65 us -> 0.02 us  [exchange(): both = jnp.stack([rim, other])]
  transfers between devices with their start and end apart: 24 -> 24, of which waited for: 12 -> 12; matrix products, arithmetic and copies ran while one was open for 3% -> 0% of each run, Pallas kernels for 18% -> 19%
where the time goes in v7:
time: 52.4 us; the launch traced here: 52.2 us
  starting transfers between devices  25.4 us (48%)
  Pallas kernels  14.9 us (28%)
  waiting for transfers between devices  10.6 us (20%)
  local copies, waits for them, and re-layouts  0.94 us (2%)
    ppermute x18, starting transfers between devices, swap(): return lax.ppermute(value, AXES, pairs)  24.4 us
    pallas_call x9, Pallas kernels, call(): pl.pallas_call(kernel, out_shape=out_shape, in_specs=[pl.BlockSpec(memory...  14.9 us
    ppermute x18, waiting for transfers between devices, swap(): return lax.ppermute(value, AXES, pairs)  6.22 us
    ppermute x6, waiting for transfers between devices, swap_cores(): lax.ppermute(value, 'gz', [(k, k ^ 1) for k in range(lax.axis_size('gz'))])  4.38 us
    ppermute x6, starting transfers between devices, swap_cores(): lax.ppermute(value, 'gz', [(k, k ^ 1) for k in range(lax.axis_size('gz'))])  1.07 us
  transfers between devices with their start and end apart: 24, of which 12 were waited for; matrix products, arithmetic and copies ran while one was open for 0% of the time, Pallas kernels for 19%

profile of v7, /device:TPU:0, one launch (start us, length us, event | category | flops | bytes accessed | tf_op | source)
XLA Modules:
  0.0 52.2 jit_solution(59243985744966887)
XLA Ops:
  0.0 0.0 copy-start
  0.0 0.8 %slice_bitcast_fusion = (bf16[1,64,256]{2,1,0:T(8,128)(2,1)S(1)}, bf16[64,256]{1,0:T(8,128)(2,1)S(1)}) fusion(bf16[64,2048]{1,0:T(8,128)(2,1)} %bitcast.24), kind=kLoop, calls=%fused_computation.21 | loop fusion | bytes 98304 | tf_op jit(solution)/shard_map/stack | solution.py:83
  0.8 0.5 collective-permute-start
  1.3 0.9 %collective-permute-done.refs_2_.refs_3_ = bf16[64,256]{1,0:T(8,128)(2,1)S(1)} collective-permute-done((bf16[64,256]{1,0:T(8,128)(2,1)S(1)}, bf16[64,256]{1,0:T(8,128)(2,1)S(1)}, u32[]{:S(2)}, u32[]{:S(2)}) %collective-permute-start) | collective-permute-done | bytes 32800 | tf_op jit(solution)/shard_map/ppermute | solution.py:75
  2.2 3.0 %collective-permute-start.2 = (bf16[2,64,256]{2,1,0:T(8,128)(2,1)S(1)}, bf16[2,64,256]{2,1,0:T(8,128)(2,1)S(1)}, u32[]{:S(2)}, u32[]{:S(2)}) collective-permute-start(bf16[2,64,256]{2,1,0:T(8,128)(2,1)S(1)} %pad_maximum_fusion), channel_id=1, source_target_pairs={{0,4},{1,3},{2,6},{3,1},{4,0},{5,9},{6,2},{7,11},{8,12},{9,5},{10,... | collective-permute-start | bytes 196616 | tf_op jit(solution)/shard_map/ppermute | solution.py:71
  5.1 1.5 %collective-permute-start.1 = (bf16[2,64,256]{2,1,0:T(8,128)(2,1)S(1)}, bf16[2,64,256]{2,1,0:T(8,128)(2,1)S(1)}, u32[]{:S(2)}, u32[]{:S(2)}) collective-permute-start(bf16[2,64,256]{2,1,0:T(8,128)(2,1)S(1)} %pad_maximum_fusion), channel_id=1, source_target_pairs={{0,2},{1,17},{2,0},{3,19},{4,6},{5,21},{6,4},{7,23},{8,10},{9,25},... | collective-permute-start | bytes 196616 | tf_op jit(solution)/shard_map/ppermute | solution.py:71
  6.6 1.5 %collective-permute-start.6 = (bf16[64,256]{1,0:T(8,128)(2,1)S(1)}, bf16[64,256]{1,0:T(8,128)(2,1)S(1)}, u32[]{:S(2)}, u32[]{:S(2)}) collective-permute-start(bf16[64,256]{1,0:T(8,128)(2,1)S(1)} %get-tuple-element.26.refs_3_.refs_4_), channel_id=1, source_target_pairs={{0,18},{1,19},{2,16},{3,17},{4,22},{5,23},{6,20},{7,21},{8,26},{9,... | collective-permute-start | bytes 98312 | tf_op jit(solution)/shard_map/ppermute | solution.py:71
  8.1 0.0 collective-permute-done.2
  8.1 1.5 %collective-permute-start.3 = (bf16[2,64,256]{2,1,0:T(8,128)(2,1)S(1)}, bf16[2,64,256]{2,1,0:T(8,128)(2,1)S(1)}, u32[]{:S(2)}, u32[]{:S(2)}) collective-permute-start(bf16[2,64,256]{2,1,0:T(8,128)(2,1)S(1)} %collective-permute-done.2), channel_id=1, source_target_pairs={{0,2},{1,3},{2,0},{3,1},{4,6},{5,7},{6,4},{7,5},{8,10},{9,11},{10,... | collective-permute-start | bytes 196616 | tf_op jit(solution)/shard_map/ppermute | solution.py:71
  9.6 1.2 %collective-permute-start.4 = (bf16[2,64,256]{2,1,0:T(8,128)(2,1)S(1)}, bf16[2,64,256]{2,1,0:T(8,128)(2,1)S(1)}, u32[]{:S(2)}, u32[]{:S(2)}) collective-permute-start(bf16[2,64,256]{2,1,0:T(8,128)(2,1)S(1)} %collective-permute-done.2), channel_id=1, source_target_pairs={{0,16},{1,17},{2,18},{3,19},{4,20},{5,21},{6,22},{7,23},{8,24},{9,... | collective-permute-start | bytes 196616 | tf_op jit(solution)/shard_map/ppermute | solution.py:71
  10.8 0.8 %collective-permute-start.5 = (bf16[2,64,256]{2,1,0:T(8,128)(2,1)S(1)}, bf16[2,64,256]{2,1,0:T(8,128)(2,1)S(1)}, u32[]{:S(2)}, u32[]{:S(2)}) collective-permute-start(bf16[2,64,256]{2,1,0:T(8,128)(2,1)S(1)} %collective-permute-done.2), channel_id=1, source_target_pairs={{0,18},{1,19},{2,16},{3,17},{4,22},{5,23},{6,20},{7,21},{8,26},{9,... | collective-permute-start | bytes 196616 | tf_op jit(solution)/shard_map/ppermute | solution.py:71
  11.6 0.0 collective-permute-done.1._
  11.6 1.8 %shard_map.64 = (bf16[2,64,256]{2,1,0:T(8,128)(2,1)S(1)}, bf16[2048,512]{1,0:T(8,128)(2,1)S(1)}, s32[8,32]{1,0:T(8,128)S(1)}, f32[64,1]{1,0:T(8,128)S(1)}) custom-call(bf16[2,64,256]{2,1,0:T(8,128)(2,1)S(1)} %collective-permute-done.1._, bf16[2048,512]{1,0:T(8,128)(2,1)} %bitcast.32, s32[8,32]{1,0:T(8,128)} %bitcast.33, ...), custom_call_target="tpu_custom_call", output_to_operand_aliasing={{0}: (0, {})} | custom-call | flops 67108864 | bytes 1048576 | tf_op jit(solution)/shard_map/pallas_call | solution.py:308
  13.4 0.0 collective-permute-done.3
  13.4 0.9 %collective-permute-done.4 = bf16[2,64,256]{2,1,0:T(8,128)(2,1)S(1)} collective-permute-done((bf16[2,64,256]{2,1,0:T(8,128)(2,1)S(1)}, bf16[2,64,256]{2,1,0:T(8,128)(2,1)S(1)}, u32[]{:S(2)}, u32[]{:S(2)}) %collective-permute-start.4) | collective-permute-done | bytes 65568 | tf_op jit(solution)/shard_map/ppermute | solution.py:71
  14.3 1.7 %collective-permute-done.5 = bf16[2,64,256]{2,1,0:T(8,128)(2,1)S(1)} collective-permute-done((bf16[2,64,256]{2,1,0:T(8,128)(2,1)S(1)}, bf16[2,64,256]{2,1,0:T(8,128)(2,1)S(1)}, u32[]{:S(2)}, u32[]{:S(2)}) %collective-permute-start.5) | collective-permute-done | bytes 65568 | tf_op jit(solution)/shard_map/ppermute | solution.py:71
  16.0 0.0 collective-permute-done.6
  16.1 0.1 collective-permute-start.7
  16.1 0.0 copy-done
  16.1 1.2 %shard_map.65.refs_5_.refs_6_ = f32[64,2048]{1,0:T(8,128)S(1)} custom-call(s32[8,32]{1,0:T(8,128)S(1)} %get-tuple-element.15.index_ref, bf16[64,2048]{1,0:T(8,128)(2,1)S(1)} %bitcast.26, bf16[2048,512]{1,0:T(8,128)(2,1)S(1)} %get-tuple-element.17.tile_ref.refs_4_.refs_5_), custom_call_target="tpu_custom_call" | custom-call | flops 67108864 | bytes 1048576 | tf_op jit(solution)/shard_map/pallas_call | solution.py:308
  17.3 0.5 collective-permute-done.7.refs_1_.refs_2_
  17.8 1.2 %shard_map.66.refs_3_.refs_4_ = bf16[64,256]{1,0:T(8,128)(2,1)S(1)} custom-call(s32[8,32]{1,0:T(8,128)S(1)} %get-tuple-element.15.index_ref, bf16[11,64,256]{2,1,0:T(8,128)(2,1)S(1)} %constant_dynamic-update-slice_fusion.refs_0_.refs_1_, bf16[11,64,256]{2,1,0:T(8,128)(2,1)S(1)} %collective-permute-done.7.refs_1_.refs_2_, ...), custom_call_target="tpu_custom_call" | custom-call | flops 8388608 | bytes 131072 | tf_op jit(solution)/shard_map/pallas_call | solution.py:308
  19.0 0.2 collective-permute-start.8
  19.2 1.1 %collective-permute-done.8.refs_2_.refs_3_ = bf16[64,256]{1,0:T(8,128)(2,1)S(1)} collective-permute-done((bf16[64,256]{1,0:T(8,128)(2,1)S(1)}, bf16[64,256]{1,0:T(8,128)(2,1)S(1)}, u32[]{:S(2)}, u32[]{:S(2)}) %collective-permute-start.8) | collective-permute-done | bytes 32800 | tf_op jit(solution)/shard_map/ppermute | solution.py:75
  20.3 1.6 %collective-permute-start.9 = (bf16[2,64,256]{2,1,0:T(8,128)(2,1)S(1)}, bf16[2,64,256]{2,1,0:T(8,128)(2,1)S(1)}, u32[]{:S(2)}, u32[]{:S(2)}) collective-permute-start(bf16[2,64,256]{2,1,0:T(8,128)(2,1)S(1)} %pad_maximum_fusion.1), channel_id=1, source_target_pairs={{0,4},{1,3},{2,6},{3,1},{4,0},{5,9},{6,2},{7,11},{8,12},{9,5},{10,... | collective-permute-start | bytes 196616 | tf_op jit(solution)/shard_map/ppermute | solution.py:71
  21.9 0.5 %collective-permute-start.13 = (bf16[2,64,256]{2,1,0:T(8,128)(2,1)S(1)}, bf16[2,64,256]{2,1,0:T(8,128)(2,1)S(1)}, u32[]{:S(2)}, u32[]{:S(2)}) collective-permute-start(bf16[2,64,256]{2,1,0:T(8,128)(2,1)S(1)} %pad_maximum_fusion.1), channel_id=1, source_target_pairs={{0,2},{1,17},{2,0},{3,19},{4,6},{5,21},{6,4},{7,23},{8,10},{9,25},... | collective-permute-start | bytes 196616 | tf_op jit(solution)/shard_map/ppermute | solution.py:71
  22.4 1.4 %collective-permute-start.14 = (bf16[64,256]{1,0:T(8,128)(2,1)S(1)}, bf16[64,256]{1,0:T(8,128)(2,1)S(1)}, u32[]{:S(2)}, u32[]{:S(2)}) collective-permute-start(bf16[64,256]{1,0:T(8,128)(2,1)S(1)} %shard_map.66.refs_3_.refs_4_), channel_id=1, source_target_pairs={{0,18},{1,19},{2,16},{3,17},{4,22},{5,23},{6,20},{7,21},{8,26},{9,... | collective-permute-start | bytes 98312 | tf_op jit(solution)/shard_map/ppermute | solution.py:71
  23.9 0.7 %collective-permute-done.9 = bf16[2,64,256]{2,1,0:T(8,128)(2,1)S(1)} collective-permute-done((bf16[2,64,256]{2,1,0:T(8,128)(2,1)S(1)}, bf16[2,64,256]{2,1,0:T(8,128)(2,1)S(1)}, u32[]{:S(2)}, u32[]{:S(2)}) %collective-permute-start.9) | collective-permute-done | bytes 65568 | tf_op jit(solution)/shard_map/ppermute | solution.py:71
  24.6 0.5 %collective-permute-start.10 = (bf16[2,64,256]{2,1,0:T(8,128)(2,1)S(1)}, bf16[2,64,256]{2,1,0:T(8,128)(2,1)S(1)}, u32[]{:S(2)}, u32[]{:S(2)}) collective-permute-start(bf16[2,64,256]{2,1,0:T(8,128)(2,1)S(1)} %collective-permute-done.9), channel_id=1, source_target_pairs={{0,2},{1,3},{2,0},{3,1},{4,6},{5,7},{6,4},{7,5},{8,10},{9,11},{10,... | collective-permute-start | bytes 196616 | tf_op jit(solution)/shard_map/ppermute | solution.py:71
  25.1 0.8 %collective-permute-start.11 = (bf16[2,64,256]{2,1,0:T(8,128)(2,1)S(1)}, bf16[2,64,256]{2,1,0:T(8,128)(2,1)S(1)}, u32[]{:S(2)}, u32[]{:S(2)}) collective-permute-start(bf16[2,64,256]{2,1,0:T(8,128)(2,1)S(1)} %collective-permute-done.9), channel_id=1, source_target_pairs={{0,16},{1,17},{2,18},{3,19},{4,20},{5,21},{6,22},{7,23},{8,24},{9,... | collective-permute-start | bytes 196616 | tf_op jit(solution)/shard_map/ppermute | solution.py:71
  25.9 2.1 %collective-permute-start.12 = (bf16[2,64,256]{2,1,0:T(8,128)(2,1)S(1)}, bf16[2,64,256]{2,1,0:T(8,128)(2,1)S(1)}, u32[]{:S(2)}, u32[]{:S(2)}) collective-permute-start(bf16[2,64,256]{2,1,0:T(8,128)(2,1)S(1)} %collective-permute-done.9), channel_id=1, source_target_pairs={{0,18},{1,19},{2,16},{3,17},{4,22},{5,23},{6,20},{7,21},{8,26},{9,... | collective-permute-start | bytes 196616 | tf_op jit(solution)/shard_map/ppermute | solution.py:71
  28.1 0.0 collective-permute-done.13.refs_0_
  28.1 2.2 %shard_map.67 = (bf16[2,64,256]{2,1,0:T(8,128)(2,1)S(1)}, f32[64,2048]{1,0:T(8,128)S(1)}, bf16[64,2048]{1,0:T(8,128)(2,1)S(1)}) custom-call(s32[8,32]{1,0:T(8,128)S(1)} %get-tuple-element.15.index_ref, bf16[2,64,256]{2,1,0:T(8,128)(2,1)S(1)} %collective-permute-done.13.refs_0_, ...), custom_call_target="tpu_custom_call", output_to_operand_aliasing={{0}: (1, {})} | custom-call | flops 67108864 | bytes 1048576 | tf_op jit(solution)/shard_map/pallas_call | solution.py:308
  30.3 0.0 collective-permute-done.10
  30.4 0.0 collective-permute-done.11
  30.4 0.7 %collective-permute-done.12 = bf16[2,64,256]{2,1,0:T(8,128)(2,1)S(1)} collective-permute-done((bf16[2,64,256]{2,1,0:T(8,128)(2,1)S(1)}, bf16[2,64,256]{2,1,0:T(8,128)(2,1)S(1)}, u32[]{:S(2)}, u32[]{:S(2)}) %collective-permute-start.12) | collective-permute-done | bytes 65568 | tf_op jit(solution)/shard_map/ppermute | solution.py:71
  31.1 0.0 collective-permute-done.14
  31.1 0.1 collective-permute-start.15
  31.2 1.2 %shard_map.68.refs_5_.refs_6_ = f32[64,2048]{1,0:T(8,128)S(1)} custom-call(s32[8,32]{1,0:T(8,128)S(1)} %get-tuple-element.15.index_ref, bf16[64,2048]{1,0:T(8,128)(2,1)S(1)} %get-tuple-element.20.value_ref, bf16[2048,512]{1,0:T(8,128)(2,1)S(1)} %get-tuple-element.17.tile_ref.refs_4_.refs_5_), custom_call_target="tpu_custom_call" | custom-call | flops 67108864 | bytes 1048576 | tf_op jit(solution)/shard_map/pallas_call | solution.py:308
  32.4 0.5 collective-permute-done.15.refs_1_.refs_2_
  32.9 1.2 %shard_map.69.refs_3_ = bf16[64,256]{1,0:T(8,128)(2,1)S(1)} custom-call(s32[8,32]{1,0:T(8,128)S(1)} %get-tuple-element.15.index_ref, bf16[11,64,256]{2,1,0:T(8,128)(2,1)S(1)} %constant_dynamic-update-slice_fusion.6.refs_0_.refs_1_, bf16[11,64,256]{2,1,0:T(8,128)(2,1)S(1)} %collective-permute-done.15.refs_1_.refs_2_, ...), custom_call_target="tpu_custom_call" | custom-call | flops 8388608 | bytes 131072 | tf_op jit(solution)/shard_map/pallas_call | solution.py:308
  34.1 0.2 collective-permute-start.16
  34.3 1.1 %collective-permute-done.16.refs_2_ = bf16[64,256]{1,0:T(8,128)(2,1)S(1)} collective-permute-done((bf16[64,256]{1,0:T(8,128)(2,1)S(1)}, bf16[64,256]{1,0:T(8,128)(2,1)S(1)}, u32[]{:S(2)}, u32[]{:S(2)}) %collective-permute-start.16) | collective-permute-done | bytes 32800 | tf_op jit(solution)/shard_map/ppermute | solution.py:75
  35.4 1.3 %collective-permute-start.17 = (bf16[2,64,256]{2,1,0:T(8,128)(2,1)S(1)}, bf16[2,64,256]{2,1,0:T(8,128)(2,1)S(1)}, u32[]{:S(2)}, u32[]{:S(2)}) collective-permute-start(bf16[2,64,256]{2,1,0:T(8,128)(2,1)S(1)} %pad_maximum_fusion.2), channel_id=1, source_target_pairs={{0,4},{1,3},{2,6},{3,1},{4,0},{5,9},{6,2},{7,11},{8,12},{9,5},{10,... | collective-permute-start | bytes 196616 | tf_op jit(solution)/shard_map/ppermute | solution.py:71
  36.7 1.5 %collective-permute-start.21 = (bf16[2,64,256]{2,1,0:T(8,128)(2,1)S(1)}, bf16[2,64,256]{2,1,0:T(8,128)(2,1)S(1)}, u32[]{:S(2)}, u32[]{:S(2)}) collective-permute-start(bf16[2,64,256]{2,1,0:T(8,128)(2,1)S(1)} %pad_maximum_fusion.2), channel_id=1, source_target_pairs={{0,2},{1,17},{2,0},{3,19},{4,6},{5,21},{6,4},{7,23},{8,10},{9,25},... | collective-permute-start | bytes 196616 | tf_op jit(solution)/shard_map/ppermute | solution.py:71
  38.2 1.5 %collective-permute-start.22 = (bf16[64,256]{1,0:T(8,128)(2,1)S(1)}, bf16[64,256]{1,0:T(8,128)(2,1)S(1)}, u32[]{:S(2)}, u32[]{:S(2)}) collective-permute-start(bf16[64,256]{1,0:T(8,128)(2,1)S(1)} %shard_map.69.refs_3_), channel_id=1, source_target_pairs={{0,18},{1,19},{2,16},{3,17},{4,22},{5,23},{6,20},{7,21},{8,26},{9,... | collective-permute-start | bytes 98312 | tf_op jit(solution)/shard_map/ppermute | solution.py:71
  39.7 0.0 collective-permute-done.17
  39.7 1.5 %collective-permute-start.18 = (bf16[2,64,256]{2,1,0:T(8,128)(2,1)S(1)}, bf16[2,64,256]{2,1,0:T(8,128)(2,1)S(1)}, u32[]{:S(2)}, u32[]{:S(2)}) collective-permute-start(bf16[2,64,256]{2,1,0:T(8,128)(2,1)S(1)} %collective-permute-done.17), channel_id=1, source_target_pairs={{0,2},{1,3},{2,0},{3,1},{4,6},{5,7},{6,4},{7,5},{8,10},{9,11},{10,... | collective-permute-start | bytes 196616 | tf_op jit(solution)/shard_map/ppermute | solution.py:71
  41.2 1.2 %collective-permute-start.19 = (bf16[2,64,256]{2,1,0:T(8,128)(2,1)S(1)}, bf16[2,64,256]{2,1,0:T(8,128)(2,1)S(1)}, u32[]{:S(2)}, u32[]{:S(2)}) collective-permute-start(bf16[2,64,256]{2,1,0:T(8,128)(2,1)S(1)} %collective-permute-done.17), channel_id=1, source_target_pairs={{0,16},{1,17},{2,18},{3,19},{4,20},{5,21},{6,22},{7,23},{8,24},{9,... | collective-permute-start | bytes 196616 | tf_op jit(solution)/shard_map/ppermute | solution.py:71
  42.4 0.8 %collective-permute-start.20 = (bf16[2,64,256]{2,1,0:T(8,128)(2,1)S(1)}, bf16[2,64,256]{2,1,0:T(8,128)(2,1)S(1)}, u32[]{:S(2)}, u32[]{:S(2)}) collective-permute-start(bf16[2,64,256]{2,1,0:T(8,128)(2,1)S(1)} %collective-permute-done.17), channel_id=1, source_target_pairs={{0,18},{1,19},{2,16},{3,17},{4,22},{5,23},{6,20},{7,21},{8,26},{9,... | collective-permute-start | bytes 196616 | tf_op jit(solution)/shard_map/ppermute | solution.py:71
  43.2 0.0 collective-permute-done.21.refs_0_
  43.2 2.2 %shard_map.70 = (bf16[2,64,256]{2,1,0:T(8,128)(2,1)S(1)}, f32[64,2048]{1,0:T(8,128)S(1)}, bf16[64,2048]{1,0:T(8,128)(2,1)S(1)}) custom-call(s32[8,32]{1,0:T(8,128)S(1)} %get-tuple-element.15.index_ref, bf16[2,64,256]{2,1,0:T(8,128)(2,1)S(1)} %collective-permute-done.21.refs_0_, ...), custom_call_target="tpu_custom_call", output_to_operand_aliasing={{0}: (1, {})} | custom-call | flops 67108864 | bytes 1048576 | tf_op jit(solution)/shard_map/pallas_call | solution.py:308
  45.4 0.0 collective-permute-done.18
  45.4 0.5 collective-permute-done.19
  45.9 1.7 %collective-permute-done.20 = bf16[2,64,256]{2,1,0:T(8,128)(2,1)S(1)} collective-permute-done((bf16[2,64,256]{2,1,0:T(8,128)(2,1)S(1)}, bf16[2,64,256]{2,1,0:T(8,128)(2,1)S(1)}, u32[]{:S(2)}, u32[]{:S(2)}) %collective-permute-start.20) | collective-permute-done | bytes 65568 | tf_op jit(solution)/shard_map/ppermute | solution.py:71
  47.6 0.0 collective-permute-done.22
  47.6 0.1 collective-permute-start.23
  47.7 1.2 %shard_map.71.refs_5_ = f32[64,2048]{1,0:T(8,128)S(1)} custom-call(s32[8,32]{1,0:T(8,128)S(1)} %get-tuple-element.15.index_ref, bf16[64,2048]{1,0:T(8,128)(2,1)S(1)} %get-tuple-element.23.value_ref, bf16[2048,512]{1,0:T(8,128)(2,1)S(1)} %get-tuple-element.17.tile_ref.refs_4_.refs_5_), custom_call_target="tpu_custom_call" | custom-call | flops 67108864 | bytes 1048576 | tf_op jit(solution)/shard_map/pallas_call | solution.py:308
  48.9 0.5 collective-permute-done.23.refs_1_
  49.3 2.8 %shard_map.72 = bf16[64,2048]{1,0:T(8,128)(2,1)} custom-call(s32[8,32]{1,0:T(8,128)S(1)} %get-tuple-element.15.index_ref, bf16[11,64,256]{2,1,0:T(8,128)(2,1)S(1)} %constant_dynamic-update-slice_fusion.12.refs_0_, bf16[11,64,256]{2,1,0:T(8,128)(2,1)S(1)} %collective-permute-done.23.refs_1_, bf16[64,256]{1,0:T(8,128)(2,1)S(1)} %collective-permute-done.16.refs_2_, ...), custom_call_target="tpu_custom_call" | custom-call | flops 67108864 | bytes 1048576 | tf_op jit(solution)/shard_map/pallas_call | solution.py:308
  (21 shorter events, 0.1 us)
Async XLA Ops:
  0.0 16.1 %copy-start = (bf16[64,1,1,2048]{3,0,2,1:T(8,128)(2,1)S(1)}, bf16[64,1,1,2048]{3,0,2,1:T(8,128)(2,1)}, u32[]{:S(2)}) copy-start(bf16[64,1,1,2048]{3,0,2,1:T(8,128)(2,1)} %param.6) | copy-start | bytes 786436
  0.8 1.3 %collective-permute-start = (bf16[64,256]{1,0:T(8,128)(2,1)S(1)}, bf16[64,256]{1,0:T(8,128)(2,1)S(1)}, u32[]{:S(2)}, u32[]{:S(2)}) collective-permute-start(bf16[64,256]{1,0:T(8,128)(2,1)S(1)} %get-tuple-element.26.refs_3_.refs_4_), channel_id=1, source_target_pairs={{0,1},{1,0},{2,3},{3,2},{4,5},{5,4},{6,7},{7,6},{8,9},{9,8},{10,11... | collective-permute-start | bytes 98312 | tf_op jit(solution)/shard_map/ppermute | solution.py:75
  2.2 6.0 %collective-permute-start.2 = (bf16[2,64,256]{2,1,0:T(8,128)(2,1)S(1)}, bf16[2,64,256]{2,1,0:T(8,128)(2,1)S(1)}, u32[]{:S(2)}, u32[]{:S(2)}) collective-permute-start(bf16[2,64,256]{2,1,0:T(8,128)(2,1)S(1)} %pad_maximum_fusion), channel_id=1, source_target_pairs={{0,4},{1,3},{2,6},{3,1},{4,0},{5,9},{6,2},{7,11},{8,12},{9,5},{10,... | collective-permute-start | bytes 196616 | tf_op jit(solution)/shard_map/ppermute | solution.py:71
  5.1 6.5 %collective-permute-start.1 = (bf16[2,64,256]{2,1,0:T(8,128)(2,1)S(1)}, bf16[2,64,256]{2,1,0:T(8,128)(2,1)S(1)}, u32[]{:S(2)}, u32[]{:S(2)}) collective-permute-start(bf16[2,64,256]{2,1,0:T(8,128)(2,1)S(1)} %pad_maximum_fusion), channel_id=1, source_target_pairs={{0,2},{1,17},{2,0},{3,19},{4,6},{5,21},{6,4},{7,23},{8,10},{9,25},... | collective-permute-start | bytes 196616 | tf_op jit(solution)/shard_map/ppermute | solution.py:71
  6.6 9.4 %collective-permute-start.6 = (bf16[64,256]{1,0:T(8,128)(2,1)S(1)}, bf16[64,256]{1,0:T(8,128)(2,1)S(1)}, u32[]{:S(2)}, u32[]{:S(2)}) collective-permute-start(bf16[64,256]{1,0:T(8,128)(2,1)S(1)} %get-tuple-element.26.refs_3_.refs_4_), channel_id=1, source_target_pairs={{0,18},{1,19},{2,16},{3,17},{4,22},{5,23},{6,20},{7,21},{8,26},{9,... | collective-permute-start | bytes 98312 | tf_op jit(solution)/shard_map/ppermute | solution.py:71
  8.1 5.3 %collective-permute-start.3 = (bf16[2,64,256]{2,1,0:T(8,128)(2,1)S(1)}, bf16[2,64,256]{2,1,0:T(8,128)(2,1)S(1)}, u32[]{:S(2)}, u32[]{:S(2)}) collective-permute-start(bf16[2,64,256]{2,1,0:T(8,128)(2,1)S(1)} %collective-permute-done.2), channel_id=1, source_target_pairs={{0,2},{1,3},{2,0},{3,1},{4,6},{5,7},{6,4},{7,5},{8,10},{9,11},{10,... | collective-permute-start | bytes 196616 | tf_op jit(solution)/shard_map/ppermute | solution.py:71
  9.6 4.7 %collective-permute-start.4 = (bf16[2,64,256]{2,1,0:T(8,128)(2,1)S(1)}, bf16[2,64,256]{2,1,0:T(8,128)(2,1)S(1)}, u32[]{:S(2)}, u32[]{:S(2)}) collective-permute-start(bf16[2,64,256]{2,1,0:T(8,128)(2,1)S(1)} %collective-permute-done.2), channel_id=1, source_target_pairs={{0,16},{1,17},{2,18},{3,19},{4,20},{5,21},{6,22},{7,23},{8,24},{9,... | collective-permute-start | bytes 196616 | tf_op jit(solution)/shard_map/ppermute | solution.py:71
  10.8 5.2 %collective-permute-start.5 = (bf16[2,64,256]{2,1,0:T(8,128)(2,1)S(1)}, bf16[2,64,256]{2,1,0:T(8,128)(2,1)S(1)}, u32[]{:S(2)}, u32[]{:S(2)}) collective-permute-start(bf16[2,64,256]{2,1,0:T(8,128)(2,1)S(1)} %collective-permute-done.2), channel_id=1, source_target_pairs={{0,18},{1,19},{2,16},{3,17},{4,22},{5,23},{6,20},{7,21},{8,26},{9,... | collective-permute-start | bytes 196616 | tf_op jit(solution)/shard_map/ppermute | solution.py:71
  16.1 1.7 %collective-permute-start.7 = (bf16[11,64,256]{2,1,0:T(8,128)(2,1)S(1)}, bf16[11,64,256]{2,1,0:T(8,128)(2,1)S(1)}, u32[]{:S(2)}, u32[]{:S(2)}) collective-permute-start(bf16[11,64,256]{2,1,0:T(8,128)(2,1)S(1)} %constant_dynamic-update-slice_fusion.refs_0_.refs_1_), channel_id=1, source_target_pairs={{0,1},{1,0},{2,3},{3,2},{4,5},{5,4},{6,7},{7,6},{8,9},{9,8},{10,11... | collective-permute-start | bytes 1081352 | tf_op jit(solution)/shard_map/ppermute | solution.py:75
  19.0 1.3 %collective-permute-start.8 = (bf16[64,256]{1,0:T(8,128)(2,1)S(1)}, bf16[64,256]{1,0:T(8,128)(2,1)S(1)}, u32[]{:S(2)}, u32[]{:S(2)}) collective-permute-start(bf16[64,256]{1,0:T(8,128)(2,1)S(1)} %shard_map.66.refs_3_.refs_4_), channel_id=1, source_target_pairs={{0,1},{1,0},{2,3},{3,2},{4,5},{5,4},{6,7},{7,6},{8,9},{9,8},{10,11... | collective-permute-start | bytes 98312 | tf_op jit(solution)/shard_map/ppermute | solution.py:75
  20.3 4.3 %collective-permute-start.9 = (bf16[2,64,256]{2,1,0:T(8,128)(2,1)S(1)}, bf16[2,64,256]{2,1,0:T(8,128)(2,1)S(1)}, u32[]{:S(2)}, u32[]{:S(2)}) collective-permute-start(bf16[2,64,256]{2,1,0:T(8,128)(2,1)S(1)} %pad_maximum_fusion.1), channel_id=1, source_target_pairs={{0,4},{1,3},{2,6},{3,1},{4,0},{5,9},{6,2},{7,11},{8,12},{9,5},{10,... | collective-permute-start | bytes 196616 | tf_op jit(solution)/shard_map/ppermute | solution.py:71
  21.9 6.2 %collective-permute-start.13 = (bf16[2,64,256]{2,1,0:T(8,128)(2,1)S(1)}, bf16[2,64,256]{2,1,0:T(8,128)(2,1)S(1)}, u32[]{:S(2)}, u32[]{:S(2)}) collective-permute-start(bf16[2,64,256]{2,1,0:T(8,128)(2,1)S(1)} %pad_maximum_fusion.1), channel_id=1, source_target_pairs={{0,2},{1,17},{2,0},{3,19},{4,6},{5,21},{6,4},{7,23},{8,10},{9,25},... | collective-permute-start | bytes 196616 | tf_op jit(solution)/shard_map/ppermute | solution.py:71
  22.4 8.7 %collective-permute-start.14 = (bf16[64,256]{1,0:T(8,128)(2,1)S(1)}, bf16[64,256]{1,0:T(8,128)(2,1)S(1)}, u32[]{:S(2)}, u32[]{:S(2)}) collective-permute-start(bf16[64,256]{1,0:T(8,128)(2,1)S(1)} %shard_map.66.refs_3_.refs_4_), channel_id=1, source_target_pairs={{0,18},{1,19},{2,16},{3,17},{4,22},{5,23},{6,20},{7,21},{8,26},{9,... | collective-permute-start | bytes 98312 | tf_op jit(solution)/shard_map/ppermute | solution.py:71
  24.6 5.7 %collective-permute-start.10 = (bf16[2,64,256]{2,1,0:T(8,128)(2,1)S(1)}, bf16[2,64,256]{2,1,0:T(8,128)(2,1)S(1)}, u32[]{:S(2)}, u32[]{:S(2)}) collective-permute-start(bf16[2,64,256]{2,1,0:T(8,128)(2,1)S(1)} %collective-permute-done.9), channel_id=1, source_target_pairs={{0,2},{1,3},{2,0},{3,1},{4,6},{5,7},{6,4},{7,5},{8,10},{9,11},{10,... | collective-permute-start | bytes 196616 | tf_op jit(solution)/shard_map/ppermute | solution.py:71
  25.1 5.2 %collective-permute-start.11 = (bf16[2,64,256]{2,1,0:T(8,128)(2,1)S(1)}, bf16[2,64,256]{2,1,0:T(8,128)(2,1)S(1)}, u32[]{:S(2)}, u32[]{:S(2)}) collective-permute-start(bf16[2,64,256]{2,1,0:T(8,128)(2,1)S(1)} %collective-permute-done.9), channel_id=1, source_target_pairs={{0,16},{1,17},{2,18},{3,19},{4,20},{5,21},{6,22},{7,23},{8,24},{9,... | collective-permute-start | bytes 196616 | tf_op jit(solution)/shard_map/ppermute | solution.py:71
  25.9 5.2 %collective-permute-start.12 = (bf16[2,64,256]{2,1,0:T(8,128)(2,1)S(1)}, bf16[2,64,256]{2,1,0:T(8,128)(2,1)S(1)}, u32[]{:S(2)}, u32[]{:S(2)}) collective-permute-start(bf16[2,64,256]{2,1,0:T(8,128)(2,1)S(1)} %collective-permute-done.9), channel_id=1, source_target_pairs={{0,18},{1,19},{2,16},{3,17},{4,22},{5,23},{6,20},{7,21},{8,26},{9,... | collective-permute-start | bytes 196616 | tf_op jit(solution)/shard_map/ppermute | solution.py:71
  31.1 1.7 %collective-permute-start.15 = (bf16[11,64,256]{2,1,0:T(8,128)(2,1)S(1)}, bf16[11,64,256]{2,1,0:T(8,128)(2,1)S(1)}, u32[]{:S(2)}, u32[]{:S(2)}) collective-permute-start(bf16[11,64,256]{2,1,0:T(8,128)(2,1)S(1)} %constant_dynamic-update-slice_fusion.6.refs_0_.refs_1_), channel_id=1, source_target_pairs={{0,1},{1,0},{2,3},{3,2},{4,5},{5,4},{6,7},{7,6},{8,9},{9,8},{10,11... | collective-permute-start | bytes 1081352 | tf_op jit(solution)/shard_map/ppermute | solution.py:75
  34.1 1.3 %collective-permute-start.16 = (bf16[64,256]{1,0:T(8,128)(2,1)S(1)}, bf16[64,256]{1,0:T(8,128)(2,1)S(1)}, u32[]{:S(2)}, u32[]{:S(2)}) collective-permute-start(bf16[64,256]{1,0:T(8,128)(2,1)S(1)} %shard_map.69.refs_3_), channel_id=1, source_target_pairs={{0,1},{1,0},{2,3},{3,2},{4,5},{5,4},{6,7},{7,6},{8,9},{9,8},{10,11... | collective-permute-start | bytes 98312 | tf_op jit(solution)/shard_map/ppermute | solution.py:75
  35.4 4.3 %collective-permute-start.17 = (bf16[2,64,256]{2,1,0:T(8,128)(2,1)S(1)}, bf16[2,64,256]{2,1,0:T(8,128)(2,1)S(1)}, u32[]{:S(2)}, u32[]{:S(2)}) collective-permute-start(bf16[2,64,256]{2,1,0:T(8,128)(2,1)S(1)} %pad_maximum_fusion.2), channel_id=1, source_target_pairs={{0,4},{1,3},{2,6},{3,1},{4,0},{5,9},{6,2},{7,11},{8,12},{9,5},{10,... | collective-permute-start | bytes 196616 | tf_op jit(solution)/shard_map/ppermute | solution.py:71
  36.7 6.5 %collective-permute-start.21 = (bf16[2,64,256]{2,1,0:T(8,128)(2,1)S(1)}, bf16[2,64,256]{2,1,0:T(8,128)(2,1)S(1)}, u32[]{:S(2)}, u32[]{:S(2)}) collective-permute-start(bf16[2,64,256]{2,1,0:T(8,128)(2,1)S(1)} %pad_maximum_fusion.2), channel_id=1, source_target_pairs={{0,2},{1,17},{2,0},{3,19},{4,6},{5,21},{6,4},{7,23},{8,10},{9,25},... | collective-permute-start | bytes 196616 | tf_op jit(solution)/shard_map/ppermute | solution.py:71
  38.2 9.4 %collective-permute-start.22 = (bf16[64,256]{1,0:T(8,128)(2,1)S(1)}, bf16[64,256]{1,0:T(8,128)(2,1)S(1)}, u32[]{:S(2)}, u32[]{:S(2)}) collective-permute-start(bf16[64,256]{1,0:T(8,128)(2,1)S(1)} %shard_map.69.refs_3_), channel_id=1, source_target_pairs={{0,18},{1,19},{2,16},{3,17},{4,22},{5,23},{6,20},{7,21},{8,26},{9,... | collective-permute-start | bytes 98312 | tf_op jit(solution)/shard_map/ppermute | solution.py:71
  39.7 5.7 %collective-permute-start.18 = (bf16[2,64,256]{2,1,0:T(8,128)(2,1)S(1)}, bf16[2,64,256]{2,1,0:T(8,128)(2,1)S(1)}, u32[]{:S(2)}, u32[]{:S(2)}) collective-permute-start(bf16[2,64,256]{2,1,0:T(8,128)(2,1)S(1)} %collective-permute-done.17), channel_id=1, source_target_pairs={{0,2},{1,3},{2,0},{3,1},{4,6},{5,7},{6,4},{7,5},{8,10},{9,11},{10,... | collective-permute-start | bytes 196616 | tf_op jit(solution)/shard_map/ppermute | solution.py:71
  41.2 4.7 %collective-permute-start.19 = (bf16[2,64,256]{2,1,0:T(8,128)(2,1)S(1)}, bf16[2,64,256]{2,1,0:T(8,128)(2,1)S(1)}, u32[]{:S(2)}, u32[]{:S(2)}) collective-permute-start(bf16[2,64,256]{2,1,0:T(8,128)(2,1)S(1)} %collective-permute-done.17), channel_id=1, source_target_pairs={{0,16},{1,17},{2,18},{3,19},{4,20},{5,21},{6,22},{7,23},{8,24},{9,... | collective-permute-start | bytes 196616 | tf_op jit(solution)/shard_map/ppermute | solution.py:71
  42.4 5.2 %collective-permute-start.20 = (bf16[2,64,256]{2,1,0:T(8,128)(2,1)S(1)}, bf16[2,64,256]{2,1,0:T(8,128)(2,1)S(1)}, u32[]{:S(2)}, u32[]{:S(2)}) collective-permute-start(bf16[2,64,256]{2,1,0:T(8,128)(2,1)S(1)} %collective-permute-done.17), channel_id=1, source_target_pairs={{0,18},{1,19},{2,16},{3,17},{4,22},{5,23},{6,20},{7,21},{8,26},{9,... | collective-permute-start | bytes 196616 | tf_op jit(solution)/shard_map/ppermute | solution.py:71
  47.6 1.7 %collective-permute-start.23 = (bf16[11,64,256]{2,1,0:T(8,128)(2,1)S(1)}, bf16[11,64,256]{2,1,0:T(8,128)(2,1)S(1)}, u32[]{:S(2)}, u32[]{:S(2)}) collective-permute-start(bf16[11,64,256]{2,1,0:T(8,128)(2,1)S(1)} %constant_dynamic-update-slice_fusion.12.refs_0_), channel_id=1, source_target_pairs={{0,1},{1,0},{2,3},{3,2},{4,5},{5,4},{6,7},{7,6},{8,9},{9,8},{10,11... | collective-permute-start | bytes 1081352 | tf_op jit(solution)/shard_map/ppermute | solution.py:75

commit v8 on v7

--- a/solution.py
+++ b/solution.py
@@ -141,8 +141,7 @@
     panels, _, rim = mine_ref.shape
     rim_count = rim // PB
 
-    @pl.loop(0, panels)
-    def _(panel):
+    for panel in range(panels):
         for t in range(rim // LANES):
             cut = slice(t * LANES, (t + 1) * LANES)
             at = panel * rim_count + 2 * t

time: 52.4 us -> 51.3 us (0.979)
  Pallas kernels: 14.9 us -> 13 us
  waiting for transfers between devices: 10.6 us -> 11.4 us
    pallas_call x9, Pallas kernels: 14.9 us -> 13 us  [call(): pl.pallas_call(kernel, out_shape=out_shape, in_specs=[pl.BlockSpec(memory...]
    ppermute x18, waiting for transfers between devices: 6.22 us -> 7.06 us  [swap(): return lax.ppermute(value, AXES, pairs)]
  transfers between devices with their start and end apart: 24 -> 24, of which waited for: 12 -> 12; matrix products, arithmetic and copies ran while one was open for 0% -> 0% of each run, Pallas kernels for 19% -> 17%
where the time goes in v8:
time: 51.3 us; the launch traced here: 51.1 us
  starting transfers between devices  25.4 us (50%)
  Pallas kernels  13 us (25%)
  waiting for transfers between devices  11.4 us (22%)
  local copies, waits for them, and re-layouts  0.94 us (2%)
    ppermute x18, starting transfers between devices, swap(): return lax.ppermute(value, AXES, pairs)  24.4 us
    pallas_call x9, Pallas kernels, call(): pl.pallas_call(kernel, out_shape=out_shape, in_specs=[pl.BlockSpec(memory...  13 us
    ppermute x18, waiting for transfers between devices, swap(): return lax.ppermute(value, AXES, pairs)  7.06 us
    ppermute x6, waiting for transfers between devices, swap_cores(): lax.ppermute(value, 'gz', [(k, k ^ 1) for k in range(lax.axis_size('gz'))])  4.38 us
    ppermute x6, starting transfers between devices, swap_cores(): lax.ppermute(value, 'gz', [(k, k ^ 1) for k in range(lax.axis_size('gz'))])  1.07 us
  transfers between devices with their start and end apart: 24, of which 12 were waited for; matrix products, arithmetic and copies ran while one was open for 0% of the time, Pallas kernels for 17%

profile of v8, /device:TPU:0, one launch (start us, length us, event | category | flops | bytes accessed | tf_op | source)
XLA Modules:
  0.0 51.1 jit_solution(6054630494045510199)
XLA Ops:
  0.0 0.0 copy-start
  0.0 0.8 %slice_bitcast_fusion = (bf16[1,64,256]{2,1,0:T(8,128)(2,1)S(1)}, bf16[64,256]{1,0:T(8,128)(2,1)S(1)}) fusion(bf16[64,2048]{1,0:T(8,128)(2,1)} %bitcast.24), kind=kLoop, calls=%fused_computation.21 | loop fusion | bytes 98304 | tf_op jit(solution)/shard_map/stack | solution.py:83
  0.8 0.5 collective-permute-start
  1.3 0.9 %collective-permute-done.refs_2_.refs_3_ = bf16[64,256]{1,0:T(8,128)(2,1)S(1)} collective-permute-done((bf16[64,256]{1,0:T(8,128)(2,1)S(1)}, bf16[64,256]{1,0:T(8,128)(2,1)S(1)}, u32[]{:S(2)}, u32[]{:S(2)}) %collective-permute-start) | collective-permute-done | bytes 32800 | tf_op jit(solution)/shard_map/ppermute | solution.py:75
  2.2 3.0 %collective-permute-start.2 = (bf16[2,64,256]{2,1,0:T(8,128)(2,1)S(1)}, bf16[2,64,256]{2,1,0:T(8,128)(2,1)S(1)}, u32[]{:S(2)}, u32[]{:S(2)}) collective-permute-start(bf16[2,64,256]{2,1,0:T(8,128)(2,1)S(1)} %pad_maximum_fusion), channel_id=1, source_target_pairs={{0,4},{1,3},{2,6},{3,1},{4,0},{5,9},{6,2},{7,11},{8,12},{9,5},{10,... | collective-permute-start | bytes 196616 | tf_op jit(solution)/shard_map/ppermute | solution.py:71
  5.1 1.5 %collective-permute-start.1 = (bf16[2,64,256]{2,1,0:T(8,128)(2,1)S(1)}, bf16[2,64,256]{2,1,0:T(8,128)(2,1)S(1)}, u32[]{:S(2)}, u32[]{:S(2)}) collective-permute-start(bf16[2,64,256]{2,1,0:T(8,128)(2,1)S(1)} %pad_maximum_fusion), channel_id=1, source_target_pairs={{0,2},{1,17},{2,0},{3,19},{4,6},{5,21},{6,4},{7,23},{8,10},{9,25},... | collective-permute-start | bytes 196616 | tf_op jit(solution)/shard_map/ppermute | solution.py:71
  6.6 1.5 %collective-permute-start.6 = (bf16[64,256]{1,0:T(8,128)(2,1)S(1)}, bf16[64,256]{1,0:T(8,128)(2,1)S(1)}, u32[]{:S(2)}, u32[]{:S(2)}) collective-permute-start(bf16[64,256]{1,0:T(8,128)(2,1)S(1)} %get-tuple-element.26.refs_3_.refs_4_), channel_id=1, source_target_pairs={{0,18},{1,19},{2,16},{3,17},{4,22},{5,23},{6,20},{7,21},{8,26},{9,... | collective-permute-start | bytes 98312 | tf_op jit(solution)/shard_map/ppermute | solution.py:71
  8.1 0.0 collective-permute-done.2
  8.1 1.5 %collective-permute-start.3 = (bf16[2,64,256]{2,1,0:T(8,128)(2,1)S(1)}, bf16[2,64,256]{2,1,0:T(8,128)(2,1)S(1)}, u32[]{:S(2)}, u32[]{:S(2)}) collective-permute-start(bf16[2,64,256]{2,1,0:T(8,128)(2,1)S(1)} %collective-permute-done.2), channel_id=1, source_target_pairs={{0,2},{1,3},{2,0},{3,1},{4,6},{5,7},{6,4},{7,5},{8,10},{9,11},{10,... | collective-permute-start | bytes 196616 | tf_op jit(solution)/shard_map/ppermute | solution.py:71
  9.6 1.2 %collective-permute-start.4 = (bf16[2,64,256]{2,1,0:T(8,128)(2,1)S(1)}, bf16[2,64,256]{2,1,0:T(8,128)(2,1)S(1)}, u32[]{:S(2)}, u32[]{:S(2)}) collective-permute-start(bf16[2,64,256]{2,1,0:T(8,128)(2,1)S(1)} %collective-permute-done.2), channel_id=1, source_target_pairs={{0,16},{1,17},{2,18},{3,19},{4,20},{5,21},{6,22},{7,23},{8,24},{9,... | collective-permute-start | bytes 196616 | tf_op jit(solution)/shard_map/ppermute | solution.py:71
  10.8 0.8 %collective-permute-start.5 = (bf16[2,64,256]{2,1,0:T(8,128)(2,1)S(1)}, bf16[2,64,256]{2,1,0:T(8,128)(2,1)S(1)}, u32[]{:S(2)}, u32[]{:S(2)}) collective-permute-start(bf16[2,64,256]{2,1,0:T(8,128)(2,1)S(1)} %collective-permute-done.2), channel_id=1, source_target_pairs={{0,18},{1,19},{2,16},{3,17},{4,22},{5,23},{6,20},{7,21},{8,26},{9,... | collective-permute-start | bytes 196616 | tf_op jit(solution)/shard_map/ppermute | solution.py:71
  11.6 0.0 collective-permute-done.1._
  11.6 1.8 %shard_map.64 = (bf16[2,64,256]{2,1,0:T(8,128)(2,1)S(1)}, bf16[2048,512]{1,0:T(8,128)(2,1)S(1)}, s32[8,32]{1,0:T(8,128)S(1)}, f32[64,1]{1,0:T(8,128)S(1)}) custom-call(bf16[2,64,256]{2,1,0:T(8,128)(2,1)S(1)} %collective-permute-done.1._, bf16[2048,512]{1,0:T(8,128)(2,1)} %bitcast.32, s32[8,32]{1,0:T(8,128)} %bitcast.33, ...), custom_call_target="tpu_custom_call", output_to_operand_aliasing={{0}: (0, {})} | custom-call | flops 67108864 | bytes 1048576 | tf_op jit(solution)/shard_map/pallas_call | solution.py:307
  13.4 0.0 collective-permute-done.3
  13.4 0.9 %collective-permute-done.4 = bf16[2,64,256]{2,1,0:T(8,128)(2,1)S(1)} collective-permute-done((bf16[2,64,256]{2,1,0:T(8,128)(2,1)S(1)}, bf16[2,64,256]{2,1,0:T(8,128)(2,1)S(1)}, u32[]{:S(2)}, u32[]{:S(2)}) %collective-permute-start.4) | collective-permute-done | bytes 65568 | tf_op jit(solution)/shard_map/ppermute | solution.py:71
  14.3 1.7 %collective-permute-done.5 = bf16[2,64,256]{2,1,0:T(8,128)(2,1)S(1)} collective-permute-done((bf16[2,64,256]{2,1,0:T(8,128)(2,1)S(1)}, bf16[2,64,256]{2,1,0:T(8,128)(2,1)S(1)}, u32[]{:S(2)}, u32[]{:S(2)}) %collective-permute-start.5) | collective-permute-done | bytes 65568 | tf_op jit(solution)/shard_map/ppermute | solution.py:71
  16.0 0.0 collective-permute-done.6
  16.1 0.1 collective-permute-start.7
  16.1 0.0 copy-done
  16.1 1.2 %shard_map.65.refs_5_.refs_6_ = f32[64,2048]{1,0:T(8,128)S(1)} custom-call(s32[8,32]{1,0:T(8,128)S(1)} %get-tuple-element.15.index_ref, bf16[64,2048]{1,0:T(8,128)(2,1)S(1)} %bitcast.26, bf16[2048,512]{1,0:T(8,128)(2,1)S(1)} %get-tuple-element.17.tile_ref.refs_4_.refs_5_), custom_call_target="tpu_custom_call" | custom-call | flops 67108864 | bytes 1048576 | tf_op jit(solution)/shard_map/pallas_call | solution.py:307
  17.3 0.5 collective-permute-done.7.refs_1_.refs_2_
  17.8 1.0 %shard_map.66.refs_3_.refs_4_ = bf16[64,256]{1,0:T(8,128)(2,1)S(1)} custom-call(s32[8,32]{1,0:T(8,128)S(1)} %get-tuple-element.15.index_ref, bf16[11,64,256]{2,1,0:T(8,128)(2,1)S(1)} %constant_dynamic-update-slice_fusion.refs_0_.refs_1_, bf16[11,64,256]{2,1,0:T(8,128)(2,1)S(1)} %collective-permute-done.7.refs_1_.refs_2_, ...), custom_call_target="tpu_custom_call" | custom-call | flops 8388608 | bytes 131072 | tf_op jit(solution)/shard_map/pallas_call | solution.py:307
  18.8 0.2 collective-permute-start.8
  19.0 1.1 %collective-permute-done.8.refs_2_.refs_3_ = bf16[64,256]{1,0:T(8,128)(2,1)S(1)} collective-permute-done((bf16[64,256]{1,0:T(8,128)(2,1)S(1)}, bf16[64,256]{1,0:T(8,128)(2,1)S(1)}, u32[]{:S(2)}, u32[]{:S(2)}) %collective-permute-start.8) | collective-permute-done | bytes 32800 | tf_op jit(solution)/shard_map/ppermute | solution.py:75
  20.1 1.6 %collective-permute-start.9 = (bf16[2,64,256]{2,1,0:T(8,128)(2,1)S(1)}, bf16[2,64,256]{2,1,0:T(8,128)(2,1)S(1)}, u32[]{:S(2)}, u32[]{:S(2)}) collective-permute-start(bf16[2,64,256]{2,1,0:T(8,128)(2,1)S(1)} %pad_maximum_fusion.1), channel_id=1, source_target_pairs={{0,4},{1,3},{2,6},{3,1},{4,0},{5,9},{6,2},{7,11},{8,12},{9,5},{10,... | collective-permute-start | bytes 196616 | tf_op jit(solution)/shard_map/ppermute | solution.py:71
  21.7 0.5 %collective-permute-start.13 = (bf16[2,64,256]{2,1,0:T(8,128)(2,1)S(1)}, bf16[2,64,256]{2,1,0:T(8,128)(2,1)S(1)}, u32[]{:S(2)}, u32[]{:S(2)}) collective-permute-start(bf16[2,64,256]{2,1,0:T(8,128)(2,1)S(1)} %pad_maximum_fusion.1), channel_id=1, source_target_pairs={{0,2},{1,17},{2,0},{3,19},{4,6},{5,21},{6,4},{7,23},{8,10},{9,25},... | collective-permute-start | bytes 196616 | tf_op jit(solution)/shard_map/ppermute | solution.py:71
  22.2 1.4 %collective-permute-start.14 = (bf16[64,256]{1,0:T(8,128)(2,1)S(1)}, bf16[64,256]{1,0:T(8,128)(2,1)S(1)}, u32[]{:S(2)}, u32[]{:S(2)}) collective-permute-start(bf16[64,256]{1,0:T(8,128)(2,1)S(1)} %shard_map.66.refs_3_.refs_4_), channel_id=1, source_target_pairs={{0,18},{1,19},{2,16},{3,17},{4,22},{5,23},{6,20},{7,21},{8,26},{9,... | collective-permute-start | bytes 98312 | tf_op jit(solution)/shard_map/ppermute | solution.py:71
  23.7 0.7 %collective-permute-done.9 = bf16[2,64,256]{2,1,0:T(8,128)(2,1)S(1)} collective-permute-done((bf16[2,64,256]{2,1,0:T(8,128)(2,1)S(1)}, bf16[2,64,256]{2,1,0:T(8,128)(2,1)S(1)}, u32[]{:S(2)}, u32[]{:S(2)}) %collective-permute-start.9) | collective-permute-done | bytes 65568 | tf_op jit(solution)/shard_map/ppermute | solution.py:71
  24.4 0.5 %collective-permute-start.10 = (bf16[2,64,256]{2,1,0:T(8,128)(2,1)S(1)}, bf16[2,64,256]{2,1,0:T(8,128)(2,1)S(1)}, u32[]{:S(2)}, u32[]{:S(2)}) collective-permute-start(bf16[2,64,256]{2,1,0:T(8,128)(2,1)S(1)} %collective-permute-done.9), channel_id=1, source_target_pairs={{0,2},{1,3},{2,0},{3,1},{4,6},{5,7},{6,4},{7,5},{8,10},{9,11},{10,... | collective-permute-start | bytes 196616 | tf_op jit(solution)/shard_map/ppermute | solution.py:71
  24.9 0.8 %collective-permute-start.11 = (bf16[2,64,256]{2,1,0:T(8,128)(2,1)S(1)}, bf16[2,64,256]{2,1,0:T(8,128)(2,1)S(1)}, u32[]{:S(2)}, u32[]{:S(2)}) collective-permute-start(bf16[2,64,256]{2,1,0:T(8,128)(2,1)S(1)} %collective-permute-done.9), channel_id=1, source_target_pairs={{0,16},{1,17},{2,18},{3,19},{4,20},{5,21},{6,22},{7,23},{8,24},{9,... | collective-permute-start | bytes 196616 | tf_op jit(solution)/shard_map/ppermute | solution.py:71
  25.7 2.1 %collective-permute-start.12 = (bf16[2,64,256]{2,1,0:T(8,128)(2,1)S(1)}, bf16[2,64,256]{2,1,0:T(8,128)(2,1)S(1)}, u32[]{:S(2)}, u32[]{:S(2)}) collective-permute-start(bf16[2,64,256]{2,1,0:T(8,128)(2,1)S(1)} %collective-permute-done.9), channel_id=1, source_target_pairs={{0,18},{1,19},{2,16},{3,17},{4,22},{5,23},{6,20},{7,21},{8,26},{9,... | collective-permute-start | bytes 196616 | tf_op jit(solution)/shard_map/ppermute | solution.py:71
  27.9 0.0 collective-permute-done.13.refs_0_
  27.9 2.1 %shard_map.67 = (bf16[2,64,256]{2,1,0:T(8,128)(2,1)S(1)}, f32[64,2048]{1,0:T(8,128)S(1)}, bf16[64,2048]{1,0:T(8,128)(2,1)S(1)}) custom-call(s32[8,32]{1,0:T(8,128)S(1)} %get-tuple-element.15.index_ref, bf16[2,64,256]{2,1,0:T(8,128)(2,1)S(1)} %collective-permute-done.13.refs_0_, ...), custom_call_target="tpu_custom_call", output_to_operand_aliasing={{0}: (1, {})} | custom-call | flops 67108864 | bytes 1048576 | tf_op jit(solution)/shard_map/pallas_call | solution.py:307
  30.0 0.0 collective-permute-done.10
  30.0 0.0 collective-permute-done.11
  30.1 0.8 %collective-permute-done.12 = bf16[2,64,256]{2,1,0:T(8,128)(2,1)S(1)} collective-permute-done((bf16[2,64,256]{2,1,0:T(8,128)(2,1)S(1)}, bf16[2,64,256]{2,1,0:T(8,128)(2,1)S(1)}, u32[]{:S(2)}, u32[]{:S(2)}) %collective-permute-start.12) | collective-permute-done | bytes 65568 | tf_op jit(solution)/shard_map/ppermute | solution.py:71
  30.9 0.0 collective-permute-done.14
  30.9 0.1 collective-permute-start.15
  31.0 1.2 %shard_map.68.refs_5_.refs_6_ = f32[64,2048]{1,0:T(8,128)S(1)} custom-call(s32[8,32]{1,0:T(8,128)S(1)} %get-tuple-element.15.index_ref, bf16[64,2048]{1,0:T(8,128)(2,1)S(1)} %get-tuple-element.20.value_ref, bf16[2048,512]{1,0:T(8,128)(2,1)S(1)} %get-tuple-element.17.tile_ref.refs_4_.refs_5_), custom_call_target="tpu_custom_call" | custom-call | flops 67108864 | bytes 1048576 | tf_op jit(solution)/shard_map/pallas_call | solution.py:307
  32.2 0.5 collective-permute-done.15.refs_1_.refs_2_
  32.7 1.0 %shard_map.69.refs_3_ = bf16[64,256]{1,0:T(8,128)(2,1)S(1)} custom-call(s32[8,32]{1,0:T(8,128)S(1)} %get-tuple-element.15.index_ref, bf16[11,64,256]{2,1,0:T(8,128)(2,1)S(1)} %constant_dynamic-update-slice_fusion.6.refs_0_.refs_1_, bf16[11,64,256]{2,1,0:T(8,128)(2,1)S(1)} %collective-permute-done.15.refs_1_.refs_2_, ...), custom_call_target="tpu_custom_call" | custom-call | flops 8388608 | bytes 131072 | tf_op jit(solution)/shard_map/pallas_call | solution.py:307
  33.7 0.2 collective-permute-start.16
  33.9 1.1 %collective-permute-done.16.refs_2_ = bf16[64,256]{1,0:T(8,128)(2,1)S(1)} collective-permute-done((bf16[64,256]{1,0:T(8,128)(2,1)S(1)}, bf16[64,256]{1,0:T(8,128)(2,1)S(1)}, u32[]{:S(2)}, u32[]{:S(2)}) %collective-permute-start.16) | collective-permute-done | bytes 32800 | tf_op jit(solution)/shard_map/ppermute | solution.py:75
  35.0 1.3 %collective-permute-start.17 = (bf16[2,64,256]{2,1,0:T(8,128)(2,1)S(1)}, bf16[2,64,256]{2,1,0:T(8,128)(2,1)S(1)}, u32[]{:S(2)}, u32[]{:S(2)}) collective-permute-start(bf16[2,64,256]{2,1,0:T(8,128)(2,1)S(1)} %pad_maximum_fusion.2), channel_id=1, source_target_pairs={{0,4},{1,3},{2,6},{3,1},{4,0},{5,9},{6,2},{7,11},{8,12},{9,5},{10,... | collective-permute-start | bytes 196616 | tf_op jit(solution)/shard_map/ppermute | solution.py:71
  36.3 1.5 %collective-permute-start.21 = (bf16[2,64,256]{2,1,0:T(8,128)(2,1)S(1)}, bf16[2,64,256]{2,1,0:T(8,128)(2,1)S(1)}, u32[]{:S(2)}, u32[]{:S(2)}) collective-permute-start(bf16[2,64,256]{2,1,0:T(8,128)(2,1)S(1)} %pad_maximum_fusion.2), channel_id=1, source_target_pairs={{0,2},{1,17},{2,0},{3,19},{4,6},{5,21},{6,4},{7,23},{8,10},{9,25},... | collective-permute-start | bytes 196616 | tf_op jit(solution)/shard_map/ppermute | solution.py:71
  37.8 1.5 %collective-permute-start.22 = (bf16[64,256]{1,0:T(8,128)(2,1)S(1)}, bf16[64,256]{1,0:T(8,128)(2,1)S(1)}, u32[]{:S(2)}, u32[]{:S(2)}) collective-permute-start(bf16[64,256]{1,0:T(8,128)(2,1)S(1)} %shard_map.69.refs_3_), channel_id=1, source_target_pairs={{0,18},{1,19},{2,16},{3,17},{4,22},{5,23},{6,20},{7,21},{8,26},{9,... | collective-permute-start | bytes 98312 | tf_op jit(solution)/shard_map/ppermute | solution.py:71
  39.3 0.0 collective-permute-done.17
  39.3 1.5 %collective-permute-start.18 = (bf16[2,64,256]{2,1,0:T(8,128)(2,1)S(1)}, bf16[2,64,256]{2,1,0:T(8,128)(2,1)S(1)}, u32[]{:S(2)}, u32[]{:S(2)}) collective-permute-start(bf16[2,64,256]{2,1,0:T(8,128)(2,1)S(1)} %collective-permute-done.17), channel_id=1, source_target_pairs={{0,2},{1,3},{2,0},{3,1},{4,6},{5,7},{6,4},{7,5},{8,10},{9,11},{10,... | collective-permute-start | bytes 196616 | tf_op jit(solution)/shard_map/ppermute | solution.py:71
  40.8 1.2 %collective-permute-start.19 = (bf16[2,64,256]{2,1,0:T(8,128)(2,1)S(1)}, bf16[2,64,256]{2,1,0:T(8,128)(2,1)S(1)}, u32[]{:S(2)}, u32[]{:S(2)}) collective-permute-start(bf16[2,64,256]{2,1,0:T(8,128)(2,1)S(1)} %collective-permute-done.17), channel_id=1, source_target_pairs={{0,16},{1,17},{2,18},{3,19},{4,20},{5,21},{6,22},{7,23},{8,24},{9,... | collective-permute-start | bytes 196616 | tf_op jit(solution)/shard_map/ppermute | solution.py:71
  42.0 0.8 %collective-permute-start.20 = (bf16[2,64,256]{2,1,0:T(8,128)(2,1)S(1)}, bf16[2,64,256]{2,1,0:T(8,128)(2,1)S(1)}, u32[]{:S(2)}, u32[]{:S(2)}) collective-permute-start(bf16[2,64,256]{2,1,0:T(8,128)(2,1)S(1)} %collective-permute-done.17), channel_id=1, source_target_pairs={{0,18},{1,19},{2,16},{3,17},{4,22},{5,23},{6,20},{7,21},{8,26},{9,... | collective-permute-start | bytes 196616 | tf_op jit(solution)/shard_map/ppermute | solution.py:71
  42.8 0.0 collective-permute-done.21.refs_0_
  42.8 1.4 %shard_map.70 = (bf16[2,64,256]{2,1,0:T(8,128)(2,1)S(1)}, f32[64,2048]{1,0:T(8,128)S(1)}, bf16[64,2048]{1,0:T(8,128)(2,1)S(1)}) custom-call(s32[8,32]{1,0:T(8,128)S(1)} %get-tuple-element.15.index_ref, bf16[2,64,256]{2,1,0:T(8,128)(2,1)S(1)} %collective-permute-done.21.refs_0_, ...), custom_call_target="tpu_custom_call", output_to_operand_aliasing={{0}: (1, {})} | custom-call | flops 67108864 | bytes 1048576 | tf_op jit(solution)/shard_map/pallas_call | solution.py:307
  44.3 0.0 collective-permute-done.18
  44.3 1.2 %collective-permute-done.19 = bf16[2,64,256]{2,1,0:T(8,128)(2,1)S(1)} collective-permute-done((bf16[2,64,256]{2,1,0:T(8,128)(2,1)S(1)}, bf16[2,64,256]{2,1,0:T(8,128)(2,1)S(1)}, u32[]{:S(2)}, u32[]{:S(2)}) %collective-permute-start.19) | collective-permute-done | bytes 65568 | tf_op jit(solution)/shard_map/ppermute | solution.py:71
  45.5 1.7 %collective-permute-done.20 = bf16[2,64,256]{2,1,0:T(8,128)(2,1)S(1)} collective-permute-done((bf16[2,64,256]{2,1,0:T(8,128)(2,1)S(1)}, bf16[2,64,256]{2,1,0:T(8,128)(2,1)S(1)}, u32[]{:S(2)}, u32[]{:S(2)}) %collective-permute-start.20) | collective-permute-done | bytes 65568 | tf_op jit(solution)/shard_map/ppermute | solution.py:71
  47.2 0.0 collective-permute-done.22
  47.2 0.1 collective-permute-start.23
  47.3 1.2 %shard_map.71.refs_5_ = f32[64,2048]{1,0:T(8,128)S(1)} custom-call(s32[8,32]{1,0:T(8,128)S(1)} %get-tuple-element.15.index_ref, bf16[64,2048]{1,0:T(8,128)(2,1)S(1)} %get-tuple-element.23.value_ref, bf16[2048,512]{1,0:T(8,128)(2,1)S(1)} %get-tuple-element.17.tile_ref.refs_4_.refs_5_), custom_call_target="tpu_custom_call" | custom-call | flops 67108864 | bytes 1048576 | tf_op jit(solution)/shard_map/pallas_call | solution.py:307
  48.5 0.5 collective-permute-done.23.refs_1_
  49.0 2.1 %shard_map.72 = bf16[64,2048]{1,0:T(8,128)(2,1)} custom-call(s32[8,32]{1,0:T(8,128)S(1)} %get-tuple-element.15.index_ref, bf16[11,64,256]{2,1,0:T(8,128)(2,1)S(1)} %constant_dynamic-update-slice_fusion.12.refs_0_, bf16[11,64,256]{2,1,0:T(8,128)(2,1)S(1)} %collective-permute-done.23.refs_1_, bf16[64,256]{1,0:T(8,128)(2,1)S(1)} %collective-permute-done.16.refs_2_, ...), custom_call_target="tpu_custom_call" | custom-call | flops 67108864 | bytes 1048576 | tf_op jit(solution)/shard_map/pallas_call | solution.py:307
  (21 shorter events, 0.1 us)
Async XLA Ops:
  0.0 16.1 %copy-start = (bf16[64,1,1,2048]{3,0,2,1:T(8,128)(2,1)S(1)}, bf16[64,1,1,2048]{3,0,2,1:T(8,128)(2,1)}, u32[]{:S(2)}) copy-start(bf16[64,1,1,2048]{3,0,2,1:T(8,128)(2,1)} %param.6) | copy-start | bytes 786436
  0.8 1.3 %collective-permute-start = (bf16[64,256]{1,0:T(8,128)(2,1)S(1)}, bf16[64,256]{1,0:T(8,128)(2,1)S(1)}, u32[]{:S(2)}, u32[]{:S(2)}) collective-permute-start(bf16[64,256]{1,0:T(8,128)(2,1)S(1)} %get-tuple-element.26.refs_3_.refs_4_), channel_id=1, source_target_pairs={{0,1},{1,0},{2,3},{3,2},{4,5},{5,4},{6,7},{7,6},{8,9},{9,8},{10,11... | collective-permute-start | bytes 98312 | tf_op jit(solution)/shard_map/ppermute | solution.py:75
  2.2 6.0 %collective-permute-start.2 = (bf16[2,64,256]{2,1,0:T(8,128)(2,1)S(1)}, bf16[2,64,256]{2,1,0:T(8,128)(2,1)S(1)}, u32[]{:S(2)}, u32[]{:S(2)}) collective-permute-start(bf16[2,64,256]{2,1,0:T(8,128)(2,1)S(1)} %pad_maximum_fusion), channel_id=1, source_target_pairs={{0,4},{1,3},{2,6},{3,1},{4,0},{5,9},{6,2},{7,11},{8,12},{9,5},{10,... | collective-permute-start | bytes 196616 | tf_op jit(solution)/shard_map/ppermute | solution.py:71
  5.1 6.5 %collective-permute-start.1 = (bf16[2,64,256]{2,1,0:T(8,128)(2,1)S(1)}, bf16[2,64,256]{2,1,0:T(8,128)(2,1)S(1)}, u32[]{:S(2)}, u32[]{:S(2)}) collective-permute-start(bf16[2,64,256]{2,1,0:T(8,128)(2,1)S(1)} %pad_maximum_fusion), channel_id=1, source_target_pairs={{0,2},{1,17},{2,0},{3,19},{4,6},{5,21},{6,4},{7,23},{8,10},{9,25},... | collective-permute-start | bytes 196616 | tf_op jit(solution)/shard_map/ppermute | solution.py:71
  6.6 9.4 %collective-permute-start.6 = (bf16[64,256]{1,0:T(8,128)(2,1)S(1)}, bf16[64,256]{1,0:T(8,128)(2,1)S(1)}, u32[]{:S(2)}, u32[]{:S(2)}) collective-permute-start(bf16[64,256]{1,0:T(8,128)(2,1)S(1)} %get-tuple-element.26.refs_3_.refs_4_), channel_id=1, source_target_pairs={{0,18},{1,19},{2,16},{3,17},{4,22},{5,23},{6,20},{7,21},{8,26},{9,... | collective-permute-start | bytes 98312 | tf_op jit(solution)/shard_map/ppermute | solution.py:71
  8.1 5.3 %collective-permute-start.3 = (bf16[2,64,256]{2,1,0:T(8,128)(2,1)S(1)}, bf16[2,64,256]{2,1,0:T(8,128)(2,1)S(1)}, u32[]{:S(2)}, u32[]{:S(2)}) collective-permute-start(bf16[2,64,256]{2,1,0:T(8,128)(2,1)S(1)} %collective-permute-done.2), channel_id=1, source_target_pairs={{0,2},{1,3},{2,0},{3,1},{4,6},{5,7},{6,4},{7,5},{8,10},{9,11},{10,... | collective-permute-start | bytes 196616 | tf_op jit(solution)/shard_map/ppermute | solution.py:71
  9.6 4.7 %collective-permute-start.4 = (bf16[2,64,256]{2,1,0:T(8,128)(2,1)S(1)}, bf16[2,64,256]{2,1,0:T(8,128)(2,1)S(1)}, u32[]{:S(2)}, u32[]{:S(2)}) collective-permute-start(bf16[2,64,256]{2,1,0:T(8,128)(2,1)S(1)} %collective-permute-done.2), channel_id=1, source_target_pairs={{0,16},{1,17},{2,18},{3,19},{4,20},{5,21},{6,22},{7,23},{8,24},{9,... | collective-permute-start | bytes 196616 | tf_op jit(solution)/shard_map/ppermute | solution.py:71
  10.8 5.2 %collective-permute-start.5 = (bf16[2,64,256]{2,1,0:T(8,128)(2,1)S(1)}, bf16[2,64,256]{2,1,0:T(8,128)(2,1)S(1)}, u32[]{:S(2)}, u32[]{:S(2)}) collective-permute-start(bf16[2,64,256]{2,1,0:T(8,128)(2,1)S(1)} %collective-permute-done.2), channel_id=1, source_target_pairs={{0,18},{1,19},{2,16},{3,17},{4,22},{5,23},{6,20},{7,21},{8,26},{9,... | collective-permute-start | bytes 196616 | tf_op jit(solution)/shard_map/ppermute | solution.py:71
  16.1 1.7 %collective-permute-start.7 = (bf16[11,64,256]{2,1,0:T(8,128)(2,1)S(1)}, bf16[11,64,256]{2,1,0:T(8,128)(2,1)S(1)}, u32[]{:S(2)}, u32[]{:S(2)}) collective-permute-start(bf16[11,64,256]{2,1,0:T(8,128)(2,1)S(1)} %constant_dynamic-update-slice_fusion.refs_0_.refs_1_), channel_id=1, source_target_pairs={{0,1},{1,0},{2,3},{3,2},{4,5},{5,4},{6,7},{7,6},{8,9},{9,8},{10,11... | collective-permute-start | bytes 1081352 | tf_op jit(solution)/shard_map/ppermute | solution.py:75
  18.8 1.3 %collective-permute-start.8 = (bf16[64,256]{1,0:T(8,128)(2,1)S(1)}, bf16[64,256]{1,0:T(8,128)(2,1)S(1)}, u32[]{:S(2)}, u32[]{:S(2)}) collective-permute-start(bf16[64,256]{1,0:T(8,128)(2,1)S(1)} %shard_map.66.refs_3_.refs_4_), channel_id=1, source_target_pairs={{0,1},{1,0},{2,3},{3,2},{4,5},{5,4},{6,7},{7,6},{8,9},{9,8},{10,11... | collective-permute-start | bytes 98312 | tf_op jit(solution)/shard_map/ppermute | solution.py:75
  20.1 4.3 %collective-permute-start.9 = (bf16[2,64,256]{2,1,0:T(8,128)(2,1)S(1)}, bf16[2,64,256]{2,1,0:T(8,128)(2,1)S(1)}, u32[]{:S(2)}, u32[]{:S(2)}) collective-permute-start(bf16[2,64,256]{2,1,0:T(8,128)(2,1)S(1)} %pad_maximum_fusion.1), channel_id=1, source_target_pairs={{0,4},{1,3},{2,6},{3,1},{4,0},{5,9},{6,2},{7,11},{8,12},{9,5},{10,... | collective-permute-start | bytes 196616 | tf_op jit(solution)/shard_map/ppermute | solution.py:71
  21.7 6.2 %collective-permute-start.13 = (bf16[2,64,256]{2,1,0:T(8,128)(2,1)S(1)}, bf16[2,64,256]{2,1,0:T(8,128)(2,1)S(1)}, u32[]{:S(2)}, u32[]{:S(2)}) collective-permute-start(bf16[2,64,256]{2,1,0:T(8,128)(2,1)S(1)} %pad_maximum_fusion.1), channel_id=1, source_target_pairs={{0,2},{1,17},{2,0},{3,19},{4,6},{5,21},{6,4},{7,23},{8,10},{9,25},... | collective-permute-start | bytes 196616 | tf_op jit(solution)/shard_map/ppermute | solution.py:71
  22.2 8.7 %collective-permute-start.14 = (bf16[64,256]{1,0:T(8,128)(2,1)S(1)}, bf16[64,256]{1,0:T(8,128)(2,1)S(1)}, u32[]{:S(2)}, u32[]{:S(2)}) collective-permute-start(bf16[64,256]{1,0:T(8,128)(2,1)S(1)} %shard_map.66.refs_3_.refs_4_), channel_id=1, source_target_pairs={{0,18},{1,19},{2,16},{3,17},{4,22},{5,23},{6,20},{7,21},{8,26},{9,... | collective-permute-start | bytes 98312 | tf_op jit(solution)/shard_map/ppermute | solution.py:71
  24.4 5.6 %collective-permute-start.10 = (bf16[2,64,256]{2,1,0:T(8,128)(2,1)S(1)}, bf16[2,64,256]{2,1,0:T(8,128)(2,1)S(1)}, u32[]{:S(2)}, u32[]{:S(2)}) collective-permute-start(bf16[2,64,256]{2,1,0:T(8,128)(2,1)S(1)} %collective-permute-done.9), channel_id=1, source_target_pairs={{0,2},{1,3},{2,0},{3,1},{4,6},{5,7},{6,4},{7,5},{8,10},{9,11},{10,... | collective-permute-start | bytes 196616 | tf_op jit(solution)/shard_map/ppermute | solution.py:71
  24.9 5.1 %collective-permute-start.11 = (bf16[2,64,256]{2,1,0:T(8,128)(2,1)S(1)}, bf16[2,64,256]{2,1,0:T(8,128)(2,1)S(1)}, u32[]{:S(2)}, u32[]{:S(2)}) collective-permute-start(bf16[2,64,256]{2,1,0:T(8,128)(2,1)S(1)} %collective-permute-done.9), channel_id=1, source_target_pairs={{0,16},{1,17},{2,18},{3,19},{4,20},{5,21},{6,22},{7,23},{8,24},{9,... | collective-permute-start | bytes 196616 | tf_op jit(solution)/shard_map/ppermute | solution.py:71
  25.7 5.2 %collective-permute-start.12 = (bf16[2,64,256]{2,1,0:T(8,128)(2,1)S(1)}, bf16[2,64,256]{2,1,0:T(8,128)(2,1)S(1)}, u32[]{:S(2)}, u32[]{:S(2)}) collective-permute-start(bf16[2,64,256]{2,1,0:T(8,128)(2,1)S(1)} %collective-permute-done.9), channel_id=1, source_target_pairs={{0,18},{1,19},{2,16},{3,17},{4,22},{5,23},{6,20},{7,21},{8,26},{9,... | collective-permute-start | bytes 196616 | tf_op jit(solution)/shard_map/ppermute | solution.py:71
  30.9 1.7 %collective-permute-start.15 = (bf16[11,64,256]{2,1,0:T(8,128)(2,1)S(1)}, bf16[11,64,256]{2,1,0:T(8,128)(2,1)S(1)}, u32[]{:S(2)}, u32[]{:S(2)}) collective-permute-start(bf16[11,64,256]{2,1,0:T(8,128)(2,1)S(1)} %constant_dynamic-update-slice_fusion.6.refs_0_.refs_1_), channel_id=1, source_target_pairs={{0,1},{1,0},{2,3},{3,2},{4,5},{5,4},{6,7},{7,6},{8,9},{9,8},{10,11... | collective-permute-start | bytes 1081352 | tf_op jit(solution)/shard_map/ppermute | solution.py:75
  33.7 1.3 %collective-permute-start.16 = (bf16[64,256]{1,0:T(8,128)(2,1)S(1)}, bf16[64,256]{1,0:T(8,128)(2,1)S(1)}, u32[]{:S(2)}, u32[]{:S(2)}) collective-permute-start(bf16[64,256]{1,0:T(8,128)(2,1)S(1)} %shard_map.69.refs_3_), channel_id=1, source_target_pairs={{0,1},{1,0},{2,3},{3,2},{4,5},{5,4},{6,7},{7,6},{8,9},{9,8},{10,11... | collective-permute-start | bytes 98312 | tf_op jit(solution)/shard_map/ppermute | solution.py:75
  35.0 4.3 %collective-permute-start.17 = (bf16[2,64,256]{2,1,0:T(8,128)(2,1)S(1)}, bf16[2,64,256]{2,1,0:T(8,128)(2,1)S(1)}, u32[]{:S(2)}, u32[]{:S(2)}) collective-permute-start(bf16[2,64,256]{2,1,0:T(8,128)(2,1)S(1)} %pad_maximum_fusion.2), channel_id=1, source_target_pairs={{0,4},{1,3},{2,6},{3,1},{4,0},{5,9},{6,2},{7,11},{8,12},{9,5},{10,... | collective-permute-start | bytes 196616 | tf_op jit(solution)/shard_map/ppermute | solution.py:71
  36.3 6.5 %collective-permute-start.21 = (bf16[2,64,256]{2,1,0:T(8,128)(2,1)S(1)}, bf16[2,64,256]{2,1,0:T(8,128)(2,1)S(1)}, u32[]{:S(2)}, u32[]{:S(2)}) collective-permute-start(bf16[2,64,256]{2,1,0:T(8,128)(2,1)S(1)} %pad_maximum_fusion.2), channel_id=1, source_target_pairs={{0,2},{1,17},{2,0},{3,19},{4,6},{5,21},{6,4},{7,23},{8,10},{9,25},... | collective-permute-start | bytes 196616 | tf_op jit(solution)/shard_map/ppermute | solution.py:71
  37.8 9.4 %collective-permute-start.22 = (bf16[64,256]{1,0:T(8,128)(2,1)S(1)}, bf16[64,256]{1,0:T(8,128)(2,1)S(1)}, u32[]{:S(2)}, u32[]{:S(2)}) collective-permute-start(bf16[64,256]{1,0:T(8,128)(2,1)S(1)} %shard_map.69.refs_3_), channel_id=1, source_target_pairs={{0,18},{1,19},{2,16},{3,17},{4,22},{5,23},{6,20},{7,21},{8,26},{9,... | collective-permute-start | bytes 98312 | tf_op jit(solution)/shard_map/ppermute | solution.py:71
  39.3 5.0 %collective-permute-start.18 = (bf16[2,64,256]{2,1,0:T(8,128)(2,1)S(1)}, bf16[2,64,256]{2,1,0:T(8,128)(2,1)S(1)}, u32[]{:S(2)}, u32[]{:S(2)}) collective-permute-start(bf16[2,64,256]{2,1,0:T(8,128)(2,1)S(1)} %collective-permute-done.17), channel_id=1, source_target_pairs={{0,2},{1,3},{2,0},{3,1},{4,6},{5,7},{6,4},{7,5},{8,10},{9,11},{10,... | collective-permute-start | bytes 196616 | tf_op jit(solution)/shard_map/ppermute | solution.py:71
  40.8 4.7 %collective-permute-start.19 = (bf16[2,64,256]{2,1,0:T(8,128)(2,1)S(1)}, bf16[2,64,256]{2,1,0:T(8,128)(2,1)S(1)}, u32[]{:S(2)}, u32[]{:S(2)}) collective-permute-start(bf16[2,64,256]{2,1,0:T(8,128)(2,1)S(1)} %collective-permute-done.17), channel_id=1, source_target_pairs={{0,16},{1,17},{2,18},{3,19},{4,20},{5,21},{6,22},{7,23},{8,24},{9,... | collective-permute-start | bytes 196616 | tf_op jit(solution)/shard_map/ppermute | solution.py:71
  42.0 5.2 %collective-permute-start.20 = (bf16[2,64,256]{2,1,0:T(8,128)(2,1)S(1)}, bf16[2,64,256]{2,1,0:T(8,128)(2,1)S(1)}, u32[]{:S(2)}, u32[]{:S(2)}) collective-permute-start(bf16[2,64,256]{2,1,0:T(8,128)(2,1)S(1)} %collective-permute-done.17), channel_id=1, source_target_pairs={{0,18},{1,19},{2,16},{3,17},{4,22},{5,23},{6,20},{7,21},{8,26},{9,... | collective-permute-start | bytes 196616 | tf_op jit(solution)/shard_map/ppermute | solution.py:71
  47.2 1.7 %collective-permute-start.23 = (bf16[11,64,256]{2,1,0:T(8,128)(2,1)S(1)}, bf16[11,64,256]{2,1,0:T(8,128)(2,1)S(1)}, u32[]{:S(2)}, u32[]{:S(2)}) collective-permute-start(bf16[11,64,256]{2,1,0:T(8,128)(2,1)S(1)} %constant_dynamic-update-slice_fusion.12.refs_0_), channel_id=1, source_target_pairs={{0,1},{1,0},{2,3},{3,2},{4,5},{5,4},{6,7},{7,6},{8,9},{9,8},{10,11... | collective-permute-start | bytes 1081352 | tf_op jit(solution)/shard_map/ppermute | solution.py:75

commit v9 on v8

--- a/solution.py
+++ b/solution.py
@@ -75,21 +75,21 @@
     return lax.ppermute(value, "gz", [(k, k ^ 1) for k in range(lax.axis_size("gz"))])
 
 
-def exchange(rim, work):
+def exchange(both, work, far_first):
     chips = partners()
     sides = len(pairings(lax.axis_size("gy")))
     plane = chips[-((len(chips) - sides) // (sides + 1)) :]
-    other = swap_cores(rim)
-    both = jnp.stack([rim, other])
+    rim = both[0]
     side = swap(both, (chips[0], chips[sides - 1]))
     alone = [swap(rim, (plane[-1], plane[-1]))] if len(plane) % 2 else []
     own = [
         swap(both, (plane[t], plane[t + 1])) for t in range(0, len(plane) - len(plane) % 2, 2)
     ]
-    passed = [swap(side, (chip, chip)) for chip in plane[::-1]]
-    own[0], *results = work(own[0])
-    received = jnp.concatenate([side] + passed[::-1] + own + [panel[None] for panel in alone])
-    return (received, swap_cores(received), other, rim), results
+    step = -1 if far_first else 1
+    passed = [swap(side, (chip, chip)) for chip in plane[::step]]
+    passed[0], *results = work(passed[0])
+    received = jnp.concatenate([side] + passed[::step] + own + [panel[None] for panel in alone])
+    return received, results
 
 
 def source_index(slots, live, count, rim_count):
@@ -112,14 +112,21 @@
     if chips % 2:
         holder = jnp.where(number == chips - 1, target, holder)
         panel = jnp.where(number == chips - 1, chips - 1, panel)
-    panel = panel + jnp.where(holder == core, 0, chips)
     here = (x_rank == 0) & (y_rank == 0) & (flip == 0)
-    panel = jnp.where(here, 2 * chips + jnp.where(target == core, 1, 0), panel)
-    zero = (2 * chips + 2) * rim_count
     place = lax.broadcasted_iota(jnp.int32, slots.shape, 0)
     used = place < live
-    far = jnp.where(x_in & y_in & used, panel * rim_count + r, zero)
-    return jnp.where(place < NEAR, jnp.where(used, slots, count), far)
+    there = x_in & y_in & used
+    all_rims = jnp.where(
+        here,
+        2 * chips + jnp.where(target == core, 1, 0),
+        panel + jnp.where(holder == core, 0, chips),
+    )
+    far = jnp.where(there, all_rims * rim_count + r, (2 * chips + 2) * rim_count)
+    index = jnp.where(place < NEAR, jnp.where(used, slots, count), far)
+    held = jnp.where(here, chips, panel) * rim_count + r
+    holder = jnp.where(here, target, holder)
+    zero = (chips + 1) * rim_count
+    return index, *(jnp.where(there & (holder == at), held, zero) for at in (core, 1 - core))
 
 
 def left_half():
@@ -136,23 +143,14 @@
     store[at + 1] = jnp.where(left_half(), turned, pair)
 
 
-def each_rim(rims, place_pair):
-    mine_ref, others_ref, other_ref, own_ref = rims
-    panels, _, rim = mine_ref.shape
-    rim_count = rim // PB
-
-    for panel in range(panels):
+def each_pair(panels_ref, first, place_pair):
+    rim = panels_ref.shape[2]
+    for panel in range(panels_ref.shape[0]):
         for t in range(rim // LANES):
-            cut = slice(t * LANES, (t + 1) * LANES)
-            at = panel * rim_count + 2 * t
-            place_pair(mine_ref[panel, :, cut], at)
-            place_pair(others_ref[panel, :, cut], at + panels * rim_count)
-
-    for t in range(rim // LANES):
-        cut = slice(t * LANES, (t + 1) * LANES)
-        at = 2 * panels * rim_count + 2 * t
-        place_pair(other_ref[:, cut], at)
-        place_pair(own_ref[:, cut], at + rim_count)
+            place_pair(
+                panels_ref[panel, :, t * LANES : (t + 1) * LANES],
+                first + panel * (rim // PB) + 2 * t,
+            )
 
 
 def product(first, second, tile):
@@ -177,7 +175,7 @@
 
 def fold_kernel(
     _, raw_hbm, slot_hbm, live_hbm, scale_hbm, time_hbm,
-    __, tile_out, index_out, time_out,
+    __, tile_out, edge_out, index_out, mine_out, theirs_out, time_out,
     raw_ref, slot_ref, live_ref, scale_ref, time_ref, arrived, *, rim_count,
 ):
     count = slot_ref.shape[1]
@@ -201,14 +199,19 @@
     eye = [lax.broadcasted_iota(jnp.int32, (FEATURES, FEATURES), n) for n in range(2)]
     column = jnp.where(eye[0] == eye[1], time_ref[...], 0.0)
     time_out[...] = jnp.sum(column, axis=1, keepdims=True)
-    index_out[...] = source_index(slot_ref[...], live_ref[...], count, rim_count)
+    indices = source_index(slot_ref[...], live_ref[...], count, rim_count)
+    for out, index in zip((index_out, mine_out, theirs_out), indices):
+        out[...] = index
     for p in range(PARTS):
         fetches[small + p].wait()
         for b in range(p * rows // PB, (p + 1) * rows // PB):
             for k in range(0, scale_ref.shape[0], 2):
                 at = pl.ds(b * PB, PB), pl.ds(k * PB, LANES)
                 scale = jnp.where(half, scale_ref[k, b], scale_ref[k + 1, b])
-                tile_out[at] = (raw_ref[at].astype(jnp.float32) * scale).astype(tile_out.dtype)
+                scaled = (raw_ref[at].astype(jnp.float32) * scale).astype(tile_out.dtype)
+                tile_out[at] = scaled
+                if b < rim_count and k >= NEAR:
+                    edge_out[pl.ds(b * PB, PB), pl.ds((k - NEAR) * PB, LANES)] = scaled
 
 
 def near_kernel(index_ref, value_ref, tile_ref, near_out, store):
@@ -228,45 +231,78 @@
     store[store.shape[0] - 1] = jnp.zeros(store.shape[1:], store.dtype)
 
 
-def rim_kernel(index_ref, *refs):
-    rims, (tile_ref, near_ref, rim_out, store) = refs[:4], refs[4:]
-
+def part_kernel(
+    index_ref, mine_ref, theirs_ref, received_ref, both_ref, tile_ref, value_ref, edge_ref,
+    part_out, store,
+):
     def keep(pair, number):
         store[number // 2] = pair
 
-    each_rim(rims, keep)
+    panels, _, rim = received_ref.shape
+    each_pair(received_ref, 0, keep)
+    each_pair(both_ref.at[pl.ds(0, 1)], panels * (rim // PB), keep)
     clear_last(store)
 
-    def sources(row):
+    def own_pair(number):
+        return value_ref[:, pl.ds(pl.multiple_of((number >> 1) * LANES, LANES), LANES)]
+
+    def far_pair(number):
+        return store[number >> 1]
+
+    def sources(fetch, blank, index_ref, first, row):
         parts = []
-        for k in range(NEAR, 2 * NEAR, 2):
+        for k in range(first, first + NEAR, 2):
             halves = []
             for side in range(2):
                 number = index_ref[k + side, row]
-                pair = store[number >> 1]
+                if blank is None:
+                    pair = fetch(number)
+                else:
+                    pair = fetch(jnp.minimum(number, blank - 1))
+                    pair = jnp.where(number < blank, pair, jnp.zeros_like(pair))
                 halves.append(jnp.where((number & 1) == side, pair, turn(pair)))
             parts.append(jnp.where(left_half(), halves[0], halves[1]))
         return jnp.concatenate(parts, axis=1)
 
-    for t in range(rim_out.shape[1] // LANES):
+    count = value_ref.shape[1] // PB
+    for t in range(rim // LANES):
         at = pl.ds(t * LANES, LANES)
-        far = product(sources(2 * t), sources(2 * t + 1), tile_ref[at, NEAR * PB :])
-        rim_out[:, at] = (near_ref[:, at] + far).astype(rim_out.dtype)
+        rows = (2 * t, 2 * t + 1)
+        near = product(
+            *(sources(own_pair, count, index_ref, 0, row) for row in rows), tile_ref[at, : NEAR * PB]
+        )
+        far = product(
+            *(sources(far_pair, None, mine_ref, NEAR, row) for row in rows),
+            tile_ref[at, NEAR * PB :],
+        )
+        part_out[0, :, at] = near + far
+        part_out[1, :, at] = product(
+            *(sources(far_pair, None, theirs_ref, NEAR, row) for row in rows), edge_ref[at, :]
+        )
 
 
 def far_kernel(step, last, index_ref, *refs):
     if not last:
         refs = refs[1:]
-    rims, (tile_ref, near_ref, times_ref, total_ref) = refs[:4], refs[4:8]
+    received_ref, others_ref, both_ref, tile_ref, near_ref, times_ref, total_ref = refs[:7]
     if last:
-        result_hbm, store, total_out, sent = refs[8:]
+        result_hbm, store, total_out, sent = refs[7:]
     else:
-        _, total_out, value_out, store, *fetching = refs[8:]
+        _, total_out, value_out, store, *fetching = refs[7:]
         if fetching:
             features_hbm, (total_ref, arrived) = total_ref, fetching
             fetch = pltpu.make_async_copy(features_hbm, total_ref, arrived)
             fetch.start()
-    each_rim(rims, lambda pair, number: spread(pair, store, number))
+    panels, _, rim = received_ref.shape
+    rim_count = rim // PB
+
+    def keep(pair, number):
+        spread(pair, store, number)
+
+    each_pair(received_ref, 0, keep)
+    each_pair(others_ref, panels * rim_count, keep)
+    each_pair(both_ref.at[pl.ds(1, 1)], 2 * panels * rim_count, keep)
+    each_pair(both_ref.at[pl.ds(0, 1)], (2 * panels + 1) * rim_count, keep)
     clear_last(store)
     if not last and fetching:
         fetch.wait()
@@ -297,8 +333,7 @@
         send.wait()
 
 
-def call(kernel, results, scratch, flops, index, *arrays, fetched=(), through=None, to_hbm=False):
-    scalars = () if index is None else (index,)
+def call(kernel, results, scratch, flops, scalars, *arrays, fetched=(), through=None, to_hbm=False):
     handed = () if through is None else (through,)
     out_shape = tuple(jax.ShapeDtypeStruct(x.shape, x.dtype) for x in handed) + results
     anywhere, vmem = pl.BlockSpec(memory_space=pl.ANY), pl.BlockSpec(memory_space=pltpu.VMEM)
@@ -324,29 +359,43 @@
     slot_count = scales.shape[3]
     rim_count = max(1, count // 8)
     points = count * PB
+    rim_points = rim_count * PB
     value = features.reshape(FEATURES, points)
-    rim = value[:, : rim_count * PB]
+    rim = value[:, :rim_points]
+    both = jnp.stack([rim, swap_cores(rim)])
     scales = scales.reshape(count, slot_count).T
     slots = slots.reshape(count, slot_count).T
-    rims_held = 2 * len(partners()) + 2
+    times_row = times.reshape(1, FEATURES)
+    chips = len(partners())
     half = FEATURES * points * width
 
     def blocks(number):
         return pltpu.VMEM((number, FEATURES, LANES), jnp.bfloat16)
 
     own_store = blocks(count + 1)
-    far_store = blocks(rims_held * rim_count + 1)
-    pair_store = blocks(rims_held * rim_count // 2 + 1)
+    far_store = blocks((2 * chips + 2) * rim_count + 1)
+    part_store = blocks((chips + 1) * rim_count // 2 + 1)
     image_shape = jax.ShapeDtypeStruct(value.shape, jnp.float32)
     value_shape = jax.ShapeDtypeStruct(value.shape, jnp.bfloat16)
-    rim_shape = jax.ShapeDtypeStruct(rim.shape, jnp.bfloat16)
+    part_shape = jax.ShapeDtypeStruct(both.shape, jnp.float32)
     tile_shape = jax.ShapeDtypeStruct((points, width), jnp.bfloat16)
+    edge_shape = jax.ShapeDtypeStruct((rim_points, width - NEAR * PB), jnp.bfloat16)
     index_shape = jax.ShapeDtypeStruct(slots.shape, jnp.int32)
+    time_shape = jax.ShapeDtypeStruct((FEATURES, 1), jnp.float32)
+
+    def image(value, scaled, index):
+        return call(near_kernel, (image_shape,), [own_store], half, (index,), value, scaled)[0]
 
     def fold(through):
+        through, scaled, edge, index, mine, theirs, times = fold_call(through)
+        edge, theirs = swap_cores(edge), swap_cores(theirs)
+        through, edge, theirs = lax.optimization_barrier((through, edge, theirs))
+        return through, scaled, edge, index, mine, theirs, times
+
+    def fold_call(through):
         return call(
             functools.partial(fold_kernel, rim_count=rim_count),
-            (tile_shape, index_shape, jax.ShapeDtypeStruct((FEATURES, 1), jnp.float32)),
+            (tile_shape, edge_shape, index_shape, index_shape, index_shape, time_shape),
             [
                 pltpu.VMEM((points, width), jnp.bfloat16),
                 pltpu.VMEM(slots.shape, jnp.int32),
@@ -356,41 +405,51 @@
                 pltpu.SemaphoreType.DMA((PARTS + 4,)),
             ],
             half,
-            None,
+            (),
             fetched=(
                 tiles.reshape(points, width),
                 slots,
                 live.reshape(1, count),
                 scales,
-                times.reshape(1, FEATURES),
+                times_row,
             ),
             through=through,
         )
 
-    rims, (scaled, index, times) = exchange(rim, fold)
-    (near,) = call(near_kernel, (image_shape,), [own_store], half, index, value, scaled)
+    received, (scaled, edge, index, mine, theirs, times) = exchange(both, fold, True)
     total = value
     for step in range(1, TERMS):
-        arrays = (index, *rims, scaled, near)
-        (rim,) = call(rim_kernel, (rim_shape,), [pair_store], half // 8, *arrays)
+        others = swap_cores(received)
+        (part,) = call(
+            part_kernel,
+            (part_shape,),
+            [part_store],
+            half // 4,
+            (index, mine, theirs),
+            *(received, both, scaled, value, edge),
+        )
 
         def rest(through):
             begun = step > 1
             fetch = [pltpu.VMEM(value.shape, jnp.bfloat16), pltpu.SemaphoreType.DMA]
-            return call(
+            through, total_now, value_now = call(
                 functools.partial(far_kernel, step, False),
                 (image_shape, value_shape),
                 [far_store] + ([] if begun else fetch),
                 half,
                 *arrays,
-                times,
                 *([total] if begun else []),
-                fetched=() if begun else (value,),
+                fetched=() if begun else (features.reshape(total.shape),),
                 through=through,
             )
-
-        rims, (total, value) = exchange(rim, rest)
-        (near,) = call(near_kernel, (image_shape,), [own_store], half, index, value, scaled)
+            return through, total_now, value_now
+
+        near = image(value, scaled, index)
+        added, others, near = lax.optimization_barrier((swap_cores(part), others, near))
+        arrays = ((index,), received, others, both, scaled, near, times)
+        both = (part + added[::-1]).astype(jnp.bfloat16)
+        received, (total, value) = exchange(both, rest, False)
+    near = image(value, scaled, index)
     (out,) = call(
         functools.partial(far_kernel, TERMS, True),
         (value_shape,),
@@ -400,8 +459,10 @@
             pltpu.SemaphoreType.DMA((PARTS,)),
         ],
         half,
-        index,
-        *rims,
+        (index,),
+        received,
+        swap_cores(received),
+        both,
         scaled,
         near,
         times,

time: 51.3 us -> 50.4 us (0.982)
  waiting for transfers between devices: 11.4 us -> 8.71 us
  starting transfers between devices: 25.4 us -> 26.8 us
    ppermute x6 -> x8, waiting for transfers between devices: 4.38 us -> 2.15 us  [swap_cores(): lax.ppermute(value, 'gz', [(k, k ^ 1) for k in range(lax.axis_size('gz'))])]
    ppermute x6 -> x8, starting transfers between devices: 1.07 us -> 2.35 us  [swap_cores(): lax.ppermute(value, 'gz', [(k, k ^ 1) for k in range(lax.axis_size('gz'))])]
  transfers between devices with their start and end apart: 24 -> 26, of which waited for: 12 -> 10; matrix products, arithmetic and copies ran while one was open for 0% -> 0% of each run, Pallas kernels for 17% -> 22%
where the time goes in v9:
time: 50.4 us; the launch traced here: 50.2 us
  starting transfers between devices  26.8 us (53%)
  Pallas kernels  13.4 us (27%)
  waiting for transfers between devices  8.71 us (17%)
  local copies, waits for them, and re-layouts  0.95 us (2%)
    ppermute x18, starting transfers between devices, swap(): return lax.ppermute(value, AXES, pairs)  24.5 us
    pallas_call x9, Pallas kernels, call(): pl.pallas_call(kernel, out_shape=out_shape, in_specs=[pl.BlockSpec(memory...  13.4 us
    ppermute x18, waiting for transfers between devices, swap(): return lax.ppermute(value, AXES, pairs)  6.56 us
    ppermute x8, starting transfers between devices, swap_cores(): lax.ppermute(value, 'gz', [(k, k ^ 1) for k in range(lax.axis_size('gz'))])  2.35 us
    ppermute x8, waiting for transfers between devices, swap_cores(): lax.ppermute(value, 'gz', [(k, k ^ 1) for k in range(lax.axis_size('gz'))])  2.15 us
  transfers between devices with their start and end apart: 26, of which 10 were waited for; matrix products, arithmetic and copies ran while one was open for 0% of the time, Pallas kernels for 22%

profile of v9, /device:TPU:0, one launch (start us, length us, event | category | flops | bytes accessed | tf_op | source)
XLA Modules:
  0.0 50.2 jit_solution(5566527205541051582)
XLA Ops:
  0.0 0.0 copy-start
  0.0 0.8 %slice_bitcast_fusion.2 = (bf16[1,64,256]{2,1,0:T(8,128)(2,1)S(1)}, bf16[64,256]{1,0:T(8,128)(2,1)S(1)}) fusion(bf16[64,2048]{1,0:T(8,128)(2,1)} %bitcast.24), kind=kLoop, calls=%fused_computation.23 | loop fusion | bytes 98304 | tf_op jit(solution)/shard_map/stack | solution.py:365
  0.8 0.5 collective-permute-start
  1.3 0.9 %collective-permute-done = bf16[64,256]{1,0:T(8,128)(2,1)S(1)} collective-permute-done((bf16[64,256]{1,0:T(8,128)(2,1)S(1)}, bf16[64,256]{1,0:T(8,128)(2,1)S(1)}, u32[]{:S(2)}, u32[]{:S(2)}) %collective-permute-start) | collective-permute-done | bytes 32800 | tf_op jit(solution)/shard_map/ppermute | solution.py:75
  2.2 3.0 %collective-permute-start.1 = (bf16[2,64,256]{2,1,0:T(8,128)(2,1)S(1)}, bf16[2,64,256]{2,1,0:T(8,128)(2,1)S(1)}, u32[]{:S(2)}, u32[]{:S(2)}) collective-permute-start(bf16[2,64,256]{2,1,0:T(8,128)(2,1)S(1)} %pad_maximum_fusion.both_ref.refs_3_), channel_id=1, source_target_pairs={{0,4},{1,3},{2,6},{3,1},{4,0},{5,9},{6,2},{7,11},{8,12},{9,5},{10,... | collective-permute-start | bytes 196616 | tf_op jit(solution)/shard_map/ppermute | solution.py:71
  5.1 2.4 %collective-permute-start.8 = (bf16[64,256]{1,0:T(8,128)(2,1)S(1)}, bf16[64,256]{1,0:T(8,128)(2,1)S(1)}, u32[]{:S(2)}, u32[]{:S(2)}) collective-permute-start(bf16[64,256]{1,0:T(8,128)(2,1)S(1)} %get-tuple-element.50), channel_id=1, source_target_pairs={{0,18},{1,19},{2,16},{3,17},{4,22},{5,23},{6,20},{7,21},{8,26},{9,... | collective-permute-start | bytes 98312 | tf_op jit(solution)/shard_map/ppermute | solution.py:71
  7.6 0.5 %collective-permute-start.7 = (bf16[2,64,256]{2,1,0:T(8,128)(2,1)S(1)}, bf16[2,64,256]{2,1,0:T(8,128)(2,1)S(1)}, u32[]{:S(2)}, u32[]{:S(2)}) collective-permute-start(bf16[2,64,256]{2,1,0:T(8,128)(2,1)S(1)} %pad_maximum_fusion.both_ref.refs_3_), channel_id=1, source_target_pairs={{0,2},{1,17},{2,0},{3,19},{4,6},{5,21},{6,4},{7,23},{8,10},{9,25},... | collective-permute-start | bytes 196616 | tf_op jit(solution)/shard_map/ppermute | solution.py:71
  8.1 0.0 collective-permute-done.1
  8.1 2.1 %collective-permute-start.2 = (bf16[2,64,256]{2,1,0:T(8,128)(2,1)S(1)}, bf16[2,64,256]{2,1,0:T(8,128)(2,1)S(1)}, u32[]{:S(2)}, u32[]{:S(2)}) collective-permute-start(bf16[2,64,256]{2,1,0:T(8,128)(2,1)S(1)} %collective-permute-done.1), channel_id=1, source_target_pairs={{0,18},{1,19},{2,16},{3,17},{4,22},{5,23},{6,20},{7,21},{8,26},{9,... | collective-permute-start | bytes 196616 | tf_op jit(solution)/shard_map/ppermute | solution.py:71
  10.3 0.5 %collective-permute-start.5 = (bf16[2,64,256]{2,1,0:T(8,128)(2,1)S(1)}, bf16[2,64,256]{2,1,0:T(8,128)(2,1)S(1)}, u32[]{:S(2)}, u32[]{:S(2)}) collective-permute-start(bf16[2,64,256]{2,1,0:T(8,128)(2,1)S(1)} %collective-permute-done.1), channel_id=1, source_target_pairs={{0,2},{1,3},{2,0},{3,1},{4,6},{5,7},{6,4},{7,5},{8,10},{9,11},{10,... | collective-permute-start | bytes 196616 | tf_op jit(solution)/shard_map/ppermute | solution.py:71
  10.8 0.8 %collective-permute-start.6 = (bf16[2,64,256]{2,1,0:T(8,128)(2,1)S(1)}, bf16[2,64,256]{2,1,0:T(8,128)(2,1)S(1)}, u32[]{:S(2)}, u32[]{:S(2)}) collective-permute-start(bf16[2,64,256]{2,1,0:T(8,128)(2,1)S(1)} %collective-permute-done.1), channel_id=1, source_target_pairs={{0,16},{1,17},{2,18},{3,19},{4,20},{5,21},{6,22},{7,23},{8,24},{9,... | collective-permute-start | bytes 196616 | tf_op jit(solution)/shard_map/ppermute | solution.py:71
  11.6 1.7 %collective-permute-done.2._ = bf16[2,64,256]{2,1,0:T(8,128)(2,1)S(1)} collective-permute-done((bf16[2,64,256]{2,1,0:T(8,128)(2,1)S(1)}, bf16[2,64,256]{2,1,0:T(8,128)(2,1)S(1)}, u32[]{:S(2)}, u32[]{:S(2)}) %collective-permute-start.2) | collective-permute-done | bytes 65568 | tf_op jit(solution)/shard_map/ppermute | solution.py:71
  13.3 1.8 %shard_map.64 = (bf16[2,64,256]{2,1,0:T(8,128)(2,1)S(1)}, bf16[2048,512]{1,0:T(8,128)(2,1)S(1)}, bf16[256,256]{1,0:T(8,128)(2,1)S(1)}, s32[8,32]{1,0:T(8,128)S(1...) custom-call(bf16[2,64,256]{2,1,0:T(8,128)(2,1)S(1)} %collective-permute-, ...), custom_call_target="tpu_custom_call", output_to_operand_aliasing={{0}: (0, {})} | custom-call | flops 67108864 | bytes 1048576 | tf_op jit(solution)/shard_map/pallas_call | solution.py:342
  15.1 0.1 collective-permute-start.3
  15.1 0.0 collective-permute-done.5
  15.1 0.5 collective-permute-start.4
  15.6 0.0 collective-permute-done.6
  15.7 0.8 %collective-permute-done.4.theirs_ref = s32[8,32]{1,0:T(8,128)S(1)} collective-permute-done((s32[8,32]{1,0:T(8,128)S(1)}, s32[8,32]{1,0:T(8,128)S(1)}, u32[]{:S(2)}, u32[]{:S(2)}) %collective-permute-start.4) | collective-permute-done | bytes 1056 | tf_op jit(solution)/shard_map/ppermute | solution.py:75
  16.5 0.0 collective-permute-done.3.edge_ref
  16.5 0.0 collective-permute-done.7
  16.5 0.0 collective-permute-done.8
  16.5 0.4 collective-permute-start.10
  16.9 0.0 copy-done
  16.9 1.2 %shard_map.65 = f32[2,64,256]{2,1,0:T(8,128)S(1)} custom-call(s32[8,32]{1,0:T(8,128)S(1)} %get-tuple-element.27.index_ref, s32[8,32]{1,0:T(8,128)S(1)} %get-tuple-element.28.mine_ref, s32[8,32]{1,0:T(8,128)S(1)} %collective-permute-done.4.theirs_ref, bf16[11,64,256]{2,1,0:T(8,128)(2,1)S(1)} %constant_dynamic-update-slice_fusion.received_ref.refs_1_, ...), custom_call_target="tpu_custom_call" | custom-call | flops 16777216 | bytes 262144 | tf_op jit(solution)/shard_map/pallas_call | solution.py:342
  18.1 0.2 collective-permute-start.9
  18.4 1.2 %shard_map.66.refs_5_ = f32[64,2048]{1,0:T(8,128)S(1)} custom-call(s32[8,32]{1,0:T(8,128)S(1)} %get-tuple-element.27.index_ref, bf16[64,2048]{1,0:T(8,128)(2,1)S(1)} %bitcast.27, bf16[2048,512]{1,0:T(8,128)(2,1)S(1)} %get-tuple-element.34.tile_ref.refs_4_.refs_3_), custom_call_target="tpu_custom_call" | custom-call | flops 67108864 | bytes 1048576 | tf_op jit(solution)/shard_map/pallas_call | solution.py:342
  19.6 0.0 collective-permute-done.9
  19.6 0.0 collective-permute-done.10.refs_2_
  19.6 1.4 %collective-permute-start.11 = (bf16[2,64,256]{2,1,0:T(8,128)(2,1)S(1)}, bf16[2,64,256]{2,1,0:T(8,128)(2,1)S(1)}, u32[]{:S(2)}, u32[]{:S(2)}) collective-permute-start(bf16[2,64,256]{2,1,0:T(8,128)(2,1)S(1)} %add_convert_fusion.1.both_ref.refs_3_), channel_id=1, source_target_pairs={{0,4},{1,3},{2,6},{3,1},{4,0},{5,9},{6,2},{7,11},{8,12},{9,5},{10,... | collective-permute-start | bytes 196616 | tf_op jit(solution)/shard_map/ppermute | solution.py:71
  21.0 1.5 %collective-permute-start.15 = (bf16[2,64,256]{2,1,0:T(8,128)(2,1)S(1)}, bf16[2,64,256]{2,1,0:T(8,128)(2,1)S(1)}, u32[]{:S(2)}, u32[]{:S(2)}) collective-permute-start(bf16[2,64,256]{2,1,0:T(8,128)(2,1)S(1)} %add_convert_fusion.1.both_ref.refs_3_), channel_id=1, source_target_pairs={{0,2},{1,17},{2,0},{3,19},{4,6},{5,21},{6,4},{7,23},{8,10},{9,25},... | collective-permute-start | bytes 196616 | tf_op jit(solution)/shard_map/ppermute | solution.py:71
  22.6 1.4 %collective-permute-start.16 = (bf16[64,256]{1,0:T(8,128)(2,1)S(1)}, bf16[64,256]{1,0:T(8,128)(2,1)S(1)}, u32[]{:S(2)}, u32[]{:S(2)}) collective-permute-start(bf16[64,256]{1,0:T(8,128)(2,1)S(1)} %slice_bitcast_fusion.1), channel_id=1, source_target_pairs={{0,18},{1,19},{2,16},{3,17},{4,22},{5,23},{6,20},{7,21},{8,26},{9,... | collective-permute-start | bytes 98312 | tf_op jit(solution)/shard_map/ppermute | solution.py:71
  24.0 0.0 collective-permute-done.11
  24.0 1.5 %collective-permute-start.12 = (bf16[2,64,256]{2,1,0:T(8,128)(2,1)S(1)}, bf16[2,64,256]{2,1,0:T(8,128)(2,1)S(1)}, u32[]{:S(2)}, u32[]{:S(2)}) collective-permute-start(bf16[2,64,256]{2,1,0:T(8,128)(2,1)S(1)} %collective-permute-done.11), channel_id=1, source_target_pairs={{0,2},{1,3},{2,0},{3,1},{4,6},{5,7},{6,4},{7,5},{8,10},{9,11},{10,... | collective-permute-start | bytes 196616 | tf_op jit(solution)/shard_map/ppermute | solution.py:71
  25.5 1.2 %collective-permute-start.13 = (bf16[2,64,256]{2,1,0:T(8,128)(2,1)S(1)}, bf16[2,64,256]{2,1,0:T(8,128)(2,1)S(1)}, u32[]{:S(2)}, u32[]{:S(2)}) collective-permute-start(bf16[2,64,256]{2,1,0:T(8,128)(2,1)S(1)} %collective-permute-done.11), channel_id=1, source_target_pairs={{0,16},{1,17},{2,18},{3,19},{4,20},{5,21},{6,22},{7,23},{8,24},{9,... | collective-permute-start | bytes 196616 | tf_op jit(solution)/shard_map/ppermute | solution.py:71
  26.7 0.8 %collective-permute-start.14 = (bf16[2,64,256]{2,1,0:T(8,128)(2,1)S(1)}, bf16[2,64,256]{2,1,0:T(8,128)(2,1)S(1)}, u32[]{:S(2)}, u32[]{:S(2)}) collective-permute-start(bf16[2,64,256]{2,1,0:T(8,128)(2,1)S(1)} %collective-permute-done.11), channel_id=1, source_target_pairs={{0,18},{1,19},{2,16},{3,17},{4,22},{5,23},{6,20},{7,21},{8,26},{9,... | collective-permute-start | bytes 196616 | tf_op jit(solution)/shard_map/ppermute | solution.py:71
  27.5 0.8 %collective-permute-done.12.refs_0_ = bf16[2,64,256]{2,1,0:T(8,128)(2,1)S(1)} collective-permute-done((bf16[2,64,256]{2,1,0:T(8,128)(2,1)S(1)}, bf16[2,64,256]{2,1,0:T(8,128)(2,1)S(1)}, u32[]{:S(2)}, u32[]{:S(2)}) %collective-permute-start.12) | collective-permute-done | bytes 65568 | tf_op jit(solution)/shard_map/ppermute | solution.py:71
  28.2 2.1 %shard_map.67 = (bf16[2,64,256]{2,1,0:T(8,128)(2,1)S(1)}, f32[64,2048]{1,0:T(8,128)S(1)}, bf16[64,2048]{1,0:T(8,128)(2,1)S(1)}) custom-call(s32[8,32]{1,0:T(8,128)S(1)} %get-tuple-element.27.index_ref, bf16[2,64,256]{2,1,0:T(8,128)(2,1)S(1)} %collective-permute-done.12.refs_0_, ...), custom_call_target="tpu_custom_call", output_to_operand_aliasing={{0}: (1, {})} | custom-call | flops 67108864 | bytes 1048576 | tf_op jit(solution)/shard_map/pallas_call | solution.py:342
  30.4 0.1 collective-permute-done.13
  30.4 1.4 %collective-permute-done.14 = bf16[2,64,256]{2,1,0:T(8,128)(2,1)S(1)} collective-permute-done((bf16[2,64,256]{2,1,0:T(8,128)(2,1)S(1)}, bf16[2,64,256]{2,1,0:T(8,128)(2,1)S(1)}, u32[]{:S(2)}, u32[]{:S(2)}) %collective-permute-start.14) | collective-permute-done | bytes 65568 | tf_op jit(solution)/shard_map/ppermute | solution.py:71
  31.9 0.0 collective-permute-done.15
  31.9 0.0 collective-permute-done.16
  31.9 0.1 collective-permute-start.18
  32.0 1.2 %shard_map.68 = f32[2,64,256]{2,1,0:T(8,128)S(1)} custom-call(s32[8,32]{1,0:T(8,128)S(1)} %get-tuple-element.27.index_ref, s32[8,32]{1,0:T(8,128)S(1)} %get-tuple-element.28.mine_ref, s32[8,32]{1,0:T(8,128)S(1)} %collective-permute-done.4.theirs_ref, bf16[11,64,256]{2,1,0:T(8,128)(2,1)S(1)} %constant_dynamic-update-slice_fusion.6.received_ref.refs_1_, ...), custom_call_target="tpu_custom_call" | custom-call | flops 16777216 | bytes 262144 | tf_op jit(solution)/shard_map/pallas_call | solution.py:342
  33.2 0.6 %collective-permute-start.17 = (f32[2,64,256]{2,1,0:T(8,128)S(1)}, f32[2,64,256]{2,1,0:T(8,128)S(1)}, u32[]{:S(2)}, u32[]{:S(2)}) collective-permute-start(f32[2,64,256]{2,1,0:T(8,128)S(1)} %shard_map.68), channel_id=1, source_target_pairs={{0,1},{1,0},{2,3},{3,2},{4,5},{5,4},{6,7},{7,6},{8,9},{9,8},{10,11... | collective-permute-start | bytes 393224 | tf_op jit(solution)/shard_map/ppermute | solution.py:75
  33.7 1.2 %shard_map.69.refs_5_ = f32[64,2048]{1,0:T(8,128)S(1)} custom-call(s32[8,32]{1,0:T(8,128)S(1)} %get-tuple-element.27.index_ref, bf16[64,2048]{1,0:T(8,128)(2,1)S(1)} %get-tuple-element.41.value_ref, bf16[2048,512]{1,0:T(8,128)(2,1)S(1)} %get-tuple-element.34.tile_ref.refs_4_.refs_3_), custom_call_target="tpu_custom_call" | custom-call | flops 67108864 | bytes 1048576 | tf_op jit(solution)/shard_map/pallas_call | solution.py:342
  34.9 0.0 collective-permute-done.17
  35.0 0.0 collective-permute-done.18.refs_2_
  35.0 1.6 %collective-permute-start.19 = (bf16[2,64,256]{2,1,0:T(8,128)(2,1)S(1)}, bf16[2,64,256]{2,1,0:T(8,128)(2,1)S(1)}, u32[]{:S(2)}, u32[]{:S(2)}) collective-permute-start(bf16[2,64,256]{2,1,0:T(8,128)(2,1)S(1)} %add_convert_fusion.refs_2_), channel_id=1, source_target_pairs={{0,4},{1,3},{2,6},{3,1},{4,0},{5,9},{6,2},{7,11},{8,12},{9,5},{10,... | collective-permute-start | bytes 196616 | tf_op jit(solution)/shard_map/ppermute | solution.py:71
  36.6 0.5 %collective-permute-start.23 = (bf16[2,64,256]{2,1,0:T(8,128)(2,1)S(1)}, bf16[2,64,256]{2,1,0:T(8,128)(2,1)S(1)}, u32[]{:S(2)}, u32[]{:S(2)}) collective-permute-start(bf16[2,64,256]{2,1,0:T(8,128)(2,1)S(1)} %add_convert_fusion.refs_2_), channel_id=1, source_target_pairs={{0,2},{1,17},{2,0},{3,19},{4,6},{5,21},{6,4},{7,23},{8,10},{9,25},... | collective-permute-start | bytes 196616 | tf_op jit(solution)/shard_map/ppermute | solution.py:71
  37.2 1.5 %collective-permute-start.24 = (bf16[64,256]{1,0:T(8,128)(2,1)S(1)}, bf16[64,256]{1,0:T(8,128)(2,1)S(1)}, u32[]{:S(2)}, u32[]{:S(2)}) collective-permute-start(bf16[64,256]{1,0:T(8,128)(2,1)S(1)} %slice_bitcast_fusion), channel_id=1, source_target_pairs={{0,18},{1,19},{2,16},{3,17},{4,22},{5,23},{6,20},{7,21},{8,26},{9,... | collective-permute-start | bytes 98312 | tf_op jit(solution)/shard_map/ppermute | solution.py:71
  38.7 0.6 %collective-permute-done.19 = bf16[2,64,256]{2,1,0:T(8,128)(2,1)S(1)} collective-permute-done((bf16[2,64,256]{2,1,0:T(8,128)(2,1)S(1)}, bf16[2,64,256]{2,1,0:T(8,128)(2,1)S(1)}, u32[]{:S(2)}, u32[]{:S(2)}) %collective-permute-start.19) | collective-permute-done | bytes 65568 | tf_op jit(solution)/shard_map/ppermute | solution.py:71
  39.3 0.7 %collective-permute-start.20 = (bf16[2,64,256]{2,1,0:T(8,128)(2,1)S(1)}, bf16[2,64,256]{2,1,0:T(8,128)(2,1)S(1)}, u32[]{:S(2)}, u32[]{:S(2)}) collective-permute-start(bf16[2,64,256]{2,1,0:T(8,128)(2,1)S(1)} %collective-permute-done.19), channel_id=1, source_target_pairs={{0,2},{1,3},{2,0},{3,1},{4,6},{5,7},{6,4},{7,5},{8,10},{9,11},{10,... | collective-permute-start | bytes 196616 | tf_op jit(solution)/shard_map/ppermute | solution.py:71
  40.1 1.1 %collective-permute-start.21 = (bf16[2,64,256]{2,1,0:T(8,128)(2,1)S(1)}, bf16[2,64,256]{2,1,0:T(8,128)(2,1)S(1)}, u32[]{:S(2)}, u32[]{:S(2)}) collective-permute-start(bf16[2,64,256]{2,1,0:T(8,128)(2,1)S(1)} %collective-permute-done.19), channel_id=1, source_target_pairs={{0,16},{1,17},{2,18},{3,19},{4,20},{5,21},{6,22},{7,23},{8,24},{9,... | collective-permute-start | bytes 196616 | tf_op jit(solution)/shard_map/ppermute | solution.py:71
  41.2 1.7 %collective-permute-start.22 = (bf16[2,64,256]{2,1,0:T(8,128)(2,1)S(1)}, bf16[2,64,256]{2,1,0:T(8,128)(2,1)S(1)}, u32[]{:S(2)}, u32[]{:S(2)}) collective-permute-start(bf16[2,64,256]{2,1,0:T(8,128)(2,1)S(1)} %collective-permute-done.19), channel_id=1, source_target_pairs={{0,18},{1,19},{2,16},{3,17},{4,22},{5,23},{6,20},{7,21},{8,26},{9,... | collective-permute-start | bytes 196616 | tf_op jit(solution)/shard_map/ppermute | solution.py:71
  42.8 1.1 %collective-permute-done.20.refs_0_ = bf16[2,64,256]{2,1,0:T(8,128)(2,1)S(1)} collective-permute-done((bf16[2,64,256]{2,1,0:T(8,128)(2,1)S(1)}, bf16[2,64,256]{2,1,0:T(8,128)(2,1)S(1)}, u32[]{:S(2)}, u32[]{:S(2)}) %collective-permute-start.20) | collective-permute-done | bytes 65568 | tf_op jit(solution)/shard_map/ppermute | solution.py:71
  43.9 1.4 %shard_map.70 = (bf16[2,64,256]{2,1,0:T(8,128)(2,1)S(1)}, f32[64,2048]{1,0:T(8,128)S(1)}, bf16[64,2048]{1,0:T(8,128)(2,1)S(1)}) custom-call(s32[8,32]{1,0:T(8,128)S(1)} %get-tuple-element.27.index_ref, bf16[2,64,256]{2,1,0:T(8,128)(2,1)S(1)} %collective-permute-done.20.refs_0_, ...), custom_call_target="tpu_custom_call", output_to_operand_aliasing={{0}: (1, {})} | custom-call | flops 67108864 | bytes 1048576 | tf_op jit(solution)/shard_map/pallas_call | solution.py:342
  45.4 0.0 collective-permute-done.21
  45.4 0.9 %collective-permute-done.22 = bf16[2,64,256]{2,1,0:T(8,128)(2,1)S(1)} collective-permute-done((bf16[2,64,256]{2,1,0:T(8,128)(2,1)S(1)}, bf16[2,64,256]{2,1,0:T(8,128)(2,1)S(1)}, u32[]{:S(2)}, u32[]{:S(2)}) %collective-permute-start.22) | collective-permute-done | bytes 65568 | tf_op jit(solution)/shard_map/ppermute | solution.py:71
  46.3 0.0 collective-permute-done.23
  46.4 0.0 collective-permute-done.24
  46.4 0.1 collective-permute-start.25
  46.5 1.2 %shard_map.71.refs_4_ = f32[64,2048]{1,0:T(8,128)S(1)} custom-call(s32[8,32]{1,0:T(8,128)S(1)} %get-tuple-element.27.index_ref, bf16[64,2048]{1,0:T(8,128)(2,1)S(1)} %get-tuple-element.47.value_ref, bf16[2048,512]{1,0:T(8,128)(2,1)S(1)} %get-tuple-element.34.tile_ref.refs_4_.refs_3_), custom_call_target="tpu_custom_call" | custom-call | flops 67108864 | bytes 1048576 | tf_op jit(solution)/shard_map/pallas_call | solution.py:342
  47.7 0.5 collective-permute-done.25.refs_1_
  48.1 2.1 %shard_map.72 = bf16[64,2048]{1,0:T(8,128)(2,1)} custom-call(s32[8,32]{1,0:T(8,128)S(1)} %get-tuple-element.27.index_ref, bf16[11,64,256]{2,1,0:T(8,128)(2,1)S(1)} %constant_dynamic-update-slice_fusion.12.refs_0_, bf16[11,64,256]{2,1,0:T(8,128)(2,1)S(1)} %collective-permute-done.25.refs_1_, bf16[2,64,256]{2,1,0:T(8,128)(2,1)S(1)} %add_convert_fusion.refs_2_, ...), custom_call_target="tpu_custom_call" | custom-call | flops 67108864 | bytes 1048576 | tf_op jit(solution)/shard_map/pallas_call | solution.py:342
  (23 shorter events, 0.2 us)
Async XLA Ops:
  0.0 16.9 %copy-start = (bf16[64,1,1,2048]{3,0,2,1:T(8,128)(2,1)S(1)}, bf16[64,1,1,2048]{3,0,2,1:T(8,128)(2,1)}, u32[]{:S(2)}) copy-start(bf16[64,1,1,2048]{3,0,2,1:T(8,128)(2,1)} %param.6) | copy-start | bytes 786436
  0.8 1.3 %collective-permute-start = (bf16[64,256]{1,0:T(8,128)(2,1)S(1)}, bf16[64,256]{1,0:T(8,128)(2,1)S(1)}, u32[]{:S(2)}, u32[]{:S(2)}) collective-permute-start(bf16[64,256]{1,0:T(8,128)(2,1)S(1)} %get-tuple-element.50), channel_id=1, source_target_pairs={{0,1},{1,0},{2,3},{3,2},{4,5},{5,4},{6,7},{7,6},{8,9},{9,8},{10,11... | collective-permute-start | bytes 98312 | tf_op jit(solution)/shard_map/ppermute | solution.py:75
  2.2 6.0 %collective-permute-start.1 = (bf16[2,64,256]{2,1,0:T(8,128)(2,1)S(1)}, bf16[2,64,256]{2,1,0:T(8,128)(2,1)S(1)}, u32[]{:S(2)}, u32[]{:S(2)}) collective-permute-start(bf16[2,64,256]{2,1,0:T(8,128)(2,1)S(1)} %pad_maximum_fusion.both_ref.refs_3_), channel_id=1, source_target_pairs={{0,4},{1,3},{2,6},{3,1},{4,0},{5,9},{6,2},{7,11},{8,12},{9,5},{10,... | collective-permute-start | bytes 196616 | tf_op jit(solution)/shard_map/ppermute | solution.py:71
  5.1 11.4 %collective-permute-start.8 = (bf16[64,256]{1,0:T(8,128)(2,1)S(1)}, bf16[64,256]{1,0:T(8,128)(2,1)S(1)}, u32[]{:S(2)}, u32[]{:S(2)}) collective-permute-start(bf16[64,256]{1,0:T(8,128)(2,1)S(1)} %get-tuple-element.50), channel_id=1, source_target_pairs={{0,18},{1,19},{2,16},{3,17},{4,22},{5,23},{6,20},{7,21},{8,26},{9,... | collective-permute-start | bytes 98312 | tf_op jit(solution)/shard_map/ppermute | solution.py:71
  7.6 8.9 %collective-permute-start.7 = (bf16[2,64,256]{2,1,0:T(8,128)(2,1)S(1)}, bf16[2,64,256]{2,1,0:T(8,128)(2,1)S(1)}, u32[]{:S(2)}, u32[]{:S(2)}) collective-permute-start(bf16[2,64,256]{2,1,0:T(8,128)(2,1)S(1)} %pad_maximum_fusion.both_ref.refs_3_), channel_id=1, source_target_pairs={{0,2},{1,17},{2,0},{3,19},{4,6},{5,21},{6,4},{7,23},{8,10},{9,25},... | collective-permute-start | bytes 196616 | tf_op jit(solution)/shard_map/ppermute | solution.py:71
  8.1 5.2 %collective-permute-start.2 = (bf16[2,64,256]{2,1,0:T(8,128)(2,1)S(1)}, bf16[2,64,256]{2,1,0:T(8,128)(2,1)S(1)}, u32[]{:S(2)}, u32[]{:S(2)}) collective-permute-start(bf16[2,64,256]{2,1,0:T(8,128)(2,1)S(1)} %collective-permute-done.1), channel_id=1, source_target_pairs={{0,18},{1,19},{2,16},{3,17},{4,22},{5,23},{6,20},{7,21},{8,26},{9,... | collective-permute-start | bytes 196616 | tf_op jit(solution)/shard_map/ppermute | solution.py:71
  10.3 4.9 %collective-permute-start.5 = (bf16[2,64,256]{2,1,0:T(8,128)(2,1)S(1)}, bf16[2,64,256]{2,1,0:T(8,128)(2,1)S(1)}, u32[]{:S(2)}, u32[]{:S(2)}) collective-permute-start(bf16[2,64,256]{2,1,0:T(8,128)(2,1)S(1)} %collective-permute-done.1), channel_id=1, source_target_pairs={{0,2},{1,3},{2,0},{3,1},{4,6},{5,7},{6,4},{7,5},{8,10},{9,11},{10,... | collective-permute-start | bytes 196616 | tf_op jit(solution)/shard_map/ppermute | solution.py:71
  10.8 4.8 %collective-permute-start.6 = (bf16[2,64,256]{2,1,0:T(8,128)(2,1)S(1)}, bf16[2,64,256]{2,1,0:T(8,128)(2,1)S(1)}, u32[]{:S(2)}, u32[]{:S(2)}) collective-permute-start(bf16[2,64,256]{2,1,0:T(8,128)(2,1)S(1)} %collective-permute-done.1), channel_id=1, source_target_pairs={{0,16},{1,17},{2,18},{3,19},{4,20},{5,21},{6,22},{7,23},{8,24},{9,... | collective-permute-start | bytes 196616 | tf_op jit(solution)/shard_map/ppermute | solution.py:71
  15.1 1.4 %collective-permute-start.3 = (bf16[256,256]{1,0:T(8,128)(2,1)S(1)}, bf16[256,256]{1,0:T(8,128)(2,1)S(1)}, u32[]{:S(2)}, u32[]{:S(2)}) collective-permute-start(bf16[256,256]{1,0:T(8,128)(2,1)S(1)} %get-tuple-element.30), channel_id=1, source_target_pairs={{0,1},{1,0},{2,3},{3,2},{4,5},{5,4},{6,7},{7,6},{8,9},{9,8},{10,11... | collective-permute-start | bytes 393224 | tf_op jit(solution)/shard_map/ppermute | solution.py:75
  15.1 1.3 %collective-permute-start.4 = (s32[8,32]{1,0:T(8,128)S(1)}, s32[8,32]{1,0:T(8,128)S(1)}, u32[]{:S(2)}, u32[]{:S(2)}) collective-permute-start(s32[8,32]{1,0:T(8,128)S(1)} %get-tuple-element.31), channel_id=1, source_target_pairs={{0,1},{1,0},{2,3},{3,2},{4,5},{5,4},{6,7},{7,6},{8,9},{9,8},{10,11... | collective-permute-start | bytes 3080 | tf_op jit(solution)/shard_map/ppermute | solution.py:75
  16.5 3.1 %collective-permute-start.10 = (bf16[11,64,256]{2,1,0:T(8,128)(2,1)S(1)}, bf16[11,64,256]{2,1,0:T(8,128)(2,1)S(1)}, u32[]{:S(2)}, u32[]{:S(2)}) collective-permute-start(bf16[11,64,256]{2,1,0:T(8,128)(2,1)S(1)} %constant_dynamic-update-slice_fusion.received_ref.refs_1_), channel_id=1, source_target_pairs={{0,1},{1,0},{2,3},{3,2},{4,5},{5,4},{6,7},{7,6},{8,9},{9,8},{10,11... | collective-permute-start | bytes 1081352 | tf_op jit(solution)/shard_map/ppermute | solution.py:75
  18.1 1.4 %collective-permute-start.9 = (f32[2,64,256]{2,1,0:T(8,128)S(1)}, f32[2,64,256]{2,1,0:T(8,128)S(1)}, u32[]{:S(2)}, u32[]{:S(2)}) collective-permute-start(f32[2,64,256]{2,1,0:T(8,128)S(1)} %shard_map.65), channel_id=1, source_target_pairs={{0,1},{1,0},{2,3},{3,2},{4,5},{5,4},{6,7},{7,6},{8,9},{9,8},{10,11... | collective-permute-start | bytes 393224 | tf_op jit(solution)/shard_map/ppermute | solution.py:75
  19.6 4.3 %collective-permute-start.11 = (bf16[2,64,256]{2,1,0:T(8,128)(2,1)S(1)}, bf16[2,64,256]{2,1,0:T(8,128)(2,1)S(1)}, u32[]{:S(2)}, u32[]{:S(2)}) collective-permute-start(bf16[2,64,256]{2,1,0:T(8,128)(2,1)S(1)} %add_convert_fusion.1.both_ref.refs_3_), channel_id=1, source_target_pairs={{0,4},{1,3},{2,6},{3,1},{4,0},{5,9},{6,2},{7,11},{8,12},{9,5},{10,... | collective-permute-start | bytes 196616 | tf_op jit(solution)/shard_map/ppermute | solution.py:71
  21.0 10.8 %collective-permute-start.15 = (bf16[2,64,256]{2,1,0:T(8,128)(2,1)S(1)}, bf16[2,64,256]{2,1,0:T(8,128)(2,1)S(1)}, u32[]{:S(2)}, u32[]{:S(2)}) collective-permute-start(bf16[2,64,256]{2,1,0:T(8,128)(2,1)S(1)} %add_convert_fusion.1.both_ref.refs_3_), channel_id=1, source_target_pairs={{0,2},{1,17},{2,0},{3,19},{4,6},{5,21},{6,4},{7,23},{8,10},{9,25},... | collective-permute-start | bytes 196616 | tf_op jit(solution)/shard_map/ppermute | solution.py:71
  22.6 9.3 %collective-permute-start.16 = (bf16[64,256]{1,0:T(8,128)(2,1)S(1)}, bf16[64,256]{1,0:T(8,128)(2,1)S(1)}, u32[]{:S(2)}, u32[]{:S(2)}) collective-permute-start(bf16[64,256]{1,0:T(8,128)(2,1)S(1)} %slice_bitcast_fusion.1), channel_id=1, source_target_pairs={{0,18},{1,19},{2,16},{3,17},{4,22},{5,23},{6,20},{7,21},{8,26},{9,... | collective-permute-start | bytes 98312 | tf_op jit(solution)/shard_map/ppermute | solution.py:71
  24.0 4.3 %collective-permute-start.12 = (bf16[2,64,256]{2,1,0:T(8,128)(2,1)S(1)}, bf16[2,64,256]{2,1,0:T(8,128)(2,1)S(1)}, u32[]{:S(2)}, u32[]{:S(2)}) collective-permute-start(bf16[2,64,256]{2,1,0:T(8,128)(2,1)S(1)} %collective-permute-done.11), channel_id=1, source_target_pairs={{0,2},{1,3},{2,0},{3,1},{4,6},{5,7},{6,4},{7,5},{8,10},{9,11},{10,... | collective-permute-start | bytes 196616 | tf_op jit(solution)/shard_map/ppermute | solution.py:71
  25.5 5.0 %collective-permute-start.13 = (bf16[2,64,256]{2,1,0:T(8,128)(2,1)S(1)}, bf16[2,64,256]{2,1,0:T(8,128)(2,1)S(1)}, u32[]{:S(2)}, u32[]{:S(2)}) collective-permute-start(bf16[2,64,256]{2,1,0:T(8,128)(2,1)S(1)} %collective-permute-done.11), channel_id=1, source_target_pairs={{0,16},{1,17},{2,18},{3,19},{4,20},{5,21},{6,22},{7,23},{8,24},{9,... | collective-permute-start | bytes 196616 | tf_op jit(solution)/shard_map/ppermute | solution.py:71
  26.7 5.2 %collective-permute-start.14 = (bf16[2,64,256]{2,1,0:T(8,128)(2,1)S(1)}, bf16[2,64,256]{2,1,0:T(8,128)(2,1)S(1)}, u32[]{:S(2)}, u32[]{:S(2)}) collective-permute-start(bf16[2,64,256]{2,1,0:T(8,128)(2,1)S(1)} %collective-permute-done.11), channel_id=1, source_target_pairs={{0,18},{1,19},{2,16},{3,17},{4,22},{5,23},{6,20},{7,21},{8,26},{9,... | collective-permute-start | bytes 196616 | tf_op jit(solution)/shard_map/ppermute | solution.py:71
  31.9 3.1 %collective-permute-start.18 = (bf16[11,64,256]{2,1,0:T(8,128)(2,1)S(1)}, bf16[11,64,256]{2,1,0:T(8,128)(2,1)S(1)}, u32[]{:S(2)}, u32[]{:S(2)}) collective-permute-start(bf16[11,64,256]{2,1,0:T(8,128)(2,1)S(1)} %constant_dynamic-update-slice_fusion.6.received_ref.refs_1_), channel_id=1, source_target_pairs={{0,1},{1,0},{2,3},{3,2},{4,5},{5,4},{6,7},{7,6},{8,9},{9,8},{10,11... | collective-permute-start | bytes 1081352 | tf_op jit(solution)/shard_map/ppermute | solution.py:75
  33.2 1.8 %collective-permute-start.17 = (f32[2,64,256]{2,1,0:T(8,128)S(1)}, f32[2,64,256]{2,1,0:T(8,128)S(1)}, u32[]{:S(2)}, u32[]{:S(2)}) collective-permute-start(f32[2,64,256]{2,1,0:T(8,128)S(1)} %shard_map.68), channel_id=1, source_target_pairs={{0,1},{1,0},{2,3},{3,2},{4,5},{5,4},{6,7},{7,6},{8,9},{9,8},{10,11... | collective-permute-start | bytes 393224 | tf_op jit(solution)/shard_map/ppermute | solution.py:75
  35.0 4.3 %collective-permute-start.19 = (bf16[2,64,256]{2,1,0:T(8,128)(2,1)S(1)}, bf16[2,64,256]{2,1,0:T(8,128)(2,1)S(1)}, u32[]{:S(2)}, u32[]{:S(2)}) collective-permute-start(bf16[2,64,256]{2,1,0:T(8,128)(2,1)S(1)} %add_convert_fusion.refs_2_), channel_id=1, source_target_pairs={{0,4},{1,3},{2,6},{3,1},{4,0},{5,9},{6,2},{7,11},{8,12},{9,5},{10,... | collective-permute-start | bytes 196616 | tf_op jit(solution)/shard_map/ppermute | solution.py:71
  36.6 9.7 %collective-permute-start.23 = (bf16[2,64,256]{2,1,0:T(8,128)(2,1)S(1)}, bf16[2,64,256]{2,1,0:T(8,128)(2,1)S(1)}, u32[]{:S(2)}, u32[]{:S(2)}) collective-permute-start(bf16[2,64,256]{2,1,0:T(8,128)(2,1)S(1)} %add_convert_fusion.refs_2_), channel_id=1, source_target_pairs={{0,2},{1,17},{2,0},{3,19},{4,6},{5,21},{6,4},{7,23},{8,10},{9,25},... | collective-permute-start | bytes 196616 | tf_op jit(solution)/shard_map/ppermute | solution.py:71
  37.2 9.2 %collective-permute-start.24 = (bf16[64,256]{1,0:T(8,128)(2,1)S(1)}, bf16[64,256]{1,0:T(8,128)(2,1)S(1)}, u32[]{:S(2)}, u32[]{:S(2)}) collective-permute-start(bf16[64,256]{1,0:T(8,128)(2,1)S(1)} %slice_bitcast_fusion), channel_id=1, source_target_pairs={{0,18},{1,19},{2,16},{3,17},{4,22},{5,23},{6,20},{7,21},{8,26},{9,... | collective-permute-start | bytes 98312 | tf_op jit(solution)/shard_map/ppermute | solution.py:71
  39.3 4.6 %collective-permute-start.20 = (bf16[2,64,256]{2,1,0:T(8,128)(2,1)S(1)}, bf16[2,64,256]{2,1,0:T(8,128)(2,1)S(1)}, u32[]{:S(2)}, u32[]{:S(2)}) collective-permute-start(bf16[2,64,256]{2,1,0:T(8,128)(2,1)S(1)} %collective-permute-done.19), channel_id=1, source_target_pairs={{0,2},{1,3},{2,0},{3,1},{4,6},{5,7},{6,4},{7,5},{8,10},{9,11},{10,... | collective-permute-start | bytes 196616 | tf_op jit(solution)/shard_map/ppermute | solution.py:71
  40.1 5.3 %collective-permute-start.21 = (bf16[2,64,256]{2,1,0:T(8,128)(2,1)S(1)}, bf16[2,64,256]{2,1,0:T(8,128)(2,1)S(1)}, u32[]{:S(2)}, u32[]{:S(2)}) collective-permute-start(bf16[2,64,256]{2,1,0:T(8,128)(2,1)S(1)} %collective-permute-done.19), channel_id=1, source_target_pairs={{0,16},{1,17},{2,18},{3,19},{4,20},{5,21},{6,22},{7,23},{8,24},{9,... | collective-permute-start | bytes 196616 | tf_op jit(solution)/shard_map/ppermute | solution.py:71
  41.2 5.2 %collective-permute-start.22 = (bf16[2,64,256]{2,1,0:T(8,128)(2,1)S(1)}, bf16[2,64,256]{2,1,0:T(8,128)(2,1)S(1)}, u32[]{:S(2)}, u32[]{:S(2)}) collective-permute-start(bf16[2,64,256]{2,1,0:T(8,128)(2,1)S(1)} %collective-permute-done.19), channel_id=1, source_target_pairs={{0,18},{1,19},{2,16},{3,17},{4,22},{5,23},{6,20},{7,21},{8,26},{9,... | collective-permute-start | bytes 196616 | tf_op jit(solution)/shard_map/ppermute | solution.py:71
  46.4 1.7 %collective-permute-start.25 = (bf16[11,64,256]{2,1,0:T(8,128)(2,1)S(1)}, bf16[11,64,256]{2,1,0:T(8,128)(2,1)S(1)}, u32[]{:S(2)}, u32[]{:S(2)}) collective-permute-start(bf16[11,64,256]{2,1,0:T(8,128)(2,1)S(1)} %constant_dynamic-update-slice_fusion.12.refs_0_), channel_id=1, source_target_pairs={{0,1},{1,0},{2,3},{3,2},{4,5},{5,4},{6,7},{7,6},{8,9},{9,8},{10,11... | collective-permute-start | bytes 1081352 | tf_op jit(solution)/shard_map/ppermute | solution.py:75

commit v10 on v9

--- a/solution.py
+++ b/solution.py
@@ -11,7 +11,7 @@
 TERMS = 3
 FEATURES = 64
 NEAR = 4
-PARTS = 4
+PARTS = 8
 VMEM_MIB = 16
 LANES = 2 * PB
 AXES = ("gx", "gy", "gz")
@@ -81,12 +81,12 @@
     plane = chips[-((len(chips) - sides) // (sides + 1)) :]
     rim = both[0]
     side = swap(both, (chips[0], chips[sides - 1]))
-    alone = [swap(rim, (plane[-1], plane[-1]))] if len(plane) % 2 else []
     own = [
         swap(both, (plane[t], plane[t + 1])) for t in range(0, len(plane) - len(plane) % 2, 2)
     ]
     step = -1 if far_first else 1
     passed = [swap(side, (chip, chip)) for chip in plane[::step]]
+    alone = [swap(rim, (plane[-1], plane[-1]))] if len(plane) % 2 else []
     passed[0], *results = work(passed[0])
     received = jnp.concatenate([side] + passed[::step] + own + [panel[None] for panel in alone])
     return received, results
@@ -445,7 +445,7 @@
             return through, total_now, value_now
 
         near = image(value, scaled, index)
-        added, others, near = lax.optimization_barrier((swap_cores(part), others, near))
+        added, others = lax.optimization_barrier((swap_cores(part), others))
         arrays = ((index,), received, others, both, scaled, near, times)
         both = (part + added[::-1]).astype(jnp.bfloat16)
         received, (total, value) = exchange(both, rest, False)

time: 50.4 us -> 50.4 us (level)
  no operation moved by 1% of the time
where the time goes in v10:
time: 50.4 us; the launch traced here: 50.2 us
  starting transfers between devices  26.8 us (53%)
  Pallas kernels  13.4 us (27%)
  waiting for transfers between devices  8.72 us (17%)
  local copies, waits for them, and re-layouts  0.95 us (2%)
    ppermute x18, starting transfers between devices, swap(): return lax.ppermute(value, AXES, pairs)  24.5 us
    pallas_call x9, Pallas kernels, call(): pl.pallas_call(kernel, out_shape=out_shape, in_specs=[pl.BlockSpec(memory...  13.4 us
    ppermute x18, waiting for transfers between devices, swap(): return lax.ppermute(value, AXES, pairs)  6.57 us
    ppermute x8, starting transfers between devices, swap_cores(): lax.ppermute(value, 'gz', [(k, k ^ 1) for k in range(lax.axis_size('gz'))])  2.36 us
    ppermute x8, waiting for transfers between devices, swap_cores(): lax.ppermute(value, 'gz', [(k, k ^ 1) for k in range(lax.axis_size('gz'))])  2.15 us
  transfers between devices with their start and end apart: 26, of which 10 were waited for; matrix products, arithmetic and copies ran while one was open for 0% of the time, Pallas kernels for 22%

profile of v10, /device:TPU:0, one launch (start us, length us, event | category | flops | bytes accessed | tf_op | source)
XLA Modules:
  0.0 50.2 jit_solution(4155403118280706564)
XLA Ops:
  0.0 0.0 copy-start
  0.0 0.8 %slice_bitcast_fusion.2 = (bf16[1,64,256]{2,1,0:T(8,128)(2,1)S(1)}, bf16[64,256]{1,0:T(8,128)(2,1)S(1)}) fusion(bf16[64,2048]{1,0:T(8,128)(2,1)} %bitcast.24), kind=kLoop, calls=%fused_computation.23 | loop fusion | bytes 98304 | tf_op jit(solution)/shard_map/stack | solution.py:365
  0.8 0.5 collective-permute-start
  1.3 0.9 %collective-permute-done = bf16[64,256]{1,0:T(8,128)(2,1)S(1)} collective-permute-done((bf16[64,256]{1,0:T(8,128)(2,1)S(1)}, bf16[64,256]{1,0:T(8,128)(2,1)S(1)}, u32[]{:S(2)}, u32[]{:S(2)}) %collective-permute-start) | collective-permute-done | bytes 32800 | tf_op jit(solution)/shard_map/ppermute | solution.py:75
  2.2 3.0 %collective-permute-start.1 = (bf16[2,64,256]{2,1,0:T(8,128)(2,1)S(1)}, bf16[2,64,256]{2,1,0:T(8,128)(2,1)S(1)}, u32[]{:S(2)}, u32[]{:S(2)}) collective-permute-start(bf16[2,64,256]{2,1,0:T(8,128)(2,1)S(1)} %pad_maximum_fusion.both_ref.refs_3_), channel_id=1, source_target_pairs={{0,4},{1,3},{2,6},{3,1},{4,0},{5,9},{6,2},{7,11},{8,12},{9,5},{10,... | collective-permute-start | bytes 196616 | tf_op jit(solution)/shard_map/ppermute | solution.py:71
  5.1 2.4 %collective-permute-start.8 = (bf16[64,256]{1,0:T(8,128)(2,1)S(1)}, bf16[64,256]{1,0:T(8,128)(2,1)S(1)}, u32[]{:S(2)}, u32[]{:S(2)}) collective-permute-start(bf16[64,256]{1,0:T(8,128)(2,1)S(1)} %get-tuple-element.46), channel_id=1, source_target_pairs={{0,18},{1,19},{2,16},{3,17},{4,22},{5,23},{6,20},{7,21},{8,26},{9,... | collective-permute-start | bytes 98312 | tf_op jit(solution)/shard_map/ppermute | solution.py:71
  7.6 0.5 %collective-permute-start.7 = (bf16[2,64,256]{2,1,0:T(8,128)(2,1)S(1)}, bf16[2,64,256]{2,1,0:T(8,128)(2,1)S(1)}, u32[]{:S(2)}, u32[]{:S(2)}) collective-permute-start(bf16[2,64,256]{2,1,0:T(8,128)(2,1)S(1)} %pad_maximum_fusion.both_ref.refs_3_), channel_id=1, source_target_pairs={{0,2},{1,17},{2,0},{3,19},{4,6},{5,21},{6,4},{7,23},{8,10},{9,25},... | collective-permute-start | bytes 196616 | tf_op jit(solution)/shard_map/ppermute | solution.py:71
  8.1 0.0 collective-permute-done.1
  8.1 2.1 %collective-permute-start.2 = (bf16[2,64,256]{2,1,0:T(8,128)(2,1)S(1)}, bf16[2,64,256]{2,1,0:T(8,128)(2,1)S(1)}, u32[]{:S(2)}, u32[]{:S(2)}) collective-permute-start(bf16[2,64,256]{2,1,0:T(8,128)(2,1)S(1)} %collective-permute-done.1), channel_id=1, source_target_pairs={{0,18},{1,19},{2,16},{3,17},{4,22},{5,23},{6,20},{7,21},{8,26},{9,... | collective-permute-start | bytes 196616 | tf_op jit(solution)/shard_map/ppermute | solution.py:71
  10.3 0.5 %collective-permute-start.5 = (bf16[2,64,256]{2,1,0:T(8,128)(2,1)S(1)}, bf16[2,64,256]{2,1,0:T(8,128)(2,1)S(1)}, u32[]{:S(2)}, u32[]{:S(2)}) collective-permute-start(bf16[2,64,256]{2,1,0:T(8,128)(2,1)S(1)} %collective-permute-done.1), channel_id=1, source_target_pairs={{0,2},{1,3},{2,0},{3,1},{4,6},{5,7},{6,4},{7,5},{8,10},{9,11},{10,... | collective-permute-start | bytes 196616 | tf_op jit(solution)/shard_map/ppermute | solution.py:71
  10.8 0.8 %collective-permute-start.6 = (bf16[2,64,256]{2,1,0:T(8,128)(2,1)S(1)}, bf16[2,64,256]{2,1,0:T(8,128)(2,1)S(1)}, u32[]{:S(2)}, u32[]{:S(2)}) collective-permute-start(bf16[2,64,256]{2,1,0:T(8,128)(2,1)S(1)} %collective-permute-done.1), channel_id=1, source_target_pairs={{0,16},{1,17},{2,18},{3,19},{4,20},{5,21},{6,22},{7,23},{8,24},{9,... | collective-permute-start | bytes 196616 | tf_op jit(solution)/shard_map/ppermute | solution.py:71
  11.6 1.7 %collective-permute-done.2._ = bf16[2,64,256]{2,1,0:T(8,128)(2,1)S(1)} collective-permute-done((bf16[2,64,256]{2,1,0:T(8,128)(2,1)S(1)}, bf16[2,64,256]{2,1,0:T(8,128)(2,1)S(1)}, u32[]{:S(2)}, u32[]{:S(2)}) %collective-permute-start.2) | collective-permute-done | bytes 65568 | tf_op jit(solution)/shard_map/ppermute | solution.py:71
  13.3 1.7 %shard_map.64 = (bf16[2,64,256]{2,1,0:T(8,128)(2,1)S(1)}, bf16[2048,512]{1,0:T(8,128)(2,1)S(1)}, bf16[256,256]{1,0:T(8,128)(2,1)S(1)}, s32[8,32]{1,0:T(8,128)S(1...) custom-call(bf16[2,64,256]{2,1,0:T(8,128)(2,1)S(1)} %collective-permute-, ...), custom_call_target="tpu_custom_call", output_to_operand_aliasing={{0}: (0, {})} | custom-call | flops 67108864 | bytes 1048576 | tf_op jit(solution)/shard_map/pallas_call | solution.py:342
  15.0 0.1 collective-permute-start.3
  15.1 0.0 collective-permute-done.5
  15.1 0.5 collective-permute-start.4
  15.6 0.0 collective-permute-done.6
  15.6 0.8 %collective-permute-done.4.theirs_ref = s32[8,32]{1,0:T(8,128)S(1)} collective-permute-done((s32[8,32]{1,0:T(8,128)S(1)}, s32[8,32]{1,0:T(8,128)S(1)}, u32[]{:S(2)}, u32[]{:S(2)}) %collective-permute-start.4) | collective-permute-done | bytes 1056 | tf_op jit(solution)/shard_map/ppermute | solution.py:75
  16.4 0.0 collective-permute-done.3.edge_ref
  16.5 0.0 collective-permute-done.7
  16.5 0.0 collective-permute-done.8
  16.5 0.4 collective-permute-start.10
  16.9 0.0 copy-done
  16.9 1.2 %shard_map.65 = f32[2,64,256]{2,1,0:T(8,128)S(1)} custom-call(s32[8,32]{1,0:T(8,128)S(1)} %get-tuple-element.25.index_ref, s32[8,32]{1,0:T(8,128)S(1)} %get-tuple-element.26.mine_ref, s32[8,32]{1,0:T(8,128)S(1)} %collective-permute-done.4.theirs_ref, bf16[11,64,256]{2,1,0:T(8,128)(2,1)S(1)} %constant_dynamic-update-slice_fusion.received_ref.refs_1_, ...), custom_call_target="tpu_custom_call" | custom-call | flops 16777216 | bytes 262144 | tf_op jit(solution)/shard_map/pallas_call | solution.py:342
  18.1 0.2 collective-permute-start.9
  18.4 1.2 %shard_map.66.refs_5_ = f32[64,2048]{1,0:T(8,128)S(1)} custom-call(s32[8,32]{1,0:T(8,128)S(1)} %get-tuple-element.25.index_ref, bf16[64,2048]{1,0:T(8,128)(2,1)S(1)} %bitcast.27, bf16[2048,512]{1,0:T(8,128)(2,1)S(1)} %get-tuple-element.32.tile_ref.refs_4_.refs_3_), custom_call_target="tpu_custom_call" | custom-call | flops 67108864 | bytes 1048576 | tf_op jit(solution)/shard_map/pallas_call | solution.py:342
  19.6 0.0 collective-permute-done.9
  19.6 0.0 collective-permute-done.10.refs_2_
  19.6 1.4 %collective-permute-start.11 = (bf16[2,64,256]{2,1,0:T(8,128)(2,1)S(1)}, bf16[2,64,256]{2,1,0:T(8,128)(2,1)S(1)}, u32[]{:S(2)}, u32[]{:S(2)}) collective-permute-start(bf16[2,64,256]{2,1,0:T(8,128)(2,1)S(1)} %add_convert_fusion.1.both_ref.refs_3_), channel_id=1, source_target_pairs={{0,4},{1,3},{2,6},{3,1},{4,0},{5,9},{6,2},{7,11},{8,12},{9,5},{10,... | collective-permute-start | bytes 196616 | tf_op jit(solution)/shard_map/ppermute | solution.py:71
  21.0 1.5 %collective-permute-start.15 = (bf16[2,64,256]{2,1,0:T(8,128)(2,1)S(1)}, bf16[2,64,256]{2,1,0:T(8,128)(2,1)S(1)}, u32[]{:S(2)}, u32[]{:S(2)}) collective-permute-start(bf16[2,64,256]{2,1,0:T(8,128)(2,1)S(1)} %add_convert_fusion.1.both_ref.refs_3_), channel_id=1, source_target_pairs={{0,2},{1,17},{2,0},{3,19},{4,6},{5,21},{6,4},{7,23},{8,10},{9,25},... | collective-permute-start | bytes 196616 | tf_op jit(solution)/shard_map/ppermute | solution.py:71
  22.5 1.4 %collective-permute-start.16 = (bf16[64,256]{1,0:T(8,128)(2,1)S(1)}, bf16[64,256]{1,0:T(8,128)(2,1)S(1)}, u32[]{:S(2)}, u32[]{:S(2)}) collective-permute-start(bf16[64,256]{1,0:T(8,128)(2,1)S(1)} %slice_bitcast_fusion.1), channel_id=1, source_target_pairs={{0,18},{1,19},{2,16},{3,17},{4,22},{5,23},{6,20},{7,21},{8,26},{9,... | collective-permute-start | bytes 98312 | tf_op jit(solution)/shard_map/ppermute | solution.py:71
  23.9 0.0 collective-permute-done.11
  23.9 1.5 %collective-permute-start.12 = (bf16[2,64,256]{2,1,0:T(8,128)(2,1)S(1)}, bf16[2,64,256]{2,1,0:T(8,128)(2,1)S(1)}, u32[]{:S(2)}, u32[]{:S(2)}) collective-permute-start(bf16[2,64,256]{2,1,0:T(8,128)(2,1)S(1)} %collective-permute-done.11), channel_id=1, source_target_pairs={{0,2},{1,3},{2,0},{3,1},{4,6},{5,7},{6,4},{7,5},{8,10},{9,11},{10,... | collective-permute-start | bytes 196616 | tf_op jit(solution)/shard_map/ppermute | solution.py:71
  25.4 1.2 %collective-permute-start.13 = (bf16[2,64,256]{2,1,0:T(8,128)(2,1)S(1)}, bf16[2,64,256]{2,1,0:T(8,128)(2,1)S(1)}, u32[]{:S(2)}, u32[]{:S(2)}) collective-permute-start(bf16[2,64,256]{2,1,0:T(8,128)(2,1)S(1)} %collective-permute-done.11), channel_id=1, source_target_pairs={{0,16},{1,17},{2,18},{3,19},{4,20},{5,21},{6,22},{7,23},{8,24},{9,... | collective-permute-start | bytes 196616 | tf_op jit(solution)/shard_map/ppermute | solution.py:71
  26.6 0.8 %collective-permute-start.14 = (bf16[2,64,256]{2,1,0:T(8,128)(2,1)S(1)}, bf16[2,64,256]{2,1,0:T(8,128)(2,1)S(1)}, u32[]{:S(2)}, u32[]{:S(2)}) collective-permute-start(bf16[2,64,256]{2,1,0:T(8,128)(2,1)S(1)} %collective-permute-done.11), channel_id=1, source_target_pairs={{0,18},{1,19},{2,16},{3,17},{4,22},{5,23},{6,20},{7,21},{8,26},{9,... | collective-permute-start | bytes 196616 | tf_op jit(solution)/shard_map/ppermute | solution.py:71
  27.4 0.8 %collective-permute-done.12.refs_0_ = bf16[2,64,256]{2,1,0:T(8,128)(2,1)S(1)} collective-permute-done((bf16[2,64,256]{2,1,0:T(8,128)(2,1)S(1)}, bf16[2,64,256]{2,1,0:T(8,128)(2,1)S(1)}, u32[]{:S(2)}, u32[]{:S(2)}) %collective-permute-start.12) | collective-permute-done | bytes 65568 | tf_op jit(solution)/shard_map/ppermute | solution.py:71
  28.2 2.1 %shard_map.67 = (bf16[2,64,256]{2,1,0:T(8,128)(2,1)S(1)}, f32[64,2048]{1,0:T(8,128)S(1)}, bf16[64,2048]{1,0:T(8,128)(2,1)S(1)}) custom-call(s32[8,32]{1,0:T(8,128)S(1)} %get-tuple-element.25.index_ref, bf16[2,64,256]{2,1,0:T(8,128)(2,1)S(1)} %collective-permute-done.12.refs_0_, ...), custom_call_target="tpu_custom_call", output_to_operand_aliasing={{0}: (1, {})} | custom-call | flops 67108864 | bytes 1048576 | tf_op jit(solution)/shard_map/pallas_call | solution.py:342
  30.3 0.1 collective-permute-done.13
  30.4 1.4 %collective-permute-done.14 = bf16[2,64,256]{2,1,0:T(8,128)(2,1)S(1)} collective-permute-done((bf16[2,64,256]{2,1,0:T(8,128)(2,1)S(1)}, bf16[2,64,256]{2,1,0:T(8,128)(2,1)S(1)}, u32[]{:S(2)}, u32[]{:S(2)}) %collective-permute-start.14) | collective-permute-done | bytes 65568 | tf_op jit(solution)/shard_map/ppermute | solution.py:71
  31.8 0.0 collective-permute-done.15
  31.8 0.0 collective-permute-done.16
  31.9 0.1 collective-permute-start.18
  31.9 1.2 %shard_map.68 = f32[2,64,256]{2,1,0:T(8,128)S(1)} custom-call(s32[8,32]{1,0:T(8,128)S(1)} %get-tuple-element.25.index_ref, s32[8,32]{1,0:T(8,128)S(1)} %get-tuple-element.26.mine_ref, s32[8,32]{1,0:T(8,128)S(1)} %collective-permute-done.4.theirs_ref, bf16[11,64,256]{2,1,0:T(8,128)(2,1)S(1)} %constant_dynamic-update-slice_fusion.6.received_ref.refs_1_, ...), custom_call_target="tpu_custom_call" | custom-call | flops 16777216 | bytes 262144 | tf_op jit(solution)/shard_map/pallas_call | solution.py:342
  33.2 0.6 %collective-permute-start.17 = (f32[2,64,256]{2,1,0:T(8,128)S(1)}, f32[2,64,256]{2,1,0:T(8,128)S(1)}, u32[]{:S(2)}, u32[]{:S(2)}) collective-permute-start(f32[2,64,256]{2,1,0:T(8,128)S(1)} %shard_map.68), channel_id=1, source_target_pairs={{0,1},{1,0},{2,3},{3,2},{4,5},{5,4},{6,7},{7,6},{8,9},{9,8},{10,11... | collective-permute-start | bytes 393224 | tf_op jit(solution)/shard_map/ppermute | solution.py:75
  33.7 1.2 %shard_map.69.refs_5_ = f32[64,2048]{1,0:T(8,128)S(1)} custom-call(s32[8,32]{1,0:T(8,128)S(1)} %get-tuple-element.25.index_ref, bf16[64,2048]{1,0:T(8,128)(2,1)S(1)} %get-tuple-element.38.value_ref, bf16[2048,512]{1,0:T(8,128)(2,1)S(1)} %get-tuple-element.32.tile_ref.refs_4_.refs_3_), custom_call_target="tpu_custom_call" | custom-call | flops 67108864 | bytes 1048576 | tf_op jit(solution)/shard_map/pallas_call | solution.py:342
  34.9 0.0 collective-permute-done.17
  34.9 0.0 collective-permute-done.18.refs_2_
  35.0 1.6 %collective-permute-start.19 = (bf16[2,64,256]{2,1,0:T(8,128)(2,1)S(1)}, bf16[2,64,256]{2,1,0:T(8,128)(2,1)S(1)}, u32[]{:S(2)}, u32[]{:S(2)}) collective-permute-start(bf16[2,64,256]{2,1,0:T(8,128)(2,1)S(1)} %add_convert_fusion.refs_2_), channel_id=1, source_target_pairs={{0,4},{1,3},{2,6},{3,1},{4,0},{5,9},{6,2},{7,11},{8,12},{9,5},{10,... | collective-permute-start | bytes 196616 | tf_op jit(solution)/shard_map/ppermute | solution.py:71
  36.6 0.5 %collective-permute-start.23 = (bf16[2,64,256]{2,1,0:T(8,128)(2,1)S(1)}, bf16[2,64,256]{2,1,0:T(8,128)(2,1)S(1)}, u32[]{:S(2)}, u32[]{:S(2)}) collective-permute-start(bf16[2,64,256]{2,1,0:T(8,128)(2,1)S(1)} %add_convert_fusion.refs_2_), channel_id=1, source_target_pairs={{0,2},{1,17},{2,0},{3,19},{4,6},{5,21},{6,4},{7,23},{8,10},{9,25},... | collective-permute-start | bytes 196616 | tf_op jit(solution)/shard_map/ppermute | solution.py:71
  37.1 1.5 %collective-permute-start.24 = (bf16[64,256]{1,0:T(8,128)(2,1)S(1)}, bf16[64,256]{1,0:T(8,128)(2,1)S(1)}, u32[]{:S(2)}, u32[]{:S(2)}) collective-permute-start(bf16[64,256]{1,0:T(8,128)(2,1)S(1)} %slice_bitcast_fusion), channel_id=1, source_target_pairs={{0,18},{1,19},{2,16},{3,17},{4,22},{5,23},{6,20},{7,21},{8,26},{9,... | collective-permute-start | bytes 98312 | tf_op jit(solution)/shard_map/ppermute | solution.py:71
  38.7 0.6 %collective-permute-done.19 = bf16[2,64,256]{2,1,0:T(8,128)(2,1)S(1)} collective-permute-done((bf16[2,64,256]{2,1,0:T(8,128)(2,1)S(1)}, bf16[2,64,256]{2,1,0:T(8,128)(2,1)S(1)}, u32[]{:S(2)}, u32[]{:S(2)}) %collective-permute-start.19) | collective-permute-done | bytes 65568 | tf_op jit(solution)/shard_map/ppermute | solution.py:71
  39.3 0.7 %collective-permute-start.20 = (bf16[2,64,256]{2,1,0:T(8,128)(2,1)S(1)}, bf16[2,64,256]{2,1,0:T(8,128)(2,1)S(1)}, u32[]{:S(2)}, u32[]{:S(2)}) collective-permute-start(bf16[2,64,256]{2,1,0:T(8,128)(2,1)S(1)} %collective-permute-done.19), channel_id=1, source_target_pairs={{0,2},{1,3},{2,0},{3,1},{4,6},{5,7},{6,4},{7,5},{8,10},{9,11},{10,... | collective-permute-start | bytes 196616 | tf_op jit(solution)/shard_map/ppermute | solution.py:71
  40.0 1.1 %collective-permute-start.21 = (bf16[2,64,256]{2,1,0:T(8,128)(2,1)S(1)}, bf16[2,64,256]{2,1,0:T(8,128)(2,1)S(1)}, u32[]{:S(2)}, u32[]{:S(2)}) collective-permute-start(bf16[2,64,256]{2,1,0:T(8,128)(2,1)S(1)} %collective-permute-done.19), channel_id=1, source_target_pairs={{0,16},{1,17},{2,18},{3,19},{4,20},{5,21},{6,22},{7,23},{8,24},{9,... | collective-permute-start | bytes 196616 | tf_op jit(solution)/shard_map/ppermute | solution.py:71
  41.1 1.7 %collective-permute-start.22 = (bf16[2,64,256]{2,1,0:T(8,128)(2,1)S(1)}, bf16[2,64,256]{2,1,0:T(8,128)(2,1)S(1)}, u32[]{:S(2)}, u32[]{:S(2)}) collective-permute-start(bf16[2,64,256]{2,1,0:T(8,128)(2,1)S(1)} %collective-permute-done.19), channel_id=1, source_target_pairs={{0,18},{1,19},{2,16},{3,17},{4,22},{5,23},{6,20},{7,21},{8,26},{9,... | collective-permute-start | bytes 196616 | tf_op jit(solution)/shard_map/ppermute | solution.py:71
  42.8 1.1 %collective-permute-done.20.refs_0_ = bf16[2,64,256]{2,1,0:T(8,128)(2,1)S(1)} collective-permute-done((bf16[2,64,256]{2,1,0:T(8,128)(2,1)S(1)}, bf16[2,64,256]{2,1,0:T(8,128)(2,1)S(1)}, u32[]{:S(2)}, u32[]{:S(2)}) %collective-permute-start.20) | collective-permute-done | bytes 65568 | tf_op jit(solution)/shard_map/ppermute | solution.py:71
  43.9 1.4 %shard_map.70 = (bf16[2,64,256]{2,1,0:T(8,128)(2,1)S(1)}, f32[64,2048]{1,0:T(8,128)S(1)}, bf16[64,2048]{1,0:T(8,128)(2,1)S(1)}) custom-call(s32[8,32]{1,0:T(8,128)S(1)} %get-tuple-element.25.index_ref, bf16[2,64,256]{2,1,0:T(8,128)(2,1)S(1)} %collective-permute-done.20.refs_0_, ...), custom_call_target="tpu_custom_call", output_to_operand_aliasing={{0}: (1, {})} | custom-call | flops 67108864 | bytes 1048576 | tf_op jit(solution)/shard_map/pallas_call | solution.py:342
  45.4 0.0 collective-permute-done.21
  45.4 0.9 %collective-permute-done.22 = bf16[2,64,256]{2,1,0:T(8,128)(2,1)S(1)} collective-permute-done((bf16[2,64,256]{2,1,0:T(8,128)(2,1)S(1)}, bf16[2,64,256]{2,1,0:T(8,128)(2,1)S(1)}, u32[]{:S(2)}, u32[]{:S(2)}) %collective-permute-start.22) | collective-permute-done | bytes 65568 | tf_op jit(solution)/shard_map/ppermute | solution.py:71
  46.3 0.0 collective-permute-done.23
  46.3 0.0 collective-permute-done.24
  46.3 0.1 collective-permute-start.25
  46.4 1.2 %shard_map.71.refs_4_ = f32[64,2048]{1,0:T(8,128)S(1)} custom-call(s32[8,32]{1,0:T(8,128)S(1)} %get-tuple-element.25.index_ref, bf16[64,2048]{1,0:T(8,128)(2,1)S(1)} %get-tuple-element.43.value_ref, bf16[2048,512]{1,0:T(8,128)(2,1)S(1)} %get-tuple-element.32.tile_ref.refs_4_.refs_3_), custom_call_target="tpu_custom_call" | custom-call | flops 67108864 | bytes 1048576 | tf_op jit(solution)/shard_map/pallas_call | solution.py:342
  47.6 0.5 collective-permute-done.25.refs_1_
  48.1 2.1 %shard_map.72 = bf16[64,2048]{1,0:T(8,128)(2,1)} custom-call(s32[8,32]{1,0:T(8,128)S(1)} %get-tuple-element.25.index_ref, bf16[11,64,256]{2,1,0:T(8,128)(2,1)S(1)} %constant_dynamic-update-slice_fusion.12.refs_0_, bf16[11,64,256]{2,1,0:T(8,128)(2,1)S(1)} %collective-permute-done.25.refs_1_, bf16[2,64,256]{2,1,0:T(8,128)(2,1)S(1)} %add_convert_fusion.refs_2_, ...), custom_call_target="tpu_custom_call" | custom-call | flops 67108864 | bytes 1048576 | tf_op jit(solution)/shard_map/pallas_call | solution.py:342
  (23 shorter events, 0.2 us)
Async XLA Ops:
  0.0 16.9 %copy-start = (bf16[64,1,1,2048]{3,0,2,1:T(8,128)(2,1)S(1)}, bf16[64,1,1,2048]{3,0,2,1:T(8,128)(2,1)}, u32[]{:S(2)}) copy-start(bf16[64,1,1,2048]{3,0,2,1:T(8,128)(2,1)} %param.6) | copy-start | bytes 786436
  0.8 1.3 %collective-permute-start = (bf16[64,256]{1,0:T(8,128)(2,1)S(1)}, bf16[64,256]{1,0:T(8,128)(2,1)S(1)}, u32[]{:S(2)}, u32[]{:S(2)}) collective-permute-start(bf16[64,256]{1,0:T(8,128)(2,1)S(1)} %get-tuple-element.46), channel_id=1, source_target_pairs={{0,1},{1,0},{2,3},{3,2},{4,5},{5,4},{6,7},{7,6},{8,9},{9,8},{10,11... | collective-permute-start | bytes 98312 | tf_op jit(solution)/shard_map/ppermute | solution.py:75
  2.2 6.0 %collective-permute-start.1 = (bf16[2,64,256]{2,1,0:T(8,128)(2,1)S(1)}, bf16[2,64,256]{2,1,0:T(8,128)(2,1)S(1)}, u32[]{:S(2)}, u32[]{:S(2)}) collective-permute-start(bf16[2,64,256]{2,1,0:T(8,128)(2,1)S(1)} %pad_maximum_fusion.both_ref.refs_3_), channel_id=1, source_target_pairs={{0,4},{1,3},{2,6},{3,1},{4,0},{5,9},{6,2},{7,11},{8,12},{9,5},{10,... | collective-permute-start | bytes 196616 | tf_op jit(solution)/shard_map/ppermute | solution.py:71
  5.1 11.3 %collective-permute-start.8 = (bf16[64,256]{1,0:T(8,128)(2,1)S(1)}, bf16[64,256]{1,0:T(8,128)(2,1)S(1)}, u32[]{:S(2)}, u32[]{:S(2)}) collective-permute-start(bf16[64,256]{1,0:T(8,128)(2,1)S(1)} %get-tuple-element.46), channel_id=1, source_target_pairs={{0,18},{1,19},{2,16},{3,17},{4,22},{5,23},{6,20},{7,21},{8,26},{9,... | collective-permute-start | bytes 98312 | tf_op jit(solution)/shard_map/ppermute | solution.py:71
  7.6 8.9 %collective-permute-start.7 = (bf16[2,64,256]{2,1,0:T(8,128)(2,1)S(1)}, bf16[2,64,256]{2,1,0:T(8,128)(2,1)S(1)}, u32[]{:S(2)}, u32[]{:S(2)}) collective-permute-start(bf16[2,64,256]{2,1,0:T(8,128)(2,1)S(1)} %pad_maximum_fusion.both_ref.refs_3_), channel_id=1, source_target_pairs={{0,2},{1,17},{2,0},{3,19},{4,6},{5,21},{6,4},{7,23},{8,10},{9,25},... | collective-permute-start | bytes 196616 | tf_op jit(solution)/shard_map/ppermute | solution.py:71
  8.1 5.2 %collective-permute-start.2 = (bf16[2,64,256]{2,1,0:T(8,128)(2,1)S(1)}, bf16[2,64,256]{2,1,0:T(8,128)(2,1)S(1)}, u32[]{:S(2)}, u32[]{:S(2)}) collective-permute-start(bf16[2,64,256]{2,1,0:T(8,128)(2,1)S(1)} %collective-permute-done.1), channel_id=1, source_target_pairs={{0,18},{1,19},{2,16},{3,17},{4,22},{5,23},{6,20},{7,21},{8,26},{9,... | collective-permute-start | bytes 196616 | tf_op jit(solution)/shard_map/ppermute | solution.py:71
  10.3 4.8 %collective-permute-start.5 = (bf16[2,64,256]{2,1,0:T(8,128)(2,1)S(1)}, bf16[2,64,256]{2,1,0:T(8,128)(2,1)S(1)}, u32[]{:S(2)}, u32[]{:S(2)}) collective-permute-start(bf16[2,64,256]{2,1,0:T(8,128)(2,1)S(1)} %collective-permute-done.1), channel_id=1, source_target_pairs={{0,2},{1,3},{2,0},{3,1},{4,6},{5,7},{6,4},{7,5},{8,10},{9,11},{10,... | collective-permute-start | bytes 196616 | tf_op jit(solution)/shard_map/ppermute | solution.py:71
  10.8 4.8 %collective-permute-start.6 = (bf16[2,64,256]{2,1,0:T(8,128)(2,1)S(1)}, bf16[2,64,256]{2,1,0:T(8,128)(2,1)S(1)}, u32[]{:S(2)}, u32[]{:S(2)}) collective-permute-start(bf16[2,64,256]{2,1,0:T(8,128)(2,1)S(1)} %collective-permute-done.1), channel_id=1, source_target_pairs={{0,16},{1,17},{2,18},{3,19},{4,20},{5,21},{6,22},{7,23},{8,24},{9,... | collective-permute-start | bytes 196616 | tf_op jit(solution)/shard_map/ppermute | solution.py:71
  15.0 1.4 %collective-permute-start.3 = (bf16[256,256]{1,0:T(8,128)(2,1)S(1)}, bf16[256,256]{1,0:T(8,128)(2,1)S(1)}, u32[]{:S(2)}, u32[]{:S(2)}) collective-permute-start(bf16[256,256]{1,0:T(8,128)(2,1)S(1)} %get-tuple-element.28), channel_id=1, source_target_pairs={{0,1},{1,0},{2,3},{3,2},{4,5},{5,4},{6,7},{7,6},{8,9},{9,8},{10,11... | collective-permute-start | bytes 393224 | tf_op jit(solution)/shard_map/ppermute | solution.py:75
  15.1 1.3 %collective-permute-start.4 = (s32[8,32]{1,0:T(8,128)S(1)}, s32[8,32]{1,0:T(8,128)S(1)}, u32[]{:S(2)}, u32[]{:S(2)}) collective-permute-start(s32[8,32]{1,0:T(8,128)S(1)} %get-tuple-element.29), channel_id=1, source_target_pairs={{0,1},{1,0},{2,3},{3,2},{4,5},{5,4},{6,7},{7,6},{8,9},{9,8},{10,11... | collective-permute-start | bytes 3080 | tf_op jit(solution)/shard_map/ppermute | solution.py:75
  16.5 3.1 %collective-permute-start.10 = (bf16[11,64,256]{2,1,0:T(8,128)(2,1)S(1)}, bf16[11,64,256]{2,1,0:T(8,128)(2,1)S(1)}, u32[]{:S(2)}, u32[]{:S(2)}) collective-permute-start(bf16[11,64,256]{2,1,0:T(8,128)(2,1)S(1)} %constant_dynamic-update-slice_fusion.received_ref.refs_1_), channel_id=1, source_target_pairs={{0,1},{1,0},{2,3},{3,2},{4,5},{5,4},{6,7},{7,6},{8,9},{9,8},{10,11... | collective-permute-start | bytes 1081352 | tf_op jit(solution)/shard_map/ppermute | solution.py:75
  18.1 1.5 %collective-permute-start.9 = (f32[2,64,256]{2,1,0:T(8,128)S(1)}, f32[2,64,256]{2,1,0:T(8,128)S(1)}, u32[]{:S(2)}, u32[]{:S(2)}) collective-permute-start(f32[2,64,256]{2,1,0:T(8,128)S(1)} %shard_map.65), channel_id=1, source_target_pairs={{0,1},{1,0},{2,3},{3,2},{4,5},{5,4},{6,7},{7,6},{8,9},{9,8},{10,11... | collective-permute-start | bytes 393224 | tf_op jit(solution)/shard_map/ppermute | solution.py:75
  19.6 4.3 %collective-permute-start.11 = (bf16[2,64,256]{2,1,0:T(8,128)(2,1)S(1)}, bf16[2,64,256]{2,1,0:T(8,128)(2,1)S(1)}, u32[]{:S(2)}, u32[]{:S(2)}) collective-permute-start(bf16[2,64,256]{2,1,0:T(8,128)(2,1)S(1)} %add_convert_fusion.1.both_ref.refs_3_), channel_id=1, source_target_pairs={{0,4},{1,3},{2,6},{3,1},{4,0},{5,9},{6,2},{7,11},{8,12},{9,5},{10,... | collective-permute-start | bytes 196616 | tf_op jit(solution)/shard_map/ppermute | solution.py:71
  21.0 10.8 %collective-permute-start.15 = (bf16[2,64,256]{2,1,0:T(8,128)(2,1)S(1)}, bf16[2,64,256]{2,1,0:T(8,128)(2,1)S(1)}, u32[]{:S(2)}, u32[]{:S(2)}) collective-permute-start(bf16[2,64,256]{2,1,0:T(8,128)(2,1)S(1)} %add_convert_fusion.1.both_ref.refs_3_), channel_id=1, source_target_pairs={{0,2},{1,17},{2,0},{3,19},{4,6},{5,21},{6,4},{7,23},{8,10},{9,25},... | collective-permute-start | bytes 196616 | tf_op jit(solution)/shard_map/ppermute | solution.py:71
  22.5 9.3 %collective-permute-start.16 = (bf16[64,256]{1,0:T(8,128)(2,1)S(1)}, bf16[64,256]{1,0:T(8,128)(2,1)S(1)}, u32[]{:S(2)}, u32[]{:S(2)}) collective-permute-start(bf16[64,256]{1,0:T(8,128)(2,1)S(1)} %slice_bitcast_fusion.1), channel_id=1, source_target_pairs={{0,18},{1,19},{2,16},{3,17},{4,22},{5,23},{6,20},{7,21},{8,26},{9,... | collective-permute-start | bytes 98312 | tf_op jit(solution)/shard_map/ppermute | solution.py:71
  23.9 4.3 %collective-permute-start.12 = (bf16[2,64,256]{2,1,0:T(8,128)(2,1)S(1)}, bf16[2,64,256]{2,1,0:T(8,128)(2,1)S(1)}, u32[]{:S(2)}, u32[]{:S(2)}) collective-permute-start(bf16[2,64,256]{2,1,0:T(8,128)(2,1)S(1)} %collective-permute-done.11), channel_id=1, source_target_pairs={{0,2},{1,3},{2,0},{3,1},{4,6},{5,7},{6,4},{7,5},{8,10},{9,11},{10,... | collective-permute-start | bytes 196616 | tf_op jit(solution)/shard_map/ppermute | solution.py:71
  25.4 5.0 %collective-permute-start.13 = (bf16[2,64,256]{2,1,0:T(8,128)(2,1)S(1)}, bf16[2,64,256]{2,1,0:T(8,128)(2,1)S(1)}, u32[]{:S(2)}, u32[]{:S(2)}) collective-permute-start(bf16[2,64,256]{2,1,0:T(8,128)(2,1)S(1)} %collective-permute-done.11), channel_id=1, source_target_pairs={{0,16},{1,17},{2,18},{3,19},{4,20},{5,21},{6,22},{7,23},{8,24},{9,... | collective-permute-start | bytes 196616 | tf_op jit(solution)/shard_map/ppermute | solution.py:71
  26.6 5.2 %collective-permute-start.14 = (bf16[2,64,256]{2,1,0:T(8,128)(2,1)S(1)}, bf16[2,64,256]{2,1,0:T(8,128)(2,1)S(1)}, u32[]{:S(2)}, u32[]{:S(2)}) collective-permute-start(bf16[2,64,256]{2,1,0:T(8,128)(2,1)S(1)} %collective-permute-done.11), channel_id=1, source_target_pairs={{0,18},{1,19},{2,16},{3,17},{4,22},{5,23},{6,20},{7,21},{8,26},{9,... | collective-permute-start | bytes 196616 | tf_op jit(solution)/shard_map/ppermute | solution.py:71
  31.9 3.1 %collective-permute-start.18 = (bf16[11,64,256]{2,1,0:T(8,128)(2,1)S(1)}, bf16[11,64,256]{2,1,0:T(8,128)(2,1)S(1)}, u32[]{:S(2)}, u32[]{:S(2)}) collective-permute-start(bf16[11,64,256]{2,1,0:T(8,128)(2,1)S(1)} %constant_dynamic-update-slice_fusion.6.received_ref.refs_1_), channel_id=1, source_target_pairs={{0,1},{1,0},{2,3},{3,2},{4,5},{5,4},{6,7},{7,6},{8,9},{9,8},{10,11... | collective-permute-start | bytes 1081352 | tf_op jit(solution)/shard_map/ppermute | solution.py:75
  33.2 1.8 %collective-permute-start.17 = (f32[2,64,256]{2,1,0:T(8,128)S(1)}, f32[2,64,256]{2,1,0:T(8,128)S(1)}, u32[]{:S(2)}, u32[]{:S(2)}) collective-permute-start(f32[2,64,256]{2,1,0:T(8,128)S(1)} %shard_map.68), channel_id=1, source_target_pairs={{0,1},{1,0},{2,3},{3,2},{4,5},{5,4},{6,7},{7,6},{8,9},{9,8},{10,11... | collective-permute-start | bytes 393224 | tf_op jit(solution)/shard_map/ppermute | solution.py:75
  35.0 4.3 %collective-permute-start.19 = (bf16[2,64,256]{2,1,0:T(8,128)(2,1)S(1)}, bf16[2,64,256]{2,1,0:T(8,128)(2,1)S(1)}, u32[]{:S(2)}, u32[]{:S(2)}) collective-permute-start(bf16[2,64,256]{2,1,0:T(8,128)(2,1)S(1)} %add_convert_fusion.refs_2_), channel_id=1, source_target_pairs={{0,4},{1,3},{2,6},{3,1},{4,0},{5,9},{6,2},{7,11},{8,12},{9,5},{10,... | collective-permute-start | bytes 196616 | tf_op jit(solution)/shard_map/ppermute | solution.py:71
  36.6 9.7 %collective-permute-start.23 = (bf16[2,64,256]{2,1,0:T(8,128)(2,1)S(1)}, bf16[2,64,256]{2,1,0:T(8,128)(2,1)S(1)}, u32[]{:S(2)}, u32[]{:S(2)}) collective-permute-start(bf16[2,64,256]{2,1,0:T(8,128)(2,1)S(1)} %add_convert_fusion.refs_2_), channel_id=1, source_target_pairs={{0,2},{1,17},{2,0},{3,19},{4,6},{5,21},{6,4},{7,23},{8,10},{9,25},... | collective-permute-start | bytes 196616 | tf_op jit(solution)/shard_map/ppermute | solution.py:71
  37.1 9.2 %collective-permute-start.24 = (bf16[64,256]{1,0:T(8,128)(2,1)S(1)}, bf16[64,256]{1,0:T(8,128)(2,1)S(1)}, u32[]{:S(2)}, u32[]{:S(2)}) collective-permute-start(bf16[64,256]{1,0:T(8,128)(2,1)S(1)} %slice_bitcast_fusion), channel_id=1, source_target_pairs={{0,18},{1,19},{2,16},{3,17},{4,22},{5,23},{6,20},{7,21},{8,26},{9,... | collective-permute-start | bytes 98312 | tf_op jit(solution)/shard_map/ppermute | solution.py:71
  39.3 4.6 %collective-permute-start.20 = (bf16[2,64,256]{2,1,0:T(8,128)(2,1)S(1)}, bf16[2,64,256]{2,1,0:T(8,128)(2,1)S(1)}, u32[]{:S(2)}, u32[]{:S(2)}) collective-permute-start(bf16[2,64,256]{2,1,0:T(8,128)(2,1)S(1)} %collective-permute-done.19), channel_id=1, source_target_pairs={{0,2},{1,3},{2,0},{3,1},{4,6},{5,7},{6,4},{7,5},{8,10},{9,11},{10,... | collective-permute-start | bytes 196616 | tf_op jit(solution)/shard_map/ppermute | solution.py:71
  40.0 5.3 %collective-permute-start.21 = (bf16[2,64,256]{2,1,0:T(8,128)(2,1)S(1)}, bf16[2,64,256]{2,1,0:T(8,128)(2,1)S(1)}, u32[]{:S(2)}, u32[]{:S(2)}) collective-permute-start(bf16[2,64,256]{2,1,0:T(8,128)(2,1)S(1)} %collective-permute-done.19), channel_id=1, source_target_pairs={{0,16},{1,17},{2,18},{3,19},{4,20},{5,21},{6,22},{7,23},{8,24},{9,... | collective-permute-start | bytes 196616 | tf_op jit(solution)/shard_map/ppermute | solution.py:71
  41.1 5.2 %collective-permute-start.22 = (bf16[2,64,256]{2,1,0:T(8,128)(2,1)S(1)}, bf16[2,64,256]{2,1,0:T(8,128)(2,1)S(1)}, u32[]{:S(2)}, u32[]{:S(2)}) collective-permute-start(bf16[2,64,256]{2,1,0:T(8,128)(2,1)S(1)} %collective-permute-done.19), channel_id=1, source_target_pairs={{0,18},{1,19},{2,16},{3,17},{4,22},{5,23},{6,20},{7,21},{8,26},{9,... | collective-permute-start | bytes 196616 | tf_op jit(solution)/shard_map/ppermute | solution.py:71
  46.3 1.7 %collective-permute-start.25 = (bf16[11,64,256]{2,1,0:T(8,128)(2,1)S(1)}, bf16[11,64,256]{2,1,0:T(8,128)(2,1)S(1)}, u32[]{:S(2)}, u32[]{:S(2)}) collective-permute-start(bf16[11,64,256]{2,1,0:T(8,128)(2,1)S(1)} %constant_dynamic-update-slice_fusion.12.refs_0_), channel_id=1, source_target_pairs={{0,1},{1,0},{2,3},{3,2},{4,5},{5,4},{6,7},{7,6},{8,9},{9,8},{10,11... | collective-permute-start | bytes 1081352 | tf_op jit(solution)/shard_map/ppermute | solution.py:75
